TPU v7x, 128 devices: a whole 4x4x4 slice. The times are simulated.
128 devices in a mesh: section: 4 (over z), dom: 32 (over y, x, core).
Axes of the slice: x: 4, y: 4, z: 4, core: 2. Of those that a mesh axis runs over, the one named last changes fastest.
Arguments:
- features: bfloat16 [8, 32768, 256], P(None, 'dom'), may hold values from -6 to 6
- tile_src: int32 [8, 256, 4], P(None, 'dom'), may hold values from 0 to 11
- tile_val: bfloat16 [8, 32768, 512], P(None, 'dom'), may hold values from -0.25 to 0.25
- boundary_rows: int32 [8, 64, 256], P(None, 'dom'), may hold values from 0 to 1023
- boundary_count: int32 [8, 64], P(None, 'dom'), may hold values from 64 to 256, as said below
- weights: bfloat16 [8, 256, 256], P('section'), may hold values from -0.375 to 0.375
- gains: bfloat16 [8, 256], P('section'), may hold values from 0.099609375 to 1.8984375
Outputs:
- output: bfloat16 [8, 32768, 256], P('section', 'dom')
Inputs may be any that keep to these rules, and one draw needn't show every extreme that they name: `boundary_count`: each micro-batch graph has a buffer with all 256 slots live.
All inputs are finite; a program needn't handle non-finite values.
Results may differ from a plain program's by a relative error of at most 0.019.
Values may be sent and summed in bfloat16 or wider, within the bound.
No kernel may reach another device: no remote copies, remote signals or barrier semaphores. Data moves between devices by JAX's collectives and lax.ppermute only.
A program may use at most 128 MiB of HBM per device.

v0:
```python
import functools

import jax
import jax.numpy as jnp
from jax import lax
from jax.experimental import pallas as pl
from jax.experimental.pallas import tpu as pltpu
from jax.sharding import PartitionSpec as P

TILE = 128
K = 4
EPS = 1e-06
BF = jnp.bfloat16
F32 = jnp.float32
VMEM = pl.BlockSpec(memory_space=pltpu.VMEM)
SMEM = pl.BlockSpec(memory_space=pltpu.SMEM)
HBM = pl.BlockSpec(memory_space=pltpu.HBM)


def call(body, outs, in_specs, name, scratch=(), limit=8, flops=0):
    return pl.pallas_call(
        body,
        out_shape=[jax.ShapeDtypeStruct(s, BF) for s in outs],
        in_specs=in_specs,
        out_specs=[VMEM] * len(outs),
        scratch_shapes=list(scratch),
        name=name,
        cost_estimate=pl.CostEstimate(flops=flops, bytes_accessed=1 << 20, transcendentals=0),
        compiler_params=pltpu.CompilerParams(vmem_limit_bytes=limit << 20),
    )


def normalise(hidden):
    mean = jnp.mean(hidden * hidden, axis=-1, keepdims=True)
    return jnp.maximum(hidden * lax.rsqrt(mean + EPS), 0.0).astype(BF)


def send_rows(chooser_ref, normed_ref, on_ref, off_ref):
    bnd = on_ref.shape[0]
    for at, out in ((bnd, off_ref), (0, on_ref)):
        out[...] = jnp.dot(
            chooser_ref[at : at + bnd, :], normed_ref[...], preferred_element_type=F32
        ).astype(BF)


def prologue_body(info_ref, count_ref, rows_ref, feat_ref, h_ref, nrm_ref, sel_ref, on_ref, off_ref, sem):
    graph, parity = info_ref[0], info_ref[1]
    copy = pltpu.make_async_copy(feat_ref.at[graph], h_ref, sem)
    copy.start()
    bnd = on_ref.shape[0]
    lane = lax.broadcasted_iota(jnp.int32, (1, bnd), 1)
    for at, buf in ((bnd, parity), (0, 1 - parity)):
        rows = rows_ref[graph, pl.ds(buf, 1), :]
        rows = jnp.where(lane < count_ref[buf, graph], rows, -1)
        column = jnp.broadcast_to(rows.astype(F32), (TILE, bnd)).T
        for c in range(sel_ref.shape[1] // TILE):
            ids = lax.broadcasted_iota(jnp.int32, (bnd, TILE), 1) + c * TILE
            hit = column == ids.astype(F32)
            sel_ref[at : at + bnd, c * TILE : (c + 1) * TILE] = jnp.where(hit, 1.0, 0.0).astype(BF)
    copy.wait()
    nrm_ref[...] = normalise(h_ref[...].astype(F32))
    send_rows(sel_ref, nrm_ref, on_ref, off_ref)


def fetch_body(info_ref, val_ref, tv_ref, sem):
    copy = pltpu.make_async_copy(val_ref.at[info_ref[0]], tv_ref, sem)
    copy.start()
    copy.wait()


def scale_body(w_ref, gain_ref, out_ref):
    width = w_ref.shape[1]
    gain = gain_ref[...].astype(F32)
    for k in range(w_ref.shape[0]):
        column = jnp.broadcast_to(gain[k : k + 1, :], (width, width)).T
        out_ref[k] = (w_ref[k].astype(F32) * column).astype(BF)


def order_body(count, info_ref, *refs):
    parts, out = refs[:count], refs[count]
    section = info_ref[2]
    per = parts[0].shape[0]
    for shift, part in enumerate(parts):
        source = lax.rem(section - shift + count, count)
        for k in range(per):
            out[source * per + k] = part[k]


def layer_body(layer, last, info_ref, src_ref, h_ref, nrm_ref, on_in, off_in, tv_ref, sel_ref, w_ref, *rest):
    if last:
        out_h, ext, agg = rest
    else:
        out_h, out_n, on_ref, off_ref, ext, agg = rest
    graph, parity = info_ref[0], info_ref[1]
    rows_dev = h_ref.shape[0]
    bnd = on_in.shape[0]
    own, half = rows_dev // TILE, bnd // TILE
    ext[0:own] = nrm_ref[...].reshape(own, TILE, -1)
    ext[own : own + half] = on_in[...].reshape(half, TILE, -1)
    ext[own + half : own + 2 * half] = off_in[...].reshape(half, TILE, -1)
    left = jnp.where(parity == 0, own + half, own)
    right = jnp.where(parity == 0, own, own + half)
    for i in range(own):
        picked = []
        for k in range(K):
            t = src_ref[graph, k, i]
            at = jnp.where(t < half, left + t, jnp.where(t < half + own, t - half, right + t - half - own))
            picked.append(ext[at])
        agg[i * TILE : (i + 1) * TILE, :] = jnp.dot(
            tv_ref[i * TILE : (i + 1) * TILE, :], jnp.concatenate(picked, axis=0), preferred_element_type=F32
        ).astype(BF)
    step = 256
    for r in range(0, rows_dev, step):
        rows = slice(r, r + step)
        update = jnp.dot(agg[rows, :], w_ref[layer], preferred_element_type=F32)
        new = (h_ref[rows, :].astype(F32) + update).astype(BF)
        out_h[rows, :] = new
        if not last:
            out_n[rows, :] = normalise(new.astype(F32))
    if not last:
        send_rows(sel_ref, out_n, on_ref, off_ref)


def on_device(features, tile_src, tile_val, boundary_rows, boundary_count, weights, gains):
    sections = lax.axis_size("section")
    doms = lax.axis_size("dom")
    section_id = lax.axis_index("section")
    dom_id = lax.axis_index("dom")
    graphs, rows_dev, width = features.shape
    bnd = boundary_rows.shape[-1]
    per_section = graphs // sections
    layers = weights.shape[0] * sections
    on_pairs = [(i, i ^ 1) for i in range(doms)]
    off_pairs = [(i, (i + (1 if i % 2 else -1)) % doms) for i in range(doms)]
    infos = [
        jnp.stack([section_id * per_section + g, dom_id % 2, section_id]).astype(jnp.int32)
        for g in range(per_section)
    ]

    def exchange(on, off):
        return lax.ppermute(on, "dom", on_pairs), lax.ppermute(off, "dom", off_pairs)

    tile_src = jnp.swapaxes(tile_src, 1, 2)
    boundary_count = jnp.swapaxes(boundary_count, 0, 1)
    features, tile_val = (pltpu.with_memory_space_constraint(x, pltpu.HBM) for x in (features, tile_val))
    state = []
    for info in infos:
        result = call(
            prologue_body,
            [(rows_dev, width), (rows_dev, width), (2 * bnd, rows_dev), (bnd, width), (bnd, width)],
            [SMEM, SMEM, VMEM, HBM],
            "prologue",
            [pltpu.SemaphoreType.DMA],
        )(info, boundary_count, boundary_rows, features)
        weights, *result = lax.optimization_barrier((weights, *result))
        h, nrm, sel, on, off = result
        state.append([h, nrm, sel, *exchange(on, off)])
    scaled = call(scale_body, [weights.shape], [VMEM, VMEM], "scale")(weights, gains)[0]
    parts = [scaled] + [
        lax.ppermute(scaled, "section", [(i, (i + shift) % sections) for i in range(sections)])
        for shift in range(1, sections)
    ]
    values = [
        call(fetch_body, [(rows_dev, K * TILE)], [SMEM, HBM], "fetch", [pltpu.SemaphoreType.DMA])(info, tile_val)[0]
        for info in infos
    ]
    w_all = call(
        functools.partial(order_body, sections), [(layers, width, width)], [SMEM] + [VMEM] * sections, "order"
    )(infos[0], *parts)[0]
    outputs = [None] * per_section
    for layer in range(layers):
        last = layer == layers - 1
        for g, info in enumerate(infos):
            h, nrm, sel, on, off = state[g]
            outs = [(rows_dev, width)]
            if not last:
                outs += [(rows_dev, width), (bnd, width), (bnd, width)]
            result = call(
                functools.partial(layer_body, layer, last),
                outs,
                [SMEM, SMEM] + [VMEM] * 7,
                "layer",
                [
                    pltpu.VMEM(((rows_dev + 2 * bnd) // TILE, TILE, width), BF),
                    pltpu.VMEM((rows_dev, width), BF),
                ],
                flops=700_000_000,
            )(info, tile_src, h, nrm, on, off, values[g], sel, w_all)
            if last:
                outputs[g] = result[0]
            else:
                h, nrm, on, off = result
                state[g] = [h, nrm, sel, *exchange(on, off)]
    return jnp.stack(outputs, axis=0)


def solution(mesh):
    in_specs = (
        P(None, "dom", None),
        P(None, "dom", None),
        P(None, "dom", None),
        P(None, "dom", None),
        P(None, "dom"),
        P("section", None, None),
        P("section", None),
    )
    return jax.shard_map(
        on_device, mesh=mesh, in_specs=in_specs, out_specs=P("section", "dom", None), check_vma=False
    )
```

profile of v0, /device:TPU:0, one launch (start us, length us, event | category | flops | bytes accessed | tf_op | source)
XLA Modules:
  0.0 107.3 jit_solution(11759799338756139963)
XLA Ops:
  0.1 0.7 copy-done.2
  0.8 0.7 copy-done.3
  1.5 2.2 %prologue.2 = (bf16[1024,256]{1,0:T(8,128)(2,1)S(1)}, bf16[1024,256]{1,0:T(8,128)(2,1)S(1)}, bf16[512,1024]{1,0:T(8,128)(2,1)S(1)}, bf16[256,256]{1,0:T(8,128)(2,1)S(1)}, bf16[256,256]{1,0:T(8,128)(2,1)S(1)}) custom-call(s32[3]{0:T(128)S(1)} %get-tuple-element.161.info_ref, s32[2,8]{1,0:T(2,128)S(1)} %bitcast.26, s32[8,2,256]{2,1,0:T(2,128)S(1)} %copy-done.2, ...), custom_call_target="tpu_custom_call" | custom-call | bytes 1048576 | tf_op jit(solution)/shard_map/prologue/pallas_call | solution.py:148
  3.7 2.2 %prologue.3 = (bf16[1024,256]{1,0:T(8,128)(2,1)S(1)}, bf16[1024,256]{1,0:T(8,128)(2,1)S(1)}, bf16[512,1024]{1,0:T(8,128)(2,1)S(1)}, bf16[256,256]{1,0:T(8,128)(2,1)S(1)}, bf16[256,256]{1,0:T(8,128)(2,1)S(1)}) custom-call(s32[3]{0:T(128)S(1)} %get-tuple-element.162.info_ref, s32[2,8]{1,0:T(2,128)S(1)} %bitcast.27, s32[8,2,256]{2,1,0:T(2,128)S(1)} %copy-done.2, ...), custom_call_target="tpu_custom_call" | custom-call | bytes 1048576 | tf_op jit(solution)/shard_map/prologue/pallas_call | solution.py:148
  5.9 0.1 scale.1.refs_0_
  6.0 2.1 %collective-permute-start.2 = (bf16[2,256,256]{2,1,0:T(8,128)(2,1)S(1)}, bf16[2,256,256]{2,1,0:T(8,128)(2,1)S(1)}, u32[]{:S(2)}, u32[]{:S(2)}) collective-permute-start(bf16[2,256,256]{2,1,0:T(8,128)(2,1)S(1)} %scale.1.refs_0_), channel_id=1, source_target_pairs={{0,32},{32,64},{64,96},{96,0},{1,33},{33,65},{65,97},{97,1},{2,34}... | collective-permute-start | bytes 786440 | tf_op jit(solution)/shard_map/ppermute | solution.py:160
  8.1 3.6 %collective-permute-start.3 = (bf16[2,256,256]{2,1,0:T(8,128)(2,1)S(1)}, bf16[2,256,256]{2,1,0:T(8,128)(2,1)S(1)}, u32[]{:S(2)}, u32[]{:S(2)}) collective-permute-start(bf16[2,256,256]{2,1,0:T(8,128)(2,1)S(1)} %scale.1.refs_0_), channel_id=1, source_target_pairs={{0,64},{32,96},{64,0},{96,32},{1,65},{33,97},{65,1},{97,33},{2,66}... | collective-permute-start | bytes 786440 | tf_op jit(solution)/shard_map/ppermute | solution.py:160
  11.7 1.0 collective-permute-start.4
  12.7 5.3 %collective-permute-start.1 = (bf16[256,256]{1,0:T(8,128)(2,1)S(1)}, bf16[256,256]{1,0:T(8,128)(2,1)S(1)}, u32[]{:S(2)}, u32[]{:S(2)}) collective-permute-start(bf16[256,256]{1,0:T(8,128)(2,1)S(1)} %get-tuple-element.91), channel_id=1, source_target_pairs={{0,31},{1,2},{2,1},{3,4},{4,3},{5,6},{6,5},{7,8},{8,7},{9,10},{10,... | collective-permute-start | bytes 393224 | tf_op jit(solution)/shard_map/ppermute | solution.py:141
  18.0 5.3 %collective-permute-done.3.refs_2_ = bf16[2,256,256]{2,1,0:T(8,128)(2,1)S(1)} collective-permute-done((bf16[2,256,256]{2,1,0:T(8,128)(2,1)S(1)}, bf16[2,256,256]{2,1,0:T(8,128)(2,1)S(1)}, u32[]{:S(2)}, u32[]{:S(2)}) %collective-permute-start.3) | collective-permute-done | bytes 262176 | tf_op jit(solution)/shard_map/ppermute | solution.py:160
  23.3 3.8 %collective-permute-start.20 = (bf16[256,256]{1,0:T(8,128)(2,1)S(1)}, bf16[256,256]{1,0:T(8,128)(2,1)S(1)}, u32[]{:S(2)}, u32[]{:S(2)}) collective-permute-start(bf16[256,256]{1,0:T(8,128)(2,1)S(1)} %get-tuple-element.131), channel_id=1, source_target_pairs={{0,31},{1,2},{2,1},{3,4},{4,3},{5,6},{6,5},{7,8},{8,7},{9,10},{10,... | collective-permute-start | bytes 393224 | tf_op jit(solution)/shard_map/ppermute | solution.py:141
  27.1 1.8 %fetch.2.tv_ref = bf16[1024,512]{1,0:T(8,128)(2,1)S(1)} custom-call(s32[3]{0:T(128)S(1)} %get-tuple-element.161.info_ref, bf16[8,1024,512]{2,1,0:T(8,128)(2,1)} %val_ref.3), custom_call_target="tpu_custom_call" | custom-call | bytes 1048576 | tf_op jit(solution)/shard_map/fetch/pallas_call | solution.py:164
  28.9 1.8 %fetch.3.tv_ref = bf16[1024,512]{1,0:T(8,128)(2,1)S(1)} custom-call(s32[3]{0:T(128)S(1)} %get-tuple-element.162.info_ref, bf16[8,1024,512]{2,1,0:T(8,128)(2,1)} %val_ref.3), custom_call_target="tpu_custom_call" | custom-call | bytes 1048576 | tf_op jit(solution)/shard_map/fetch/pallas_call | solution.py:164
  30.7 0.6 order.1.w_ref
  31.3 2.0 %layer.16 = (bf16[1024,256]{1,0:T(8,128)(2,1)S(1)}, bf16[1024,256]{1,0:T(8,128)(2,1)S(1)}, bf16[256,256]{1,0:T(8,128)(2,1)S(1)}, bf16[256,256]{1,0:T(8,128)(2,1)S(1)}) custom-call(s32[3]{0:T(128)S(1)} %get-tuple-element.161.info_ref, s32[8,4,8]{2,1,0:T(4,128)S(1)} %bitcast.8, bf16[1024,256]{1,0:T(8,128)(2,1)S(1)} %get-tuple-element.88.h_ref, ...), custom_call_target="tpu_custom_call" | custom-call | flops 700000000 | bytes 1048576 | tf_op jit(solution)/shard_map/layer/pallas_call | solution.py:178
  33.3 0.1 collective-permute-start.5
  33.4 1.5 %collective-permute-start.6 = (bf16[256,256]{1,0:T(8,128)(2,1)S(1)}, bf16[256,256]{1,0:T(8,128)(2,1)S(1)}, u32[]{:S(2)}, u32[]{:S(2)}) collective-permute-start(bf16[256,256]{1,0:T(8,128)(2,1)S(1)} %get-tuple-element.103), channel_id=1, source_target_pairs={{0,31},{1,2},{2,1},{3,4},{4,3},{5,6},{6,5},{7,8},{8,7},{9,10},{10,... | collective-permute-start | bytes 393224 | tf_op jit(solution)/shard_map/ppermute | solution.py:141
  35.0 2.0 %layer.24 = (bf16[1024,256]{1,0:T(8,128)(2,1)S(1)}, bf16[1024,256]{1,0:T(8,128)(2,1)S(1)}, bf16[256,256]{1,0:T(8,128)(2,1)S(1)}, bf16[256,256]{1,0:T(8,128)(2,1)S(1)}) custom-call(s32[3]{0:T(128)S(1)} %get-tuple-element.162.info_ref, s32[8,4,8]{2,1,0:T(4,128)S(1)} %bitcast.9, bf16[1024,256]{1,0:T(8,128)(2,1)S(1)} %get-tuple-element.128.h_ref, ...), custom_call_target="tpu_custom_call" | custom-call | flops 700000000 | bytes 1048576 | tf_op jit(solution)/shard_map/layer/pallas_call | solution.py:178
  37.0 0.1 collective-permute-start.21
  37.1 3.7 %collective-permute-start.22 = (bf16[256,256]{1,0:T(8,128)(2,1)S(1)}, bf16[256,256]{1,0:T(8,128)(2,1)S(1)}, u32[]{:S(2)}, u32[]{:S(2)}) collective-permute-start(bf16[256,256]{1,0:T(8,128)(2,1)S(1)} %get-tuple-element.136), channel_id=1, source_target_pairs={{0,31},{1,2},{2,1},{3,4},{4,3},{5,6},{6,5},{7,8},{8,7},{9,10},{10,... | collective-permute-start | bytes 393224 | tf_op jit(solution)/shard_map/ppermute | solution.py:141
  40.8 0.5 collective-permute-done.6.off_in
  41.2 2.0 %layer.17 = (bf16[1024,256]{1,0:T(8,128)(2,1)S(1)}, bf16[1024,256]{1,0:T(8,128)(2,1)S(1)}, bf16[256,256]{1,0:T(8,128)(2,1)S(1)}, bf16[256,256]{1,0:T(8,128)(2,1)S(1)}) custom-call(s32[3]{0:T(128)S(1)} %get-tuple-element.161.info_ref, s32[8,4,8]{2,1,0:T(4,128)S(1)} %bitcast.10, bf16[1024,256]{1,0:T(8,128)(2,1)S(1)} %get-tuple-element.100.h_ref, ...), custom_call_target="tpu_custom_call" | custom-call | flops 700000000 | bytes 1048576 | tf_op jit(solution)/shard_map/layer/pallas_call | solution.py:178
  43.2 0.1 collective-permute-start.7
  43.3 1.5 %collective-permute-start.8 = (bf16[256,256]{1,0:T(8,128)(2,1)S(1)}, bf16[256,256]{1,0:T(8,128)(2,1)S(1)}, u32[]{:S(2)}, u32[]{:S(2)}) collective-permute-start(bf16[256,256]{1,0:T(8,128)(2,1)S(1)} %get-tuple-element.107), channel_id=1, source_target_pairs={{0,31},{1,2},{2,1},{3,4},{4,3},{5,6},{6,5},{7,8},{8,7},{9,10},{10,... | collective-permute-start | bytes 393224 | tf_op jit(solution)/shard_map/ppermute | solution.py:141
  44.9 2.0 %layer.25 = (bf16[1024,256]{1,0:T(8,128)(2,1)S(1)}, bf16[1024,256]{1,0:T(8,128)(2,1)S(1)}, bf16[256,256]{1,0:T(8,128)(2,1)S(1)}, bf16[256,256]{1,0:T(8,128)(2,1)S(1)}) custom-call(s32[3]{0:T(128)S(1)} %get-tuple-element.162.info_ref, s32[8,4,8]{2,1,0:T(4,128)S(1)} %bitcast.11, bf16[1024,256]{1,0:T(8,128)(2,1)S(1)} %get-tuple-element.133.h_ref, ...), custom_call_target="tpu_custom_call" | custom-call | flops 700000000 | bytes 1048576 | tf_op jit(solution)/shard_map/layer/pallas_call | solution.py:178
  46.9 0.1 collective-permute-start.23
  47.0 3.7 %collective-permute-start.24 = (bf16[256,256]{1,0:T(8,128)(2,1)S(1)}, bf16[256,256]{1,0:T(8,128)(2,1)S(1)}, u32[]{:S(2)}, u32[]{:S(2)}) collective-permute-start(bf16[256,256]{1,0:T(8,128)(2,1)S(1)} %get-tuple-element.140), channel_id=1, source_target_pairs={{0,31},{1,2},{2,1},{3,4},{4,3},{5,6},{6,5},{7,8},{8,7},{9,10},{10,... | collective-permute-start | bytes 393224 | tf_op jit(solution)/shard_map/ppermute | solution.py:141
  50.6 0.5 collective-permute-done.8.off_in
  51.1 2.0 %layer.18 = (bf16[1024,256]{1,0:T(8,128)(2,1)S(1)}, bf16[1024,256]{1,0:T(8,128)(2,1)S(1)}, bf16[256,256]{1,0:T(8,128)(2,1)S(1)}, bf16[256,256]{1,0:T(8,128)(2,1)S(1)}) custom-call(s32[3]{0:T(128)S(1)} %get-tuple-element.161.info_ref, s32[8,4,8]{2,1,0:T(4,128)S(1)} %bitcast.12, bf16[1024,256]{1,0:T(8,128)(2,1)S(1)} %get-tuple-element.104.h_ref, ...), custom_call_target="tpu_custom_call" | custom-call | flops 700000000 | bytes 1048576 | tf_op jit(solution)/shard_map/layer/pallas_call | solution.py:178
  53.1 1.6 %collective-permute-start.10 = (bf16[256,256]{1,0:T(8,128)(2,1)S(1)}, bf16[256,256]{1,0:T(8,128)(2,1)S(1)}, u32[]{:S(2)}, u32[]{:S(2)}) collective-permute-start(bf16[256,256]{1,0:T(8,128)(2,1)S(1)} %get-tuple-element.111), channel_id=1, source_target_pairs={{0,31},{1,2},{2,1},{3,4},{4,3},{5,6},{6,5},{7,8},{8,7},{9,10},{10,... | collective-permute-start | bytes 393224 | tf_op jit(solution)/shard_map/ppermute | solution.py:141
  54.7 0.1 collective-permute-done.24.off_in
  54.8 2.0 %layer.26 = (bf16[1024,256]{1,0:T(8,128)(2,1)S(1)}, bf16[1024,256]{1,0:T(8,128)(2,1)S(1)}, bf16[256,256]{1,0:T(8,128)(2,1)S(1)}, bf16[256,256]{1,0:T(8,128)(2,1)S(1)}) custom-call(s32[3]{0:T(128)S(1)} %get-tuple-element.162.info_ref, s32[8,4,8]{2,1,0:T(4,128)S(1)} %bitcast.13, bf16[1024,256]{1,0:T(8,128)(2,1)S(1)} %get-tuple-element.137.h_ref, ...), custom_call_target="tpu_custom_call" | custom-call | flops 700000000 | bytes 1048576 | tf_op jit(solution)/shard_map/layer/pallas_call | solution.py:178
  56.8 0.5 collective-permute-start.25
  57.3 3.6 %collective-permute-start.26 = (bf16[256,256]{1,0:T(8,128)(2,1)S(1)}, bf16[256,256]{1,0:T(8,128)(2,1)S(1)}, u32[]{:S(2)}, u32[]{:S(2)}) collective-permute-start(bf16[256,256]{1,0:T(8,128)(2,1)S(1)} %get-tuple-element.144), channel_id=1, source_target_pairs={{0,31},{1,2},{2,1},{3,4},{4,3},{5,6},{6,5},{7,8},{8,7},{9,10},{10,... | collective-permute-start | bytes 393224 | tf_op jit(solution)/shard_map/ppermute | solution.py:141
  60.9 2.0 %layer.19 = (bf16[1024,256]{1,0:T(8,128)(2,1)S(1)}, bf16[1024,256]{1,0:T(8,128)(2,1)S(1)}, bf16[256,256]{1,0:T(8,128)(2,1)S(1)}, bf16[256,256]{1,0:T(8,128)(2,1)S(1)}) custom-call(s32[3]{0:T(128)S(1)} %get-tuple-element.161.info_ref, s32[8,4,8]{2,1,0:T(4,128)S(1)} %bitcast.14, bf16[1024,256]{1,0:T(8,128)(2,1)S(1)} %get-tuple-element.108.h_ref, ...), custom_call_target="tpu_custom_call" | custom-call | flops 700000000 | bytes 1048576 | tf_op jit(solution)/shard_map/layer/pallas_call | solution.py:178
  62.9 0.1 collective-permute-start.11
  63.0 1.6 %collective-permute-start.12 = (bf16[256,256]{1,0:T(8,128)(2,1)S(1)}, bf16[256,256]{1,0:T(8,128)(2,1)S(1)}, u32[]{:S(2)}, u32[]{:S(2)}) collective-permute-start(bf16[256,256]{1,0:T(8,128)(2,1)S(1)} %get-tuple-element.115), channel_id=1, source_target_pairs={{0,31},{1,2},{2,1},{3,4},{4,3},{5,6},{6,5},{7,8},{8,7},{9,10},{10,... | collective-permute-start | bytes 393224 | tf_op jit(solution)/shard_map/ppermute | solution.py:141
  64.6 0.4 collective-permute-done.26.off_in
  65.0 2.0 %layer.27 = (bf16[1024,256]{1,0:T(8,128)(2,1)S(1)}, bf16[1024,256]{1,0:T(8,128)(2,1)S(1)}, bf16[256,256]{1,0:T(8,128)(2,1)S(1)}, bf16[256,256]{1,0:T(8,128)(2,1)S(1)}) custom-call(s32[3]{0:T(128)S(1)} %get-tuple-element.162.info_ref, s32[8,4,8]{2,1,0:T(4,128)S(1)} %bitcast.15, bf16[1024,256]{1,0:T(8,128)(2,1)S(1)} %get-tuple-element.141.h_ref, ...), custom_call_target="tpu_custom_call" | custom-call | flops 700000000 | bytes 1048576 | tf_op jit(solution)/shard_map/layer/pallas_call | solution.py:178
  67.0 0.1 collective-permute-start.27
  67.1 3.7 %collective-permute-start.28 = (bf16[256,256]{1,0:T(8,128)(2,1)S(1)}, bf16[256,256]{1,0:T(8,128)(2,1)S(1)}, u32[]{:S(2)}, u32[]{:S(2)}) collective-permute-start(bf16[256,256]{1,0:T(8,128)(2,1)S(1)} %get-tuple-element.148), channel_id=1, source_target_pairs={{0,31},{1,2},{2,1},{3,4},{4,3},{5,6},{6,5},{7,8},{8,7},{9,10},{10,... | collective-permute-start | bytes 393224 | tf_op jit(solution)/shard_map/ppermute | solution.py:141
  70.8 2.0 %layer.20 = (bf16[1024,256]{1,0:T(8,128)(2,1)S(1)}, bf16[1024,256]{1,0:T(8,128)(2,1)S(1)}, bf16[256,256]{1,0:T(8,128)(2,1)S(1)}, bf16[256,256]{1,0:T(8,128)(2,1)S(1)}) custom-call(s32[3]{0:T(128)S(1)} %get-tuple-element.161.info_ref, s32[8,4,8]{2,1,0:T(4,128)S(1)} %bitcast.16, bf16[1024,256]{1,0:T(8,128)(2,1)S(1)} %get-tuple-element.112.h_ref, ...), custom_call_target="tpu_custom_call" | custom-call | flops 700000000 | bytes 1048576 | tf_op jit(solution)/shard_map/layer/pallas_call | solution.py:178
  72.8 0.1 collective-permute-start.13
  72.9 1.6 %collective-permute-start.14 = (bf16[256,256]{1,0:T(8,128)(2,1)S(1)}, bf16[256,256]{1,0:T(8,128)(2,1)S(1)}, u32[]{:S(2)}, u32[]{:S(2)}) collective-permute-start(bf16[256,256]{1,0:T(8,128)(2,1)S(1)} %get-tuple-element.119), channel_id=1, source_target_pairs={{0,31},{1,2},{2,1},{3,4},{4,3},{5,6},{6,5},{7,8},{8,7},{9,10},{10,... | collective-permute-start | bytes 393224 | tf_op jit(solution)/shard_map/ppermute | solution.py:141
  74.5 0.4 collective-permute-done.28.off_in
  74.9 2.0 %layer.28 = (bf16[1024,256]{1,0:T(8,128)(2,1)S(1)}, bf16[1024,256]{1,0:T(8,128)(2,1)S(1)}, bf16[256,256]{1,0:T(8,128)(2,1)S(1)}, bf16[256,256]{1,0:T(8,128)(2,1)S(1)}) custom-call(s32[3]{0:T(128)S(1)} %get-tuple-element.162.info_ref, s32[8,4,8]{2,1,0:T(4,128)S(1)} %bitcast.17, bf16[1024,256]{1,0:T(8,128)(2,1)S(1)} %get-tuple-element.145.h_ref, ...), custom_call_target="tpu_custom_call" | custom-call | flops 700000000 | bytes 1048576 | tf_op jit(solution)/shard_map/layer/pallas_call | solution.py:178
  76.9 0.1 collective-permute-start.29
  77.0 3.7 %collective-permute-start.30 = (bf16[256,256]{1,0:T(8,128)(2,1)S(1)}, bf16[256,256]{1,0:T(8,128)(2,1)S(1)}, u32[]{:S(2)}, u32[]{:S(2)}) collective-permute-start(bf16[256,256]{1,0:T(8,128)(2,1)S(1)} %get-tuple-element.152), channel_id=1, source_target_pairs={{0,31},{1,2},{2,1},{3,4},{4,3},{5,6},{6,5},{7,8},{8,7},{9,10},{10,... | collective-permute-start | bytes 393224 | tf_op jit(solution)/shard_map/ppermute | solution.py:141
  80.7 2.0 %layer.21 = (bf16[1024,256]{1,0:T(8,128)(2,1)S(1)}, bf16[1024,256]{1,0:T(8,128)(2,1)S(1)}, bf16[256,256]{1,0:T(8,128)(2,1)S(1)}, bf16[256,256]{1,0:T(8,128)(2,1)S(1)}) custom-call(s32[3]{0:T(128)S(1)} %get-tuple-element.161.info_ref, s32[8,4,8]{2,1,0:T(4,128)S(1)} %bitcast.18, bf16[1024,256]{1,0:T(8,128)(2,1)S(1)} %get-tuple-element.116.h_ref, ...), custom_call_target="tpu_custom_call" | custom-call | flops 700000000 | bytes 1048576 | tf_op jit(solution)/shard_map/layer/pallas_call | solution.py:178
  82.7 0.1 collective-permute-start.15
  82.8 1.6 %collective-permute-start.16 = (bf16[256,256]{1,0:T(8,128)(2,1)S(1)}, bf16[256,256]{1,0:T(8,128)(2,1)S(1)}, u32[]{:S(2)}, u32[]{:S(2)}) collective-permute-start(bf16[256,256]{1,0:T(8,128)(2,1)S(1)} %get-tuple-element.123), channel_id=1, source_target_pairs={{0,31},{1,2},{2,1},{3,4},{4,3},{5,6},{6,5},{7,8},{8,7},{9,10},{10,... | collective-permute-start | bytes 393224 | tf_op jit(solution)/shard_map/ppermute | solution.py:141
  84.4 0.4 collective-permute-done.30.off_in
  84.8 2.0 %layer.29 = (bf16[1024,256]{1,0:T(8,128)(2,1)S(1)}, bf16[1024,256]{1,0:T(8,128)(2,1)S(1)}, bf16[256,256]{1,0:T(8,128)(2,1)S(1)}, bf16[256,256]{1,0:T(8,128)(2,1)S(1)}) custom-call(s32[3]{0:T(128)S(1)} %get-tuple-element.162.info_ref, s32[8,4,8]{2,1,0:T(4,128)S(1)} %bitcast.19, bf16[1024,256]{1,0:T(8,128)(2,1)S(1)} %get-tuple-element.149.h_ref, ...), custom_call_target="tpu_custom_call" | custom-call | flops 700000000 | bytes 1048576 | tf_op jit(solution)/shard_map/layer/pallas_call | solution.py:178
  86.8 0.1 collective-permute-start.31
  86.9 3.9 %collective-permute-start.32 = (bf16[256,256]{1,0:T(8,128)(2,1)S(1)}, bf16[256,256]{1,0:T(8,128)(2,1)S(1)}, u32[]{:S(2)}, u32[]{:S(2)}) collective-permute-start(bf16[256,256]{1,0:T(8,128)(2,1)S(1)} %get-tuple-element.156), channel_id=1, source_target_pairs={{0,31},{1,2},{2,1},{3,4},{4,3},{5,6},{6,5},{7,8},{8,7},{9,10},{10,... | collective-permute-start | bytes 393224 | tf_op jit(solution)/shard_map/ppermute | solution.py:141
  90.8 2.0 %layer.22 = (bf16[1024,256]{1,0:T(8,128)(2,1)S(1)}, bf16[1024,256]{1,0:T(8,128)(2,1)S(1)}, bf16[256,256]{1,0:T(8,128)(2,1)S(1)}, bf16[256,256]{1,0:T(8,128)(2,1)S(1)}) custom-call(s32[3]{0:T(128)S(1)} %get-tuple-element.161.info_ref, s32[8,4,8]{2,1,0:T(4,128)S(1)} %bitcast.20, bf16[1024,256]{1,0:T(8,128)(2,1)S(1)} %get-tuple-element.120.h_ref, ...), custom_call_target="tpu_custom_call" | custom-call | flops 700000000 | bytes 1048576 | tf_op jit(solution)/shard_map/layer/pallas_call | solution.py:178
  92.9 1.5 %collective-permute-start.18 = (bf16[256,256]{1,0:T(8,128)(2,1)S(1)}, bf16[256,256]{1,0:T(8,128)(2,1)S(1)}, u32[]{:S(2)}, u32[]{:S(2)}) collective-permute-start(bf16[256,256]{1,0:T(8,128)(2,1)S(1)} %get-tuple-element.127), channel_id=1, source_target_pairs={{0,31},{1,2},{2,1},{3,4},{4,3},{5,6},{6,5},{7,8},{8,7},{9,10},{10,... | collective-permute-start | bytes 393224 | tf_op jit(solution)/shard_map/ppermute | solution.py:141
  94.4 0.5 collective-permute-done.32.off_in
  94.9 2.0 %layer.30 = (bf16[1024,256]{1,0:T(8,128)(2,1)S(1)}, bf16[1024,256]{1,0:T(8,128)(2,1)S(1)}, bf16[256,256]{1,0:T(8,128)(2,1)S(1)}, bf16[256,256]{1,0:T(8,128)(2,1)S(1)}) custom-call(s32[3]{0:T(128)S(1)} %get-tuple-element.162.info_ref, s32[8,4,8]{2,1,0:T(4,128)S(1)} %bitcast.21, bf16[1024,256]{1,0:T(8,128)(2,1)S(1)} %get-tuple-element.153.h_ref, ...), custom_call_target="tpu_custom_call" | custom-call | flops 700000000 | bytes 1048576 | tf_op jit(solution)/shard_map/layer/pallas_call | solution.py:178
  97.0 3.7 %collective-permute-start.34 = (bf16[256,256]{1,0:T(8,128)(2,1)S(1)}, bf16[256,256]{1,0:T(8,128)(2,1)S(1)}, u32[]{:S(2)}, u32[]{:S(2)}) collective-permute-start(bf16[256,256]{1,0:T(8,128)(2,1)S(1)} %get-tuple-element.160), channel_id=1, source_target_pairs={{0,31},{1,2},{2,1},{3,4},{4,3},{5,6},{6,5},{7,8},{8,7},{9,10},{10,... | collective-permute-start | bytes 393224 | tf_op jit(solution)/shard_map/ppermute | solution.py:141
  100.7 1.4 %layer.23 = bf16[1024,256]{1,0:T(8,128)(2,1)S(1)} custom-call(s32[3]{0:T(128)S(1)} %get-tuple-element.161.info_ref, s32[8,4,8]{2,1,0:T(4,128)S(1)} %bitcast.22, bf16[1024,256]{1,0:T(8,128)(2,1)S(1)} %get-tuple-element.124.h_ref, bf16[1024,256]{1,0:T(8,128)(2,1)S(1)} %get-tuple-element.125.nrm_ref, bf16[256,256]{1,0:T(8,128)(2,1)S(1)} %collective-permute-done.17.on_in, ...), custom_call_target="tpu_custom_call" | custom-call | flops 700000000 | bytes 1048576 | tf_op jit(solution)/shard_map/layer/pallas_call | solution.py:178
  102.1 2.6 %collective-permute-done.34.off_in = bf16[256,256]{1,0:T(8,128)(2,1)S(1)} collective-permute-done((bf16[256,256]{1,0:T(8,128)(2,1)S(1)}, bf16[256,256]{1,0:T(8,128)(2,1)S(1)}, u32[]{:S(2)}, u32[]{:S(2)}) %collective-permute-start.34) | collective-permute-done | bytes 131104 | tf_op jit(solution)/shard_map/ppermute | solution.py:141
  104.8 1.4 %layer.31 = bf16[1024,256]{1,0:T(8,128)(2,1)S(1)} custom-call(s32[3]{0:T(128)S(1)} %get-tuple-element.162.info_ref, s32[8,4,8]{2,1,0:T(4,128)S(1)} %bitcast.23, bf16[1024,256]{1,0:T(8,128)(2,1)S(1)} %get-tuple-element.157.h_ref, bf16[1024,256]{1,0:T(8,128)(2,1)S(1)} %get-tuple-element.158.nrm_ref, bf16[256,256]{1,0:T(8,128)(2,1)S(1)} %collective-permute-done.33.on_in, ...), custom_call_target="tpu_custom_call" | custom-call | flops 700000000 | bytes 1048576 | tf_op jit(solution)/shard_map/layer/pallas_call | solution.py:178
  106.2 1.1 pad_maximum_fusion
  (40 shorter events, 0.4 us)
Async XLA Ops:
  0.0 5.8 %copy-start.1 = (bf16[2,256,256]{2,1,0:T(8,128)(2,1)S(1)}, bf16[2,256,256]{2,1,0:T(8,128)(2,1)}, u32[]{:S(2)}) copy-start(bf16[2,256,256]{2,1,0:T(8,128)(2,1)} %w_ref) | copy-start | bytes 786436
  0.1 0.7 copy-start.2
  0.8 0.7 copy-start.3
  1.5 4.4 %copy-start.4 = (bf16[2,256]{1,0:T(2,128)(2,1)S(1)}, bf16[2,256]{1,0:T(2,128)(2,1)}, u32[]{:S(2)}) copy-start(bf16[2,256]{1,0:T(2,128)(2,1)} %gain_ref.1) | copy-start | bytes 3076
  6.0 25.3 %copy-start = (s32[8,8,4]{1,2,0:T(4,128)S(1)}, s32[8,8,4]{1,2,0:T(4,128)}, u32[]{:S(2)}) copy-start(s32[8,8,4]{1,2,0:T(4,128)} %param.8) | copy-start | bytes 3076
  6.0 12.0 %collective-permute-start.2 = (bf16[2,256,256]{2,1,0:T(8,128)(2,1)S(1)}, bf16[2,256,256]{2,1,0:T(8,128)(2,1)S(1)}, u32[]{:S(2)}, u32[]{:S(2)}) collective-permute-start(bf16[2,256,256]{2,1,0:T(8,128)(2,1)S(1)} %scale.1.refs_0_), channel_id=1, source_target_pairs={{0,32},{32,64},{64,96},{96,0},{1,33},{33,65},{65,97},{97,1},{2,34}... | collective-permute-start | bytes 786440 | tf_op jit(solution)/shard_map/ppermute | solution.py:160
  8.1 15.2 %collective-permute-start.3 = (bf16[2,256,256]{2,1,0:T(8,128)(2,1)S(1)}, bf16[2,256,256]{2,1,0:T(8,128)(2,1)S(1)}, u32[]{:S(2)}, u32[]{:S(2)}) collective-permute-start(bf16[2,256,256]{2,1,0:T(8,128)(2,1)S(1)} %scale.1.refs_0_), channel_id=1, source_target_pairs={{0,64},{32,96},{64,0},{96,32},{1,65},{33,97},{65,1},{97,33},{2,66}... | collective-permute-start | bytes 786440 | tf_op jit(solution)/shard_map/ppermute | solution.py:160
  11.7 19.0 %collective-permute-start.4 = (bf16[2,256,256]{2,1,0:T(8,128)(2,1)S(1)}, bf16[2,256,256]{2,1,0:T(8,128)(2,1)S(1)}, u32[]{:S(2)}, u32[]{:S(2)}) collective-permute-start(bf16[2,256,256]{2,1,0:T(8,128)(2,1)S(1)} %scale.1.refs_0_), channel_id=1, source_target_pairs={{0,96},{32,0},{64,32},{96,64},{1,97},{33,1},{65,33},{97,65},{2,98}... | collective-permute-start | bytes 786440 | tf_op jit(solution)/shard_map/ppermute | solution.py:160
  12.7 18.6 %collective-permute-start = (bf16[256,256]{1,0:T(8,128)(2,1)S(1)}, bf16[256,256]{1,0:T(8,128)(2,1)S(1)}, u32[]{:S(2)}, u32[]{:S(2)}) collective-permute-start(bf16[256,256]{1,0:T(8,128)(2,1)S(1)} %get-tuple-element.90), channel_id=1, source_target_pairs={{0,1},{1,0},{2,3},{3,2},{4,5},{5,4},{6,7},{7,6},{8,9},{9,8},{10,11... | collective-permute-start | bytes 393224 | tf_op jit(solution)/shard_map/ppermute | solution.py:141
  12.7 18.6 %collective-permute-start.1 = (bf16[256,256]{1,0:T(8,128)(2,1)S(1)}, bf16[256,256]{1,0:T(8,128)(2,1)S(1)}, u32[]{:S(2)}, u32[]{:S(2)}) collective-permute-start(bf16[256,256]{1,0:T(8,128)(2,1)S(1)} %get-tuple-element.91), channel_id=1, source_target_pairs={{0,31},{1,2},{2,1},{3,4},{4,3},{5,6},{6,5},{7,8},{8,7},{9,10},{10,... | collective-permute-start | bytes 393224 | tf_op jit(solution)/shard_map/ppermute | solution.py:141
  18.0 17.0 %collective-permute-start.19 = (bf16[256,256]{1,0:T(8,128)(2,1)S(1)}, bf16[256,256]{1,0:T(8,128)(2,1)S(1)}, u32[]{:S(2)}, u32[]{:S(2)}) collective-permute-start(bf16[256,256]{1,0:T(8,128)(2,1)S(1)} %get-tuple-element.130), channel_id=1, source_target_pairs={{0,1},{1,0},{2,3},{3,2},{4,5},{5,4},{6,7},{7,6},{8,9},{9,8},{10,11... | collective-permute-start | bytes 393224 | tf_op jit(solution)/shard_map/ppermute | solution.py:141
  23.3 11.7 %collective-permute-start.20 = (bf16[256,256]{1,0:T(8,128)(2,1)S(1)}, bf16[256,256]{1,0:T(8,128)(2,1)S(1)}, u32[]{:S(2)}, u32[]{:S(2)}) collective-permute-start(bf16[256,256]{1,0:T(8,128)(2,1)S(1)} %get-tuple-element.131), channel_id=1, source_target_pairs={{0,31},{1,2},{2,1},{3,4},{4,3},{5,6},{6,5},{7,8},{8,7},{9,10},{10,... | collective-permute-start | bytes 393224 | tf_op jit(solution)/shard_map/ppermute | solution.py:141
  33.3 7.4 %collective-permute-start.5 = (bf16[256,256]{1,0:T(8,128)(2,1)S(1)}, bf16[256,256]{1,0:T(8,128)(2,1)S(1)}, u32[]{:S(2)}, u32[]{:S(2)}) collective-permute-start(bf16[256,256]{1,0:T(8,128)(2,1)S(1)} %get-tuple-element.102), channel_id=1, source_target_pairs={{0,1},{1,0},{2,3},{3,2},{4,5},{5,4},{6,7},{7,6},{8,9},{9,8},{10,11... | collective-permute-start | bytes 393224 | tf_op jit(solution)/shard_map/ppermute | solution.py:141
  33.4 7.8 %collective-permute-start.6 = (bf16[256,256]{1,0:T(8,128)(2,1)S(1)}, bf16[256,256]{1,0:T(8,128)(2,1)S(1)}, u32[]{:S(2)}, u32[]{:S(2)}) collective-permute-start(bf16[256,256]{1,0:T(8,128)(2,1)S(1)} %get-tuple-element.103), channel_id=1, source_target_pairs={{0,31},{1,2},{2,1},{3,4},{4,3},{5,6},{6,5},{7,8},{8,7},{9,10},{10,... | collective-permute-start | bytes 393224 | tf_op jit(solution)/shard_map/ppermute | solution.py:141
  37.0 7.9 %collective-permute-start.21 = (bf16[256,256]{1,0:T(8,128)(2,1)S(1)}, bf16[256,256]{1,0:T(8,128)(2,1)S(1)}, u32[]{:S(2)}, u32[]{:S(2)}) collective-permute-start(bf16[256,256]{1,0:T(8,128)(2,1)S(1)} %get-tuple-element.135), channel_id=1, source_target_pairs={{0,1},{1,0},{2,3},{3,2},{4,5},{5,4},{6,7},{7,6},{8,9},{9,8},{10,11... | collective-permute-start | bytes 393224 | tf_op jit(solution)/shard_map/ppermute | solution.py:141
  37.1 7.8 %collective-permute-start.22 = (bf16[256,256]{1,0:T(8,128)(2,1)S(1)}, bf16[256,256]{1,0:T(8,128)(2,1)S(1)}, u32[]{:S(2)}, u32[]{:S(2)}) collective-permute-start(bf16[256,256]{1,0:T(8,128)(2,1)S(1)} %get-tuple-element.136), channel_id=1, source_target_pairs={{0,31},{1,2},{2,1},{3,4},{4,3},{5,6},{6,5},{7,8},{8,7},{9,10},{10,... | collective-permute-start | bytes 393224 | tf_op jit(solution)/shard_map/ppermute | solution.py:141
  43.2 7.4 %collective-permute-start.7 = (bf16[256,256]{1,0:T(8,128)(2,1)S(1)}, bf16[256,256]{1,0:T(8,128)(2,1)S(1)}, u32[]{:S(2)}, u32[]{:S(2)}) collective-permute-start(bf16[256,256]{1,0:T(8,128)(2,1)S(1)} %get-tuple-element.106), channel_id=1, source_target_pairs={{0,1},{1,0},{2,3},{3,2},{4,5},{5,4},{6,7},{7,6},{8,9},{9,8},{10,11... | collective-permute-start | bytes 393224 | tf_op jit(solution)/shard_map/ppermute | solution.py:141
  43.3 7.8 %collective-permute-start.8 = (bf16[256,256]{1,0:T(8,128)(2,1)S(1)}, bf16[256,256]{1,0:T(8,128)(2,1)S(1)}, u32[]{:S(2)}, u32[]{:S(2)}) collective-permute-start(bf16[256,256]{1,0:T(8,128)(2,1)S(1)} %get-tuple-element.107), channel_id=1, source_target_pairs={{0,31},{1,2},{2,1},{3,4},{4,3},{5,6},{6,5},{7,8},{8,7},{9,10},{10,... | collective-permute-start | bytes 393224 | tf_op jit(solution)/shard_map/ppermute | solution.py:141
  46.9 7.8 %collective-permute-start.23 = (bf16[256,256]{1,0:T(8,128)(2,1)S(1)}, bf16[256,256]{1,0:T(8,128)(2,1)S(1)}, u32[]{:S(2)}, u32[]{:S(2)}) collective-permute-start(bf16[256,256]{1,0:T(8,128)(2,1)S(1)} %get-tuple-element.139), channel_id=1, source_target_pairs={{0,1},{1,0},{2,3},{3,2},{4,5},{5,4},{6,7},{7,6},{8,9},{9,8},{10,11... | collective-permute-start | bytes 393224 | tf_op jit(solution)/shard_map/ppermute | solution.py:141
  47.0 7.8 %collective-permute-start.24 = (bf16[256,256]{1,0:T(8,128)(2,1)S(1)}, bf16[256,256]{1,0:T(8,128)(2,1)S(1)}, u32[]{:S(2)}, u32[]{:S(2)}) collective-permute-start(bf16[256,256]{1,0:T(8,128)(2,1)S(1)} %get-tuple-element.140), channel_id=1, source_target_pairs={{0,31},{1,2},{2,1},{3,4},{4,3},{5,6},{6,5},{7,8},{8,7},{9,10},{10,... | collective-permute-start | bytes 393224 | tf_op jit(solution)/shard_map/ppermute | solution.py:141
  53.1 7.8 %collective-permute-start.10 = (bf16[256,256]{1,0:T(8,128)(2,1)S(1)}, bf16[256,256]{1,0:T(8,128)(2,1)S(1)}, u32[]{:S(2)}, u32[]{:S(2)}) collective-permute-start(bf16[256,256]{1,0:T(8,128)(2,1)S(1)} %get-tuple-element.111), channel_id=1, source_target_pairs={{0,31},{1,2},{2,1},{3,4},{4,3},{5,6},{6,5},{7,8},{8,7},{9,10},{10,... | collective-permute-start | bytes 393224 | tf_op jit(solution)/shard_map/ppermute | solution.py:141
  54.7 6.2 %collective-permute-start.9 = (bf16[256,256]{1,0:T(8,128)(2,1)S(1)}, bf16[256,256]{1,0:T(8,128)(2,1)S(1)}, u32[]{:S(2)}, u32[]{:S(2)}) collective-permute-start(bf16[256,256]{1,0:T(8,128)(2,1)S(1)} %get-tuple-element.110), channel_id=1, source_target_pairs={{0,1},{1,0},{2,3},{3,2},{4,5},{5,4},{6,7},{7,6},{8,9},{9,8},{10,11... | collective-permute-start | bytes 393224 | tf_op jit(solution)/shard_map/ppermute | solution.py:141
  56.8 7.8 %collective-permute-start.25 = (bf16[256,256]{1,0:T(8,128)(2,1)S(1)}, bf16[256,256]{1,0:T(8,128)(2,1)S(1)}, u32[]{:S(2)}, u32[]{:S(2)}) collective-permute-start(bf16[256,256]{1,0:T(8,128)(2,1)S(1)} %get-tuple-element.143), channel_id=1, source_target_pairs={{0,1},{1,0},{2,3},{3,2},{4,5},{5,4},{6,7},{7,6},{8,9},{9,8},{10,11... | collective-permute-start | bytes 393224 | tf_op jit(solution)/shard_map/ppermute | solution.py:141
  57.3 7.7 %collective-permute-start.26 = (bf16[256,256]{1,0:T(8,128)(2,1)S(1)}, bf16[256,256]{1,0:T(8,128)(2,1)S(1)}, u32[]{:S(2)}, u32[]{:S(2)}) collective-permute-start(bf16[256,256]{1,0:T(8,128)(2,1)S(1)} %get-tuple-element.144), channel_id=1, source_target_pairs={{0,31},{1,2},{2,1},{3,4},{4,3},{5,6},{6,5},{7,8},{8,7},{9,10},{10,... | collective-permute-start | bytes 393224 | tf_op jit(solution)/shard_map/ppermute | solution.py:141
  62.9 7.9 %collective-permute-start.11 = (bf16[256,256]{1,0:T(8,128)(2,1)S(1)}, bf16[256,256]{1,0:T(8,128)(2,1)S(1)}, u32[]{:S(2)}, u32[]{:S(2)}) collective-permute-start(bf16[256,256]{1,0:T(8,128)(2,1)S(1)} %get-tuple-element.114), channel_id=1, source_target_pairs={{0,1},{1,0},{2,3},{3,2},{4,5},{5,4},{6,7},{7,6},{8,9},{9,8},{10,11... | collective-permute-start | bytes 393224 | tf_op jit(solution)/shard_map/ppermute | solution.py:141
  63.0 7.8 %collective-permute-start.12 = (bf16[256,256]{1,0:T(8,128)(2,1)S(1)}, bf16[256,256]{1,0:T(8,128)(2,1)S(1)}, u32[]{:S(2)}, u32[]{:S(2)}) collective-permute-start(bf16[256,256]{1,0:T(8,128)(2,1)S(1)} %get-tuple-element.115), channel_id=1, source_target_pairs={{0,31},{1,2},{2,1},{3,4},{4,3},{5,6},{6,5},{7,8},{8,7},{9,10},{10,... | collective-permute-start | bytes 393224 | tf_op jit(solution)/shard_map/ppermute | solution.py:141
  67.0 7.5 %collective-permute-start.27 = (bf16[256,256]{1,0:T(8,128)(2,1)S(1)}, bf16[256,256]{1,0:T(8,128)(2,1)S(1)}, u32[]{:S(2)}, u32[]{:S(2)}) collective-permute-start(bf16[256,256]{1,0:T(8,128)(2,1)S(1)} %get-tuple-element.147), channel_id=1, source_target_pairs={{0,1},{1,0},{2,3},{3,2},{4,5},{5,4},{6,7},{7,6},{8,9},{9,8},{10,11... | collective-permute-start | bytes 393224 | tf_op jit(solution)/shard_map/ppermute | solution.py:141
  67.1 7.8 %collective-permute-start.28 = (bf16[256,256]{1,0:T(8,128)(2,1)S(1)}, bf16[256,256]{1,0:T(8,128)(2,1)S(1)}, u32[]{:S(2)}, u32[]{:S(2)}) collective-permute-start(bf16[256,256]{1,0:T(8,128)(2,1)S(1)} %get-tuple-element.148), channel_id=1, source_target_pairs={{0,31},{1,2},{2,1},{3,4},{4,3},{5,6},{6,5},{7,8},{8,7},{9,10},{10,... | collective-permute-start | bytes 393224 | tf_op jit(solution)/shard_map/ppermute | solution.py:141
  72.8 7.9 %collective-permute-start.13 = (bf16[256,256]{1,0:T(8,128)(2,1)S(1)}, bf16[256,256]{1,0:T(8,128)(2,1)S(1)}, u32[]{:S(2)}, u32[]{:S(2)}) collective-permute-start(bf16[256,256]{1,0:T(8,128)(2,1)S(1)} %get-tuple-element.118), channel_id=1, source_target_pairs={{0,1},{1,0},{2,3},{3,2},{4,5},{5,4},{6,7},{7,6},{8,9},{9,8},{10,11... | collective-permute-start | bytes 393224 | tf_op jit(solution)/shard_map/ppermute | solution.py:141
  72.9 7.8 %collective-permute-start.14 = (bf16[256,256]{1,0:T(8,128)(2,1)S(1)}, bf16[256,256]{1,0:T(8,128)(2,1)S(1)}, u32[]{:S(2)}, u32[]{:S(2)}) collective-permute-start(bf16[256,256]{1,0:T(8,128)(2,1)S(1)} %get-tuple-element.119), channel_id=1, source_target_pairs={{0,31},{1,2},{2,1},{3,4},{4,3},{5,6},{6,5},{7,8},{8,7},{9,10},{10,... | collective-permute-start | bytes 393224 | tf_op jit(solution)/shard_map/ppermute | solution.py:141
  76.9 7.5 %collective-permute-start.29 = (bf16[256,256]{1,0:T(8,128)(2,1)S(1)}, bf16[256,256]{1,0:T(8,128)(2,1)S(1)}, u32[]{:S(2)}, u32[]{:S(2)}) collective-permute-start(bf16[256,256]{1,0:T(8,128)(2,1)S(1)} %get-tuple-element.151), channel_id=1, source_target_pairs={{0,1},{1,0},{2,3},{3,2},{4,5},{5,4},{6,7},{7,6},{8,9},{9,8},{10,11... | collective-permute-start | bytes 393224 | tf_op jit(solution)/shard_map/ppermute | solution.py:141
  77.0 7.8 %collective-permute-start.30 = (bf16[256,256]{1,0:T(8,128)(2,1)S(1)}, bf16[256,256]{1,0:T(8,128)(2,1)S(1)}, u32[]{:S(2)}, u32[]{:S(2)}) collective-permute-start(bf16[256,256]{1,0:T(8,128)(2,1)S(1)} %get-tuple-element.152), channel_id=1, source_target_pairs={{0,31},{1,2},{2,1},{3,4},{4,3},{5,6},{6,5},{7,8},{8,7},{9,10},{10,... | collective-permute-start | bytes 393224 | tf_op jit(solution)/shard_map/ppermute | solution.py:141
  82.7 8.1 %collective-permute-start.15 = (bf16[256,256]{1,0:T(8,128)(2,1)S(1)}, bf16[256,256]{1,0:T(8,128)(2,1)S(1)}, u32[]{:S(2)}, u32[]{:S(2)}) collective-permute-start(bf16[256,256]{1,0:T(8,128)(2,1)S(1)} %get-tuple-element.122), channel_id=1, source_target_pairs={{0,1},{1,0},{2,3},{3,2},{4,5},{5,4},{6,7},{7,6},{8,9},{9,8},{10,11... | collective-permute-start | bytes 393224 | tf_op jit(solution)/shard_map/ppermute | solution.py:141
  82.8 8.0 %collective-permute-start.16 = (bf16[256,256]{1,0:T(8,128)(2,1)S(1)}, bf16[256,256]{1,0:T(8,128)(2,1)S(1)}, u32[]{:S(2)}, u32[]{:S(2)}) collective-permute-start(bf16[256,256]{1,0:T(8,128)(2,1)S(1)} %get-tuple-element.123), channel_id=1, source_target_pairs={{0,31},{1,2},{2,1},{3,4},{4,3},{5,6},{6,5},{7,8},{8,7},{9,10},{10,... | collective-permute-start | bytes 393224 | tf_op jit(solution)/shard_map/ppermute | solution.py:141
  86.8 7.6 %collective-permute-start.31 = (bf16[256,256]{1,0:T(8,128)(2,1)S(1)}, bf16[256,256]{1,0:T(8,128)(2,1)S(1)}, u32[]{:S(2)}, u32[]{:S(2)}) collective-permute-start(bf16[256,256]{1,0:T(8,128)(2,1)S(1)} %get-tuple-element.155), channel_id=1, source_target_pairs={{0,1},{1,0},{2,3},{3,2},{4,5},{5,4},{6,7},{7,6},{8,9},{9,8},{10,11... | collective-permute-start | bytes 393224 | tf_op jit(solution)/shard_map/ppermute | solution.py:141
  86.9 8.0 %collective-permute-start.32 = (bf16[256,256]{1,0:T(8,128)(2,1)S(1)}, bf16[256,256]{1,0:T(8,128)(2,1)S(1)}, u32[]{:S(2)}, u32[]{:S(2)}) collective-permute-start(bf16[256,256]{1,0:T(8,128)(2,1)S(1)} %get-tuple-element.156), channel_id=1, source_target_pairs={{0,31},{1,2},{2,1},{3,4},{4,3},{5,6},{6,5},{7,8},{8,7},{9,10},{10,... | collective-permute-start | bytes 393224 | tf_op jit(solution)/shard_map/ppermute | solution.py:141
  92.8 7.9 %collective-permute-start.17 = (bf16[256,256]{1,0:T(8,128)(2,1)S(1)}, bf16[256,256]{1,0:T(8,128)(2,1)S(1)}, u32[]{:S(2)}, u32[]{:S(2)}) collective-permute-start(bf16[256,256]{1,0:T(8,128)(2,1)S(1)} %get-tuple-element.126), channel_id=1, source_target_pairs={{0,1},{1,0},{2,3},{3,2},{4,5},{5,4},{6,7},{7,6},{8,9},{9,8},{10,11... | collective-permute-start | bytes 393224 | tf_op jit(solution)/shard_map/ppermute | solution.py:141
  92.9 7.8 %collective-permute-start.18 = (bf16[256,256]{1,0:T(8,128)(2,1)S(1)}, bf16[256,256]{1,0:T(8,128)(2,1)S(1)}, u32[]{:S(2)}, u32[]{:S(2)}) collective-permute-start(bf16[256,256]{1,0:T(8,128)(2,1)S(1)} %get-tuple-element.127), channel_id=1, source_target_pairs={{0,31},{1,2},{2,1},{3,4},{4,3},{5,6},{6,5},{7,8},{8,7},{9,10},{10,... | collective-permute-start | bytes 393224 | tf_op jit(solution)/shard_map/ppermute | solution.py:141
  96.9 5.2 %collective-permute-start.33 = (bf16[256,256]{1,0:T(8,128)(2,1)S(1)}, bf16[256,256]{1,0:T(8,128)(2,1)S(1)}, u32[]{:S(2)}, u32[]{:S(2)}) collective-permute-start(bf16[256,256]{1,0:T(8,128)(2,1)S(1)} %get-tuple-element.159), channel_id=1, source_target_pairs={{0,1},{1,0},{2,3},{3,2},{4,5},{5,4},{6,7},{7,6},{8,9},{9,8},{10,11... | collective-permute-start | bytes 393224 | tf_op jit(solution)/shard_map/ppermute | solution.py:141
  97.0 7.8 %collective-permute-start.34 = (bf16[256,256]{1,0:T(8,128)(2,1)S(1)}, bf16[256,256]{1,0:T(8,128)(2,1)S(1)}, u32[]{:S(2)}, u32[]{:S(2)}) collective-permute-start(bf16[256,256]{1,0:T(8,128)(2,1)S(1)} %get-tuple-element.160), channel_id=1, source_target_pairs={{0,31},{1,2},{2,1},{3,4},{4,3},{5,6},{6,5},{7,8},{8,7},{9,10},{10,... | collective-permute-start | bytes 393224 | tf_op jit(solution)/shard_map/ppermute | solution.py:141
where the time goes:
time: 108 us; the launch traced here: 107 us
  starting transfers between devices  54 us (50%)
  Pallas kernels  39.5 us (37%)
  waiting for transfers between devices  10.9 us (10%)
  local copies, waits for them, and re-layouts  1.41 us (1%)
  other arithmetic  1.14 us (1%)
    ppermute x16, starting transfers between devices, exchange(): lax.ppermute(off, 'dom', off_pairs)  45.8 us
    pallas_call x16, Pallas kernels, on_device(): call(functools.partial(layer_body, layer, last), outs, [SMEM, SMEM] + [VM...  30.9 us
    ppermute x3, starting transfers between devices, on_device(): lax.ppermute(scaled, 'section', [(i, (i + shift) % sections) for i in ran...  6.66 us
    ppermute x16, waiting for transfers between devices, exchange(): lax.ppermute(off, 'dom', off_pairs)  5.52 us
    ppermute x3, waiting for transfers between devices, on_device(): lax.ppermute(scaled, 'section', [(i, (i + shift) % sections) for i in ran...  5.3 us
    pallas_call x2, Pallas kernels, on_device(): call(prologue_body, [(rows_dev, width), (rows_dev, width), (2 * bnd, rows...  4.35 us
    pallas_call x2, Pallas kernels, on_device(): call(fetch_body, [(rows_dev, K * TILE)], [SMEM, HBM], 'fetch', [pltpu.Sem...  3.55 us
  transfers between devices with their start and end apart: 35, of which 9 were waited for; matrix products, arithmetic and copies ran while one was open for 0% of the time, Pallas kernels for 31%

commit v1 on v0

v1 whole, which is shorter than its diff:
```python
import functools

import jax
import jax.numpy as jnp
from jax import lax
from jax.experimental import pallas as pl
from jax.experimental.pallas import tpu as pltpu
from jax.sharding import PartitionSpec as P

TILE = 128
K = 4
EPS = 1e-06
BF = jnp.bfloat16
F32 = jnp.float32
VMEM = pl.BlockSpec(memory_space=pltpu.VMEM)
HBM = pl.BlockSpec(memory_space=pltpu.HBM)


def call(body, outs, in_specs, name, scratch=(), limit=8, flops=0, ints=(), hbm_out=False):
    return pl.pallas_call(
        body,
        out_shape=[jax.ShapeDtypeStruct(s, BF) for s in outs] + [jax.ShapeDtypeStruct(s, jnp.int32) for s in ints],
        in_specs=in_specs,
        out_specs=[HBM if hbm_out else VMEM] * (len(outs) + len(ints)),
        scratch_shapes=list(scratch),
        name=name,
        cost_estimate=pl.CostEstimate(flops=flops, bytes_accessed=1 << 10, transcendentals=0),
        compiler_params=pltpu.CompilerParams(vmem_limit_bytes=limit << 20),
    )


def normalise(hidden):
    mean = jnp.mean(hidden * hidden, axis=-1, keepdims=True)
    return jnp.maximum(hidden * lax.rsqrt(mean + EPS), 0.0).astype(BF)


def send_rows(chooser_ref, normed_ref, on_ref, off_ref):
    bnd = on_ref.shape[0]
    for at, out in ((bnd, off_ref), (0, on_ref)):
        out[...] = jnp.dot(
            chooser_ref[at : at + bnd, :], normed_ref[...], preferred_element_type=F32
        ).astype(BF)


def dom_parity():
    return lax.rem(lax.axis_index("dom"), 2)


def graph_of(local, per_section):
    return lax.axis_index("section") * per_section + local


def chunked(source, target, sems):
    count = sems.shape[0]
    step = target.shape[0] // count
    copies = []
    for c in range(count):
        rows = pl.ds(c * step, step)
        copies.append(pltpu.make_async_copy(source.at[rows], target.at[rows], sems.at[c]))
    for copy in copies:
        copy.start()
    return copies


def prologue_body(local, per_section, early, *refs):
    feat, rows_hbm, count_hbm, src_hbm = refs[:4]
    refs = refs[4 + early :]
    h_ref, nrm_ref, sel_ref, on_ref, off_ref, idx_ref = refs[:6]
    rows_ref, count_ref, src_ref, sems, feat_sems = refs[6:]
    graph, parity = graph_of(local, per_section), dom_parity()
    small = [
        pltpu.make_async_copy(rows_hbm.at[graph], rows_ref, sems.at[0]),
        pltpu.make_async_copy(count_hbm, count_ref, sems.at[1]),
        pltpu.make_async_copy(src_hbm.at[graph], src_ref, sems.at[2]),
    ]
    for copy in small:
        copy.start()
    copies = chunked(feat.at[graph], h_ref, feat_sems)
    for copy in small:
        copy.wait()
    rows_dev = h_ref.shape[0]
    bnd = on_ref.shape[0]
    own, half = rows_dev // TILE, bnd // TILE
    counts = count_ref[...]
    here = lax.broadcasted_iota(jnp.int32, counts.shape, 1) == graph
    live = jnp.sum(jnp.where(here, counts, 0), axis=1, keepdims=True)
    lane = lax.broadcasted_iota(jnp.int32, rows_ref.shape, 1)
    rows = jnp.where(lane < live, rows_ref[...], -1).astype(F32)
    first = jnp.broadcast_to(rows[0:1, :], (TILE, bnd))
    second = jnp.broadcast_to(rows[1:2, :], (TILE, bnd))
    even = parity == 0
    for at, picked in ((0, jnp.where(even, second, first)), (bnd, jnp.where(even, first, second))):
        column = picked.T
        for c in range(rows_dev // TILE):
            ids = lax.broadcasted_iota(jnp.int32, (bnd, TILE), 1) + c * TILE
            hit = column == ids.astype(F32)
            sel_ref[at : at + bnd, c * TILE : (c + 1) * TILE] = jnp.where(hit, 1.0, 0.0).astype(BF)
    t = src_ref[...]
    left = jnp.where(even, own + half, own)
    right = jnp.where(even, own, own + half)
    table = jnp.where(t < half, left + t, jnp.where(t < half + own, t - half, right + t - half - own))
    for i in range(own):
        for k in range(K):
            idx_ref[i * K + k : i * K + k + 1, :] = jnp.broadcast_to(table[k : k + 1, i : i + 1], (1, TILE))
    for c, copy in enumerate(copies):
        copy.wait()
        block = slice(c * rows_dev // len(copies), (c + 1) * rows_dev // len(copies))
        nrm_ref[block, :] = normalise(h_ref[block, :].astype(F32))
    send_rows(sel_ref, nrm_ref, on_ref, off_ref)


def fetch_body(per_section, val_ref, after_ref, *refs):
    outs, sems = refs[:per_section], refs[per_section]
    copies = []
    for g, out in enumerate(outs):
        copies += chunked(val_ref.at[graph_of(g, per_section)], out, sems.at[g])
    for copy in copies:
        copy.wait()


def scale_body(w_ref, gain_ref, after_ref, out_ref):
    width = w_ref.shape[1]
    gain = gain_ref[...].astype(F32)
    for k in range(w_ref.shape[0]):
        column = jnp.broadcast_to(gain[k : k + 1, :], (width, width)).T
        out_ref[k] = (w_ref[k].astype(F32) * column).astype(BF)


def order_body(count, *refs):
    parts, out = refs[:count], refs[count]
    section = lax.axis_index("section")
    per = parts[0].shape[0]
    for shift, part in enumerate(parts):
        source = lax.rem(section - shift + count, count)
        for k in range(per):
            out[source * per + k] = part[k]


def layer_body(layer, last, others, idx_ref, h_ref, nrm_ref, on_in, off_in, tv_ref, sel_ref, w_ref, *rest):
    done, rest = rest[:others], rest[others:]
    if last and others:
        out_ref, ext, agg, out_h, sems = rest
        copies = [pltpu.make_async_copy(done[g], out_ref.at[g], sems.at[g]) for g in range(others)]
        for copy in copies:
            copy.start()
    elif last:
        out_h, ext, agg = rest
    else:
        out_h, out_n, on_ref, off_ref, ext, agg = rest
    rows_dev = h_ref.shape[0]
    bnd = on_in.shape[0]
    own, half = rows_dev // TILE, bnd // TILE
    index = [idx_ref[j, 0] for j in range(own * K)]
    ext[0:own] = nrm_ref[...].reshape(own, TILE, -1)
    ext[own : own + half] = on_in[...].reshape(half, TILE, -1)
    ext[own + half : own + 2 * half] = off_in[...].reshape(half, TILE, -1)
    for i in range(own):
        picked = [ext[index[i * K + k]] for k in range(K)]
        agg[i * TILE : (i + 1) * TILE, :] = jnp.dot(
            tv_ref[i * TILE : (i + 1) * TILE, :], jnp.concatenate(picked, axis=0), preferred_element_type=F32
        ).astype(BF)
    step = 256
    for r in range(0, rows_dev, step):
        rows = slice(r, r + step)
        update = jnp.dot(agg[rows, :], w_ref[layer], preferred_element_type=F32)
        new = (h_ref[rows, :].astype(F32) + update).astype(BF)
        out_h[rows, :] = new
        if not last:
            out_n[rows, :] = normalise(new.astype(F32))
    if not last:
        send_rows(sel_ref, out_n, on_ref, off_ref)
    elif others:
        copies.append(pltpu.make_async_copy(out_h, out_ref.at[others], sems.at[others]))
        copies[-1].start()
        for copy in copies:
            copy.wait()


def on_device(features, tile_src, tile_val, boundary_rows, boundary_count, weights, gains):
    sections = lax.axis_size("section")
    doms = lax.axis_size("dom")
    graphs, rows_dev, width = features.shape
    bnd = boundary_rows.shape[-1]
    per_section = graphs // sections
    layers = weights.shape[0] * sections
    tiles = rows_dev // TILE
    on_pairs = [(i, i ^ 1) for i in range(doms)]
    off_pairs = [(i, (i + (1 if i % 2 else -1)) % doms) for i in range(doms)]

    def exchange(on, off):
        return lax.ppermute(on, "dom", on_pairs), lax.ppermute(off, "dom", off_pairs)

    tile_src = jnp.swapaxes(tile_src, 1, 2)
    boundary_count = jnp.swapaxes(boundary_count, 0, 1)
    features, tile_val, boundary_rows, boundary_count, tile_src = (
        pltpu.with_memory_space_constraint(x, pltpu.HBM)
        for x in (features, tile_val, boundary_rows, boundary_count, tile_src)
    )
    state = []
    early = ()
    for g in range(per_section):
        h, nrm, sel, on, off, idx = call(
            functools.partial(prologue_body, g, per_section, len(early)),
            [(rows_dev, width), (rows_dev, width), (2 * bnd, rows_dev), (bnd, width), (bnd, width)],
            [HBM] * 4 + [VMEM] * len(early),
            "prologue",
            [
                pltpu.VMEM((2, bnd), jnp.int32),
                pltpu.VMEM((2, graphs), jnp.int32),
                pltpu.VMEM((K, tiles), jnp.int32),
                pltpu.SemaphoreType.DMA((3,)),
                pltpu.SemaphoreType.DMA((4,)),
            ],
            ints=[(tiles * K, TILE)],
        )(features, boundary_rows, boundary_count, tile_src, *early)
        on, off = exchange(on, off)
        state.append([h, nrm, on, off, sel, idx])
        early = (state[0][2],)
    scaled = call(scale_body, [weights.shape], [VMEM] * 3, "scale")(weights, gains, *early)[0]
    parts = [scaled] + [
        lax.ppermute(scaled, "section", [(i, (i + shift) % sections) for i in range(sections)])
        for shift in range(1, sections)
    ]
    values = call(
        functools.partial(fetch_body, per_section),
        [(rows_dev, K * TILE)] * per_section,
        [HBM, VMEM],
        "fetch",
        [pltpu.SemaphoreType.DMA((per_section, 4))],
    )(tile_val, *early)
    w_all = call(functools.partial(order_body, sections), [(layers, width, width)], [VMEM] * sections, "order")(
        *parts
    )[0]
    outputs = []
    for layer in range(layers):
        last = layer == layers - 1
        for g in range(per_section):
            h, nrm, on, off, sel, idx = state[g]
            scratch = [pltpu.VMEM((tiles + 2 * bnd // TILE, TILE, width), BF), pltpu.VMEM((rows_dev, width), BF)]
            final = last and g == per_section - 1
            others = len(outputs) if final else 0
            if final:
                outs = [(per_section, rows_dev, width)]
                scratch += [pltpu.VMEM((rows_dev, width), BF), pltpu.SemaphoreType.DMA((per_section,))]
            elif last:
                outs = [(rows_dev, width)]
            else:
                outs = [(rows_dev, width), (rows_dev, width), (bnd, width), (bnd, width)]
            result = call(
                functools.partial(layer_body, layer, last, others),
                outs,
                [VMEM] * (8 + others),
                "layer",
                scratch,
                flops=1_000_000,
                hbm_out=final,
            )(idx, h, nrm, on, off, values[g], sel, w_all, *outputs[:others])
            if last:
                outputs.append(result[0])
            else:
                h, nrm, on, off = result
                state[g] = [h, nrm, *exchange(on, off), sel, idx]
    return outputs[-1]


def solution(mesh):
    in_specs = (
        P(None, "dom", None),
        P(None, "dom", None),
        P(None, "dom", None),
        P(None, "dom", None),
        P(None, "dom"),
        P("section", None, None),
        P("section", None),
    )
    return jax.shard_map(
        on_device, mesh=mesh, in_specs=in_specs, out_specs=P("section", "dom", None), check_vma=False
    )
```

time: 108 us -> 97.3 us (0.901)
  Pallas kernels: 39.5 us -> 25.4 us
  waiting for transfers between devices: 10.9 us -> 17.5 us
  starting transfers between devices: 54 us -> 52 us
  other arithmetic: 1.14 us -> 0 us
    pallas_call x21 -> x20, Pallas kernels: 38.9 us -> 25.3 us  [the longest x16 19.4 us: on_device(): call(functools.partial(layer_body, layer, last, others), outs, [VMEM] * (...]
    ppermute x16, waiting for transfers between devices: 5.52 us -> 12.3 us  [exchange(): lax.ppermute(off, 'dom', off_pairs)]
    ppermute x3, waiting for transfers between devices: 5.3 us -> 3.88 us  [on_device(): lax.ppermute(scaled, 'section', [(i, (i + shift) % sections) for i in ran...]
    ppermute x16, waiting for transfers between devices: 0.04 us -> 1.37 us  [exchange(): lax.ppermute(on, 'dom', on_pairs)]
    ppermute x3, starting transfers between devices: 6.66 us -> 5.45 us  [on_device(): lax.ppermute(scaled, 'section', [(i, (i + shift) % sections) for i in ran...]
    another operation x2 -> x0, other arithmetic: 1.14 us -> none  [the longest x1 1.06 us: on_device(): return jnp.stack(outputs, axis=0)]
  transfers between devices with their start and end apart: 35 -> 35, of which waited for: 9 -> 11; matrix products, arithmetic and copies ran while one was open for 0% -> 0% of each run, Pallas kernels for 31% -> 22%
where the time goes in v1:
time: 97.3 us; the launch traced here: 97.1 us
  starting transfers between devices  52 us (53%)
  Pallas kernels  25.4 us (26%)
  waiting for transfers between devices  17.5 us (18%)
  local copies, waits for them, and re-layouts  1.63 us (2%)
    ppermute x16, starting transfers between devices, exchange(): lax.ppermute(off, 'dom', off_pairs)  45.2 us
    pallas_call x16, Pallas kernels, on_device(): call(functools.partial(layer_body, layer, last, others), outs, [VMEM] * (...  19.4 us
    ppermute x16, waiting for transfers between devices, exchange(): lax.ppermute(off, 'dom', off_pairs)  12.3 us
    ppermute x3, starting transfers between devices, on_device(): lax.ppermute(scaled, 'section', [(i, (i + shift) % sections) for i in ran...  5.45 us
    pallas_call x2, Pallas kernels, on_device(): call(functools.partial(prologue_body, g, per_section, len(early)), [(rows...  4.27 us
    ppermute x3, waiting for transfers between devices, on_device(): lax.ppermute(scaled, 'section', [(i, (i + shift) % sections) for i in ran...  3.88 us
  transfers between devices with their start and end apart: 35, of which 11 were waited for; matrix products, arithmetic and copies ran while one was open for 0% of the time, Pallas kernels for 22%

profile of v1, /device:TPU:0, one launch (start us, length us, event | category | flops | bytes accessed | tf_op | source)
XLA Modules:
  0.0 97.1 jit_solution(6092936631073011840)
XLA Ops:
  0.0 2.1 %prologue.2 = (bf16[1024,256]{1,0:T(8,128)(2,1)S(1)}, bf16[1024,256]{1,0:T(8,128)(2,1)S(1)}, bf16[512,1024]{1,0:T(8,128)(2,1)S(1)}, bf16[256,256]{1,0:T(8,128)(2...) custom-call(bf16[8,1024,256]{2,1,0:T(8,128)(2,1)} %refs_0_.3, s32[8,2,256]{2,1,0:T(2,128)} %refs_1_.3, ...), custom_call_target="tpu_custom_call" | custom-call | bytes 1024 | tf_op jit(solution)/shard_map/prologue/pallas_call | solution.py:202
  2.1 0.1 collective-permute-start
  2.2 1.3 %collective-permute-done.refs_4_.after_ref.on_in = bf16[256,256]{1,0:T(8,128)(2,1)S(1)} collective-permute-done((bf16[256,256]{1,0:T(8,128)(2,1)S(1)}, bf16[256,256]{1,0:T(8,128)(2,1)S(1)}, u32[]{:S(2)}, u32[]{:S(2)}) %collective-permute-start) | collective-permute-done | bytes 131104 | tf_op jit(solution)/shard_map/ppermute | solution.py:191
  3.6 0.9 copy-done
  4.5 0.7 copy-done.1
  5.2 0.1 scale.1.refs_0_
  5.3 4.2 %collective-permute-start.5 = (bf16[2,256,256]{2,1,0:T(8,128)(2,1)S(1)}, bf16[2,256,256]{2,1,0:T(8,128)(2,1)S(1)}, u32[]{:S(2)}, u32[]{:S(2)}) collective-permute-start(bf16[2,256,256]{2,1,0:T(8,128)(2,1)S(1)} %scale.1.refs_0_), channel_id=1, source_target_pairs={{0,96},{32,0},{64,32},{96,64},{1,97},{33,1},{65,33},{97,65},{2,98}... | collective-permute-start | bytes 786440 | tf_op jit(solution)/shard_map/ppermute | solution.py:221
  9.5 1.3 %collective-permute-start.3 = (bf16[2,256,256]{2,1,0:T(8,128)(2,1)S(1)}, bf16[2,256,256]{2,1,0:T(8,128)(2,1)S(1)}, u32[]{:S(2)}, u32[]{:S(2)}) collective-permute-start(bf16[2,256,256]{2,1,0:T(8,128)(2,1)S(1)} %scale.1.refs_0_), channel_id=1, source_target_pairs={{0,32},{32,64},{64,96},{96,0},{1,33},{33,65},{65,97},{97,1},{2,34}... | collective-permute-start | bytes 786440 | tf_op jit(solution)/shard_map/ppermute | solution.py:221
  10.8 4.1 %collective-permute-start.20 = (bf16[256,256]{1,0:T(8,128)(2,1)S(1)}, bf16[256,256]{1,0:T(8,128)(2,1)S(1)}, u32[]{:S(2)}, u32[]{:S(2)}) collective-permute-start(bf16[256,256]{1,0:T(8,128)(2,1)S(1)} %get-tuple-element.114), channel_id=1, source_target_pairs={{0,31},{1,2},{2,1},{3,4},{4,3},{5,6},{6,5},{7,8},{8,7},{9,10},{10,... | collective-permute-start | bytes 393224 | tf_op jit(solution)/shard_map/ppermute | solution.py:191
  14.9 2.1 %prologue.3 = (bf16[1024,256]{1,0:T(8,128)(2,1)S(1)}, bf16[1024,256]{1,0:T(8,128)(2,1)S(1)}, bf16[512,1024]{1,0:T(8,128)(2,1)S(1)}, bf16[256,256]{1,0:T(8,128)(2...) custom-call(bf16[8,1024,256]{2,1,0:T(8,128)(2,1)} %refs_0_.3, s32[8,2,256]{2,1,0:T(2,128)} %refs_1_.3, ...), custom_call_target="tpu_custom_call" | custom-call | bytes 1024 | tf_op jit(solution)/shard_map/prologue/pallas_call | solution.py:202
  17.1 0.1 collective-permute-start.1
  17.2 3.9 %collective-permute-done.5.refs_3_ = bf16[2,256,256]{2,1,0:T(8,128)(2,1)S(1)} collective-permute-done((bf16[2,256,256]{2,1,0:T(8,128)(2,1)S(1)}, bf16[2,256,256]{2,1,0:T(8,128)(2,1)S(1)}, u32[]{:S(2)}, u32[]{:S(2)}) %collective-permute-start.5) | collective-permute-done | bytes 262176 | tf_op jit(solution)/shard_map/ppermute | solution.py:221
  21.0 4.1 %collective-permute-start.2 = (bf16[256,256]{1,0:T(8,128)(2,1)S(1)}, bf16[256,256]{1,0:T(8,128)(2,1)S(1)}, u32[]{:S(2)}, u32[]{:S(2)}) collective-permute-start(bf16[256,256]{1,0:T(8,128)(2,1)S(1)} %get-tuple-element.80), channel_id=1, source_target_pairs={{0,31},{1,2},{2,1},{3,4},{4,3},{5,6},{6,5},{7,8},{8,7},{9,10},{10,... | collective-permute-start | bytes 393224 | tf_op jit(solution)/shard_map/ppermute | solution.py:191
  25.2 1.6 %fetch.1 = (bf16[1024,512]{1,0:T(8,128)(2,1)S(1)}, bf16[1024,512]{1,0:T(8,128)(2,1)S(1)}) custom-call(bf16[8,1024,512]{2,1,0:T(8,128)(2,1)} %val_ref.1, bf16[256,256]{1,0:T(8,128)(2,1)S(1)} %collective-permute-done.refs_4_.after_ref.on_in), custom_call_target="tpu_custom_call" | custom-call | bytes 1024 | tf_op jit(solution)/shard_map/fetch/pallas_call | solution.py:224
  26.8 0.1 order.1.w_ref
  26.9 1.2 %layer.23 = (bf16[1024,256]{1,0:T(8,128)(2,1)S(1)}, bf16[1024,256]{1,0:T(8,128)(2,1)S(1)}, bf16[256,256]{1,0:T(8,128)(2,1)S(1)}, bf16[256,256]{1,0:T(8,128)(2,1)S(1)}) custom-call(s32[32,128]{1,0:T(8,128)S(1)} %get-tuple-element.111.idx_ref, bf16[1024,256]{1,0:T(8,128)(2,1)S(1)} %get-tuple-element.112.h_ref, ...), custom_call_target="tpu_custom_call" | custom-call | flops 1000000 | bytes 1024 | tf_op jit(solution)/shard_map/layer/pallas_call | solution.py:249
  28.1 0.1 collective-permute-start.21
  28.2 3.0 %collective-permute-start.22 = (bf16[256,256]{1,0:T(8,128)(2,1)S(1)}, bf16[256,256]{1,0:T(8,128)(2,1)S(1)}, u32[]{:S(2)}, u32[]{:S(2)}) collective-permute-start(bf16[256,256]{1,0:T(8,128)(2,1)S(1)} %get-tuple-element.120), channel_id=1, source_target_pairs={{0,31},{1,2},{2,1},{3,4},{4,3},{5,6},{6,5},{7,8},{8,7},{9,10},{10,... | collective-permute-start | bytes 393224 | tf_op jit(solution)/shard_map/ppermute | solution.py:191
  31.2 1.2 %layer.16 = (bf16[1024,256]{1,0:T(8,128)(2,1)S(1)}, bf16[1024,256]{1,0:T(8,128)(2,1)S(1)}, bf16[256,256]{1,0:T(8,128)(2,1)S(1)}, bf16[256,256]{1,0:T(8,128)(2,1)S(1)}) custom-call(s32[32,128]{1,0:T(8,128)S(1)} %get-tuple-element.76.idx_ref, bf16[1024,256]{1,0:T(8,128)(2,1)S(1)} %get-tuple-element.77.h_ref, bf16[1024,256]{1,0:T(8,128)(2,1)S(1)} %get-tuple-element.78.nrm_ref, ...), custom_call_target="tpu_custom_call" | custom-call | flops 1000000 | bytes 1024 | tf_op jit(solution)/shard_map/layer/pallas_call | solution.py:249
  32.4 0.1 collective-permute-start.6
  32.5 2.2 %collective-permute-start.7 = (bf16[256,256]{1,0:T(8,128)(2,1)S(1)}, bf16[256,256]{1,0:T(8,128)(2,1)S(1)}, u32[]{:S(2)}, u32[]{:S(2)}) collective-permute-start(bf16[256,256]{1,0:T(8,128)(2,1)S(1)} %get-tuple-element.86), channel_id=1, source_target_pairs={{0,31},{1,2},{2,1},{3,4},{4,3},{5,6},{6,5},{7,8},{8,7},{9,10},{10,... | collective-permute-start | bytes 393224 | tf_op jit(solution)/shard_map/ppermute | solution.py:191
  34.8 1.2 %collective-permute-done.22.off_in = bf16[256,256]{1,0:T(8,128)(2,1)S(1)} collective-permute-done((bf16[256,256]{1,0:T(8,128)(2,1)S(1)}, bf16[256,256]{1,0:T(8,128)(2,1)S(1)}, u32[]{:S(2)}, u32[]{:S(2)}) %collective-permute-start.22) | collective-permute-done | bytes 131104 | tf_op jit(solution)/shard_map/ppermute | solution.py:191
  36.0 1.2 %layer.24 = (bf16[1024,256]{1,0:T(8,128)(2,1)S(1)}, bf16[1024,256]{1,0:T(8,128)(2,1)S(1)}, bf16[256,256]{1,0:T(8,128)(2,1)S(1)}, bf16[256,256]{1,0:T(8,128)(2,1)S(1)}) custom-call(s32[32,128]{1,0:T(8,128)S(1)} %get-tuple-element.111.idx_ref, bf16[1024,256]{1,0:T(8,128)(2,1)S(1)} %get-tuple-element.117.h_ref, ...), custom_call_target="tpu_custom_call" | custom-call | flops 1000000 | bytes 1024 | tf_op jit(solution)/shard_map/layer/pallas_call | solution.py:249
  37.2 0.1 collective-permute-start.23
  37.3 3.0 %collective-permute-start.24 = (bf16[256,256]{1,0:T(8,128)(2,1)S(1)}, bf16[256,256]{1,0:T(8,128)(2,1)S(1)}, u32[]{:S(2)}, u32[]{:S(2)}) collective-permute-start(bf16[256,256]{1,0:T(8,128)(2,1)S(1)} %get-tuple-element.124), channel_id=1, source_target_pairs={{0,31},{1,2},{2,1},{3,4},{4,3},{5,6},{6,5},{7,8},{8,7},{9,10},{10,... | collective-permute-start | bytes 393224 | tf_op jit(solution)/shard_map/ppermute | solution.py:191
  40.3 1.2 %layer.17 = (bf16[1024,256]{1,0:T(8,128)(2,1)S(1)}, bf16[1024,256]{1,0:T(8,128)(2,1)S(1)}, bf16[256,256]{1,0:T(8,128)(2,1)S(1)}, bf16[256,256]{1,0:T(8,128)(2,1)S(1)}) custom-call(s32[32,128]{1,0:T(8,128)S(1)} %get-tuple-element.76.idx_ref, bf16[1024,256]{1,0:T(8,128)(2,1)S(1)} %get-tuple-element.83.h_ref, bf16[1024,256]{1,0:T(8,128)(2,1)S(1)} %get-tuple-element.84.nrm_ref, ...), custom_call_target="tpu_custom_call" | custom-call | flops 1000000 | bytes 1024 | tf_op jit(solution)/shard_map/layer/pallas_call | solution.py:249
  41.5 0.1 collective-permute-start.8
  41.6 2.2 %collective-permute-start.9 = (bf16[256,256]{1,0:T(8,128)(2,1)S(1)}, bf16[256,256]{1,0:T(8,128)(2,1)S(1)}, u32[]{:S(2)}, u32[]{:S(2)}) collective-permute-start(bf16[256,256]{1,0:T(8,128)(2,1)S(1)} %get-tuple-element.90), channel_id=1, source_target_pairs={{0,31},{1,2},{2,1},{3,4},{4,3},{5,6},{6,5},{7,8},{8,7},{9,10},{10,... | collective-permute-start | bytes 393224 | tf_op jit(solution)/shard_map/ppermute | solution.py:191
  43.9 1.2 %collective-permute-done.24.off_in = bf16[256,256]{1,0:T(8,128)(2,1)S(1)} collective-permute-done((bf16[256,256]{1,0:T(8,128)(2,1)S(1)}, bf16[256,256]{1,0:T(8,128)(2,1)S(1)}, u32[]{:S(2)}, u32[]{:S(2)}) %collective-permute-start.24) | collective-permute-done | bytes 131104 | tf_op jit(solution)/shard_map/ppermute | solution.py:191
  45.1 1.2 %layer.25 = (bf16[1024,256]{1,0:T(8,128)(2,1)S(1)}, bf16[1024,256]{1,0:T(8,128)(2,1)S(1)}, bf16[256,256]{1,0:T(8,128)(2,1)S(1)}, bf16[256,256]{1,0:T(8,128)(2,1)S(1)}) custom-call(s32[32,128]{1,0:T(8,128)S(1)} %get-tuple-element.111.idx_ref, bf16[1024,256]{1,0:T(8,128)(2,1)S(1)} %get-tuple-element.121.h_ref, ...), custom_call_target="tpu_custom_call" | custom-call | flops 1000000 | bytes 1024 | tf_op jit(solution)/shard_map/layer/pallas_call | solution.py:249
  46.3 0.1 collective-permute-start.25
  46.4 3.2 %collective-permute-start.26 = (bf16[256,256]{1,0:T(8,128)(2,1)S(1)}, bf16[256,256]{1,0:T(8,128)(2,1)S(1)}, u32[]{:S(2)}, u32[]{:S(2)}) collective-permute-start(bf16[256,256]{1,0:T(8,128)(2,1)S(1)} %get-tuple-element.128), channel_id=1, source_target_pairs={{0,31},{1,2},{2,1},{3,4},{4,3},{5,6},{6,5},{7,8},{8,7},{9,10},{10,... | collective-permute-start | bytes 393224 | tf_op jit(solution)/shard_map/ppermute | solution.py:191
  49.6 1.2 %layer.18 = (bf16[1024,256]{1,0:T(8,128)(2,1)S(1)}, bf16[1024,256]{1,0:T(8,128)(2,1)S(1)}, bf16[256,256]{1,0:T(8,128)(2,1)S(1)}, bf16[256,256]{1,0:T(8,128)(2,1)S(1)}) custom-call(s32[32,128]{1,0:T(8,128)S(1)} %get-tuple-element.76.idx_ref, bf16[1024,256]{1,0:T(8,128)(2,1)S(1)} %get-tuple-element.87.h_ref, bf16[1024,256]{1,0:T(8,128)(2,1)S(1)} %get-tuple-element.88.nrm_ref, ...), custom_call_target="tpu_custom_call" | custom-call | flops 1000000 | bytes 1024 | tf_op jit(solution)/shard_map/layer/pallas_call | solution.py:249
  50.8 0.1 collective-permute-start.10
  50.9 2.2 %collective-permute-start.11 = (bf16[256,256]{1,0:T(8,128)(2,1)S(1)}, bf16[256,256]{1,0:T(8,128)(2,1)S(1)}, u32[]{:S(2)}, u32[]{:S(2)}) collective-permute-start(bf16[256,256]{1,0:T(8,128)(2,1)S(1)} %get-tuple-element.94), channel_id=1, source_target_pairs={{0,31},{1,2},{2,1},{3,4},{4,3},{5,6},{6,5},{7,8},{8,7},{9,10},{10,... | collective-permute-start | bytes 393224 | tf_op jit(solution)/shard_map/ppermute | solution.py:191
  53.2 1.2 %collective-permute-done.26.off_in = bf16[256,256]{1,0:T(8,128)(2,1)S(1)} collective-permute-done((bf16[256,256]{1,0:T(8,128)(2,1)S(1)}, bf16[256,256]{1,0:T(8,128)(2,1)S(1)}, u32[]{:S(2)}, u32[]{:S(2)}) %collective-permute-start.26) | collective-permute-done | bytes 131104 | tf_op jit(solution)/shard_map/ppermute | solution.py:191
  54.4 1.2 %layer.26 = (bf16[1024,256]{1,0:T(8,128)(2,1)S(1)}, bf16[1024,256]{1,0:T(8,128)(2,1)S(1)}, bf16[256,256]{1,0:T(8,128)(2,1)S(1)}, bf16[256,256]{1,0:T(8,128)(2,1)S(1)}) custom-call(s32[32,128]{1,0:T(8,128)S(1)} %get-tuple-element.111.idx_ref, bf16[1024,256]{1,0:T(8,128)(2,1)S(1)} %get-tuple-element.125.h_ref, ...), custom_call_target="tpu_custom_call" | custom-call | flops 1000000 | bytes 1024 | tf_op jit(solution)/shard_map/layer/pallas_call | solution.py:249
  55.6 0.1 collective-permute-start.27
  55.7 3.0 %collective-permute-start.28 = (bf16[256,256]{1,0:T(8,128)(2,1)S(1)}, bf16[256,256]{1,0:T(8,128)(2,1)S(1)}, u32[]{:S(2)}, u32[]{:S(2)}) collective-permute-start(bf16[256,256]{1,0:T(8,128)(2,1)S(1)} %get-tuple-element.132), channel_id=1, source_target_pairs={{0,31},{1,2},{2,1},{3,4},{4,3},{5,6},{6,5},{7,8},{8,7},{9,10},{10,... | collective-permute-start | bytes 393224 | tf_op jit(solution)/shard_map/ppermute | solution.py:191
  58.7 1.2 %layer.19 = (bf16[1024,256]{1,0:T(8,128)(2,1)S(1)}, bf16[1024,256]{1,0:T(8,128)(2,1)S(1)}, bf16[256,256]{1,0:T(8,128)(2,1)S(1)}, bf16[256,256]{1,0:T(8,128)(2,1)S(1)}) custom-call(s32[32,128]{1,0:T(8,128)S(1)} %get-tuple-element.76.idx_ref, bf16[1024,256]{1,0:T(8,128)(2,1)S(1)} %get-tuple-element.91.h_ref, bf16[1024,256]{1,0:T(8,128)(2,1)S(1)} %get-tuple-element.92.nrm_ref, ...), custom_call_target="tpu_custom_call" | custom-call | flops 1000000 | bytes 1024 | tf_op jit(solution)/shard_map/layer/pallas_call | solution.py:249
  60.0 0.1 collective-permute-start.12
  60.1 2.2 %collective-permute-start.13 = (bf16[256,256]{1,0:T(8,128)(2,1)S(1)}, bf16[256,256]{1,0:T(8,128)(2,1)S(1)}, u32[]{:S(2)}, u32[]{:S(2)}) collective-permute-start(bf16[256,256]{1,0:T(8,128)(2,1)S(1)} %get-tuple-element.98), channel_id=1, source_target_pairs={{0,31},{1,2},{2,1},{3,4},{4,3},{5,6},{6,5},{7,8},{8,7},{9,10},{10,... | collective-permute-start | bytes 393224 | tf_op jit(solution)/shard_map/ppermute | solution.py:191
  62.3 1.2 %collective-permute-done.28.off_in = bf16[256,256]{1,0:T(8,128)(2,1)S(1)} collective-permute-done((bf16[256,256]{1,0:T(8,128)(2,1)S(1)}, bf16[256,256]{1,0:T(8,128)(2,1)S(1)}, u32[]{:S(2)}, u32[]{:S(2)}) %collective-permute-start.28) | collective-permute-done | bytes 131104 | tf_op jit(solution)/shard_map/ppermute | solution.py:191
  63.5 1.2 %layer.27 = (bf16[1024,256]{1,0:T(8,128)(2,1)S(1)}, bf16[1024,256]{1,0:T(8,128)(2,1)S(1)}, bf16[256,256]{1,0:T(8,128)(2,1)S(1)}, bf16[256,256]{1,0:T(8,128)(2,1)S(1)}) custom-call(s32[32,128]{1,0:T(8,128)S(1)} %get-tuple-element.111.idx_ref, bf16[1024,256]{1,0:T(8,128)(2,1)S(1)} %get-tuple-element.129.h_ref, ...), custom_call_target="tpu_custom_call" | custom-call | flops 1000000 | bytes 1024 | tf_op jit(solution)/shard_map/layer/pallas_call | solution.py:249
  64.8 0.1 collective-permute-start.29
  64.9 3.0 %collective-permute-start.30 = (bf16[256,256]{1,0:T(8,128)(2,1)S(1)}, bf16[256,256]{1,0:T(8,128)(2,1)S(1)}, u32[]{:S(2)}, u32[]{:S(2)}) collective-permute-start(bf16[256,256]{1,0:T(8,128)(2,1)S(1)} %get-tuple-element.136), channel_id=1, source_target_pairs={{0,31},{1,2},{2,1},{3,4},{4,3},{5,6},{6,5},{7,8},{8,7},{9,10},{10,... | collective-permute-start | bytes 393224 | tf_op jit(solution)/shard_map/ppermute | solution.py:191
  67.9 1.2 %layer.20 = (bf16[1024,256]{1,0:T(8,128)(2,1)S(1)}, bf16[1024,256]{1,0:T(8,128)(2,1)S(1)}, bf16[256,256]{1,0:T(8,128)(2,1)S(1)}, bf16[256,256]{1,0:T(8,128)(2,1)S(1)}) custom-call(s32[32,128]{1,0:T(8,128)S(1)} %get-tuple-element.76.idx_ref, bf16[1024,256]{1,0:T(8,128)(2,1)S(1)} %get-tuple-element.95.h_ref, bf16[1024,256]{1,0:T(8,128)(2,1)S(1)} %get-tuple-element.96.nrm_ref, ...), custom_call_target="tpu_custom_call" | custom-call | flops 1000000 | bytes 1024 | tf_op jit(solution)/shard_map/layer/pallas_call | solution.py:249
  69.1 0.1 collective-permute-start.14
  69.2 2.2 %collective-permute-start.15 = (bf16[256,256]{1,0:T(8,128)(2,1)S(1)}, bf16[256,256]{1,0:T(8,128)(2,1)S(1)}, u32[]{:S(2)}, u32[]{:S(2)}) collective-permute-start(bf16[256,256]{1,0:T(8,128)(2,1)S(1)} %get-tuple-element.102), channel_id=1, source_target_pairs={{0,31},{1,2},{2,1},{3,4},{4,3},{5,6},{6,5},{7,8},{8,7},{9,10},{10,... | collective-permute-start | bytes 393224 | tf_op jit(solution)/shard_map/ppermute | solution.py:191
  71.4 1.2 %collective-permute-done.30.off_in = bf16[256,256]{1,0:T(8,128)(2,1)S(1)} collective-permute-done((bf16[256,256]{1,0:T(8,128)(2,1)S(1)}, bf16[256,256]{1,0:T(8,128)(2,1)S(1)}, u32[]{:S(2)}, u32[]{:S(2)}) %collective-permute-start.30) | collective-permute-done | bytes 131104 | tf_op jit(solution)/shard_map/ppermute | solution.py:191
  72.6 1.2 %layer.28 = (bf16[1024,256]{1,0:T(8,128)(2,1)S(1)}, bf16[1024,256]{1,0:T(8,128)(2,1)S(1)}, bf16[256,256]{1,0:T(8,128)(2,1)S(1)}, bf16[256,256]{1,0:T(8,128)(2,1)S(1)}) custom-call(s32[32,128]{1,0:T(8,128)S(1)} %get-tuple-element.111.idx_ref, bf16[1024,256]{1,0:T(8,128)(2,1)S(1)} %get-tuple-element.133.h_ref, ...), custom_call_target="tpu_custom_call" | custom-call | flops 1000000 | bytes 1024 | tf_op jit(solution)/shard_map/layer/pallas_call | solution.py:249
  74.0 3.0 %collective-permute-start.32 = (bf16[256,256]{1,0:T(8,128)(2,1)S(1)}, bf16[256,256]{1,0:T(8,128)(2,1)S(1)}, u32[]{:S(2)}, u32[]{:S(2)}) collective-permute-start(bf16[256,256]{1,0:T(8,128)(2,1)S(1)} %get-tuple-element.140), channel_id=1, source_target_pairs={{0,31},{1,2},{2,1},{3,4},{4,3},{5,6},{6,5},{7,8},{8,7},{9,10},{10,... | collective-permute-start | bytes 393224 | tf_op jit(solution)/shard_map/ppermute | solution.py:191
  77.0 1.2 %layer.21 = (bf16[1024,256]{1,0:T(8,128)(2,1)S(1)}, bf16[1024,256]{1,0:T(8,128)(2,1)S(1)}, bf16[256,256]{1,0:T(8,128)(2,1)S(1)}, bf16[256,256]{1,0:T(8,128)(2,1)S(1)}) custom-call(s32[32,128]{1,0:T(8,128)S(1)} %get-tuple-element.76.idx_ref, bf16[1024,256]{1,0:T(8,128)(2,1)S(1)} %get-tuple-element.99.h_ref, bf16[1024,256]{1,0:T(8,128)(2,1)S(1)} %get-tuple-element.100.nrm_ref, ...), custom_call_target="tpu_custom_call" | custom-call | flops 1000000 | bytes 1024 | tf_op jit(solution)/shard_map/layer/pallas_call | solution.py:249
  78.3 2.5 %collective-permute-start.17 = (bf16[256,256]{1,0:T(8,128)(2,1)S(1)}, bf16[256,256]{1,0:T(8,128)(2,1)S(1)}, u32[]{:S(2)}, u32[]{:S(2)}) collective-permute-start(bf16[256,256]{1,0:T(8,128)(2,1)S(1)} %get-tuple-element.106), channel_id=1, source_target_pairs={{0,31},{1,2},{2,1},{3,4},{4,3},{5,6},{6,5},{7,8},{8,7},{9,10},{10,... | collective-permute-start | bytes 393224 | tf_op jit(solution)/shard_map/ppermute | solution.py:191
  80.8 1.0 %collective-permute-done.32.off_in = bf16[256,256]{1,0:T(8,128)(2,1)S(1)} collective-permute-done((bf16[256,256]{1,0:T(8,128)(2,1)S(1)}, bf16[256,256]{1,0:T(8,128)(2,1)S(1)}, u32[]{:S(2)}, u32[]{:S(2)}) %collective-permute-start.32) | collective-permute-done | bytes 131104 | tf_op jit(solution)/shard_map/ppermute | solution.py:191
  81.8 1.2 %layer.29 = (bf16[1024,256]{1,0:T(8,128)(2,1)S(1)}, bf16[1024,256]{1,0:T(8,128)(2,1)S(1)}, bf16[256,256]{1,0:T(8,128)(2,1)S(1)}, bf16[256,256]{1,0:T(8,128)(2,1)S(1)}) custom-call(s32[32,128]{1,0:T(8,128)S(1)} %get-tuple-element.111.idx_ref, bf16[1024,256]{1,0:T(8,128)(2,1)S(1)} %get-tuple-element.137.h_ref, ...), custom_call_target="tpu_custom_call" | custom-call | flops 1000000 | bytes 1024 | tf_op jit(solution)/shard_map/layer/pallas_call | solution.py:249
  83.1 3.0 %collective-permute-start.34 = (bf16[256,256]{1,0:T(8,128)(2,1)S(1)}, bf16[256,256]{1,0:T(8,128)(2,1)S(1)}, u32[]{:S(2)}, u32[]{:S(2)}) collective-permute-start(bf16[256,256]{1,0:T(8,128)(2,1)S(1)} %get-tuple-element.144), channel_id=1, source_target_pairs={{0,31},{1,2},{2,1},{3,4},{4,3},{5,6},{6,5},{7,8},{8,7},{9,10},{10,... | collective-permute-start | bytes 393224 | tf_op jit(solution)/shard_map/ppermute | solution.py:191
  86.1 0.2 collective-permute-done.17.off_in
  86.3 1.2 %layer.22 = (bf16[1024,256]{1,0:T(8,128)(2,1)S(1)}, bf16[1024,256]{1,0:T(8,128)(2,1)S(1)}, bf16[256,256]{1,0:T(8,128)(2,1)S(1)}, bf16[256,256]{1,0:T(8,128)(2,1)S(1)}) custom-call(s32[32,128]{1,0:T(8,128)S(1)} %get-tuple-element.76.idx_ref, bf16[1024,256]{1,0:T(8,128)(2,1)S(1)} %get-tuple-element.103.h_ref, ...), custom_call_target="tpu_custom_call" | custom-call | flops 1000000 | bytes 1024 | tf_op jit(solution)/shard_map/layer/pallas_call | solution.py:249
  87.6 2.2 %collective-permute-start.19 = (bf16[256,256]{1,0:T(8,128)(2,1)S(1)}, bf16[256,256]{1,0:T(8,128)(2,1)S(1)}, u32[]{:S(2)}, u32[]{:S(2)}) collective-permute-start(bf16[256,256]{1,0:T(8,128)(2,1)S(1)} %get-tuple-element.110), channel_id=1, source_target_pairs={{0,31},{1,2},{2,1},{3,4},{4,3},{5,6},{6,5},{7,8},{8,7},{9,10},{10,... | collective-permute-start | bytes 393224 | tf_op jit(solution)/shard_map/ppermute | solution.py:191
  89.9 1.0 %collective-permute-done.34.off_in = bf16[256,256]{1,0:T(8,128)(2,1)S(1)} collective-permute-done((bf16[256,256]{1,0:T(8,128)(2,1)S(1)}, bf16[256,256]{1,0:T(8,128)(2,1)S(1)}, u32[]{:S(2)}, u32[]{:S(2)}) %collective-permute-start.34) | collective-permute-done | bytes 131104 | tf_op jit(solution)/shard_map/ppermute | solution.py:191
  90.9 0.7 layer.30.rest_0_
  91.6 3.8 %collective-permute-done.19.off_in = bf16[256,256]{1,0:T(8,128)(2,1)S(1)} collective-permute-done((bf16[256,256]{1,0:T(8,128)(2,1)S(1)}, bf16[256,256]{1,0:T(8,128)(2,1)S(1)}, u32[]{:S(2)}, u32[]{:S(2)}) %collective-permute-start.19) | collective-permute-done | bytes 131104 | tf_op jit(solution)/shard_map/ppermute | solution.py:191
  95.4 1.5 %layer.31 = bf16[2,1024,256]{2,1,0:T(8,128)(2,1)} custom-call(s32[32,128]{1,0:T(8,128)S(1)} %get-tuple-element.76.idx_ref, bf16[1024,256]{1,0:T(8,128)(2,1)S(1)} %get-tuple-element.107.h_ref, bf16[1024,256]{1,0:T(8,128)(2,1)S(1)} %get-tuple-element.108.nrm_ref, bf16[256,256]{1,0:T(8,128)(2,1)S(1)} %collective-permute-done.18.on_in, ...), custom_call_target="tpu_custom_call" | custom-call | flops 1000000 | bytes 1024 | tf_op jit(solution)/shard_map/layer/pallas_call | solution.py:249
  (31 shorter events, 0.4 us)
Async XLA Ops:
  2.1 1.4 %collective-permute-start = (bf16[256,256]{1,0:T(8,128)(2,1)S(1)}, bf16[256,256]{1,0:T(8,128)(2,1)S(1)}, u32[]{:S(2)}, u32[]{:S(2)}) collective-permute-start(bf16[256,256]{1,0:T(8,128)(2,1)S(1)} %get-tuple-element.75), channel_id=1, source_target_pairs={{0,1},{1,0},{2,3},{3,2},{4,5},{5,4},{6,7},{7,6},{8,9},{9,8},{10,11... | collective-permute-start | bytes 393224 | tf_op jit(solution)/shard_map/ppermute | solution.py:191
  3.6 1.0 copy-start
  4.5 0.7 copy-start.1
  5.3 15.7 %collective-permute-start.5 = (bf16[2,256,256]{2,1,0:T(8,128)(2,1)S(1)}, bf16[2,256,256]{2,1,0:T(8,128)(2,1)S(1)}, u32[]{:S(2)}, u32[]{:S(2)}) collective-permute-start(bf16[2,256,256]{2,1,0:T(8,128)(2,1)S(1)} %scale.1.refs_0_), channel_id=1, source_target_pairs={{0,96},{32,0},{64,32},{96,64},{1,97},{33,1},{65,33},{97,65},{2,98}... | collective-permute-start | bytes 786440 | tf_op jit(solution)/shard_map/ppermute | solution.py:221
  9.5 17.2 %collective-permute-start.4 = (bf16[2,256,256]{2,1,0:T(8,128)(2,1)S(1)}, bf16[2,256,256]{2,1,0:T(8,128)(2,1)S(1)}, u32[]{:S(2)}, u32[]{:S(2)}) collective-permute-start(bf16[2,256,256]{2,1,0:T(8,128)(2,1)S(1)} %scale.1.refs_0_), channel_id=1, source_target_pairs={{0,64},{32,96},{64,0},{96,32},{1,65},{33,97},{65,1},{97,33},{2,66}... | collective-permute-start | bytes 786440 | tf_op jit(solution)/shard_map/ppermute | solution.py:221
  9.5 17.2 %collective-permute-start.3 = (bf16[2,256,256]{2,1,0:T(8,128)(2,1)S(1)}, bf16[2,256,256]{2,1,0:T(8,128)(2,1)S(1)}, u32[]{:S(2)}, u32[]{:S(2)}) collective-permute-start(bf16[2,256,256]{2,1,0:T(8,128)(2,1)S(1)} %scale.1.refs_0_), channel_id=1, source_target_pairs={{0,32},{32,64},{64,96},{96,0},{1,33},{33,65},{65,97},{97,1},{2,34}... | collective-permute-start | bytes 786440 | tf_op jit(solution)/shard_map/ppermute | solution.py:221
  10.8 16.1 %collective-permute-start.20 = (bf16[256,256]{1,0:T(8,128)(2,1)S(1)}, bf16[256,256]{1,0:T(8,128)(2,1)S(1)}, u32[]{:S(2)}, u32[]{:S(2)}) collective-permute-start(bf16[256,256]{1,0:T(8,128)(2,1)S(1)} %get-tuple-element.114), channel_id=1, source_target_pairs={{0,31},{1,2},{2,1},{3,4},{4,3},{5,6},{6,5},{7,8},{8,7},{9,10},{10,... | collective-permute-start | bytes 393224 | tf_op jit(solution)/shard_map/ppermute | solution.py:191
  17.1 14.1 %collective-permute-start.1 = (bf16[256,256]{1,0:T(8,128)(2,1)S(1)}, bf16[256,256]{1,0:T(8,128)(2,1)S(1)}, u32[]{:S(2)}, u32[]{:S(2)}) collective-permute-start(bf16[256,256]{1,0:T(8,128)(2,1)S(1)} %get-tuple-element.79), channel_id=1, source_target_pairs={{0,1},{1,0},{2,3},{3,2},{4,5},{5,4},{6,7},{7,6},{8,9},{9,8},{10,11... | collective-permute-start | bytes 393224 | tf_op jit(solution)/shard_map/ppermute | solution.py:191
  21.0 10.2 %collective-permute-start.2 = (bf16[256,256]{1,0:T(8,128)(2,1)S(1)}, bf16[256,256]{1,0:T(8,128)(2,1)S(1)}, u32[]{:S(2)}, u32[]{:S(2)}) collective-permute-start(bf16[256,256]{1,0:T(8,128)(2,1)S(1)} %get-tuple-element.80), channel_id=1, source_target_pairs={{0,31},{1,2},{2,1},{3,4},{4,3},{5,6},{6,5},{7,8},{8,7},{9,10},{10,... | collective-permute-start | bytes 393224 | tf_op jit(solution)/shard_map/ppermute | solution.py:191
  28.1 6.7 %collective-permute-start.21 = (bf16[256,256]{1,0:T(8,128)(2,1)S(1)}, bf16[256,256]{1,0:T(8,128)(2,1)S(1)}, u32[]{:S(2)}, u32[]{:S(2)}) collective-permute-start(bf16[256,256]{1,0:T(8,128)(2,1)S(1)} %get-tuple-element.119), channel_id=1, source_target_pairs={{0,1},{1,0},{2,3},{3,2},{4,5},{5,4},{6,7},{7,6},{8,9},{9,8},{10,11... | collective-permute-start | bytes 393224 | tf_op jit(solution)/shard_map/ppermute | solution.py:191
  28.2 7.8 %collective-permute-start.22 = (bf16[256,256]{1,0:T(8,128)(2,1)S(1)}, bf16[256,256]{1,0:T(8,128)(2,1)S(1)}, u32[]{:S(2)}, u32[]{:S(2)}) collective-permute-start(bf16[256,256]{1,0:T(8,128)(2,1)S(1)} %get-tuple-element.120), channel_id=1, source_target_pairs={{0,31},{1,2},{2,1},{3,4},{4,3},{5,6},{6,5},{7,8},{8,7},{9,10},{10,... | collective-permute-start | bytes 393224 | tf_op jit(solution)/shard_map/ppermute | solution.py:191
  32.4 7.9 %collective-permute-start.6 = (bf16[256,256]{1,0:T(8,128)(2,1)S(1)}, bf16[256,256]{1,0:T(8,128)(2,1)S(1)}, u32[]{:S(2)}, u32[]{:S(2)}) collective-permute-start(bf16[256,256]{1,0:T(8,128)(2,1)S(1)} %get-tuple-element.85), channel_id=1, source_target_pairs={{0,1},{1,0},{2,3},{3,2},{4,5},{5,4},{6,7},{7,6},{8,9},{9,8},{10,11... | collective-permute-start | bytes 393224 | tf_op jit(solution)/shard_map/ppermute | solution.py:191
  32.5 7.8 %collective-permute-start.7 = (bf16[256,256]{1,0:T(8,128)(2,1)S(1)}, bf16[256,256]{1,0:T(8,128)(2,1)S(1)}, u32[]{:S(2)}, u32[]{:S(2)}) collective-permute-start(bf16[256,256]{1,0:T(8,128)(2,1)S(1)} %get-tuple-element.86), channel_id=1, source_target_pairs={{0,31},{1,2},{2,1},{3,4},{4,3},{5,6},{6,5},{7,8},{8,7},{9,10},{10,... | collective-permute-start | bytes 393224 | tf_op jit(solution)/shard_map/ppermute | solution.py:191
  37.2 6.7 %collective-permute-start.23 = (bf16[256,256]{1,0:T(8,128)(2,1)S(1)}, bf16[256,256]{1,0:T(8,128)(2,1)S(1)}, u32[]{:S(2)}, u32[]{:S(2)}) collective-permute-start(bf16[256,256]{1,0:T(8,128)(2,1)S(1)} %get-tuple-element.123), channel_id=1, source_target_pairs={{0,1},{1,0},{2,3},{3,2},{4,5},{5,4},{6,7},{7,6},{8,9},{9,8},{10,11... | collective-permute-start | bytes 393224 | tf_op jit(solution)/shard_map/ppermute | solution.py:191
  37.3 7.8 %collective-permute-start.24 = (bf16[256,256]{1,0:T(8,128)(2,1)S(1)}, bf16[256,256]{1,0:T(8,128)(2,1)S(1)}, u32[]{:S(2)}, u32[]{:S(2)}) collective-permute-start(bf16[256,256]{1,0:T(8,128)(2,1)S(1)} %get-tuple-element.124), channel_id=1, source_target_pairs={{0,31},{1,2},{2,1},{3,4},{4,3},{5,6},{6,5},{7,8},{8,7},{9,10},{10,... | collective-permute-start | bytes 393224 | tf_op jit(solution)/shard_map/ppermute | solution.py:191
  41.5 8.1 %collective-permute-start.8 = (bf16[256,256]{1,0:T(8,128)(2,1)S(1)}, bf16[256,256]{1,0:T(8,128)(2,1)S(1)}, u32[]{:S(2)}, u32[]{:S(2)}) collective-permute-start(bf16[256,256]{1,0:T(8,128)(2,1)S(1)} %get-tuple-element.89), channel_id=1, source_target_pairs={{0,1},{1,0},{2,3},{3,2},{4,5},{5,4},{6,7},{7,6},{8,9},{9,8},{10,11... | collective-permute-start | bytes 393224 | tf_op jit(solution)/shard_map/ppermute | solution.py:191
  41.6 8.0 %collective-permute-start.9 = (bf16[256,256]{1,0:T(8,128)(2,1)S(1)}, bf16[256,256]{1,0:T(8,128)(2,1)S(1)}, u32[]{:S(2)}, u32[]{:S(2)}) collective-permute-start(bf16[256,256]{1,0:T(8,128)(2,1)S(1)} %get-tuple-element.90), channel_id=1, source_target_pairs={{0,31},{1,2},{2,1},{3,4},{4,3},{5,6},{6,5},{7,8},{8,7},{9,10},{10,... | collective-permute-start | bytes 393224 | tf_op jit(solution)/shard_map/ppermute | solution.py:191
  46.3 6.8 %collective-permute-start.25 = (bf16[256,256]{1,0:T(8,128)(2,1)S(1)}, bf16[256,256]{1,0:T(8,128)(2,1)S(1)}, u32[]{:S(2)}, u32[]{:S(2)}) collective-permute-start(bf16[256,256]{1,0:T(8,128)(2,1)S(1)} %get-tuple-element.127), channel_id=1, source_target_pairs={{0,1},{1,0},{2,3},{3,2},{4,5},{5,4},{6,7},{7,6},{8,9},{9,8},{10,11... | collective-permute-start | bytes 393224 | tf_op jit(solution)/shard_map/ppermute | solution.py:191
  46.4 8.0 %collective-permute-start.26 = (bf16[256,256]{1,0:T(8,128)(2,1)S(1)}, bf16[256,256]{1,0:T(8,128)(2,1)S(1)}, u32[]{:S(2)}, u32[]{:S(2)}) collective-permute-start(bf16[256,256]{1,0:T(8,128)(2,1)S(1)} %get-tuple-element.128), channel_id=1, source_target_pairs={{0,31},{1,2},{2,1},{3,4},{4,3},{5,6},{6,5},{7,8},{8,7},{9,10},{10,... | collective-permute-start | bytes 393224 | tf_op jit(solution)/shard_map/ppermute | solution.py:191
  50.8 7.9 %collective-permute-start.10 = (bf16[256,256]{1,0:T(8,128)(2,1)S(1)}, bf16[256,256]{1,0:T(8,128)(2,1)S(1)}, u32[]{:S(2)}, u32[]{:S(2)}) collective-permute-start(bf16[256,256]{1,0:T(8,128)(2,1)S(1)} %get-tuple-element.93), channel_id=1, source_target_pairs={{0,1},{1,0},{2,3},{3,2},{4,5},{5,4},{6,7},{7,6},{8,9},{9,8},{10,11... | collective-permute-start | bytes 393224 | tf_op jit(solution)/shard_map/ppermute | solution.py:191
  50.9 7.8 %collective-permute-start.11 = (bf16[256,256]{1,0:T(8,128)(2,1)S(1)}, bf16[256,256]{1,0:T(8,128)(2,1)S(1)}, u32[]{:S(2)}, u32[]{:S(2)}) collective-permute-start(bf16[256,256]{1,0:T(8,128)(2,1)S(1)} %get-tuple-element.94), channel_id=1, source_target_pairs={{0,31},{1,2},{2,1},{3,4},{4,3},{5,6},{6,5},{7,8},{8,7},{9,10},{10,... | collective-permute-start | bytes 393224 | tf_op jit(solution)/shard_map/ppermute | solution.py:191
  55.6 6.7 %collective-permute-start.27 = (bf16[256,256]{1,0:T(8,128)(2,1)S(1)}, bf16[256,256]{1,0:T(8,128)(2,1)S(1)}, u32[]{:S(2)}, u32[]{:S(2)}) collective-permute-start(bf16[256,256]{1,0:T(8,128)(2,1)S(1)} %get-tuple-element.131), channel_id=1, source_target_pairs={{0,1},{1,0},{2,3},{3,2},{4,5},{5,4},{6,7},{7,6},{8,9},{9,8},{10,11... | collective-permute-start | bytes 393224 | tf_op jit(solution)/shard_map/ppermute | solution.py:191
  55.7 7.8 %collective-permute-start.28 = (bf16[256,256]{1,0:T(8,128)(2,1)S(1)}, bf16[256,256]{1,0:T(8,128)(2,1)S(1)}, u32[]{:S(2)}, u32[]{:S(2)}) collective-permute-start(bf16[256,256]{1,0:T(8,128)(2,1)S(1)} %get-tuple-element.132), channel_id=1, source_target_pairs={{0,31},{1,2},{2,1},{3,4},{4,3},{5,6},{6,5},{7,8},{8,7},{9,10},{10,... | collective-permute-start | bytes 393224 | tf_op jit(solution)/shard_map/ppermute | solution.py:191
  60.0 7.9 %collective-permute-start.12 = (bf16[256,256]{1,0:T(8,128)(2,1)S(1)}, bf16[256,256]{1,0:T(8,128)(2,1)S(1)}, u32[]{:S(2)}, u32[]{:S(2)}) collective-permute-start(bf16[256,256]{1,0:T(8,128)(2,1)S(1)} %get-tuple-element.97), channel_id=1, source_target_pairs={{0,1},{1,0},{2,3},{3,2},{4,5},{5,4},{6,7},{7,6},{8,9},{9,8},{10,11... | collective-permute-start | bytes 393224 | tf_op jit(solution)/shard_map/ppermute | solution.py:191
  60.1 7.8 %collective-permute-start.13 = (bf16[256,256]{1,0:T(8,128)(2,1)S(1)}, bf16[256,256]{1,0:T(8,128)(2,1)S(1)}, u32[]{:S(2)}, u32[]{:S(2)}) collective-permute-start(bf16[256,256]{1,0:T(8,128)(2,1)S(1)} %get-tuple-element.98), channel_id=1, source_target_pairs={{0,31},{1,2},{2,1},{3,4},{4,3},{5,6},{6,5},{7,8},{8,7},{9,10},{10,... | collective-permute-start | bytes 393224 | tf_op jit(solution)/shard_map/ppermute | solution.py:191
  64.8 6.7 %collective-permute-start.29 = (bf16[256,256]{1,0:T(8,128)(2,1)S(1)}, bf16[256,256]{1,0:T(8,128)(2,1)S(1)}, u32[]{:S(2)}, u32[]{:S(2)}) collective-permute-start(bf16[256,256]{1,0:T(8,128)(2,1)S(1)} %get-tuple-element.135), channel_id=1, source_target_pairs={{0,1},{1,0},{2,3},{3,2},{4,5},{5,4},{6,7},{7,6},{8,9},{9,8},{10,11... | collective-permute-start | bytes 393224 | tf_op jit(solution)/shard_map/ppermute | solution.py:191
  64.9 7.8 %collective-permute-start.30 = (bf16[256,256]{1,0:T(8,128)(2,1)S(1)}, bf16[256,256]{1,0:T(8,128)(2,1)S(1)}, u32[]{:S(2)}, u32[]{:S(2)}) collective-permute-start(bf16[256,256]{1,0:T(8,128)(2,1)S(1)} %get-tuple-element.136), channel_id=1, source_target_pairs={{0,31},{1,2},{2,1},{3,4},{4,3},{5,6},{6,5},{7,8},{8,7},{9,10},{10,... | collective-permute-start | bytes 393224 | tf_op jit(solution)/shard_map/ppermute | solution.py:191
  69.1 7.9 %collective-permute-start.14 = (bf16[256,256]{1,0:T(8,128)(2,1)S(1)}, bf16[256,256]{1,0:T(8,128)(2,1)S(1)}, u32[]{:S(2)}, u32[]{:S(2)}) collective-permute-start(bf16[256,256]{1,0:T(8,128)(2,1)S(1)} %get-tuple-element.101), channel_id=1, source_target_pairs={{0,1},{1,0},{2,3},{3,2},{4,5},{5,4},{6,7},{7,6},{8,9},{9,8},{10,11... | collective-permute-start | bytes 393224 | tf_op jit(solution)/shard_map/ppermute | solution.py:191
  69.2 7.8 %collective-permute-start.15 = (bf16[256,256]{1,0:T(8,128)(2,1)S(1)}, bf16[256,256]{1,0:T(8,128)(2,1)S(1)}, u32[]{:S(2)}, u32[]{:S(2)}) collective-permute-start(bf16[256,256]{1,0:T(8,128)(2,1)S(1)} %get-tuple-element.102), channel_id=1, source_target_pairs={{0,31},{1,2},{2,1},{3,4},{4,3},{5,6},{6,5},{7,8},{8,7},{9,10},{10,... | collective-permute-start | bytes 393224 | tf_op jit(solution)/shard_map/ppermute | solution.py:191
  73.9 6.9 %collective-permute-start.31 = (bf16[256,256]{1,0:T(8,128)(2,1)S(1)}, bf16[256,256]{1,0:T(8,128)(2,1)S(1)}, u32[]{:S(2)}, u32[]{:S(2)}) collective-permute-start(bf16[256,256]{1,0:T(8,128)(2,1)S(1)} %get-tuple-element.139), channel_id=1, source_target_pairs={{0,1},{1,0},{2,3},{3,2},{4,5},{5,4},{6,7},{7,6},{8,9},{9,8},{10,11... | collective-permute-start | bytes 393224 | tf_op jit(solution)/shard_map/ppermute | solution.py:191
  74.0 7.8 %collective-permute-start.32 = (bf16[256,256]{1,0:T(8,128)(2,1)S(1)}, bf16[256,256]{1,0:T(8,128)(2,1)S(1)}, u32[]{:S(2)}, u32[]{:S(2)}) collective-permute-start(bf16[256,256]{1,0:T(8,128)(2,1)S(1)} %get-tuple-element.140), channel_id=1, source_target_pairs={{0,31},{1,2},{2,1},{3,4},{4,3},{5,6},{6,5},{7,8},{8,7},{9,10},{10,... | collective-permute-start | bytes 393224 | tf_op jit(solution)/shard_map/ppermute | solution.py:191
  78.2 7.9 %collective-permute-start.16 = (bf16[256,256]{1,0:T(8,128)(2,1)S(1)}, bf16[256,256]{1,0:T(8,128)(2,1)S(1)}, u32[]{:S(2)}, u32[]{:S(2)}) collective-permute-start(bf16[256,256]{1,0:T(8,128)(2,1)S(1)} %get-tuple-element.105), channel_id=1, source_target_pairs={{0,1},{1,0},{2,3},{3,2},{4,5},{5,4},{6,7},{7,6},{8,9},{9,8},{10,11... | collective-permute-start | bytes 393224 | tf_op jit(solution)/shard_map/ppermute | solution.py:191
  78.3 8.0 %collective-permute-start.17 = (bf16[256,256]{1,0:T(8,128)(2,1)S(1)}, bf16[256,256]{1,0:T(8,128)(2,1)S(1)}, u32[]{:S(2)}, u32[]{:S(2)}) collective-permute-start(bf16[256,256]{1,0:T(8,128)(2,1)S(1)} %get-tuple-element.106), channel_id=1, source_target_pairs={{0,31},{1,2},{2,1},{3,4},{4,3},{5,6},{6,5},{7,8},{8,7},{9,10},{10,... | collective-permute-start | bytes 393224 | tf_op jit(solution)/shard_map/ppermute | solution.py:191
  83.0 6.9 %collective-permute-start.33 = (bf16[256,256]{1,0:T(8,128)(2,1)S(1)}, bf16[256,256]{1,0:T(8,128)(2,1)S(1)}, u32[]{:S(2)}, u32[]{:S(2)}) collective-permute-start(bf16[256,256]{1,0:T(8,128)(2,1)S(1)} %get-tuple-element.143), channel_id=1, source_target_pairs={{0,1},{1,0},{2,3},{3,2},{4,5},{5,4},{6,7},{7,6},{8,9},{9,8},{10,11... | collective-permute-start | bytes 393224 | tf_op jit(solution)/shard_map/ppermute | solution.py:191
  83.1 7.8 %collective-permute-start.34 = (bf16[256,256]{1,0:T(8,128)(2,1)S(1)}, bf16[256,256]{1,0:T(8,128)(2,1)S(1)}, u32[]{:S(2)}, u32[]{:S(2)}) collective-permute-start(bf16[256,256]{1,0:T(8,128)(2,1)S(1)} %get-tuple-element.144), channel_id=1, source_target_pairs={{0,31},{1,2},{2,1},{3,4},{4,3},{5,6},{6,5},{7,8},{8,7},{9,10},{10,... | collective-permute-start | bytes 393224 | tf_op jit(solution)/shard_map/ppermute | solution.py:191
  87.5 4.0 %collective-permute-start.18 = (bf16[256,256]{1,0:T(8,128)(2,1)S(1)}, bf16[256,256]{1,0:T(8,128)(2,1)S(1)}, u32[]{:S(2)}, u32[]{:S(2)}) collective-permute-start(bf16[256,256]{1,0:T(8,128)(2,1)S(1)} %get-tuple-element.109), channel_id=1, source_target_pairs={{0,1},{1,0},{2,3},{3,2},{4,5},{5,4},{6,7},{7,6},{8,9},{9,8},{10,11... | collective-permute-start | bytes 393224 | tf_op jit(solution)/shard_map/ppermute | solution.py:191
  87.6 7.8 %collective-permute-start.19 = (bf16[256,256]{1,0:T(8,128)(2,1)S(1)}, bf16[256,256]{1,0:T(8,128)(2,1)S(1)}, u32[]{:S(2)}, u32[]{:S(2)}) collective-permute-start(bf16[256,256]{1,0:T(8,128)(2,1)S(1)} %get-tuple-element.110), channel_id=1, source_target_pairs={{0,31},{1,2},{2,1},{3,4},{4,3},{5,6},{6,5},{7,8},{8,7},{9,10},{10,... | collective-permute-start | bytes 393224 | tf_op jit(solution)/shard_map/ppermute | solution.py:191

commit v2 on v1

--- a/solution.py
+++ b/solution.py
@@ -62,63 +62,80 @@
     return copies
 
 
-def prologue_body(local, per_section, early, *refs):
-    feat, rows_hbm, count_hbm, src_hbm = refs[:4]
-    refs = refs[4 + early :]
-    h_ref, nrm_ref, sel_ref, on_ref, off_ref, idx_ref = refs[:6]
-    rows_ref, count_ref, src_ref, sems, feat_sems = refs[6:]
-    graph, parity = graph_of(local, per_section), dom_parity()
+def prologue_body(per_section, *refs):
+    feat, rows_hbm, count_hbm, src_hbm, val_hbm, w_hbm, gain_hbm = refs[:7]
+    graph_outs = [refs[7 + 6 * g : 13 + 6 * g] for g in range(per_section)]
+    scaled_ref, *tables = refs[7 + 6 * per_section : 8 + 7 * per_section]
+    rows_all, count_ref, src_all, w_ref, gain_ref, sems, small_sems, feat_sems, val_sems = refs[8 + 7 * per_section :]
+    even = dom_parity() == 0
+    graphs = [graph_of(g, per_section) for g in range(per_section)]
+    count_copy = pltpu.make_async_copy(count_hbm, count_ref, sems.at[0])
+    count_copy.start()
     small = [
-        pltpu.make_async_copy(rows_hbm.at[graph], rows_ref, sems.at[0]),
-        pltpu.make_async_copy(count_hbm, count_ref, sems.at[1]),
-        pltpu.make_async_copy(src_hbm.at[graph], src_ref, sems.at[2]),
+        [
+            pltpu.make_async_copy(rows_hbm.at[graph], rows_all.at[g], small_sems.at[g, 0]),
+            pltpu.make_async_copy(src_hbm.at[graph], src_all.at[g], small_sems.at[g, 1]),
+        ]
+        for g, graph in enumerate(graphs)
     ]
-    for copy in small:
+    for pair in small:
+        for copy in pair:
+            copy.start()
+    feat_copies = [
+        chunked(feat.at[graph], graph_outs[g][0], feat_sems.at[g]) for g, graph in enumerate(graphs)
+    ]
+    later = [
+        pltpu.make_async_copy(gain_hbm, gain_ref, sems.at[1]),
+        pltpu.make_async_copy(w_hbm, w_ref, sems.at[2]),
+    ]
+    for copy in later:
         copy.start()
-    copies = chunked(feat.at[graph], h_ref, feat_sems)
-    for copy in small:
+    val_copies = []
+    for g, graph in enumerate(graphs):
+        val_copies += chunked(val_hbm.at[graph], graph_outs[g][5], val_sems.at[g])
+    count_copy.wait()
+    for g, graph in enumerate(graphs):
+        h_ref, nrm_ref, sel_ref, on_ref, off_ref, _ = graph_outs[g]
+        rows_dev = h_ref.shape[0]
+        bnd = on_ref.shape[0]
+        own, half = rows_dev // TILE, bnd // TILE
+        for copy in small[g]:
+            copy.wait()
+        counts = count_ref[...]
+        here = lax.broadcasted_iota(jnp.int32, counts.shape, 1) == graph
+        live = jnp.sum(jnp.where(here, counts, 0), axis=1, keepdims=True)
+        raw = rows_all[g]
+        lane = lax.broadcasted_iota(jnp.int32, raw.shape, 1)
+        rows = jnp.where(lane < live, raw, -1).astype(F32)
+        first = jnp.broadcast_to(rows[0:1, :], (TILE, bnd))
+        second = jnp.broadcast_to(rows[1:2, :], (TILE, bnd))
+        for at, picked in ((0, jnp.where(even, second, first)), (bnd, jnp.where(even, first, second))):
+            column = picked.T
+            for c in range(rows_dev // TILE):
+                ids = lax.broadcasted_iota(jnp.int32, (bnd, TILE), 1) + c * TILE
+                hit = column == ids.astype(F32)
+                sel_ref[at : at + bnd, c * TILE : (c + 1) * TILE] = jnp.where(hit, 1.0, 0.0).astype(BF)
+        t = src_all[g]
+        left = jnp.where(even, own + half, own)
+        right = jnp.where(even, own, own + half)
+        table = jnp.where(t < half, left + t, jnp.where(t < half + own, t - half, right + t - half - own))
+        for i in range(own):
+            for k in range(K):
+                tables[g][i * K + k : i * K + k + 1, :] = jnp.broadcast_to(table[k : k + 1, i : i + 1], (1, TILE))
+        for c, copy in enumerate(feat_copies[g]):
+            copy.wait()
+            step = rows_dev // len(feat_copies[g])
+            block = slice(c * step, (c + 1) * step)
+            nrm_ref[block, :] = normalise(h_ref[block, :].astype(F32))
+        send_rows(sel_ref, nrm_ref, on_ref, off_ref)
+    for copy in later:
         copy.wait()
-    rows_dev = h_ref.shape[0]
-    bnd = on_ref.shape[0]
-    own, half = rows_dev // TILE, bnd // TILE
-    counts = count_ref[...]
-    here = lax.broadcasted_iota(jnp.int32, counts.shape, 1) == graph
-    live = jnp.sum(jnp.where(here, counts, 0), axis=1, keepdims=True)
-    lane = lax.broadcasted_iota(jnp.int32, rows_ref.shape, 1)
-    rows = jnp.where(lane < live, rows_ref[...], -1).astype(F32)
-    first = jnp.broadcast_to(rows[0:1, :], (TILE, bnd))
-    second = jnp.broadcast_to(rows[1:2, :], (TILE, bnd))
-    even = parity == 0
-    for at, picked in ((0, jnp.where(even, second, first)), (bnd, jnp.where(even, first, second))):
-        column = picked.T
-        for c in range(rows_dev // TILE):
-            ids = lax.broadcasted_iota(jnp.int32, (bnd, TILE), 1) + c * TILE
-            hit = column == ids.astype(F32)
-            sel_ref[at : at + bnd, c * TILE : (c + 1) * TILE] = jnp.where(hit, 1.0, 0.0).astype(BF)
-    t = src_ref[...]
-    left = jnp.where(even, own + half, own)
-    right = jnp.where(even, own, own + half)
-    table = jnp.where(t < half, left + t, jnp.where(t < half + own, t - half, right + t - half - own))
-    for i in range(own):
-        for k in range(K):
-            idx_ref[i * K + k : i * K + k + 1, :] = jnp.broadcast_to(table[k : k + 1, i : i + 1], (1, TILE))
-    for c, copy in enumerate(copies):
+    scale(w_ref, gain_ref, scaled_ref)
+    for copy in val_copies:
         copy.wait()
-        block = slice(c * rows_dev // len(copies), (c + 1) * rows_dev // len(copies))
-        nrm_ref[block, :] = normalise(h_ref[block, :].astype(F32))
-    send_rows(sel_ref, nrm_ref, on_ref, off_ref)
-
-
-def fetch_body(per_section, val_ref, after_ref, *refs):
-    outs, sems = refs[:per_section], refs[per_section]
-    copies = []
-    for g, out in enumerate(outs):
-        copies += chunked(val_ref.at[graph_of(g, per_section)], out, sems.at[g])
-    for copy in copies:
-        copy.wait()
-
-
-def scale_body(w_ref, gain_ref, after_ref, out_ref):
+
+
+def scale(w_ref, gain_ref, out_ref):
     width = w_ref.shape[1]
     gain = gain_ref[...].astype(F32)
     for k in range(w_ref.shape[0]):
@@ -126,8 +143,12 @@
         out_ref[k] = (w_ref[k].astype(F32) * column).astype(BF)
 
 
+def gate_body(after_ref, out_ref):
+    out_ref[...] = after_ref[: out_ref.shape[0], : out_ref.shape[1]]
+
+
 def order_body(count, *refs):
-    parts, out = refs[:count], refs[count]
+    parts, out = refs[:count], refs[-1]
     section = lax.axis_index("section")
     per = parts[0].shape[0]
     for shift, part in enumerate(parts):
@@ -192,45 +213,48 @@
 
     tile_src = jnp.swapaxes(tile_src, 1, 2)
     boundary_count = jnp.swapaxes(boundary_count, 0, 1)
-    features, tile_val, boundary_rows, boundary_count, tile_src = (
+    features, tile_val, boundary_rows, boundary_count, tile_src, weights, gains = (
         pltpu.with_memory_space_constraint(x, pltpu.HBM)
-        for x in (features, tile_val, boundary_rows, boundary_count, tile_src)
+        for x in (features, tile_val, boundary_rows, boundary_count, tile_src, weights, gains)
     )
-    state = []
-    early = ()
+    per_graph = [(rows_dev, width), (rows_dev, width), (2 * bnd, rows_dev), (bnd, width), (bnd, width)]
+    per_graph += [(rows_dev, K * TILE)]
+    results = call(
+        functools.partial(prologue_body, per_section),
+        per_graph * per_section + [weights.shape],
+        [HBM] * 7,
+        "prologue",
+        [
+            pltpu.VMEM((per_section, 2, bnd), jnp.int32),
+            pltpu.VMEM((2, graphs), jnp.int32),
+            pltpu.VMEM((per_section, K, tiles), jnp.int32),
+            pltpu.VMEM(weights.shape, BF),
+            pltpu.VMEM(gains.shape, BF),
+            pltpu.SemaphoreType.DMA((3,)),
+            pltpu.SemaphoreType.DMA((per_section, 2)),
+            pltpu.SemaphoreType.DMA((per_section, 4)),
+            pltpu.SemaphoreType.DMA((per_section, 4)),
+        ],
+        limit=16,
+        ints=[(tiles * K, TILE)] * per_section,
+    )(features, boundary_rows, boundary_count, tile_src, tile_val, weights, gains)
+    scaled, *tables = results[6 * per_section :]
+    state, values = [], []
     for g in range(per_section):
-        h, nrm, sel, on, off, idx = call(
-            functools.partial(prologue_body, g, per_section, len(early)),
-            [(rows_dev, width), (rows_dev, width), (2 * bnd, rows_dev), (bnd, width), (bnd, width)],
-            [HBM] * 4 + [VMEM] * len(early),
-            "prologue",
-            [
-                pltpu.VMEM((2, bnd), jnp.int32),
-                pltpu.VMEM((2, graphs), jnp.int32),
-                pltpu.VMEM((K, tiles), jnp.int32),
-                pltpu.SemaphoreType.DMA((3,)),
-                pltpu.SemaphoreType.DMA((4,)),
-            ],
-            ints=[(tiles * K, TILE)],
-        )(features, boundary_rows, boundary_count, tile_src, *early)
-        on, off = exchange(on, off)
-        state.append([h, nrm, on, off, sel, idx])
-        early = (state[0][2],)
-    scaled = call(scale_body, [weights.shape], [VMEM] * 3, "scale")(weights, gains, *early)[0]
+        h, nrm, sel, on, off, value = results[6 * g : 6 * g + 6]
+        values.append(value)
+        on = lax.ppermute(on, "dom", on_pairs)
+        off, on = lax.optimization_barrier((off, on))
+        off = lax.ppermute(off, "dom", off_pairs)
+        state.append([h, nrm, on, off, sel, tables[g]])
     parts = [scaled] + [
         lax.ppermute(scaled, "section", [(i, (i + shift) % sections) for i in range(sections)])
         for shift in range(1, sections)
     ]
-    values = call(
-        functools.partial(fetch_body, per_section),
-        [(rows_dev, K * TILE)] * per_section,
-        [HBM, VMEM],
-        "fetch",
-        [pltpu.SemaphoreType.DMA((per_section, 4))],
-    )(tile_val, *early)
-    w_all = call(functools.partial(order_body, sections), [(layers, width, width)], [VMEM] * sections, "order")(
-        *parts
-    )[0]
+    gate = call(gate_body, [(16, TILE)], [VMEM], "gate")(state[0][3])[0]
+    w_all = call(
+        functools.partial(order_body, sections), [(layers, width, width)], [VMEM] * (sections + 1), "order"
+    )(*parts, gate)[0]
     outputs = []
     for layer in range(layers):
         last = layer == layers - 1

time: 97.3 us -> 96.3 us (0.990)
  starting transfers between devices: 52 us -> 55 us
  Pallas kernels: 25.4 us -> 23.6 us
  local copies, waits for them, and re-layouts: 1.63 us -> 0 us
    ppermute x0 -> x4, starting transfers between devices: none -> 6.39 us  [the longest x2 6.3 us: on_device(): off = lax.ppermute(off, 'dom', off_pairs)]
    ppermute x16 -> x14, starting transfers between devices: 45.2 us -> 42.1 us  [exchange(): lax.ppermute(off, 'dom', off_pairs)]
    ppermute x16 -> x14, waiting for transfers between devices: 12.3 us -> 9.44 us  [exchange(): lax.ppermute(off, 'dom', off_pairs)]
    ppermute x3, waiting for transfers between devices: 3.88 us -> 5.96 us  [on_device(): lax.ppermute(scaled, 'section', [(i, (i + shift) % sections) for i in ran...]
    pallas_call x4 -> x2, Pallas kernels: 5.98 us -> 4.14 us  [the longest x1 4.13 us: on_device(): call(functools.partial(prologue_body, per_section), per_graph * per_secti...]
    ppermute x0 -> x4, waiting for transfers between devices: none -> 1.67 us  [the longest x2 1.67 us: on_device(): off = lax.ppermute(off, 'dom', off_pairs)]
    unnamed x4 -> x0, local copies, waits for them, and re-layouts: 1.63 us -> none
    ppermute x16 -> x14, waiting for transfers between devices: 1.37 us -> 0.04 us  [exchange(): lax.ppermute(on, 'dom', on_pairs)]
  transfers between devices with their start and end apart: 35 -> 35, of which waited for: 11 -> 12; matrix products, arithmetic and copies ran while one was open for 0% -> 0% of each run, Pallas kernels for 22% -> 19%
where the time goes in v2:
time: 96.3 us; the launch traced here: 96.2 us
  starting transfers between devices  55 us (57%)
  Pallas kernels  23.6 us (25%)
  waiting for transfers between devices  17.1 us (18%)
    ppermute x14, starting transfers between devices, exchange(): lax.ppermute(off, 'dom', off_pairs)  42.1 us
    pallas_call x16, Pallas kernels, on_device(): call(functools.partial(layer_body, layer, last, others), outs, [VMEM] * (...  19.4 us
    ppermute x14, waiting for transfers between devices, exchange(): lax.ppermute(off, 'dom', off_pairs)  9.44 us
    ppermute x2, starting transfers between devices, on_device(): off = lax.ppermute(off, 'dom', off_pairs)  6.3 us
    ppermute x3, waiting for transfers between devices, on_device(): lax.ppermute(scaled, 'section', [(i, (i + shift) % sections) for i in ran...  5.96 us
    ppermute x3, starting transfers between devices, on_device(): lax.ppermute(scaled, 'section', [(i, (i + shift) % sections) for i in ran...  5.35 us
    pallas_call x1, Pallas kernels, on_device(): call(functools.partial(prologue_body, per_section), per_graph * per_secti...  4.13 us
  transfers between devices with their start and end apart: 35, of which 12 were waited for; matrix products, arithmetic and copies ran while one was open for 0% of the time, Pallas kernels for 19%

profile of v2, /device:TPU:0, one launch (start us, length us, event | category | flops | bytes accessed | tf_op | source)
XLA Modules:
  0.0 96.2 jit_solution(11348006759238933064)
XLA Ops:
  0.0 4.1 %prologue.1 = (bf16[1024,256]{1,0:T(8,128)(2,1)S(1)}, bf16[1024,256]{1,0:T(8,128)(2,1)S(1)}, bf16[512,1024]{1,0:T(8,128)(2,1)S(1)}, bf16[256,256]{1,0:T(8,128)(2...) custom-call(bf16[8,1024,256]{2,1,0:T(8,128)(2,1)} %refs_0_.1, ...), custom_call_target="tpu_custom_call" | custom-call | bytes 1024 | tf_op jit(solution)/shard_map/prologue/pallas_call | solution.py:222
  4.1 0.1 collective-permute-start.5
  4.2 4.1 %collective-permute-start.4 = (bf16[2,256,256]{2,1,0:T(8,128)(2,1)S(1)}, bf16[2,256,256]{2,1,0:T(8,128)(2,1)S(1)}, u32[]{:S(2)}, u32[]{:S(2)}) collective-permute-start(bf16[2,256,256]{2,1,0:T(8,128)(2,1)S(1)} %get-tuple-element.89.refs_0_), channel_id=1, source_target_pairs={{0,96},{32,0},{64,32},{96,64},{1,97},{33,1},{65,33},{97,65},{2,98}... | collective-permute-start | bytes 786440 | tf_op jit(solution)/shard_map/ppermute | solution.py:251
  8.3 1.3 %collective-permute-start.2 = (bf16[2,256,256]{2,1,0:T(8,128)(2,1)S(1)}, bf16[2,256,256]{2,1,0:T(8,128)(2,1)S(1)}, u32[]{:S(2)}, u32[]{:S(2)}) collective-permute-start(bf16[2,256,256]{2,1,0:T(8,128)(2,1)S(1)} %get-tuple-element.89.refs_0_), channel_id=1, source_target_pairs={{0,32},{32,64},{64,96},{96,0},{1,33},{33,65},{65,97},{97,1},{2,34}... | collective-permute-start | bytes 786440 | tf_op jit(solution)/shard_map/ppermute | solution.py:251
  9.6 5.3 %collective-permute-start.6 = (bf16[256,256]{1,0:T(8,128)(2,1)S(1)}, bf16[256,256]{1,0:T(8,128)(2,1)S(1)}, u32[]{:S(2)}, u32[]{:S(2)}) collective-permute-start(bf16[256,256]{1,0:T(8,128)(2,1)S(1)} %get-tuple-element.92), channel_id=1, source_target_pairs={{0,31},{1,2},{2,1},{3,4},{4,3},{5,6},{6,5},{7,8},{8,7},{9,10},{10,... | collective-permute-start | bytes 393224 | tf_op jit(solution)/shard_map/ppermute | solution.py:248
  14.9 1.0 %collective-permute-start.1 = (bf16[256,256]{1,0:T(8,128)(2,1)S(1)}, bf16[256,256]{1,0:T(8,128)(2,1)S(1)}, u32[]{:S(2)}, u32[]{:S(2)}) collective-permute-start(bf16[256,256]{1,0:T(8,128)(2,1)S(1)} %get-tuple-element.86), channel_id=1, source_target_pairs={{0,31},{1,2},{2,1},{3,4},{4,3},{5,6},{6,5},{7,8},{8,7},{9,10},{10,... | collective-permute-start | bytes 393224 | tf_op jit(solution)/shard_map/ppermute | solution.py:248
  15.9 1.7 %collective-permute-done.6.after_ref.off_in = bf16[256,256]{1,0:T(8,128)(2,1)S(1)} collective-permute-done((bf16[256,256]{1,0:T(8,128)(2,1)S(1)}, bf16[256,256]{1,0:T(8,128)(2,1)S(1)}, u32[]{:S(2)}, u32[]{:S(2)}) %collective-permute-start.6) | collective-permute-done | bytes 131104 | tf_op jit(solution)/shard_map/ppermute | solution.py:248
  17.6 2.5 %collective-permute-done.4.refs_3_ = bf16[2,256,256]{2,1,0:T(8,128)(2,1)S(1)} collective-permute-done((bf16[2,256,256]{2,1,0:T(8,128)(2,1)S(1)}, bf16[2,256,256]{2,1,0:T(8,128)(2,1)S(1)}, u32[]{:S(2)}, u32[]{:S(2)}) %collective-permute-start.4) | collective-permute-done | bytes 262176 | tf_op jit(solution)/shard_map/ppermute | solution.py:251
  20.1 3.4 %collective-permute-done.2.refs_1_ = bf16[2,256,256]{2,1,0:T(8,128)(2,1)S(1)} collective-permute-done((bf16[2,256,256]{2,1,0:T(8,128)(2,1)S(1)}, bf16[2,256,256]{2,1,0:T(8,128)(2,1)S(1)}, u32[]{:S(2)}, u32[]{:S(2)}) %collective-permute-start.2) | collective-permute-done | bytes 262176 | tf_op jit(solution)/shard_map/ppermute | solution.py:251
  23.5 0.1 order.1.w_ref
  23.6 1.2 %layer.23 = (bf16[1024,256]{1,0:T(8,128)(2,1)S(1)}, bf16[1024,256]{1,0:T(8,128)(2,1)S(1)}, bf16[256,256]{1,0:T(8,128)(2,1)S(1)}, bf16[256,256]{1,0:T(8,128)(2,1)S(1)}) custom-call(s32[32,128]{1,0:T(8,128)S(1)} %get-tuple-element.121.idx_ref, bf16[1024,256]{1,0:T(8,128)(2,1)S(1)} %get-tuple-element.122.h_ref, ...), custom_call_target="tpu_custom_call" | custom-call | flops 1000000 | bytes 1024 | tf_op jit(solution)/shard_map/layer/pallas_call | solution.py:273
  24.9 0.1 collective-permute-start.21
  24.9 5.3 %collective-permute-start.22 = (bf16[256,256]{1,0:T(8,128)(2,1)S(1)}, bf16[256,256]{1,0:T(8,128)(2,1)S(1)}, u32[]{:S(2)}, u32[]{:S(2)}) collective-permute-start(bf16[256,256]{1,0:T(8,128)(2,1)S(1)} %get-tuple-element.130), channel_id=1, source_target_pairs={{0,31},{1,2},{2,1},{3,4},{4,3},{5,6},{6,5},{7,8},{8,7},{9,10},{10,... | collective-permute-start | bytes 393224 | tf_op jit(solution)/shard_map/ppermute | solution.py:212
  30.3 1.2 %layer.16 = (bf16[1024,256]{1,0:T(8,128)(2,1)S(1)}, bf16[1024,256]{1,0:T(8,128)(2,1)S(1)}, bf16[256,256]{1,0:T(8,128)(2,1)S(1)}, bf16[256,256]{1,0:T(8,128)(2,1)S(1)}) custom-call(s32[32,128]{1,0:T(8,128)S(1)} %get-tuple-element.80.idx_ref, bf16[1024,256]{1,0:T(8,128)(2,1)S(1)} %get-tuple-element.81.h_ref, bf16[1024,256]{1,0:T(8,128)(2,1)S(1)} %get-tuple-element.82.nrm_ref, ...), custom_call_target="tpu_custom_call" | custom-call | flops 1000000 | bytes 1024 | tf_op jit(solution)/shard_map/layer/pallas_call | solution.py:273
  31.5 0.1 collective-permute-start.7
  31.6 0.9 collective-permute-start.8
  32.5 0.4 collective-permute-done.22.off_in
  32.9 1.2 %layer.24 = (bf16[1024,256]{1,0:T(8,128)(2,1)S(1)}, bf16[1024,256]{1,0:T(8,128)(2,1)S(1)}, bf16[256,256]{1,0:T(8,128)(2,1)S(1)}, bf16[256,256]{1,0:T(8,128)(2,1)S(1)}) custom-call(s32[32,128]{1,0:T(8,128)S(1)} %get-tuple-element.121.idx_ref, bf16[1024,256]{1,0:T(8,128)(2,1)S(1)} %get-tuple-element.127.h_ref, ...), custom_call_target="tpu_custom_call" | custom-call | flops 1000000 | bytes 1024 | tf_op jit(solution)/shard_map/layer/pallas_call | solution.py:273
  34.1 0.1 collective-permute-start.23
  34.2 5.1 %collective-permute-start.24 = (bf16[256,256]{1,0:T(8,128)(2,1)S(1)}, bf16[256,256]{1,0:T(8,128)(2,1)S(1)}, u32[]{:S(2)}, u32[]{:S(2)}) collective-permute-start(bf16[256,256]{1,0:T(8,128)(2,1)S(1)} %get-tuple-element.134), channel_id=1, source_target_pairs={{0,31},{1,2},{2,1},{3,4},{4,3},{5,6},{6,5},{7,8},{8,7},{9,10},{10,... | collective-permute-start | bytes 393224 | tf_op jit(solution)/shard_map/ppermute | solution.py:212
  39.4 1.2 %layer.17 = (bf16[1024,256]{1,0:T(8,128)(2,1)S(1)}, bf16[1024,256]{1,0:T(8,128)(2,1)S(1)}, bf16[256,256]{1,0:T(8,128)(2,1)S(1)}, bf16[256,256]{1,0:T(8,128)(2,1)S(1)}) custom-call(s32[32,128]{1,0:T(8,128)S(1)} %get-tuple-element.80.idx_ref, bf16[1024,256]{1,0:T(8,128)(2,1)S(1)} %get-tuple-element.93.h_ref, bf16[1024,256]{1,0:T(8,128)(2,1)S(1)} %get-tuple-element.94.nrm_ref, ...), custom_call_target="tpu_custom_call" | custom-call | flops 1000000 | bytes 1024 | tf_op jit(solution)/shard_map/layer/pallas_call | solution.py:273
  40.6 0.1 collective-permute-start.9
  40.7 0.9 collective-permute-start.10
  41.6 0.4 collective-permute-done.24.off_in
  42.0 1.2 %layer.25 = (bf16[1024,256]{1,0:T(8,128)(2,1)S(1)}, bf16[1024,256]{1,0:T(8,128)(2,1)S(1)}, bf16[256,256]{1,0:T(8,128)(2,1)S(1)}, bf16[256,256]{1,0:T(8,128)(2,1)S(1)}) custom-call(s32[32,128]{1,0:T(8,128)S(1)} %get-tuple-element.121.idx_ref, bf16[1024,256]{1,0:T(8,128)(2,1)S(1)} %get-tuple-element.131.h_ref, ...), custom_call_target="tpu_custom_call" | custom-call | flops 1000000 | bytes 1024 | tf_op jit(solution)/shard_map/layer/pallas_call | solution.py:273
  43.3 0.1 collective-permute-start.25
  43.4 5.3 %collective-permute-start.26 = (bf16[256,256]{1,0:T(8,128)(2,1)S(1)}, bf16[256,256]{1,0:T(8,128)(2,1)S(1)}, u32[]{:S(2)}, u32[]{:S(2)}) collective-permute-start(bf16[256,256]{1,0:T(8,128)(2,1)S(1)} %get-tuple-element.138), channel_id=1, source_target_pairs={{0,31},{1,2},{2,1},{3,4},{4,3},{5,6},{6,5},{7,8},{8,7},{9,10},{10,... | collective-permute-start | bytes 393224 | tf_op jit(solution)/shard_map/ppermute | solution.py:212
  48.7 1.2 %layer.18 = (bf16[1024,256]{1,0:T(8,128)(2,1)S(1)}, bf16[1024,256]{1,0:T(8,128)(2,1)S(1)}, bf16[256,256]{1,0:T(8,128)(2,1)S(1)}, bf16[256,256]{1,0:T(8,128)(2,1)S(1)}) custom-call(s32[32,128]{1,0:T(8,128)S(1)} %get-tuple-element.80.idx_ref, bf16[1024,256]{1,0:T(8,128)(2,1)S(1)} %get-tuple-element.97.h_ref, bf16[1024,256]{1,0:T(8,128)(2,1)S(1)} %get-tuple-element.98.nrm_ref, ...), custom_call_target="tpu_custom_call" | custom-call | flops 1000000 | bytes 1024 | tf_op jit(solution)/shard_map/layer/pallas_call | solution.py:273
  49.9 0.1 collective-permute-start.11
  50.0 0.7 collective-permute-start.12
  50.8 0.6 collective-permute-done.26.off_in
  51.3 1.2 %layer.26 = (bf16[1024,256]{1,0:T(8,128)(2,1)S(1)}, bf16[1024,256]{1,0:T(8,128)(2,1)S(1)}, bf16[256,256]{1,0:T(8,128)(2,1)S(1)}, bf16[256,256]{1,0:T(8,128)(2,1)S(1)}) custom-call(s32[32,128]{1,0:T(8,128)S(1)} %get-tuple-element.121.idx_ref, bf16[1024,256]{1,0:T(8,128)(2,1)S(1)} %get-tuple-element.135.h_ref, ...), custom_call_target="tpu_custom_call" | custom-call | flops 1000000 | bytes 1024 | tf_op jit(solution)/shard_map/layer/pallas_call | solution.py:273
  52.6 0.1 collective-permute-start.27
  52.7 5.1 %collective-permute-start.28 = (bf16[256,256]{1,0:T(8,128)(2,1)S(1)}, bf16[256,256]{1,0:T(8,128)(2,1)S(1)}, u32[]{:S(2)}, u32[]{:S(2)}) collective-permute-start(bf16[256,256]{1,0:T(8,128)(2,1)S(1)} %get-tuple-element.142), channel_id=1, source_target_pairs={{0,31},{1,2},{2,1},{3,4},{4,3},{5,6},{6,5},{7,8},{8,7},{9,10},{10,... | collective-permute-start | bytes 393224 | tf_op jit(solution)/shard_map/ppermute | solution.py:212
  57.8 0.0 collective-permute-done.12.off_in
  57.8 1.2 %layer.19 = (bf16[1024,256]{1,0:T(8,128)(2,1)S(1)}, bf16[1024,256]{1,0:T(8,128)(2,1)S(1)}, bf16[256,256]{1,0:T(8,128)(2,1)S(1)}, bf16[256,256]{1,0:T(8,128)(2,1)S(1)}) custom-call(s32[32,128]{1,0:T(8,128)S(1)} %get-tuple-element.80.idx_ref, bf16[1024,256]{1,0:T(8,128)(2,1)S(1)} %get-tuple-element.101.h_ref, ...), custom_call_target="tpu_custom_call" | custom-call | flops 1000000 | bytes 1024 | tf_op jit(solution)/shard_map/layer/pallas_call | solution.py:273
  59.0 0.1 collective-permute-start.13
  59.1 0.7 collective-permute-start.14
  59.9 0.6 collective-permute-done.28.off_in
  60.5 1.2 %layer.27 = (bf16[1024,256]{1,0:T(8,128)(2,1)S(1)}, bf16[1024,256]{1,0:T(8,128)(2,1)S(1)}, bf16[256,256]{1,0:T(8,128)(2,1)S(1)}, bf16[256,256]{1,0:T(8,128)(2,1)S(1)}) custom-call(s32[32,128]{1,0:T(8,128)S(1)} %get-tuple-element.121.idx_ref, bf16[1024,256]{1,0:T(8,128)(2,1)S(1)} %get-tuple-element.139.h_ref, ...), custom_call_target="tpu_custom_call" | custom-call | flops 1000000 | bytes 1024 | tf_op jit(solution)/shard_map/layer/pallas_call | solution.py:273
  61.7 0.1 collective-permute-start.29
  61.8 5.1 %collective-permute-start.30 = (bf16[256,256]{1,0:T(8,128)(2,1)S(1)}, bf16[256,256]{1,0:T(8,128)(2,1)S(1)}, u32[]{:S(2)}, u32[]{:S(2)}) collective-permute-start(bf16[256,256]{1,0:T(8,128)(2,1)S(1)} %get-tuple-element.146), channel_id=1, source_target_pairs={{0,31},{1,2},{2,1},{3,4},{4,3},{5,6},{6,5},{7,8},{8,7},{9,10},{10,... | collective-permute-start | bytes 393224 | tf_op jit(solution)/shard_map/ppermute | solution.py:212
  66.9 1.2 %layer.20 = (bf16[1024,256]{1,0:T(8,128)(2,1)S(1)}, bf16[1024,256]{1,0:T(8,128)(2,1)S(1)}, bf16[256,256]{1,0:T(8,128)(2,1)S(1)}, bf16[256,256]{1,0:T(8,128)(2,1)S(1)}) custom-call(s32[32,128]{1,0:T(8,128)S(1)} %get-tuple-element.80.idx_ref, bf16[1024,256]{1,0:T(8,128)(2,1)S(1)} %get-tuple-element.105.h_ref, ...), custom_call_target="tpu_custom_call" | custom-call | flops 1000000 | bytes 1024 | tf_op jit(solution)/shard_map/layer/pallas_call | solution.py:273
  68.2 0.1 collective-permute-start.15
  68.3 0.7 collective-permute-start.16
  69.0 0.6 collective-permute-done.30.off_in
  69.6 1.2 %layer.28 = (bf16[1024,256]{1,0:T(8,128)(2,1)S(1)}, bf16[1024,256]{1,0:T(8,128)(2,1)S(1)}, bf16[256,256]{1,0:T(8,128)(2,1)S(1)}, bf16[256,256]{1,0:T(8,128)(2,1)S(1)}) custom-call(s32[32,128]{1,0:T(8,128)S(1)} %get-tuple-element.121.idx_ref, bf16[1024,256]{1,0:T(8,128)(2,1)S(1)} %get-tuple-element.143.h_ref, ...), custom_call_target="tpu_custom_call" | custom-call | flops 1000000 | bytes 1024 | tf_op jit(solution)/shard_map/layer/pallas_call | solution.py:273
  70.8 0.1 collective-permute-start.31
  70.9 5.1 %collective-permute-start.32 = (bf16[256,256]{1,0:T(8,128)(2,1)S(1)}, bf16[256,256]{1,0:T(8,128)(2,1)S(1)}, u32[]{:S(2)}, u32[]{:S(2)}) collective-permute-start(bf16[256,256]{1,0:T(8,128)(2,1)S(1)} %get-tuple-element.150), channel_id=1, source_target_pairs={{0,31},{1,2},{2,1},{3,4},{4,3},{5,6},{6,5},{7,8},{8,7},{9,10},{10,... | collective-permute-start | bytes 393224 | tf_op jit(solution)/shard_map/ppermute | solution.py:212
  76.0 1.2 %layer.21 = (bf16[1024,256]{1,0:T(8,128)(2,1)S(1)}, bf16[1024,256]{1,0:T(8,128)(2,1)S(1)}, bf16[256,256]{1,0:T(8,128)(2,1)S(1)}, bf16[256,256]{1,0:T(8,128)(2,1)S(1)}) custom-call(s32[32,128]{1,0:T(8,128)S(1)} %get-tuple-element.80.idx_ref, bf16[1024,256]{1,0:T(8,128)(2,1)S(1)} %get-tuple-element.109.h_ref, ...), custom_call_target="tpu_custom_call" | custom-call | flops 1000000 | bytes 1024 | tf_op jit(solution)/shard_map/layer/pallas_call | solution.py:273
  77.3 0.1 collective-permute-start.17
  77.4 1.0 collective-permute-start.18
  78.3 0.4 collective-permute-done.32.off_in
  78.7 1.2 %layer.29 = (bf16[1024,256]{1,0:T(8,128)(2,1)S(1)}, bf16[1024,256]{1,0:T(8,128)(2,1)S(1)}, bf16[256,256]{1,0:T(8,128)(2,1)S(1)}, bf16[256,256]{1,0:T(8,128)(2,1)S(1)}) custom-call(s32[32,128]{1,0:T(8,128)S(1)} %get-tuple-element.121.idx_ref, bf16[1024,256]{1,0:T(8,128)(2,1)S(1)} %get-tuple-element.147.h_ref, ...), custom_call_target="tpu_custom_call" | custom-call | flops 1000000 | bytes 1024 | tf_op jit(solution)/shard_map/layer/pallas_call | solution.py:273
  79.9 0.1 collective-permute-start.33
  80.0 5.1 %collective-permute-start.34 = (bf16[256,256]{1,0:T(8,128)(2,1)S(1)}, bf16[256,256]{1,0:T(8,128)(2,1)S(1)}, u32[]{:S(2)}, u32[]{:S(2)}) collective-permute-start(bf16[256,256]{1,0:T(8,128)(2,1)S(1)} %get-tuple-element.154), channel_id=1, source_target_pairs={{0,31},{1,2},{2,1},{3,4},{4,3},{5,6},{6,5},{7,8},{8,7},{9,10},{10,... | collective-permute-start | bytes 393224 | tf_op jit(solution)/shard_map/ppermute | solution.py:212
  85.2 0.2 collective-permute-done.18.off_in
  85.4 1.2 %layer.22 = (bf16[1024,256]{1,0:T(8,128)(2,1)S(1)}, bf16[1024,256]{1,0:T(8,128)(2,1)S(1)}, bf16[256,256]{1,0:T(8,128)(2,1)S(1)}, bf16[256,256]{1,0:T(8,128)(2,1)S(1)}) custom-call(s32[32,128]{1,0:T(8,128)S(1)} %get-tuple-element.80.idx_ref, bf16[1024,256]{1,0:T(8,128)(2,1)S(1)} %get-tuple-element.113.h_ref, ...), custom_call_target="tpu_custom_call" | custom-call | flops 1000000 | bytes 1024 | tf_op jit(solution)/shard_map/layer/pallas_call | solution.py:273
  86.6 0.1 collective-permute-start.19
  86.7 0.7 collective-permute-start.20
  87.5 0.4 collective-permute-done.34.off_in
  87.8 0.7 layer.30.rest_0_
  88.5 6.0 %collective-permute-done.20.off_in = bf16[256,256]{1,0:T(8,128)(2,1)S(1)} collective-permute-done((bf16[256,256]{1,0:T(8,128)(2,1)S(1)}, bf16[256,256]{1,0:T(8,128)(2,1)S(1)}, u32[]{:S(2)}, u32[]{:S(2)}) %collective-permute-start.20) | collective-permute-done | bytes 131104 | tf_op jit(solution)/shard_map/ppermute | solution.py:212
  94.5 1.5 %layer.31 = bf16[2,1024,256]{2,1,0:T(8,128)(2,1)} custom-call(s32[32,128]{1,0:T(8,128)S(1)} %get-tuple-element.80.idx_ref, bf16[1024,256]{1,0:T(8,128)(2,1)S(1)} %get-tuple-element.117.h_ref, bf16[1024,256]{1,0:T(8,128)(2,1)S(1)} %get-tuple-element.118.nrm_ref, bf16[256,256]{1,0:T(8,128)(2,1)S(1)} %collective-permute-done.19.on_in, ...), custom_call_target="tpu_custom_call" | custom-call | flops 1000000 | bytes 1024 | tf_op jit(solution)/shard_map/layer/pallas_call | solution.py:273
  (25 shorter events, 0.1 us)
Async XLA Ops:
  4.1 5.4 %collective-permute-start.5 = (bf16[256,256]{1,0:T(8,128)(2,1)S(1)}, bf16[256,256]{1,0:T(8,128)(2,1)S(1)}, u32[]{:S(2)}, u32[]{:S(2)}) collective-permute-start(bf16[256,256]{1,0:T(8,128)(2,1)S(1)} %get-tuple-element.91), channel_id=1, source_target_pairs={{0,1},{1,0},{2,3},{3,2},{4,5},{5,4},{6,7},{7,6},{8,9},{9,8},{10,11... | collective-permute-start | bytes 393224 | tf_op jit(solution)/shard_map/ppermute | solution.py:246
  4.2 15.9 %collective-permute-start.4 = (bf16[2,256,256]{2,1,0:T(8,128)(2,1)S(1)}, bf16[2,256,256]{2,1,0:T(8,128)(2,1)S(1)}, u32[]{:S(2)}, u32[]{:S(2)}) collective-permute-start(bf16[2,256,256]{2,1,0:T(8,128)(2,1)S(1)} %get-tuple-element.89.refs_0_), channel_id=1, source_target_pairs={{0,96},{32,0},{64,32},{96,64},{1,97},{33,1},{65,33},{97,65},{2,98}... | collective-permute-start | bytes 786440 | tf_op jit(solution)/shard_map/ppermute | solution.py:251
  8.3 11.8 %collective-permute-start.3 = (bf16[2,256,256]{2,1,0:T(8,128)(2,1)S(1)}, bf16[2,256,256]{2,1,0:T(8,128)(2,1)S(1)}, u32[]{:S(2)}, u32[]{:S(2)}) collective-permute-start(bf16[2,256,256]{2,1,0:T(8,128)(2,1)S(1)} %get-tuple-element.89.refs_0_), channel_id=1, source_target_pairs={{0,64},{32,96},{64,0},{96,32},{1,65},{33,97},{65,1},{97,33},{2,66}... | collective-permute-start | bytes 786440 | tf_op jit(solution)/shard_map/ppermute | solution.py:251
  8.3 15.2 %collective-permute-start.2 = (bf16[2,256,256]{2,1,0:T(8,128)(2,1)S(1)}, bf16[2,256,256]{2,1,0:T(8,128)(2,1)S(1)}, u32[]{:S(2)}, u32[]{:S(2)}) collective-permute-start(bf16[2,256,256]{2,1,0:T(8,128)(2,1)S(1)} %get-tuple-element.89.refs_0_), channel_id=1, source_target_pairs={{0,32},{32,64},{64,96},{96,0},{1,33},{33,65},{65,97},{97,1},{2,34}... | collective-permute-start | bytes 786440 | tf_op jit(solution)/shard_map/ppermute | solution.py:251
  9.6 5.3 %collective-permute-start = (bf16[256,256]{1,0:T(8,128)(2,1)S(1)}, bf16[256,256]{1,0:T(8,128)(2,1)S(1)}, u32[]{:S(2)}, u32[]{:S(2)}) collective-permute-start(bf16[256,256]{1,0:T(8,128)(2,1)S(1)} %get-tuple-element.84), channel_id=1, source_target_pairs={{0,1},{1,0},{2,3},{3,2},{4,5},{5,4},{6,7},{7,6},{8,9},{9,8},{10,11... | collective-permute-start | bytes 393224 | tf_op jit(solution)/shard_map/ppermute | solution.py:246
  9.6 8.0 %collective-permute-start.6 = (bf16[256,256]{1,0:T(8,128)(2,1)S(1)}, bf16[256,256]{1,0:T(8,128)(2,1)S(1)}, u32[]{:S(2)}, u32[]{:S(2)}) collective-permute-start(bf16[256,256]{1,0:T(8,128)(2,1)S(1)} %get-tuple-element.92), channel_id=1, source_target_pairs={{0,31},{1,2},{2,1},{3,4},{4,3},{5,6},{6,5},{7,8},{8,7},{9,10},{10,... | collective-permute-start | bytes 393224 | tf_op jit(solution)/shard_map/ppermute | solution.py:248
  14.9 15.3 %collective-permute-start.1 = (bf16[256,256]{1,0:T(8,128)(2,1)S(1)}, bf16[256,256]{1,0:T(8,128)(2,1)S(1)}, u32[]{:S(2)}, u32[]{:S(2)}) collective-permute-start(bf16[256,256]{1,0:T(8,128)(2,1)S(1)} %get-tuple-element.86), channel_id=1, source_target_pairs={{0,31},{1,2},{2,1},{3,4},{4,3},{5,6},{6,5},{7,8},{8,7},{9,10},{10,... | collective-permute-start | bytes 393224 | tf_op jit(solution)/shard_map/ppermute | solution.py:248
  24.9 7.7 %collective-permute-start.21 = (bf16[256,256]{1,0:T(8,128)(2,1)S(1)}, bf16[256,256]{1,0:T(8,128)(2,1)S(1)}, u32[]{:S(2)}, u32[]{:S(2)}) collective-permute-start(bf16[256,256]{1,0:T(8,128)(2,1)S(1)} %get-tuple-element.129), channel_id=1, source_target_pairs={{0,1},{1,0},{2,3},{3,2},{4,5},{5,4},{6,7},{7,6},{8,9},{9,8},{10,11... | collective-permute-start | bytes 393224 | tf_op jit(solution)/shard_map/ppermute | solution.py:212
  24.9 8.0 %collective-permute-start.22 = (bf16[256,256]{1,0:T(8,128)(2,1)S(1)}, bf16[256,256]{1,0:T(8,128)(2,1)S(1)}, u32[]{:S(2)}, u32[]{:S(2)}) collective-permute-start(bf16[256,256]{1,0:T(8,128)(2,1)S(1)} %get-tuple-element.130), channel_id=1, source_target_pairs={{0,31},{1,2},{2,1},{3,4},{4,3},{5,6},{6,5},{7,8},{8,7},{9,10},{10,... | collective-permute-start | bytes 393224 | tf_op jit(solution)/shard_map/ppermute | solution.py:212
  31.5 7.9 %collective-permute-start.7 = (bf16[256,256]{1,0:T(8,128)(2,1)S(1)}, bf16[256,256]{1,0:T(8,128)(2,1)S(1)}, u32[]{:S(2)}, u32[]{:S(2)}) collective-permute-start(bf16[256,256]{1,0:T(8,128)(2,1)S(1)} %get-tuple-element.95), channel_id=1, source_target_pairs={{0,1},{1,0},{2,3},{3,2},{4,5},{5,4},{6,7},{7,6},{8,9},{9,8},{10,11... | collective-permute-start | bytes 393224 | tf_op jit(solution)/shard_map/ppermute | solution.py:212
  31.6 7.8 %collective-permute-start.8 = (bf16[256,256]{1,0:T(8,128)(2,1)S(1)}, bf16[256,256]{1,0:T(8,128)(2,1)S(1)}, u32[]{:S(2)}, u32[]{:S(2)}) collective-permute-start(bf16[256,256]{1,0:T(8,128)(2,1)S(1)} %get-tuple-element.96), channel_id=1, source_target_pairs={{0,31},{1,2},{2,1},{3,4},{4,3},{5,6},{6,5},{7,8},{8,7},{9,10},{10,... | collective-permute-start | bytes 393224 | tf_op jit(solution)/shard_map/ppermute | solution.py:212
  34.1 7.5 %collective-permute-start.23 = (bf16[256,256]{1,0:T(8,128)(2,1)S(1)}, bf16[256,256]{1,0:T(8,128)(2,1)S(1)}, u32[]{:S(2)}, u32[]{:S(2)}) collective-permute-start(bf16[256,256]{1,0:T(8,128)(2,1)S(1)} %get-tuple-element.133), channel_id=1, source_target_pairs={{0,1},{1,0},{2,3},{3,2},{4,5},{5,4},{6,7},{7,6},{8,9},{9,8},{10,11... | collective-permute-start | bytes 393224 | tf_op jit(solution)/shard_map/ppermute | solution.py:212
  34.2 7.8 %collective-permute-start.24 = (bf16[256,256]{1,0:T(8,128)(2,1)S(1)}, bf16[256,256]{1,0:T(8,128)(2,1)S(1)}, u32[]{:S(2)}, u32[]{:S(2)}) collective-permute-start(bf16[256,256]{1,0:T(8,128)(2,1)S(1)} %get-tuple-element.134), channel_id=1, source_target_pairs={{0,31},{1,2},{2,1},{3,4},{4,3},{5,6},{6,5},{7,8},{8,7},{9,10},{10,... | collective-permute-start | bytes 393224 | tf_op jit(solution)/shard_map/ppermute | solution.py:212
  40.6 8.1 %collective-permute-start.9 = (bf16[256,256]{1,0:T(8,128)(2,1)S(1)}, bf16[256,256]{1,0:T(8,128)(2,1)S(1)}, u32[]{:S(2)}, u32[]{:S(2)}) collective-permute-start(bf16[256,256]{1,0:T(8,128)(2,1)S(1)} %get-tuple-element.99), channel_id=1, source_target_pairs={{0,1},{1,0},{2,3},{3,2},{4,5},{5,4},{6,7},{7,6},{8,9},{9,8},{10,11... | collective-permute-start | bytes 393224 | tf_op jit(solution)/shard_map/ppermute | solution.py:212
  40.7 8.0 %collective-permute-start.10 = (bf16[256,256]{1,0:T(8,128)(2,1)S(1)}, bf16[256,256]{1,0:T(8,128)(2,1)S(1)}, u32[]{:S(2)}, u32[]{:S(2)}) collective-permute-start(bf16[256,256]{1,0:T(8,128)(2,1)S(1)} %get-tuple-element.100), channel_id=1, source_target_pairs={{0,31},{1,2},{2,1},{3,4},{4,3},{5,6},{6,5},{7,8},{8,7},{9,10},{10,... | collective-permute-start | bytes 393224 | tf_op jit(solution)/shard_map/ppermute | solution.py:212
  43.3 7.5 %collective-permute-start.25 = (bf16[256,256]{1,0:T(8,128)(2,1)S(1)}, bf16[256,256]{1,0:T(8,128)(2,1)S(1)}, u32[]{:S(2)}, u32[]{:S(2)}) collective-permute-start(bf16[256,256]{1,0:T(8,128)(2,1)S(1)} %get-tuple-element.137), channel_id=1, source_target_pairs={{0,1},{1,0},{2,3},{3,2},{4,5},{5,4},{6,7},{7,6},{8,9},{9,8},{10,11... | collective-permute-start | bytes 393224 | tf_op jit(solution)/shard_map/ppermute | solution.py:212
  43.4 8.0 %collective-permute-start.26 = (bf16[256,256]{1,0:T(8,128)(2,1)S(1)}, bf16[256,256]{1,0:T(8,128)(2,1)S(1)}, u32[]{:S(2)}, u32[]{:S(2)}) collective-permute-start(bf16[256,256]{1,0:T(8,128)(2,1)S(1)} %get-tuple-element.138), channel_id=1, source_target_pairs={{0,31},{1,2},{2,1},{3,4},{4,3},{5,6},{6,5},{7,8},{8,7},{9,10},{10,... | collective-permute-start | bytes 393224 | tf_op jit(solution)/shard_map/ppermute | solution.py:212
  49.9 7.9 %collective-permute-start.11 = (bf16[256,256]{1,0:T(8,128)(2,1)S(1)}, bf16[256,256]{1,0:T(8,128)(2,1)S(1)}, u32[]{:S(2)}, u32[]{:S(2)}) collective-permute-start(bf16[256,256]{1,0:T(8,128)(2,1)S(1)} %get-tuple-element.103), channel_id=1, source_target_pairs={{0,1},{1,0},{2,3},{3,2},{4,5},{5,4},{6,7},{7,6},{8,9},{9,8},{10,11... | collective-permute-start | bytes 393224 | tf_op jit(solution)/shard_map/ppermute | solution.py:212
  50.0 7.8 %collective-permute-start.12 = (bf16[256,256]{1,0:T(8,128)(2,1)S(1)}, bf16[256,256]{1,0:T(8,128)(2,1)S(1)}, u32[]{:S(2)}, u32[]{:S(2)}) collective-permute-start(bf16[256,256]{1,0:T(8,128)(2,1)S(1)} %get-tuple-element.104), channel_id=1, source_target_pairs={{0,31},{1,2},{2,1},{3,4},{4,3},{5,6},{6,5},{7,8},{8,7},{9,10},{10,... | collective-permute-start | bytes 393224 | tf_op jit(solution)/shard_map/ppermute | solution.py:212
  52.6 7.3 %collective-permute-start.27 = (bf16[256,256]{1,0:T(8,128)(2,1)S(1)}, bf16[256,256]{1,0:T(8,128)(2,1)S(1)}, u32[]{:S(2)}, u32[]{:S(2)}) collective-permute-start(bf16[256,256]{1,0:T(8,128)(2,1)S(1)} %get-tuple-element.141), channel_id=1, source_target_pairs={{0,1},{1,0},{2,3},{3,2},{4,5},{5,4},{6,7},{7,6},{8,9},{9,8},{10,11... | collective-permute-start | bytes 393224 | tf_op jit(solution)/shard_map/ppermute | solution.py:212
  52.7 7.8 %collective-permute-start.28 = (bf16[256,256]{1,0:T(8,128)(2,1)S(1)}, bf16[256,256]{1,0:T(8,128)(2,1)S(1)}, u32[]{:S(2)}, u32[]{:S(2)}) collective-permute-start(bf16[256,256]{1,0:T(8,128)(2,1)S(1)} %get-tuple-element.142), channel_id=1, source_target_pairs={{0,31},{1,2},{2,1},{3,4},{4,3},{5,6},{6,5},{7,8},{8,7},{9,10},{10,... | collective-permute-start | bytes 393224 | tf_op jit(solution)/shard_map/ppermute | solution.py:212
  59.0 7.9 %collective-permute-start.13 = (bf16[256,256]{1,0:T(8,128)(2,1)S(1)}, bf16[256,256]{1,0:T(8,128)(2,1)S(1)}, u32[]{:S(2)}, u32[]{:S(2)}) collective-permute-start(bf16[256,256]{1,0:T(8,128)(2,1)S(1)} %get-tuple-element.107), channel_id=1, source_target_pairs={{0,1},{1,0},{2,3},{3,2},{4,5},{5,4},{6,7},{7,6},{8,9},{9,8},{10,11... | collective-permute-start | bytes 393224 | tf_op jit(solution)/shard_map/ppermute | solution.py:212
  59.1 7.8 %collective-permute-start.14 = (bf16[256,256]{1,0:T(8,128)(2,1)S(1)}, bf16[256,256]{1,0:T(8,128)(2,1)S(1)}, u32[]{:S(2)}, u32[]{:S(2)}) collective-permute-start(bf16[256,256]{1,0:T(8,128)(2,1)S(1)} %get-tuple-element.108), channel_id=1, source_target_pairs={{0,31},{1,2},{2,1},{3,4},{4,3},{5,6},{6,5},{7,8},{8,7},{9,10},{10,... | collective-permute-start | bytes 393224 | tf_op jit(solution)/shard_map/ppermute | solution.py:212
  61.7 7.3 %collective-permute-start.29 = (bf16[256,256]{1,0:T(8,128)(2,1)S(1)}, bf16[256,256]{1,0:T(8,128)(2,1)S(1)}, u32[]{:S(2)}, u32[]{:S(2)}) collective-permute-start(bf16[256,256]{1,0:T(8,128)(2,1)S(1)} %get-tuple-element.145), channel_id=1, source_target_pairs={{0,1},{1,0},{2,3},{3,2},{4,5},{5,4},{6,7},{7,6},{8,9},{9,8},{10,11... | collective-permute-start | bytes 393224 | tf_op jit(solution)/shard_map/ppermute | solution.py:212
  61.8 7.8 %collective-permute-start.30 = (bf16[256,256]{1,0:T(8,128)(2,1)S(1)}, bf16[256,256]{1,0:T(8,128)(2,1)S(1)}, u32[]{:S(2)}, u32[]{:S(2)}) collective-permute-start(bf16[256,256]{1,0:T(8,128)(2,1)S(1)} %get-tuple-element.146), channel_id=1, source_target_pairs={{0,31},{1,2},{2,1},{3,4},{4,3},{5,6},{6,5},{7,8},{8,7},{9,10},{10,... | collective-permute-start | bytes 393224 | tf_op jit(solution)/shard_map/ppermute | solution.py:212
  68.2 7.9 %collective-permute-start.15 = (bf16[256,256]{1,0:T(8,128)(2,1)S(1)}, bf16[256,256]{1,0:T(8,128)(2,1)S(1)}, u32[]{:S(2)}, u32[]{:S(2)}) collective-permute-start(bf16[256,256]{1,0:T(8,128)(2,1)S(1)} %get-tuple-element.111), channel_id=1, source_target_pairs={{0,1},{1,0},{2,3},{3,2},{4,5},{5,4},{6,7},{7,6},{8,9},{9,8},{10,11... | collective-permute-start | bytes 393224 | tf_op jit(solution)/shard_map/ppermute | solution.py:212
  68.3 7.8 %collective-permute-start.16 = (bf16[256,256]{1,0:T(8,128)(2,1)S(1)}, bf16[256,256]{1,0:T(8,128)(2,1)S(1)}, u32[]{:S(2)}, u32[]{:S(2)}) collective-permute-start(bf16[256,256]{1,0:T(8,128)(2,1)S(1)} %get-tuple-element.112), channel_id=1, source_target_pairs={{0,31},{1,2},{2,1},{3,4},{4,3},{5,6},{6,5},{7,8},{8,7},{9,10},{10,... | collective-permute-start | bytes 393224 | tf_op jit(solution)/shard_map/ppermute | solution.py:212
  70.8 7.5 %collective-permute-start.31 = (bf16[256,256]{1,0:T(8,128)(2,1)S(1)}, bf16[256,256]{1,0:T(8,128)(2,1)S(1)}, u32[]{:S(2)}, u32[]{:S(2)}) collective-permute-start(bf16[256,256]{1,0:T(8,128)(2,1)S(1)} %get-tuple-element.149), channel_id=1, source_target_pairs={{0,1},{1,0},{2,3},{3,2},{4,5},{5,4},{6,7},{7,6},{8,9},{9,8},{10,11... | collective-permute-start | bytes 393224 | tf_op jit(solution)/shard_map/ppermute | solution.py:212
  70.9 7.8 %collective-permute-start.32 = (bf16[256,256]{1,0:T(8,128)(2,1)S(1)}, bf16[256,256]{1,0:T(8,128)(2,1)S(1)}, u32[]{:S(2)}, u32[]{:S(2)}) collective-permute-start(bf16[256,256]{1,0:T(8,128)(2,1)S(1)} %get-tuple-element.150), channel_id=1, source_target_pairs={{0,31},{1,2},{2,1},{3,4},{4,3},{5,6},{6,5},{7,8},{8,7},{9,10},{10,... | collective-permute-start | bytes 393224 | tf_op jit(solution)/shard_map/ppermute | solution.py:212
  77.3 7.9 %collective-permute-start.17 = (bf16[256,256]{1,0:T(8,128)(2,1)S(1)}, bf16[256,256]{1,0:T(8,128)(2,1)S(1)}, u32[]{:S(2)}, u32[]{:S(2)}) collective-permute-start(bf16[256,256]{1,0:T(8,128)(2,1)S(1)} %get-tuple-element.115), channel_id=1, source_target_pairs={{0,1},{1,0},{2,3},{3,2},{4,5},{5,4},{6,7},{7,6},{8,9},{9,8},{10,11... | collective-permute-start | bytes 393224 | tf_op jit(solution)/shard_map/ppermute | solution.py:212
  77.4 8.0 %collective-permute-start.18 = (bf16[256,256]{1,0:T(8,128)(2,1)S(1)}, bf16[256,256]{1,0:T(8,128)(2,1)S(1)}, u32[]{:S(2)}, u32[]{:S(2)}) collective-permute-start(bf16[256,256]{1,0:T(8,128)(2,1)S(1)} %get-tuple-element.116), channel_id=1, source_target_pairs={{0,31},{1,2},{2,1},{3,4},{4,3},{5,6},{6,5},{7,8},{8,7},{9,10},{10,... | collective-permute-start | bytes 393224 | tf_op jit(solution)/shard_map/ppermute | solution.py:212
  79.9 7.5 %collective-permute-start.33 = (bf16[256,256]{1,0:T(8,128)(2,1)S(1)}, bf16[256,256]{1,0:T(8,128)(2,1)S(1)}, u32[]{:S(2)}, u32[]{:S(2)}) collective-permute-start(bf16[256,256]{1,0:T(8,128)(2,1)S(1)} %get-tuple-element.153), channel_id=1, source_target_pairs={{0,1},{1,0},{2,3},{3,2},{4,5},{5,4},{6,7},{7,6},{8,9},{9,8},{10,11... | collective-permute-start | bytes 393224 | tf_op jit(solution)/shard_map/ppermute | solution.py:212
  80.0 7.8 %collective-permute-start.34 = (bf16[256,256]{1,0:T(8,128)(2,1)S(1)}, bf16[256,256]{1,0:T(8,128)(2,1)S(1)}, u32[]{:S(2)}, u32[]{:S(2)}) collective-permute-start(bf16[256,256]{1,0:T(8,128)(2,1)S(1)} %get-tuple-element.154), channel_id=1, source_target_pairs={{0,31},{1,2},{2,1},{3,4},{4,3},{5,6},{6,5},{7,8},{8,7},{9,10},{10,... | collective-permute-start | bytes 393224 | tf_op jit(solution)/shard_map/ppermute | solution.py:212
  86.6 1.9 %collective-permute-start.19 = (bf16[256,256]{1,0:T(8,128)(2,1)S(1)}, bf16[256,256]{1,0:T(8,128)(2,1)S(1)}, u32[]{:S(2)}, u32[]{:S(2)}) collective-permute-start(bf16[256,256]{1,0:T(8,128)(2,1)S(1)} %get-tuple-element.119), channel_id=1, source_target_pairs={{0,1},{1,0},{2,3},{3,2},{4,5},{5,4},{6,7},{7,6},{8,9},{9,8},{10,11... | collective-permute-start | bytes 393224 | tf_op jit(solution)/shard_map/ppermute | solution.py:212
  86.7 7.8 %collective-permute-start.20 = (bf16[256,256]{1,0:T(8,128)(2,1)S(1)}, bf16[256,256]{1,0:T(8,128)(2,1)S(1)}, u32[]{:S(2)}, u32[]{:S(2)}) collective-permute-start(bf16[256,256]{1,0:T(8,128)(2,1)S(1)} %get-tuple-element.120), channel_id=1, source_target_pairs={{0,31},{1,2},{2,1},{3,4},{4,3},{5,6},{6,5},{7,8},{8,7},{9,10},{10,... | collective-permute-start | bytes 393224 | tf_op jit(solution)/shard_map/ppermute | solution.py:212

commit v3 on v2

--- a/solution.py
+++ b/solution.py
@@ -65,8 +65,8 @@
 def prologue_body(per_section, *refs):
     feat, rows_hbm, count_hbm, src_hbm, val_hbm, w_hbm, gain_hbm = refs[:7]
     graph_outs = [refs[7 + 6 * g : 13 + 6 * g] for g in range(per_section)]
-    scaled_ref, *tables = refs[7 + 6 * per_section : 8 + 7 * per_section]
-    rows_all, count_ref, src_all, w_ref, gain_ref, sems, small_sems, feat_sems, val_sems = refs[8 + 7 * per_section :]
+    scaled_ref, mine_ref, *tables = refs[7 + 6 * per_section : 9 + 7 * per_section]
+    rows_all, count_ref, src_all, w_ref, gain_ref, sems, small_sems, feat_sems, val_sems = refs[9 + 7 * per_section :]
     even = dom_parity() == 0
     graphs = [graph_of(g, per_section) for g in range(per_section)]
     count_copy = pltpu.make_async_copy(count_hbm, count_ref, sems.at[0])
@@ -131,6 +131,7 @@
     for copy in later:
         copy.wait()
     scale(w_ref, gain_ref, scaled_ref)
+    mine_ref[...] = scaled_ref[dom_parity()]
     for copy in val_copies:
         copy.wait()
 
@@ -143,18 +144,21 @@
         out_ref[k] = (w_ref[k].astype(F32) * column).astype(BF)
 
 
-def gate_body(after_ref, out_ref):
-    out_ref[...] = after_ref[: out_ref.shape[0], : out_ref.shape[1]]
-
-
-def order_body(count, *refs):
-    parts, out = refs[:count], refs[-1]
+def pack_body(after_ref, *refs):
+    for k, part in enumerate(refs[:-1]):
+        refs[-1][k] = part[...]
+
+
+def order_body(scaled_ref, mine_ref, swapped_ref, out_ref):
     section = lax.axis_index("section")
-    per = parts[0].shape[0]
-    for shift, part in enumerate(parts):
+    parity = dom_parity()
+    count = mine_ref.shape[0] + 1
+    for k in range(2):
+        out_ref[section * 2 + k] = scaled_ref[k]
+    for shift in range(1, count):
         source = lax.rem(section - shift + count, count)
-        for k in range(per):
-            out[source * per + k] = part[k]
+        out_ref[source * 2 + parity] = mine_ref[shift - 1]
+        out_ref[source * 2 + 1 - parity] = swapped_ref[shift - 1]
 
 
 def layer_body(layer, last, others, idx_ref, h_ref, nrm_ref, on_in, off_in, tv_ref, sel_ref, w_ref, *rest):
@@ -217,11 +221,12 @@
         pltpu.with_memory_space_constraint(x, pltpu.HBM)
         for x in (features, tile_val, boundary_rows, boundary_count, tile_src, weights, gains)
     )
+    square = (width, width)
     per_graph = [(rows_dev, width), (rows_dev, width), (2 * bnd, rows_dev), (bnd, width), (bnd, width)]
     per_graph += [(rows_dev, K * TILE)]
     results = call(
         functools.partial(prologue_body, per_section),
-        per_graph * per_section + [weights.shape],
+        per_graph * per_section + [weights.shape, square],
         [HBM] * 7,
         "prologue",
         [
@@ -238,7 +243,7 @@
         limit=16,
         ints=[(tiles * K, TILE)] * per_section,
     )(features, boundary_rows, boundary_count, tile_src, tile_val, weights, gains)
-    scaled, *tables = results[6 * per_section :]
+    scaled, mine, *tables = results[6 * per_section :]
     state, values = [], []
     for g in range(per_section):
         h, nrm, sel, on, off, value = results[6 * g : 6 * g + 6]
@@ -247,14 +252,13 @@
         off, on = lax.optimization_barrier((off, on))
         off = lax.ppermute(off, "dom", off_pairs)
         state.append([h, nrm, on, off, sel, tables[g]])
-    parts = [scaled] + [
-        lax.ppermute(scaled, "section", [(i, (i + shift) % sections) for i in range(sections)])
+    parts = [
+        lax.ppermute(mine, "section", [(i, (i + shift) % sections) for i in range(sections)])
         for shift in range(1, sections)
     ]
-    gate = call(gate_body, [(16, TILE)], [VMEM], "gate")(state[0][3])[0]
-    w_all = call(
-        functools.partial(order_body, sections), [(layers, width, width)], [VMEM] * (sections + 1), "order"
-    )(*parts, gate)[0]
+    packed = call(pack_body, [(sections - 1, *square)], [VMEM] * sections, "pack")(state[0][3], *parts)[0]
+    swapped = lax.ppermute(packed, "dom", on_pairs)
+    w_all = call(order_body, [(layers, *square)], [VMEM] * 3, "order")(scaled, packed, swapped)[0]
     outputs = []
     for layer in range(layers):
         last = layer == layers - 1

time: 96.3 us -> 93.7 us (0.973)
  waiting for transfers between devices: 17.1 us -> 11.1 us
  starting transfers between devices: 55 us -> 58.2 us
    ppermute x14, waiting for transfers between devices: 9.44 us -> 5.31 us  [exchange(): lax.ppermute(off, 'dom', off_pairs)]
    ppermute x2, starting transfers between devices: 6.3 us -> 9.37 us  [on_device(): off = lax.ppermute(off, 'dom', off_pairs)]
    ppermute x3 -> x4, waiting for transfers between devices: 5.96 us -> 3.91 us  [the longest x3 3.9 us: on_device(): lax.ppermute(mine, 'section', [(i, (i + shift) % sections) for i in range...]
    ppermute x2, waiting for transfers between devices: 0.01 us -> 1.4 us  [on_device(): on = lax.ppermute(on, 'dom', on_pairs)]
    ppermute x2, waiting for transfers between devices: 1.67 us -> 0.42 us  [on_device(): off = lax.ppermute(off, 'dom', off_pairs)]
    ppermute x3 -> x4, starting transfers between devices: 5.35 us -> 5.43 us  [the longest x3 5.35 us: on_device(): lax.ppermute(mine, 'section', [(i, (i + shift) % sections) for i in range...]
  transfers between devices with their start and end apart: 35 -> 36, of which waited for: 12 -> 15; matrix products, arithmetic and copies ran while one was open for 0% -> 0% of each run, Pallas kernels for 19% -> 19%
where the time goes in v3:
time: 93.7 us; the launch traced here: 93.4 us
  starting transfers between devices  58.2 us (62%)
  Pallas kernels  23.6 us (25%)
  waiting for transfers between devices  11.1 us (12%)
    ppermute x14, starting transfers between devices, exchange(): lax.ppermute(off, 'dom', off_pairs)  41.6 us
    pallas_call x16, Pallas kernels, on_device(): call(functools.partial(layer_body, layer, last, others), outs, [VMEM] * (...  19.4 us
    ppermute x2, starting transfers between devices, on_device(): off = lax.ppermute(off, 'dom', off_pairs)  9.37 us
    ppermute x3, starting transfers between devices, on_device(): lax.ppermute(mine, 'section', [(i, (i + shift) % sections) for i in range...  5.35 us
    ppermute x14, waiting for transfers between devices, exchange(): lax.ppermute(off, 'dom', off_pairs)  5.31 us
    pallas_call x1, Pallas kernels, on_device(): call(functools.partial(prologue_body, per_section), per_graph * per_secti...  4.15 us
    ppermute x3, waiting for transfers between devices, on_device(): lax.ppermute(mine, 'section', [(i, (i + shift) % sections) for i in range...  3.9 us
  transfers between devices with their start and end apart: 36, of which 15 were waited for; matrix products, arithmetic and copies ran while one was open for 0% of the time, Pallas kernels for 19%

profile of v3, /device:TPU:0, one launch (start us, length us, event | category | flops | bytes accessed | tf_op | source)
XLA Modules:
  0.0 93.4 jit_solution(836853939418447723)
XLA Ops:
  0.0 4.2 %prologue.1 = (bf16[1024,256]{1,0:T(8,128)(2,1)S(1)}, bf16[1024,256]{1,0:T(8,128)(2,1)S(1)}, bf16[512,1024]{1,0:T(8,128)(2,1)S(1)}, bf16[256,256]{1,0:T(8,128)(2...) custom-call(bf16[8,1024,256]{2,1,0:T(8,128)(2,1)} %refs_0_.1, ...), custom_call_target="tpu_custom_call" | custom-call | bytes 1024 | tf_op jit(solution)/shard_map/prologue/pallas_call | solution.py:227
  4.2 0.1 collective-permute-start.2
  4.3 4.1 %collective-permute-start.6 = (bf16[256,256]{1,0:T(8,128)(2,1)S(1)}, bf16[256,256]{1,0:T(8,128)(2,1)S(1)}, u32[]{:S(2)}, u32[]{:S(2)}) collective-permute-start(bf16[256,256]{1,0:T(8,128)(2,1)S(1)} %get-tuple-element.94), channel_id=1, source_target_pairs={{0,96},{32,0},{64,32},{96,64},{1,97},{33,1},{65,33},{97,65},{2,98}... | collective-permute-start | bytes 393224 | tf_op jit(solution)/shard_map/ppermute | solution.py:256
  8.3 1.3 %collective-permute-start.4 = (bf16[256,256]{1,0:T(8,128)(2,1)S(1)}, bf16[256,256]{1,0:T(8,128)(2,1)S(1)}, u32[]{:S(2)}, u32[]{:S(2)}) collective-permute-start(bf16[256,256]{1,0:T(8,128)(2,1)S(1)} %get-tuple-element.94), channel_id=1, source_target_pairs={{0,32},{32,64},{64,96},{96,0},{1,33},{33,65},{65,97},{97,1},{2,34}... | collective-permute-start | bytes 393224 | tf_op jit(solution)/shard_map/ppermute | solution.py:256
  9.6 4.4 %collective-permute-start.3 = (bf16[256,256]{1,0:T(8,128)(2,1)S(1)}, bf16[256,256]{1,0:T(8,128)(2,1)S(1)}, u32[]{:S(2)}, u32[]{:S(2)}) collective-permute-start(bf16[256,256]{1,0:T(8,128)(2,1)S(1)} %get-tuple-element.93), channel_id=1, source_target_pairs={{0,31},{1,2},{2,1},{3,4},{4,3},{5,6},{6,5},{7,8},{8,7},{9,10},{10,... | collective-permute-start | bytes 393224 | tf_op jit(solution)/shard_map/ppermute | solution.py:253
  14.0 0.5 collective-permute-done.6.refs_2_
  14.5 1.7 %collective-permute-done.5.refs_1_ = bf16[256,256]{1,0:T(8,128)(2,1)S(1)} collective-permute-done((bf16[256,256]{1,0:T(8,128)(2,1)S(1)}, bf16[256,256]{1,0:T(8,128)(2,1)S(1)}, u32[]{:S(2)}, u32[]{:S(2)}) %collective-permute-start.5) | collective-permute-done | bytes 131104 | tf_op jit(solution)/shard_map/ppermute | solution.py:256
  16.2 1.7 %collective-permute-done.4.refs_0_ = bf16[256,256]{1,0:T(8,128)(2,1)S(1)} collective-permute-done((bf16[256,256]{1,0:T(8,128)(2,1)S(1)}, bf16[256,256]{1,0:T(8,128)(2,1)S(1)}, u32[]{:S(2)}, u32[]{:S(2)}) %collective-permute-start.4) | collective-permute-done | bytes 131104 | tf_op jit(solution)/shard_map/ppermute | solution.py:256
  18.0 0.1 collective-permute-start.7
  18.1 0.5 collective-permute-start
  18.6 1.4 %collective-permute-done.on_in = bf16[256,256]{1,0:T(8,128)(2,1)S(1)} collective-permute-done((bf16[256,256]{1,0:T(8,128)(2,1)S(1)}, bf16[256,256]{1,0:T(8,128)(2,1)S(1)}, u32[]{:S(2)}, u32[]{:S(2)}) %collective-permute-start) | collective-permute-done | bytes 131104 | tf_op jit(solution)/shard_map/ppermute | solution.py:251
  20.0 5.0 %collective-permute-start.1 = (bf16[256,256]{1,0:T(8,128)(2,1)S(1)}, bf16[256,256]{1,0:T(8,128)(2,1)S(1)}, u32[]{:S(2)}, u32[]{:S(2)}) collective-permute-start(bf16[256,256]{1,0:T(8,128)(2,1)S(1)} %get-tuple-element.87), channel_id=1, source_target_pairs={{0,31},{1,2},{2,1},{3,4},{4,3},{5,6},{6,5},{7,8},{8,7},{9,10},{10,... | collective-permute-start | bytes 393224 | tf_op jit(solution)/shard_map/ppermute | solution.py:253
  25.0 1.2 %layer.23 = (bf16[1024,256]{1,0:T(8,128)(2,1)S(1)}, bf16[1024,256]{1,0:T(8,128)(2,1)S(1)}, bf16[256,256]{1,0:T(8,128)(2,1)S(1)}, bf16[256,256]{1,0:T(8,128)(2,1)S(1)}) custom-call(s32[32,128]{1,0:T(8,128)S(1)} %get-tuple-element.123.idx_ref, bf16[1024,256]{1,0:T(8,128)(2,1)S(1)} %get-tuple-element.124.h_ref, ...), custom_call_target="tpu_custom_call" | custom-call | flops 1000000 | bytes 1024 | tf_op jit(solution)/shard_map/layer/pallas_call | solution.py:277
  26.2 0.1 collective-permute-start.22
  26.3 0.9 collective-permute-start.23
  27.3 0.4 collective-permute-done.1.off_in
  27.7 1.2 %layer.16 = (bf16[1024,256]{1,0:T(8,128)(2,1)S(1)}, bf16[1024,256]{1,0:T(8,128)(2,1)S(1)}, bf16[256,256]{1,0:T(8,128)(2,1)S(1)}, bf16[256,256]{1,0:T(8,128)(2,1)S(1)}) custom-call(s32[32,128]{1,0:T(8,128)S(1)} %get-tuple-element.81.idx_ref, bf16[1024,256]{1,0:T(8,128)(2,1)S(1)} %get-tuple-element.82.h_ref, bf16[1024,256]{1,0:T(8,128)(2,1)S(1)} %get-tuple-element.83.nrm_ref, ...), custom_call_target="tpu_custom_call" | custom-call | flops 1000000 | bytes 1024 | tf_op jit(solution)/shard_map/layer/pallas_call | solution.py:277
  28.9 0.1 collective-permute-start.8
  29.0 5.0 %collective-permute-start.9 = (bf16[256,256]{1,0:T(8,128)(2,1)S(1)}, bf16[256,256]{1,0:T(8,128)(2,1)S(1)}, u32[]{:S(2)}, u32[]{:S(2)}) collective-permute-start(bf16[256,256]{1,0:T(8,128)(2,1)S(1)} %get-tuple-element.98), channel_id=1, source_target_pairs={{0,31},{1,2},{2,1},{3,4},{4,3},{5,6},{6,5},{7,8},{8,7},{9,10},{10,... | collective-permute-start | bytes 393224 | tf_op jit(solution)/shard_map/ppermute | solution.py:216
  34.0 0.1 collective-permute-done.23.off_in
  34.1 1.2 %layer.24 = (bf16[1024,256]{1,0:T(8,128)(2,1)S(1)}, bf16[1024,256]{1,0:T(8,128)(2,1)S(1)}, bf16[256,256]{1,0:T(8,128)(2,1)S(1)}, bf16[256,256]{1,0:T(8,128)(2,1)S(1)}) custom-call(s32[32,128]{1,0:T(8,128)S(1)} %get-tuple-element.123.idx_ref, bf16[1024,256]{1,0:T(8,128)(2,1)S(1)} %get-tuple-element.129.h_ref, ...), custom_call_target="tpu_custom_call" | custom-call | flops 1000000 | bytes 1024 | tf_op jit(solution)/shard_map/layer/pallas_call | solution.py:277
  35.3 0.1 collective-permute-start.24
  35.4 0.9 collective-permute-start.25
  36.4 0.4 collective-permute-done.9.off_in
  36.8 1.2 %layer.17 = (bf16[1024,256]{1,0:T(8,128)(2,1)S(1)}, bf16[1024,256]{1,0:T(8,128)(2,1)S(1)}, bf16[256,256]{1,0:T(8,128)(2,1)S(1)}, bf16[256,256]{1,0:T(8,128)(2,1)S(1)}) custom-call(s32[32,128]{1,0:T(8,128)S(1)} %get-tuple-element.81.idx_ref, bf16[1024,256]{1,0:T(8,128)(2,1)S(1)} %get-tuple-element.95.h_ref, bf16[1024,256]{1,0:T(8,128)(2,1)S(1)} %get-tuple-element.96.nrm_ref, ...), custom_call_target="tpu_custom_call" | custom-call | flops 1000000 | bytes 1024 | tf_op jit(solution)/shard_map/layer/pallas_call | solution.py:277
  38.0 0.1 collective-permute-start.10
  38.1 5.2 %collective-permute-start.11 = (bf16[256,256]{1,0:T(8,128)(2,1)S(1)}, bf16[256,256]{1,0:T(8,128)(2,1)S(1)}, u32[]{:S(2)}, u32[]{:S(2)}) collective-permute-start(bf16[256,256]{1,0:T(8,128)(2,1)S(1)} %get-tuple-element.102), channel_id=1, source_target_pairs={{0,31},{1,2},{2,1},{3,4},{4,3},{5,6},{6,5},{7,8},{8,7},{9,10},{10,... | collective-permute-start | bytes 393224 | tf_op jit(solution)/shard_map/ppermute | solution.py:216
  43.3 1.2 %layer.25 = (bf16[1024,256]{1,0:T(8,128)(2,1)S(1)}, bf16[1024,256]{1,0:T(8,128)(2,1)S(1)}, bf16[256,256]{1,0:T(8,128)(2,1)S(1)}, bf16[256,256]{1,0:T(8,128)(2,1)S(1)}) custom-call(s32[32,128]{1,0:T(8,128)S(1)} %get-tuple-element.123.idx_ref, bf16[1024,256]{1,0:T(8,128)(2,1)S(1)} %get-tuple-element.133.h_ref, ...), custom_call_target="tpu_custom_call" | custom-call | flops 1000000 | bytes 1024 | tf_op jit(solution)/shard_map/layer/pallas_call | solution.py:277
  44.6 0.1 collective-permute-start.26
  44.7 0.8 collective-permute-start.27
  45.5 0.6 collective-permute-done.11.off_in
  46.1 1.2 %layer.18 = (bf16[1024,256]{1,0:T(8,128)(2,1)S(1)}, bf16[1024,256]{1,0:T(8,128)(2,1)S(1)}, bf16[256,256]{1,0:T(8,128)(2,1)S(1)}, bf16[256,256]{1,0:T(8,128)(2,1)S(1)}) custom-call(s32[32,128]{1,0:T(8,128)S(1)} %get-tuple-element.81.idx_ref, bf16[1024,256]{1,0:T(8,128)(2,1)S(1)} %get-tuple-element.99.h_ref, bf16[1024,256]{1,0:T(8,128)(2,1)S(1)} %get-tuple-element.100.nrm_ref, ...), custom_call_target="tpu_custom_call" | custom-call | flops 1000000 | bytes 1024 | tf_op jit(solution)/shard_map/layer/pallas_call | solution.py:277
  47.3 0.1 collective-permute-start.12
  47.4 5.0 %collective-permute-start.13 = (bf16[256,256]{1,0:T(8,128)(2,1)S(1)}, bf16[256,256]{1,0:T(8,128)(2,1)S(1)}, u32[]{:S(2)}, u32[]{:S(2)}) collective-permute-start(bf16[256,256]{1,0:T(8,128)(2,1)S(1)} %get-tuple-element.106), channel_id=1, source_target_pairs={{0,31},{1,2},{2,1},{3,4},{4,3},{5,6},{6,5},{7,8},{8,7},{9,10},{10,... | collective-permute-start | bytes 393224 | tf_op jit(solution)/shard_map/ppermute | solution.py:216
  52.5 1.2 %layer.26 = (bf16[1024,256]{1,0:T(8,128)(2,1)S(1)}, bf16[1024,256]{1,0:T(8,128)(2,1)S(1)}, bf16[256,256]{1,0:T(8,128)(2,1)S(1)}, bf16[256,256]{1,0:T(8,128)(2,1)S(1)}) custom-call(s32[32,128]{1,0:T(8,128)S(1)} %get-tuple-element.123.idx_ref, bf16[1024,256]{1,0:T(8,128)(2,1)S(1)} %get-tuple-element.137.h_ref, ...), custom_call_target="tpu_custom_call" | custom-call | flops 1000000 | bytes 1024 | tf_op jit(solution)/shard_map/layer/pallas_call | solution.py:277
  53.7 0.1 collective-permute-start.28
  53.8 0.8 collective-permute-start.29
  54.6 0.6 collective-permute-done.13.off_in
  55.2 1.2 %layer.19 = (bf16[1024,256]{1,0:T(8,128)(2,1)S(1)}, bf16[1024,256]{1,0:T(8,128)(2,1)S(1)}, bf16[256,256]{1,0:T(8,128)(2,1)S(1)}, bf16[256,256]{1,0:T(8,128)(2,1)S(1)}) custom-call(s32[32,128]{1,0:T(8,128)S(1)} %get-tuple-element.81.idx_ref, bf16[1024,256]{1,0:T(8,128)(2,1)S(1)} %get-tuple-element.103.h_ref, ...), custom_call_target="tpu_custom_call" | custom-call | flops 1000000 | bytes 1024 | tf_op jit(solution)/shard_map/layer/pallas_call | solution.py:277
  56.4 0.1 collective-permute-start.14
  56.5 5.0 %collective-permute-start.15 = (bf16[256,256]{1,0:T(8,128)(2,1)S(1)}, bf16[256,256]{1,0:T(8,128)(2,1)S(1)}, u32[]{:S(2)}, u32[]{:S(2)}) collective-permute-start(bf16[256,256]{1,0:T(8,128)(2,1)S(1)} %get-tuple-element.110), channel_id=1, source_target_pairs={{0,31},{1,2},{2,1},{3,4},{4,3},{5,6},{6,5},{7,8},{8,7},{9,10},{10,... | collective-permute-start | bytes 393224 | tf_op jit(solution)/shard_map/ppermute | solution.py:216
  61.6 1.2 %layer.27 = (bf16[1024,256]{1,0:T(8,128)(2,1)S(1)}, bf16[1024,256]{1,0:T(8,128)(2,1)S(1)}, bf16[256,256]{1,0:T(8,128)(2,1)S(1)}, bf16[256,256]{1,0:T(8,128)(2,1)S(1)}) custom-call(s32[32,128]{1,0:T(8,128)S(1)} %get-tuple-element.123.idx_ref, bf16[1024,256]{1,0:T(8,128)(2,1)S(1)} %get-tuple-element.141.h_ref, ...), custom_call_target="tpu_custom_call" | custom-call | flops 1000000 | bytes 1024 | tf_op jit(solution)/shard_map/layer/pallas_call | solution.py:277
  62.8 0.1 collective-permute-start.30
  62.9 0.8 collective-permute-start.31
  63.7 0.6 collective-permute-done.15.off_in
  64.3 1.2 %layer.20 = (bf16[1024,256]{1,0:T(8,128)(2,1)S(1)}, bf16[1024,256]{1,0:T(8,128)(2,1)S(1)}, bf16[256,256]{1,0:T(8,128)(2,1)S(1)}, bf16[256,256]{1,0:T(8,128)(2,1)S(1)}) custom-call(s32[32,128]{1,0:T(8,128)S(1)} %get-tuple-element.81.idx_ref, bf16[1024,256]{1,0:T(8,128)(2,1)S(1)} %get-tuple-element.107.h_ref, ...), custom_call_target="tpu_custom_call" | custom-call | flops 1000000 | bytes 1024 | tf_op jit(solution)/shard_map/layer/pallas_call | solution.py:277
  65.6 0.1 collective-permute-start.16
  65.7 5.0 %collective-permute-start.17 = (bf16[256,256]{1,0:T(8,128)(2,1)S(1)}, bf16[256,256]{1,0:T(8,128)(2,1)S(1)}, u32[]{:S(2)}, u32[]{:S(2)}) collective-permute-start(bf16[256,256]{1,0:T(8,128)(2,1)S(1)} %get-tuple-element.114), channel_id=1, source_target_pairs={{0,31},{1,2},{2,1},{3,4},{4,3},{5,6},{6,5},{7,8},{8,7},{9,10},{10,... | collective-permute-start | bytes 393224 | tf_op jit(solution)/shard_map/ppermute | solution.py:216
  70.7 1.2 %layer.28 = (bf16[1024,256]{1,0:T(8,128)(2,1)S(1)}, bf16[1024,256]{1,0:T(8,128)(2,1)S(1)}, bf16[256,256]{1,0:T(8,128)(2,1)S(1)}, bf16[256,256]{1,0:T(8,128)(2,1)S(1)}) custom-call(s32[32,128]{1,0:T(8,128)S(1)} %get-tuple-element.123.idx_ref, bf16[1024,256]{1,0:T(8,128)(2,1)S(1)} %get-tuple-element.145.h_ref, ...), custom_call_target="tpu_custom_call" | custom-call | flops 1000000 | bytes 1024 | tf_op jit(solution)/shard_map/layer/pallas_call | solution.py:277
  71.9 0.1 collective-permute-start.32
  72.0 1.1 %collective-permute-start.33 = (bf16[256,256]{1,0:T(8,128)(2,1)S(1)}, bf16[256,256]{1,0:T(8,128)(2,1)S(1)}, u32[]{:S(2)}, u32[]{:S(2)}) collective-permute-start(bf16[256,256]{1,0:T(8,128)(2,1)S(1)} %get-tuple-element.152), channel_id=1, source_target_pairs={{0,31},{1,2},{2,1},{3,4},{4,3},{5,6},{6,5},{7,8},{8,7},{9,10},{10,... | collective-permute-start | bytes 393224 | tf_op jit(solution)/shard_map/ppermute | solution.py:216
  73.1 0.4 collective-permute-done.17.off_in
  73.4 1.2 %layer.21 = (bf16[1024,256]{1,0:T(8,128)(2,1)S(1)}, bf16[1024,256]{1,0:T(8,128)(2,1)S(1)}, bf16[256,256]{1,0:T(8,128)(2,1)S(1)}, bf16[256,256]{1,0:T(8,128)(2,1)S(1)}) custom-call(s32[32,128]{1,0:T(8,128)S(1)} %get-tuple-element.81.idx_ref, bf16[1024,256]{1,0:T(8,128)(2,1)S(1)} %get-tuple-element.111.h_ref, ...), custom_call_target="tpu_custom_call" | custom-call | flops 1000000 | bytes 1024 | tf_op jit(solution)/shard_map/layer/pallas_call | solution.py:277
  74.8 5.0 %collective-permute-start.19 = (bf16[256,256]{1,0:T(8,128)(2,1)S(1)}, bf16[256,256]{1,0:T(8,128)(2,1)S(1)}, u32[]{:S(2)}, u32[]{:S(2)}) collective-permute-start(bf16[256,256]{1,0:T(8,128)(2,1)S(1)} %get-tuple-element.118), channel_id=1, source_target_pairs={{0,31},{1,2},{2,1},{3,4},{4,3},{5,6},{6,5},{7,8},{8,7},{9,10},{10,... | collective-permute-start | bytes 393224 | tf_op jit(solution)/shard_map/ppermute | solution.py:216
  79.8 0.2 collective-permute-done.33.off_in
  80.0 1.2 %layer.29 = (bf16[1024,256]{1,0:T(8,128)(2,1)S(1)}, bf16[1024,256]{1,0:T(8,128)(2,1)S(1)}, bf16[256,256]{1,0:T(8,128)(2,1)S(1)}, bf16[256,256]{1,0:T(8,128)(2,1)S(1)}) custom-call(s32[32,128]{1,0:T(8,128)S(1)} %get-tuple-element.123.idx_ref, bf16[1024,256]{1,0:T(8,128)(2,1)S(1)} %get-tuple-element.149.h_ref, ...), custom_call_target="tpu_custom_call" | custom-call | flops 1000000 | bytes 1024 | tf_op jit(solution)/shard_map/layer/pallas_call | solution.py:277
  81.4 0.8 collective-permute-start.35
  82.2 0.4 collective-permute-done.19.off_in
  82.6 1.2 %layer.22 = (bf16[1024,256]{1,0:T(8,128)(2,1)S(1)}, bf16[1024,256]{1,0:T(8,128)(2,1)S(1)}, bf16[256,256]{1,0:T(8,128)(2,1)S(1)}, bf16[256,256]{1,0:T(8,128)(2,1)S(1)}) custom-call(s32[32,128]{1,0:T(8,128)S(1)} %get-tuple-element.81.idx_ref, bf16[1024,256]{1,0:T(8,128)(2,1)S(1)} %get-tuple-element.115.h_ref, ...), custom_call_target="tpu_custom_call" | custom-call | flops 1000000 | bytes 1024 | tf_op jit(solution)/shard_map/layer/pallas_call | solution.py:277
  83.9 5.0 %collective-permute-start.21 = (bf16[256,256]{1,0:T(8,128)(2,1)S(1)}, bf16[256,256]{1,0:T(8,128)(2,1)S(1)}, u32[]{:S(2)}, u32[]{:S(2)}) collective-permute-start(bf16[256,256]{1,0:T(8,128)(2,1)S(1)} %get-tuple-element.122), channel_id=1, source_target_pairs={{0,31},{1,2},{2,1},{3,4},{4,3},{5,6},{6,5},{7,8},{8,7},{9,10},{10,... | collective-permute-start | bytes 393224 | tf_op jit(solution)/shard_map/ppermute | solution.py:216
  88.9 0.2 collective-permute-done.35.off_in
  89.2 0.7 layer.30.rest_0_
  89.9 1.8 %collective-permute-done.21.off_in = bf16[256,256]{1,0:T(8,128)(2,1)S(1)} collective-permute-done((bf16[256,256]{1,0:T(8,128)(2,1)S(1)}, bf16[256,256]{1,0:T(8,128)(2,1)S(1)}, u32[]{:S(2)}, u32[]{:S(2)}) %collective-permute-start.21) | collective-permute-done | bytes 131104 | tf_op jit(solution)/shard_map/ppermute | solution.py:216
  91.7 1.5 %layer.31 = bf16[2,1024,256]{2,1,0:T(8,128)(2,1)} custom-call(s32[32,128]{1,0:T(8,128)S(1)} %get-tuple-element.81.idx_ref, bf16[1024,256]{1,0:T(8,128)(2,1)S(1)} %get-tuple-element.119.h_ref, bf16[1024,256]{1,0:T(8,128)(2,1)S(1)} %get-tuple-element.120.nrm_ref, bf16[256,256]{1,0:T(8,128)(2,1)S(1)} %collective-permute-done.20.on_in, ...), custom_call_target="tpu_custom_call" | custom-call | flops 1000000 | bytes 1024 | tf_op jit(solution)/shard_map/layer/pallas_call | solution.py:277
  (27 shorter events, 0.4 us)
Async XLA Ops:
  4.2 5.4 %collective-permute-start.2 = (bf16[256,256]{1,0:T(8,128)(2,1)S(1)}, bf16[256,256]{1,0:T(8,128)(2,1)S(1)}, u32[]{:S(2)}, u32[]{:S(2)}) collective-permute-start(bf16[256,256]{1,0:T(8,128)(2,1)S(1)} %get-tuple-element.92), channel_id=1, source_target_pairs={{0,1},{1,0},{2,3},{3,2},{4,5},{5,4},{6,7},{7,6},{8,9},{9,8},{10,11... | collective-permute-start | bytes 393224 | tf_op jit(solution)/shard_map/ppermute | solution.py:251
  4.3 10.3 %collective-permute-start.6 = (bf16[256,256]{1,0:T(8,128)(2,1)S(1)}, bf16[256,256]{1,0:T(8,128)(2,1)S(1)}, u32[]{:S(2)}, u32[]{:S(2)}) collective-permute-start(bf16[256,256]{1,0:T(8,128)(2,1)S(1)} %get-tuple-element.94), channel_id=1, source_target_pairs={{0,96},{32,0},{64,32},{96,64},{1,97},{33,1},{65,33},{97,65},{2,98}... | collective-permute-start | bytes 393224 | tf_op jit(solution)/shard_map/ppermute | solution.py:256
  8.3 7.9 %collective-permute-start.5 = (bf16[256,256]{1,0:T(8,128)(2,1)S(1)}, bf16[256,256]{1,0:T(8,128)(2,1)S(1)}, u32[]{:S(2)}, u32[]{:S(2)}) collective-permute-start(bf16[256,256]{1,0:T(8,128)(2,1)S(1)} %get-tuple-element.94), channel_id=1, source_target_pairs={{0,64},{32,96},{64,0},{96,32},{1,65},{33,97},{65,1},{97,33},{2,66}... | collective-permute-start | bytes 393224 | tf_op jit(solution)/shard_map/ppermute | solution.py:256
  8.3 9.6 %collective-permute-start.4 = (bf16[256,256]{1,0:T(8,128)(2,1)S(1)}, bf16[256,256]{1,0:T(8,128)(2,1)S(1)}, u32[]{:S(2)}, u32[]{:S(2)}) collective-permute-start(bf16[256,256]{1,0:T(8,128)(2,1)S(1)} %get-tuple-element.94), channel_id=1, source_target_pairs={{0,32},{32,64},{64,96},{96,0},{1,33},{33,65},{65,97},{97,1},{2,34}... | collective-permute-start | bytes 393224 | tf_op jit(solution)/shard_map/ppermute | solution.py:256
  9.6 8.3 %collective-permute-start.3 = (bf16[256,256]{1,0:T(8,128)(2,1)S(1)}, bf16[256,256]{1,0:T(8,128)(2,1)S(1)}, u32[]{:S(2)}, u32[]{:S(2)}) collective-permute-start(bf16[256,256]{1,0:T(8,128)(2,1)S(1)} %get-tuple-element.93), channel_id=1, source_target_pairs={{0,31},{1,2},{2,1},{3,4},{4,3},{5,6},{6,5},{7,8},{8,7},{9,10},{10,... | collective-permute-start | bytes 393224 | tf_op jit(solution)/shard_map/ppermute | solution.py:253
  18.0 6.9 %collective-permute-start.7 = (bf16[3,256,256]{2,1,0:T(8,128)(2,1)S(1)}, bf16[3,256,256]{2,1,0:T(8,128)(2,1)S(1)}, u32[]{:S(2)}, u32[]{:S(2)}) collective-permute-start(bf16[3,256,256]{2,1,0:T(8,128)(2,1)S(1)} %pack.1.mine_ref), channel_id=1, source_target_pairs={{0,1},{1,0},{2,3},{3,2},{4,5},{5,4},{6,7},{7,6},{8,9},{9,8},{10,11... | collective-permute-start | bytes 1179656 | tf_op jit(solution)/shard_map/ppermute | solution.py:260
  18.1 1.9 %collective-permute-start = (bf16[256,256]{1,0:T(8,128)(2,1)S(1)}, bf16[256,256]{1,0:T(8,128)(2,1)S(1)}, u32[]{:S(2)}, u32[]{:S(2)}) collective-permute-start(bf16[256,256]{1,0:T(8,128)(2,1)S(1)} %get-tuple-element.85), channel_id=1, source_target_pairs={{0,1},{1,0},{2,3},{3,2},{4,5},{5,4},{6,7},{7,6},{8,9},{9,8},{10,11... | collective-permute-start | bytes 393224 | tf_op jit(solution)/shard_map/ppermute | solution.py:251
  20.0 7.7 %collective-permute-start.1 = (bf16[256,256]{1,0:T(8,128)(2,1)S(1)}, bf16[256,256]{1,0:T(8,128)(2,1)S(1)}, u32[]{:S(2)}, u32[]{:S(2)}) collective-permute-start(bf16[256,256]{1,0:T(8,128)(2,1)S(1)} %get-tuple-element.87), channel_id=1, source_target_pairs={{0,31},{1,2},{2,1},{3,4},{4,3},{5,6},{6,5},{7,8},{8,7},{9,10},{10,... | collective-permute-start | bytes 393224 | tf_op jit(solution)/shard_map/ppermute | solution.py:253
  26.2 7.8 %collective-permute-start.22 = (bf16[256,256]{1,0:T(8,128)(2,1)S(1)}, bf16[256,256]{1,0:T(8,128)(2,1)S(1)}, u32[]{:S(2)}, u32[]{:S(2)}) collective-permute-start(bf16[256,256]{1,0:T(8,128)(2,1)S(1)} %get-tuple-element.131), channel_id=1, source_target_pairs={{0,1},{1,0},{2,3},{3,2},{4,5},{5,4},{6,7},{7,6},{8,9},{9,8},{10,11... | collective-permute-start | bytes 393224 | tf_op jit(solution)/shard_map/ppermute | solution.py:216
  26.3 7.8 %collective-permute-start.23 = (bf16[256,256]{1,0:T(8,128)(2,1)S(1)}, bf16[256,256]{1,0:T(8,128)(2,1)S(1)}, u32[]{:S(2)}, u32[]{:S(2)}) collective-permute-start(bf16[256,256]{1,0:T(8,128)(2,1)S(1)} %get-tuple-element.132), channel_id=1, source_target_pairs={{0,31},{1,2},{2,1},{3,4},{4,3},{5,6},{6,5},{7,8},{8,7},{9,10},{10,... | collective-permute-start | bytes 393224 | tf_op jit(solution)/shard_map/ppermute | solution.py:216
  28.9 7.5 %collective-permute-start.8 = (bf16[256,256]{1,0:T(8,128)(2,1)S(1)}, bf16[256,256]{1,0:T(8,128)(2,1)S(1)}, u32[]{:S(2)}, u32[]{:S(2)}) collective-permute-start(bf16[256,256]{1,0:T(8,128)(2,1)S(1)} %get-tuple-element.97), channel_id=1, source_target_pairs={{0,1},{1,0},{2,3},{3,2},{4,5},{5,4},{6,7},{7,6},{8,9},{9,8},{10,11... | collective-permute-start | bytes 393224 | tf_op jit(solution)/shard_map/ppermute | solution.py:216
  29.0 7.8 %collective-permute-start.9 = (bf16[256,256]{1,0:T(8,128)(2,1)S(1)}, bf16[256,256]{1,0:T(8,128)(2,1)S(1)}, u32[]{:S(2)}, u32[]{:S(2)}) collective-permute-start(bf16[256,256]{1,0:T(8,128)(2,1)S(1)} %get-tuple-element.98), channel_id=1, source_target_pairs={{0,31},{1,2},{2,1},{3,4},{4,3},{5,6},{6,5},{7,8},{8,7},{9,10},{10,... | collective-permute-start | bytes 393224 | tf_op jit(solution)/shard_map/ppermute | solution.py:216
  35.3 8.0 %collective-permute-start.24 = (bf16[256,256]{1,0:T(8,128)(2,1)S(1)}, bf16[256,256]{1,0:T(8,128)(2,1)S(1)}, u32[]{:S(2)}, u32[]{:S(2)}) collective-permute-start(bf16[256,256]{1,0:T(8,128)(2,1)S(1)} %get-tuple-element.135), channel_id=1, source_target_pairs={{0,1},{1,0},{2,3},{3,2},{4,5},{5,4},{6,7},{7,6},{8,9},{9,8},{10,11... | collective-permute-start | bytes 393224 | tf_op jit(solution)/shard_map/ppermute | solution.py:216
  35.4 7.9 %collective-permute-start.25 = (bf16[256,256]{1,0:T(8,128)(2,1)S(1)}, bf16[256,256]{1,0:T(8,128)(2,1)S(1)}, u32[]{:S(2)}, u32[]{:S(2)}) collective-permute-start(bf16[256,256]{1,0:T(8,128)(2,1)S(1)} %get-tuple-element.136), channel_id=1, source_target_pairs={{0,31},{1,2},{2,1},{3,4},{4,3},{5,6},{6,5},{7,8},{8,7},{9,10},{10,... | collective-permute-start | bytes 393224 | tf_op jit(solution)/shard_map/ppermute | solution.py:216
  38.0 7.5 %collective-permute-start.10 = (bf16[256,256]{1,0:T(8,128)(2,1)S(1)}, bf16[256,256]{1,0:T(8,128)(2,1)S(1)}, u32[]{:S(2)}, u32[]{:S(2)}) collective-permute-start(bf16[256,256]{1,0:T(8,128)(2,1)S(1)} %get-tuple-element.101), channel_id=1, source_target_pairs={{0,1},{1,0},{2,3},{3,2},{4,5},{5,4},{6,7},{7,6},{8,9},{9,8},{10,11... | collective-permute-start | bytes 393224 | tf_op jit(solution)/shard_map/ppermute | solution.py:216
  38.1 8.0 %collective-permute-start.11 = (bf16[256,256]{1,0:T(8,128)(2,1)S(1)}, bf16[256,256]{1,0:T(8,128)(2,1)S(1)}, u32[]{:S(2)}, u32[]{:S(2)}) collective-permute-start(bf16[256,256]{1,0:T(8,128)(2,1)S(1)} %get-tuple-element.102), channel_id=1, source_target_pairs={{0,31},{1,2},{2,1},{3,4},{4,3},{5,6},{6,5},{7,8},{8,7},{9,10},{10,... | collective-permute-start | bytes 393224 | tf_op jit(solution)/shard_map/ppermute | solution.py:216
  44.6 7.9 %collective-permute-start.26 = (bf16[256,256]{1,0:T(8,128)(2,1)S(1)}, bf16[256,256]{1,0:T(8,128)(2,1)S(1)}, u32[]{:S(2)}, u32[]{:S(2)}) collective-permute-start(bf16[256,256]{1,0:T(8,128)(2,1)S(1)} %get-tuple-element.139), channel_id=1, source_target_pairs={{0,1},{1,0},{2,3},{3,2},{4,5},{5,4},{6,7},{7,6},{8,9},{9,8},{10,11... | collective-permute-start | bytes 393224 | tf_op jit(solution)/shard_map/ppermute | solution.py:216
  44.7 7.8 %collective-permute-start.27 = (bf16[256,256]{1,0:T(8,128)(2,1)S(1)}, bf16[256,256]{1,0:T(8,128)(2,1)S(1)}, u32[]{:S(2)}, u32[]{:S(2)}) collective-permute-start(bf16[256,256]{1,0:T(8,128)(2,1)S(1)} %get-tuple-element.140), channel_id=1, source_target_pairs={{0,31},{1,2},{2,1},{3,4},{4,3},{5,6},{6,5},{7,8},{8,7},{9,10},{10,... | collective-permute-start | bytes 393224 | tf_op jit(solution)/shard_map/ppermute | solution.py:216
  47.3 7.3 %collective-permute-start.12 = (bf16[256,256]{1,0:T(8,128)(2,1)S(1)}, bf16[256,256]{1,0:T(8,128)(2,1)S(1)}, u32[]{:S(2)}, u32[]{:S(2)}) collective-permute-start(bf16[256,256]{1,0:T(8,128)(2,1)S(1)} %get-tuple-element.105), channel_id=1, source_target_pairs={{0,1},{1,0},{2,3},{3,2},{4,5},{5,4},{6,7},{7,6},{8,9},{9,8},{10,11... | collective-permute-start | bytes 393224 | tf_op jit(solution)/shard_map/ppermute | solution.py:216
  47.4 7.8 %collective-permute-start.13 = (bf16[256,256]{1,0:T(8,128)(2,1)S(1)}, bf16[256,256]{1,0:T(8,128)(2,1)S(1)}, u32[]{:S(2)}, u32[]{:S(2)}) collective-permute-start(bf16[256,256]{1,0:T(8,128)(2,1)S(1)} %get-tuple-element.106), channel_id=1, source_target_pairs={{0,31},{1,2},{2,1},{3,4},{4,3},{5,6},{6,5},{7,8},{8,7},{9,10},{10,... | collective-permute-start | bytes 393224 | tf_op jit(solution)/shard_map/ppermute | solution.py:216
  53.7 7.9 %collective-permute-start.28 = (bf16[256,256]{1,0:T(8,128)(2,1)S(1)}, bf16[256,256]{1,0:T(8,128)(2,1)S(1)}, u32[]{:S(2)}, u32[]{:S(2)}) collective-permute-start(bf16[256,256]{1,0:T(8,128)(2,1)S(1)} %get-tuple-element.143), channel_id=1, source_target_pairs={{0,1},{1,0},{2,3},{3,2},{4,5},{5,4},{6,7},{7,6},{8,9},{9,8},{10,11... | collective-permute-start | bytes 393224 | tf_op jit(solution)/shard_map/ppermute | solution.py:216
  53.8 7.8 %collective-permute-start.29 = (bf16[256,256]{1,0:T(8,128)(2,1)S(1)}, bf16[256,256]{1,0:T(8,128)(2,1)S(1)}, u32[]{:S(2)}, u32[]{:S(2)}) collective-permute-start(bf16[256,256]{1,0:T(8,128)(2,1)S(1)} %get-tuple-element.144), channel_id=1, source_target_pairs={{0,31},{1,2},{2,1},{3,4},{4,3},{5,6},{6,5},{7,8},{8,7},{9,10},{10,... | collective-permute-start | bytes 393224 | tf_op jit(solution)/shard_map/ppermute | solution.py:216
  56.4 7.3 %collective-permute-start.14 = (bf16[256,256]{1,0:T(8,128)(2,1)S(1)}, bf16[256,256]{1,0:T(8,128)(2,1)S(1)}, u32[]{:S(2)}, u32[]{:S(2)}) collective-permute-start(bf16[256,256]{1,0:T(8,128)(2,1)S(1)} %get-tuple-element.109), channel_id=1, source_target_pairs={{0,1},{1,0},{2,3},{3,2},{4,5},{5,4},{6,7},{7,6},{8,9},{9,8},{10,11... | collective-permute-start | bytes 393224 | tf_op jit(solution)/shard_map/ppermute | solution.py:216
  56.5 7.8 %collective-permute-start.15 = (bf16[256,256]{1,0:T(8,128)(2,1)S(1)}, bf16[256,256]{1,0:T(8,128)(2,1)S(1)}, u32[]{:S(2)}, u32[]{:S(2)}) collective-permute-start(bf16[256,256]{1,0:T(8,128)(2,1)S(1)} %get-tuple-element.110), channel_id=1, source_target_pairs={{0,31},{1,2},{2,1},{3,4},{4,3},{5,6},{6,5},{7,8},{8,7},{9,10},{10,... | collective-permute-start | bytes 393224 | tf_op jit(solution)/shard_map/ppermute | solution.py:216
  62.8 7.9 %collective-permute-start.30 = (bf16[256,256]{1,0:T(8,128)(2,1)S(1)}, bf16[256,256]{1,0:T(8,128)(2,1)S(1)}, u32[]{:S(2)}, u32[]{:S(2)}) collective-permute-start(bf16[256,256]{1,0:T(8,128)(2,1)S(1)} %get-tuple-element.147), channel_id=1, source_target_pairs={{0,1},{1,0},{2,3},{3,2},{4,5},{5,4},{6,7},{7,6},{8,9},{9,8},{10,11... | collective-permute-start | bytes 393224 | tf_op jit(solution)/shard_map/ppermute | solution.py:216
  62.9 7.8 %collective-permute-start.31 = (bf16[256,256]{1,0:T(8,128)(2,1)S(1)}, bf16[256,256]{1,0:T(8,128)(2,1)S(1)}, u32[]{:S(2)}, u32[]{:S(2)}) collective-permute-start(bf16[256,256]{1,0:T(8,128)(2,1)S(1)} %get-tuple-element.148), channel_id=1, source_target_pairs={{0,31},{1,2},{2,1},{3,4},{4,3},{5,6},{6,5},{7,8},{8,7},{9,10},{10,... | collective-permute-start | bytes 393224 | tf_op jit(solution)/shard_map/ppermute | solution.py:216
  65.6 7.5 %collective-permute-start.16 = (bf16[256,256]{1,0:T(8,128)(2,1)S(1)}, bf16[256,256]{1,0:T(8,128)(2,1)S(1)}, u32[]{:S(2)}, u32[]{:S(2)}) collective-permute-start(bf16[256,256]{1,0:T(8,128)(2,1)S(1)} %get-tuple-element.113), channel_id=1, source_target_pairs={{0,1},{1,0},{2,3},{3,2},{4,5},{5,4},{6,7},{7,6},{8,9},{9,8},{10,11... | collective-permute-start | bytes 393224 | tf_op jit(solution)/shard_map/ppermute | solution.py:216
  65.7 7.8 %collective-permute-start.17 = (bf16[256,256]{1,0:T(8,128)(2,1)S(1)}, bf16[256,256]{1,0:T(8,128)(2,1)S(1)}, u32[]{:S(2)}, u32[]{:S(2)}) collective-permute-start(bf16[256,256]{1,0:T(8,128)(2,1)S(1)} %get-tuple-element.114), channel_id=1, source_target_pairs={{0,31},{1,2},{2,1},{3,4},{4,3},{5,6},{6,5},{7,8},{8,7},{9,10},{10,... | collective-permute-start | bytes 393224 | tf_op jit(solution)/shard_map/ppermute | solution.py:216
  71.9 7.9 %collective-permute-start.32 = (bf16[256,256]{1,0:T(8,128)(2,1)S(1)}, bf16[256,256]{1,0:T(8,128)(2,1)S(1)}, u32[]{:S(2)}, u32[]{:S(2)}) collective-permute-start(bf16[256,256]{1,0:T(8,128)(2,1)S(1)} %get-tuple-element.151), channel_id=1, source_target_pairs={{0,1},{1,0},{2,3},{3,2},{4,5},{5,4},{6,7},{7,6},{8,9},{9,8},{10,11... | collective-permute-start | bytes 393224 | tf_op jit(solution)/shard_map/ppermute | solution.py:216
  72.0 8.0 %collective-permute-start.33 = (bf16[256,256]{1,0:T(8,128)(2,1)S(1)}, bf16[256,256]{1,0:T(8,128)(2,1)S(1)}, u32[]{:S(2)}, u32[]{:S(2)}) collective-permute-start(bf16[256,256]{1,0:T(8,128)(2,1)S(1)} %get-tuple-element.152), channel_id=1, source_target_pairs={{0,31},{1,2},{2,1},{3,4},{4,3},{5,6},{6,5},{7,8},{8,7},{9,10},{10,... | collective-permute-start | bytes 393224 | tf_op jit(solution)/shard_map/ppermute | solution.py:216
  74.7 7.5 %collective-permute-start.18 = (bf16[256,256]{1,0:T(8,128)(2,1)S(1)}, bf16[256,256]{1,0:T(8,128)(2,1)S(1)}, u32[]{:S(2)}, u32[]{:S(2)}) collective-permute-start(bf16[256,256]{1,0:T(8,128)(2,1)S(1)} %get-tuple-element.117), channel_id=1, source_target_pairs={{0,1},{1,0},{2,3},{3,2},{4,5},{5,4},{6,7},{7,6},{8,9},{9,8},{10,11... | collective-permute-start | bytes 393224 | tf_op jit(solution)/shard_map/ppermute | solution.py:216
  74.8 7.8 %collective-permute-start.19 = (bf16[256,256]{1,0:T(8,128)(2,1)S(1)}, bf16[256,256]{1,0:T(8,128)(2,1)S(1)}, u32[]{:S(2)}, u32[]{:S(2)}) collective-permute-start(bf16[256,256]{1,0:T(8,128)(2,1)S(1)} %get-tuple-element.118), channel_id=1, source_target_pairs={{0,31},{1,2},{2,1},{3,4},{4,3},{5,6},{6,5},{7,8},{8,7},{9,10},{10,... | collective-permute-start | bytes 393224 | tf_op jit(solution)/shard_map/ppermute | solution.py:216
  81.3 7.7 %collective-permute-start.34 = (bf16[256,256]{1,0:T(8,128)(2,1)S(1)}, bf16[256,256]{1,0:T(8,128)(2,1)S(1)}, u32[]{:S(2)}, u32[]{:S(2)}) collective-permute-start(bf16[256,256]{1,0:T(8,128)(2,1)S(1)} %get-tuple-element.155), channel_id=1, source_target_pairs={{0,1},{1,0},{2,3},{3,2},{4,5},{5,4},{6,7},{7,6},{8,9},{9,8},{10,11... | collective-permute-start | bytes 393224 | tf_op jit(solution)/shard_map/ppermute | solution.py:216
  81.4 7.8 %collective-permute-start.35 = (bf16[256,256]{1,0:T(8,128)(2,1)S(1)}, bf16[256,256]{1,0:T(8,128)(2,1)S(1)}, u32[]{:S(2)}, u32[]{:S(2)}) collective-permute-start(bf16[256,256]{1,0:T(8,128)(2,1)S(1)} %get-tuple-element.156), channel_id=1, source_target_pairs={{0,31},{1,2},{2,1},{3,4},{4,3},{5,6},{6,5},{7,8},{8,7},{9,10},{10,... | collective-permute-start | bytes 393224 | tf_op jit(solution)/shard_map/ppermute | solution.py:216
  83.8 6.1 %collective-permute-start.20 = (bf16[256,256]{1,0:T(8,128)(2,1)S(1)}, bf16[256,256]{1,0:T(8,128)(2,1)S(1)}, u32[]{:S(2)}, u32[]{:S(2)}) collective-permute-start(bf16[256,256]{1,0:T(8,128)(2,1)S(1)} %get-tuple-element.121), channel_id=1, source_target_pairs={{0,1},{1,0},{2,3},{3,2},{4,5},{5,4},{6,7},{7,6},{8,9},{9,8},{10,11... | collective-permute-start | bytes 393224 | tf_op jit(solution)/shard_map/ppermute | solution.py:216
  83.9 7.8 %collective-permute-start.21 = (bf16[256,256]{1,0:T(8,128)(2,1)S(1)}, bf16[256,256]{1,0:T(8,128)(2,1)S(1)}, u32[]{:S(2)}, u32[]{:S(2)}) collective-permute-start(bf16[256,256]{1,0:T(8,128)(2,1)S(1)} %get-tuple-element.122), channel_id=1, source_target_pairs={{0,31},{1,2},{2,1},{3,4},{4,3},{5,6},{6,5},{7,8},{8,7},{9,10},{10,... | collective-permute-start | bytes 393224 | tf_op jit(solution)/shard_map/ppermute | solution.py:216

commit v4 on v3

--- a/solution.py
+++ b/solution.py
@@ -63,10 +63,10 @@
 
 
 def prologue_body(per_section, *refs):
-    feat, rows_hbm, count_hbm, src_hbm, val_hbm, w_hbm, gain_hbm = refs[:7]
-    graph_outs = [refs[7 + 6 * g : 13 + 6 * g] for g in range(per_section)]
-    scaled_ref, mine_ref, *tables = refs[7 + 6 * per_section : 9 + 7 * per_section]
-    rows_all, count_ref, src_all, w_ref, gain_ref, sems, small_sems, feat_sems, val_sems = refs[9 + 7 * per_section :]
+    feat, rows_hbm, count_hbm, src_hbm, w_hbm, gain_hbm = refs[:6]
+    graph_outs = [refs[6 + 3 * g : 9 + 3 * g] for g in range(per_section)]
+    on_all, off_all, scaled_ref, mine_ref, *tables = refs[6 + 3 * per_section : 10 + 4 * per_section]
+    rows_all, count_ref, src_all, w_ref, gain_ref, sems, small_sems, feat_sems = refs[10 + 4 * per_section :]
     even = dom_parity() == 0
     graphs = [graph_of(g, per_section) for g in range(per_section)]
     count_copy = pltpu.make_async_copy(count_hbm, count_ref, sems.at[0])
@@ -90,14 +90,11 @@
     ]
     for copy in later:
         copy.start()
-    val_copies = []
-    for g, graph in enumerate(graphs):
-        val_copies += chunked(val_hbm.at[graph], graph_outs[g][5], val_sems.at[g])
     count_copy.wait()
     for g, graph in enumerate(graphs):
-        h_ref, nrm_ref, sel_ref, on_ref, off_ref, _ = graph_outs[g]
+        h_ref, nrm_ref, sel_ref = graph_outs[g]
         rows_dev = h_ref.shape[0]
-        bnd = on_ref.shape[0]
+        bnd = on_all.shape[1]
         own, half = rows_dev // TILE, bnd // TILE
         for copy in small[g]:
             copy.wait()
@@ -127,12 +124,19 @@
             step = rows_dev // len(feat_copies[g])
             block = slice(c * step, (c + 1) * step)
             nrm_ref[block, :] = normalise(h_ref[block, :].astype(F32))
-        send_rows(sel_ref, nrm_ref, on_ref, off_ref)
+        send_rows(sel_ref, nrm_ref, on_all.at[g], off_all.at[g])
     for copy in later:
         copy.wait()
     scale(w_ref, gain_ref, scaled_ref)
     mine_ref[...] = scaled_ref[dom_parity()]
-    for copy in val_copies:
+
+
+def fetch_body(per_section, val_ref, after_ref, *refs):
+    outs, sems = refs[:per_section], refs[per_section]
+    copies = []
+    for g, out in enumerate(outs):
+        copies += chunked(val_ref.at[graph_of(g, per_section)], out, sems.at[g])
+    for copy in copies:
         copy.wait()
 
 
@@ -144,7 +148,8 @@
         out_ref[k] = (w_ref[k].astype(F32) * column).astype(BF)
 
 
-def pack_body(after_ref, *refs):
+def pack_body(*refs):
+    refs = refs[-4:]
     for k, part in enumerate(refs[:-1]):
         refs[-1][k] = part[...]
 
@@ -161,7 +166,7 @@
         out_ref[source * 2 + 1 - parity] = swapped_ref[shift - 1]
 
 
-def layer_body(layer, last, others, idx_ref, h_ref, nrm_ref, on_in, off_in, tv_ref, sel_ref, w_ref, *rest):
+def layer_body(layer, graph, last, others, idx_ref, h_ref, nrm_ref, on_in, off_in, tv_ref, sel_ref, w_ref, *rest):
     done, rest = rest[:others], rest[others:]
     if last and others:
         out_ref, ext, agg, out_h, sems = rest
@@ -172,6 +177,8 @@
         out_h, ext, agg = rest
     else:
         out_h, out_n, on_ref, off_ref, ext, agg = rest
+    if len(on_in.shape) == 3:
+        on_in, off_in = on_in.at[graph], off_in.at[graph]
     rows_dev = h_ref.shape[0]
     bnd = on_in.shape[0]
     own, half = rows_dev // TILE, bnd // TILE
@@ -190,13 +197,15 @@
         update = jnp.dot(agg[rows, :], w_ref[layer], preferred_element_type=F32)
         new = (h_ref[rows, :].astype(F32) + update).astype(BF)
         out_h[rows, :] = new
+        if last and others:
+            at = pl.ds(r, step)
+            copies.append(pltpu.make_async_copy(out_h.at[at], out_ref.at[others, at], sems.at[others + r // step]))
+            copies[-1].start()
         if not last:
             out_n[rows, :] = normalise(new.astype(F32))
     if not last:
         send_rows(sel_ref, out_n, on_ref, off_ref)
     elif others:
-        copies.append(pltpu.make_async_copy(out_h, out_ref.at[others], sems.at[others]))
-        copies[-1].start()
         for copy in copies:
             copy.wait()
 
@@ -222,12 +231,11 @@
         for x in (features, tile_val, boundary_rows, boundary_count, tile_src, weights, gains)
     )
     square = (width, width)
-    per_graph = [(rows_dev, width), (rows_dev, width), (2 * bnd, rows_dev), (bnd, width), (bnd, width)]
-    per_graph += [(rows_dev, K * TILE)]
+    per_graph = [(rows_dev, width), (rows_dev, width), (2 * bnd, rows_dev)]
     results = call(
         functools.partial(prologue_body, per_section),
-        per_graph * per_section + [weights.shape, square],
-        [HBM] * 7,
+        per_graph * per_section + [(per_section, bnd, width)] * 2 + [weights.shape, square],
+        [HBM] * 6,
         "prologue",
         [
             pltpu.VMEM((per_section, 2, bnd), jnp.int32),
@@ -238,25 +246,29 @@
             pltpu.SemaphoreType.DMA((3,)),
             pltpu.SemaphoreType.DMA((per_section, 2)),
             pltpu.SemaphoreType.DMA((per_section, 4)),
-            pltpu.SemaphoreType.DMA((per_section, 4)),
         ],
         limit=16,
         ints=[(tiles * K, TILE)] * per_section,
-    )(features, boundary_rows, boundary_count, tile_src, tile_val, weights, gains)
-    scaled, mine, *tables = results[6 * per_section :]
-    state, values = [], []
+    )(features, boundary_rows, boundary_count, tile_src, weights, gains)
+    on_all, off_all, scaled, mine, *tables = results[3 * per_section :]
+    on_all = lax.ppermute(on_all, "dom", on_pairs)
+    off_all = lax.ppermute(off_all, "dom", off_pairs)
+    state = []
     for g in range(per_section):
-        h, nrm, sel, on, off, value = results[6 * g : 6 * g + 6]
-        values.append(value)
-        on = lax.ppermute(on, "dom", on_pairs)
-        off, on = lax.optimization_barrier((off, on))
-        off = lax.ppermute(off, "dom", off_pairs)
-        state.append([h, nrm, on, off, sel, tables[g]])
+        h, nrm, sel = results[3 * g : 3 * g + 3]
+        state.append([h, nrm, on_all, off_all, sel, tables[g]])
+    values = call(
+        functools.partial(fetch_body, per_section),
+        [(rows_dev, K * TILE)] * per_section,
+        [HBM, VMEM],
+        "fetch",
+        [pltpu.SemaphoreType.DMA((per_section, 4))],
+    )(tile_val, on_all)
     parts = [
         lax.ppermute(mine, "section", [(i, (i + shift) % sections) for i in range(sections)])
         for shift in range(1, sections)
     ]
-    packed = call(pack_body, [(sections - 1, *square)], [VMEM] * sections, "pack")(state[0][3], *parts)[0]
+    packed = call(pack_body, [(sections - 1, *square)], [VMEM] * (sections + 1), "pack")(off_all, values[0], *parts)[0]
     swapped = lax.ppermute(packed, "dom", on_pairs)
     w_all = call(order_body, [(layers, *square)], [VMEM] * 3, "order")(scaled, packed, swapped)[0]
     outputs = []
@@ -269,13 +281,13 @@
             others = len(outputs) if final else 0
             if final:
                 outs = [(per_section, rows_dev, width)]
-                scratch += [pltpu.VMEM((rows_dev, width), BF), pltpu.SemaphoreType.DMA((per_section,))]
+                scratch += [pltpu.VMEM((rows_dev, width), BF), pltpu.SemaphoreType.DMA((others + 4,))]
             elif last:
                 outs = [(rows_dev, width)]
             else:
                 outs = [(rows_dev, width), (rows_dev, width), (bnd, width), (bnd, width)]
             result = call(
-                functools.partial(layer_body, layer, last, others),
+                functools.partial(layer_body, layer, g, last, others),
                 outs,
                 [VMEM] * (8 + others),
                 "layer",

time: 93.7 us -> 92.1 us (0.983)
  starting transfers between devices: 58.2 us -> 49.1 us
  waiting for transfers between devices: 11.1 us -> 17.8 us
  Pallas kernels: 23.6 us -> 24.6 us
    ppermute x14, waiting for transfers between devices: 5.31 us -> 11.3 us  [exchange(): lax.ppermute(off, 'dom', off_pairs)]
    ppermute x14, starting transfers between devices: 41.6 us -> 36.9 us  [exchange(): lax.ppermute(off, 'dom', off_pairs)]
    ppermute x4 -> x2, starting transfers between devices: 9.95 us -> 5.48 us  [the longest x1 5.39 us: on_device(): off_all = lax.ppermute(off_all, 'dom', off_pairs)]
    ppermute x4 -> x2, waiting for transfers between devices: 1.82 us -> 0.01 us  [the longest x1 0.01 us: on_device(): on_all = lax.ppermute(on_all, 'dom', on_pairs)]
    ppermute x1, waiting for transfers between devices: 0.01 us -> 1.71 us  [on_device(): swapped = lax.ppermute(packed, 'dom', on_pairs)]
    pallas_call x17 -> x18, Pallas kernels: 19.4 us -> 20.9 us  [the longest x16 19.3 us: on_device(): call(functools.partial(layer_body, layer, g, last, others), outs, [VMEM]...]
  transfers between devices with their start and end apart: 36 -> 34, of which waited for: 15 -> 13; matrix products, arithmetic and copies ran while one was open for 0% -> 0% of each run, Pallas kernels for 19% -> 20%
where the time goes in v4:
time: 92.1 us; the launch traced here: 91.9 us
  starting transfers between devices  49.1 us (53%)
  Pallas kernels  24.6 us (27%)
  waiting for transfers between devices  17.8 us (19%)
    ppermute x14, starting transfers between devices, exchange(): lax.ppermute(off, 'dom', off_pairs)  36.9 us
    pallas_call x16, Pallas kernels, on_device(): call(functools.partial(layer_body, layer, g, last, others), outs, [VMEM]...  19.3 us
    ppermute x14, waiting for transfers between devices, exchange(): lax.ppermute(off, 'dom', off_pairs)  11.3 us
    ppermute x1, starting transfers between devices, on_device(): off_all = lax.ppermute(off_all, 'dom', off_pairs)  5.39 us
    ppermute x3, starting transfers between devices, on_device(): lax.ppermute(mine, 'section', [(i, (i + shift) % sections) for i in range...  5.3 us
    ppermute x3, waiting for transfers between devices, on_device(): lax.ppermute(mine, 'section', [(i, (i + shift) % sections) for i in range...  4.74 us
    pallas_call x1, Pallas kernels, on_device(): call(functools.partial(prologue_body, per_section), per_graph * per_secti...  3.65 us
  transfers between devices with their start and end apart: 34, of which 13 were waited for; matrix products, arithmetic and copies ran while one was open for 0% of the time, Pallas kernels for 20%

profile of v4, /device:TPU:0, one launch (start us, length us, event | category | flops | bytes accessed | tf_op | source)
XLA Modules:
  0.0 91.9 jit_solution(13304909801917867351)
XLA Ops:
  0.0 3.7 %prologue.1 = (bf16[1024,256]{1,0:T(8,128)(2,1)S(1)}, bf16[1024,256]{1,0:T(8,128)(2,1)S(1)}, bf16[512,1024]{1,0:T(8,128)(2,1)S(1)}, bf16[1024,256]{1,0:T(8,128)(...) custom-call(bf16[8,1024,256]{2,1,0:T(8,128)(2,1)} %refs_0_.1, ...), custom_call_target="tpu_custom_call" | custom-call | bytes 1024 | tf_op jit(solution)/shard_map/prologue/pallas_call | solution.py:235
  3.7 0.1 collective-permute-start
  3.8 5.4 %collective-permute-start.1 = (bf16[2,256,256]{2,1,0:T(8,128)(2,1)S(1)}, bf16[2,256,256]{2,1,0:T(8,128)(2,1)S(1)}, u32[]{:S(2)}, u32[]{:S(2)}) collective-permute-start(bf16[2,256,256]{2,1,0:T(8,128)(2,1)S(1)} %get-tuple-element.79), channel_id=1, source_target_pairs={{0,31},{1,2},{2,1},{3,4},{4,3},{5,6},{6,5},{7,8},{8,7},{9,10},{10,... | collective-permute-start | bytes 786440 | tf_op jit(solution)/shard_map/ppermute | solution.py:255
  9.1 4.0 %collective-permute-start.4 = (bf16[256,256]{1,0:T(8,128)(2,1)S(1)}, bf16[256,256]{1,0:T(8,128)(2,1)S(1)}, u32[]{:S(2)}, u32[]{:S(2)}) collective-permute-start(bf16[256,256]{1,0:T(8,128)(2,1)S(1)} %get-tuple-element.84), channel_id=1, source_target_pairs={{0,96},{32,0},{64,32},{96,64},{1,97},{33,1},{65,33},{97,65},{2,98}... | collective-permute-start | bytes 393224 | tf_op jit(solution)/shard_map/ppermute | solution.py:268
  13.2 1.3 %collective-permute-start.2 = (bf16[256,256]{1,0:T(8,128)(2,1)S(1)}, bf16[256,256]{1,0:T(8,128)(2,1)S(1)}, u32[]{:S(2)}, u32[]{:S(2)}) collective-permute-start(bf16[256,256]{1,0:T(8,128)(2,1)S(1)} %get-tuple-element.84), channel_id=1, source_target_pairs={{0,32},{32,64},{64,96},{96,0},{1,33},{33,65},{65,97},{97,1},{2,34}... | collective-permute-start | bytes 393224 | tf_op jit(solution)/shard_map/ppermute | solution.py:268
  14.4 1.6 %fetch.1 = (bf16[1024,512]{1,0:T(8,128)(2,1)S(1)}, bf16[1024,512]{1,0:T(8,128)(2,1)S(1)}) custom-call(bf16[8,1024,512]{2,1,0:T(8,128)(2,1)} %val_ref.1, bf16[2,256,256]{2,1,0:T(8,128)(2,1)S(1)} %collective-permute-done.after_ref.on_in), custom_call_target="tpu_custom_call" | custom-call | bytes 1024 | tf_op jit(solution)/shard_map/fetch/pallas_call | solution.py:260
  16.0 1.1 %collective-permute-done.4.refs_4_ = bf16[256,256]{1,0:T(8,128)(2,1)S(1)} collective-permute-done((bf16[256,256]{1,0:T(8,128)(2,1)S(1)}, bf16[256,256]{1,0:T(8,128)(2,1)S(1)}, u32[]{:S(2)}, u32[]{:S(2)}) %collective-permute-start.4) | collective-permute-done | bytes 131104 | tf_op jit(solution)/shard_map/ppermute | solution.py:268
  17.1 2.7 %collective-permute-done.3.refs_3_ = bf16[256,256]{1,0:T(8,128)(2,1)S(1)} collective-permute-done((bf16[256,256]{1,0:T(8,128)(2,1)S(1)}, bf16[256,256]{1,0:T(8,128)(2,1)S(1)}, u32[]{:S(2)}, u32[]{:S(2)}) %collective-permute-start.3) | collective-permute-done | bytes 131104 | tf_op jit(solution)/shard_map/ppermute | solution.py:268
  19.8 1.0 %collective-permute-done.2.refs_2_ = bf16[256,256]{1,0:T(8,128)(2,1)S(1)} collective-permute-done((bf16[256,256]{1,0:T(8,128)(2,1)S(1)}, bf16[256,256]{1,0:T(8,128)(2,1)S(1)}, u32[]{:S(2)}, u32[]{:S(2)}) %collective-permute-start.2) | collective-permute-done | bytes 131104 | tf_op jit(solution)/shard_map/ppermute | solution.py:268
  20.8 0.1 collective-permute-start.5
  20.9 1.7 %collective-permute-done.5.swapped_ref = bf16[3,256,256]{2,1,0:T(8,128)(2,1)S(1)} collective-permute-done((bf16[3,256,256]{2,1,0:T(8,128)(2,1)S(1)}, bf16[3,256,256]{2,1,0:T(8,128)(2,1)S(1)}, u32[]{:S(2)}, u32[]{:S(2)}) %collective-permute-start.5) | collective-permute-done | bytes 393248 | tf_op jit(solution)/shard_map/ppermute | solution.py:272
  22.7 1.2 %layer.23 = (bf16[1024,256]{1,0:T(8,128)(2,1)S(1)}, bf16[1024,256]{1,0:T(8,128)(2,1)S(1)}, bf16[256,256]{1,0:T(8,128)(2,1)S(1)}, bf16[256,256]{1,0:T(8,128)(2,1)S(1)}) custom-call(s32[32,128]{1,0:T(8,128)S(1)} %get-tuple-element.113.idx_ref, bf16[1024,256]{1,0:T(8,128)(2,1)S(1)} %get-tuple-element.114.h_ref, ...), custom_call_target="tpu_custom_call" | custom-call | flops 1000000 | bytes 1024 | tf_op jit(solution)/shard_map/layer/pallas_call | solution.py:289
  23.9 0.2 collective-permute-start.20
  24.1 1.9 %collective-permute-start.21 = (bf16[256,256]{1,0:T(8,128)(2,1)S(1)}, bf16[256,256]{1,0:T(8,128)(2,1)S(1)}, u32[]{:S(2)}, u32[]{:S(2)}) collective-permute-start(bf16[256,256]{1,0:T(8,128)(2,1)S(1)} %get-tuple-element.120), channel_id=1, source_target_pairs={{0,31},{1,2},{2,1},{3,4},{4,3},{5,6},{6,5},{7,8},{8,7},{9,10},{10,... | collective-permute-start | bytes 393224 | tf_op jit(solution)/shard_map/ppermute | solution.py:225
  26.1 1.2 %layer.16 = (bf16[1024,256]{1,0:T(8,128)(2,1)S(1)}, bf16[1024,256]{1,0:T(8,128)(2,1)S(1)}, bf16[256,256]{1,0:T(8,128)(2,1)S(1)}, bf16[256,256]{1,0:T(8,128)(2,1)S(1)}) custom-call(s32[32,128]{1,0:T(8,128)S(1)} %get-tuple-element.75.idx_ref, bf16[1024,256]{1,0:T(8,128)(2,1)S(1)} %get-tuple-element.76.h_ref, bf16[1024,256]{1,0:T(8,128)(2,1)S(1)} %get-tuple-element.77.nrm_ref, ...), custom_call_target="tpu_custom_call" | custom-call | flops 1000000 | bytes 1024 | tf_op jit(solution)/shard_map/layer/pallas_call | solution.py:289
  27.3 0.1 collective-permute-start.6
  27.4 3.2 %collective-permute-start.7 = (bf16[256,256]{1,0:T(8,128)(2,1)S(1)}, bf16[256,256]{1,0:T(8,128)(2,1)S(1)}, u32[]{:S(2)}, u32[]{:S(2)}) collective-permute-start(bf16[256,256]{1,0:T(8,128)(2,1)S(1)} %get-tuple-element.88), channel_id=1, source_target_pairs={{0,31},{1,2},{2,1},{3,4},{4,3},{5,6},{6,5},{7,8},{8,7},{9,10},{10,... | collective-permute-start | bytes 393224 | tf_op jit(solution)/shard_map/ppermute | solution.py:225
  30.6 1.2 %collective-permute-done.21.off_in = bf16[256,256]{1,0:T(8,128)(2,1)S(1)} collective-permute-done((bf16[256,256]{1,0:T(8,128)(2,1)S(1)}, bf16[256,256]{1,0:T(8,128)(2,1)S(1)}, u32[]{:S(2)}, u32[]{:S(2)}) %collective-permute-start.21) | collective-permute-done | bytes 131104 | tf_op jit(solution)/shard_map/ppermute | solution.py:225
  31.9 1.2 %layer.24 = (bf16[1024,256]{1,0:T(8,128)(2,1)S(1)}, bf16[1024,256]{1,0:T(8,128)(2,1)S(1)}, bf16[256,256]{1,0:T(8,128)(2,1)S(1)}, bf16[256,256]{1,0:T(8,128)(2,1)S(1)}) custom-call(s32[32,128]{1,0:T(8,128)S(1)} %get-tuple-element.113.idx_ref, bf16[1024,256]{1,0:T(8,128)(2,1)S(1)} %get-tuple-element.117.h_ref, ...), custom_call_target="tpu_custom_call" | custom-call | flops 1000000 | bytes 1024 | tf_op jit(solution)/shard_map/layer/pallas_call | solution.py:289
  33.1 0.1 collective-permute-start.22
  33.2 2.0 %collective-permute-start.23 = (bf16[256,256]{1,0:T(8,128)(2,1)S(1)}, bf16[256,256]{1,0:T(8,128)(2,1)S(1)}, u32[]{:S(2)}, u32[]{:S(2)}) collective-permute-start(bf16[256,256]{1,0:T(8,128)(2,1)S(1)} %get-tuple-element.124), channel_id=1, source_target_pairs={{0,31},{1,2},{2,1},{3,4},{4,3},{5,6},{6,5},{7,8},{8,7},{9,10},{10,... | collective-permute-start | bytes 393224 | tf_op jit(solution)/shard_map/ppermute | solution.py:225
  35.2 1.2 %layer.17 = (bf16[1024,256]{1,0:T(8,128)(2,1)S(1)}, bf16[1024,256]{1,0:T(8,128)(2,1)S(1)}, bf16[256,256]{1,0:T(8,128)(2,1)S(1)}, bf16[256,256]{1,0:T(8,128)(2,1)S(1)}) custom-call(s32[32,128]{1,0:T(8,128)S(1)} %get-tuple-element.75.idx_ref, bf16[1024,256]{1,0:T(8,128)(2,1)S(1)} %get-tuple-element.85.h_ref, bf16[1024,256]{1,0:T(8,128)(2,1)S(1)} %get-tuple-element.86.nrm_ref, ...), custom_call_target="tpu_custom_call" | custom-call | flops 1000000 | bytes 1024 | tf_op jit(solution)/shard_map/layer/pallas_call | solution.py:289
  36.4 0.1 collective-permute-start.8
  36.5 3.2 %collective-permute-start.9 = (bf16[256,256]{1,0:T(8,128)(2,1)S(1)}, bf16[256,256]{1,0:T(8,128)(2,1)S(1)}, u32[]{:S(2)}, u32[]{:S(2)}) collective-permute-start(bf16[256,256]{1,0:T(8,128)(2,1)S(1)} %get-tuple-element.92), channel_id=1, source_target_pairs={{0,31},{1,2},{2,1},{3,4},{4,3},{5,6},{6,5},{7,8},{8,7},{9,10},{10,... | collective-permute-start | bytes 393224 | tf_op jit(solution)/shard_map/ppermute | solution.py:225
  39.7 1.2 %collective-permute-done.23.off_in = bf16[256,256]{1,0:T(8,128)(2,1)S(1)} collective-permute-done((bf16[256,256]{1,0:T(8,128)(2,1)S(1)}, bf16[256,256]{1,0:T(8,128)(2,1)S(1)}, u32[]{:S(2)}, u32[]{:S(2)}) %collective-permute-start.23) | collective-permute-done | bytes 131104 | tf_op jit(solution)/shard_map/ppermute | solution.py:225
  41.0 1.2 %layer.25 = (bf16[1024,256]{1,0:T(8,128)(2,1)S(1)}, bf16[1024,256]{1,0:T(8,128)(2,1)S(1)}, bf16[256,256]{1,0:T(8,128)(2,1)S(1)}, bf16[256,256]{1,0:T(8,128)(2,1)S(1)}) custom-call(s32[32,128]{1,0:T(8,128)S(1)} %get-tuple-element.113.idx_ref, bf16[1024,256]{1,0:T(8,128)(2,1)S(1)} %get-tuple-element.121.h_ref, ...), custom_call_target="tpu_custom_call" | custom-call | flops 1000000 | bytes 1024 | tf_op jit(solution)/shard_map/layer/pallas_call | solution.py:289
  42.2 0.1 collective-permute-start.24
  42.3 2.2 %collective-permute-start.25 = (bf16[256,256]{1,0:T(8,128)(2,1)S(1)}, bf16[256,256]{1,0:T(8,128)(2,1)S(1)}, u32[]{:S(2)}, u32[]{:S(2)}) collective-permute-start(bf16[256,256]{1,0:T(8,128)(2,1)S(1)} %get-tuple-element.128), channel_id=1, source_target_pairs={{0,31},{1,2},{2,1},{3,4},{4,3},{5,6},{6,5},{7,8},{8,7},{9,10},{10,... | collective-permute-start | bytes 393224 | tf_op jit(solution)/shard_map/ppermute | solution.py:225
  44.5 1.2 %layer.18 = (bf16[1024,256]{1,0:T(8,128)(2,1)S(1)}, bf16[1024,256]{1,0:T(8,128)(2,1)S(1)}, bf16[256,256]{1,0:T(8,128)(2,1)S(1)}, bf16[256,256]{1,0:T(8,128)(2,1)S(1)}) custom-call(s32[32,128]{1,0:T(8,128)S(1)} %get-tuple-element.75.idx_ref, bf16[1024,256]{1,0:T(8,128)(2,1)S(1)} %get-tuple-element.89.h_ref, bf16[1024,256]{1,0:T(8,128)(2,1)S(1)} %get-tuple-element.90.nrm_ref, ...), custom_call_target="tpu_custom_call" | custom-call | flops 1000000 | bytes 1024 | tf_op jit(solution)/shard_map/layer/pallas_call | solution.py:289
  45.7 0.1 collective-permute-start.10
  45.8 3.2 %collective-permute-start.11 = (bf16[256,256]{1,0:T(8,128)(2,1)S(1)}, bf16[256,256]{1,0:T(8,128)(2,1)S(1)}, u32[]{:S(2)}, u32[]{:S(2)}) collective-permute-start(bf16[256,256]{1,0:T(8,128)(2,1)S(1)} %get-tuple-element.96), channel_id=1, source_target_pairs={{0,31},{1,2},{2,1},{3,4},{4,3},{5,6},{6,5},{7,8},{8,7},{9,10},{10,... | collective-permute-start | bytes 393224 | tf_op jit(solution)/shard_map/ppermute | solution.py:225
  49.0 1.2 %collective-permute-done.25.off_in = bf16[256,256]{1,0:T(8,128)(2,1)S(1)} collective-permute-done((bf16[256,256]{1,0:T(8,128)(2,1)S(1)}, bf16[256,256]{1,0:T(8,128)(2,1)S(1)}, u32[]{:S(2)}, u32[]{:S(2)}) %collective-permute-start.25) | collective-permute-done | bytes 131104 | tf_op jit(solution)/shard_map/ppermute | solution.py:225
  50.3 1.2 %layer.26 = (bf16[1024,256]{1,0:T(8,128)(2,1)S(1)}, bf16[1024,256]{1,0:T(8,128)(2,1)S(1)}, bf16[256,256]{1,0:T(8,128)(2,1)S(1)}, bf16[256,256]{1,0:T(8,128)(2,1)S(1)}) custom-call(s32[32,128]{1,0:T(8,128)S(1)} %get-tuple-element.113.idx_ref, bf16[1024,256]{1,0:T(8,128)(2,1)S(1)} %get-tuple-element.125.h_ref, ...), custom_call_target="tpu_custom_call" | custom-call | flops 1000000 | bytes 1024 | tf_op jit(solution)/shard_map/layer/pallas_call | solution.py:289
  51.5 0.1 collective-permute-start.26
  51.6 2.0 %collective-permute-start.27 = (bf16[256,256]{1,0:T(8,128)(2,1)S(1)}, bf16[256,256]{1,0:T(8,128)(2,1)S(1)}, u32[]{:S(2)}, u32[]{:S(2)}) collective-permute-start(bf16[256,256]{1,0:T(8,128)(2,1)S(1)} %get-tuple-element.132), channel_id=1, source_target_pairs={{0,31},{1,2},{2,1},{3,4},{4,3},{5,6},{6,5},{7,8},{8,7},{9,10},{10,... | collective-permute-start | bytes 393224 | tf_op jit(solution)/shard_map/ppermute | solution.py:225
  53.6 1.2 %layer.19 = (bf16[1024,256]{1,0:T(8,128)(2,1)S(1)}, bf16[1024,256]{1,0:T(8,128)(2,1)S(1)}, bf16[256,256]{1,0:T(8,128)(2,1)S(1)}, bf16[256,256]{1,0:T(8,128)(2,1)S(1)}) custom-call(s32[32,128]{1,0:T(8,128)S(1)} %get-tuple-element.75.idx_ref, bf16[1024,256]{1,0:T(8,128)(2,1)S(1)} %get-tuple-element.93.h_ref, bf16[1024,256]{1,0:T(8,128)(2,1)S(1)} %get-tuple-element.94.nrm_ref, ...), custom_call_target="tpu_custom_call" | custom-call | flops 1000000 | bytes 1024 | tf_op jit(solution)/shard_map/layer/pallas_call | solution.py:289
  54.9 0.1 collective-permute-start.12
  55.0 3.2 %collective-permute-start.13 = (bf16[256,256]{1,0:T(8,128)(2,1)S(1)}, bf16[256,256]{1,0:T(8,128)(2,1)S(1)}, u32[]{:S(2)}, u32[]{:S(2)}) collective-permute-start(bf16[256,256]{1,0:T(8,128)(2,1)S(1)} %get-tuple-element.100), channel_id=1, source_target_pairs={{0,31},{1,2},{2,1},{3,4},{4,3},{5,6},{6,5},{7,8},{8,7},{9,10},{10,... | collective-permute-start | bytes 393224 | tf_op jit(solution)/shard_map/ppermute | solution.py:225
  58.2 1.2 %collective-permute-done.27.off_in = bf16[256,256]{1,0:T(8,128)(2,1)S(1)} collective-permute-done((bf16[256,256]{1,0:T(8,128)(2,1)S(1)}, bf16[256,256]{1,0:T(8,128)(2,1)S(1)}, u32[]{:S(2)}, u32[]{:S(2)}) %collective-permute-start.27) | collective-permute-done | bytes 131104 | tf_op jit(solution)/shard_map/ppermute | solution.py:225
  59.4 1.2 %layer.27 = (bf16[1024,256]{1,0:T(8,128)(2,1)S(1)}, bf16[1024,256]{1,0:T(8,128)(2,1)S(1)}, bf16[256,256]{1,0:T(8,128)(2,1)S(1)}, bf16[256,256]{1,0:T(8,128)(2,1)S(1)}) custom-call(s32[32,128]{1,0:T(8,128)S(1)} %get-tuple-element.113.idx_ref, bf16[1024,256]{1,0:T(8,128)(2,1)S(1)} %get-tuple-element.129.h_ref, ...), custom_call_target="tpu_custom_call" | custom-call | flops 1000000 | bytes 1024 | tf_op jit(solution)/shard_map/layer/pallas_call | solution.py:289
  60.6 0.1 collective-permute-start.28
  60.7 2.0 %collective-permute-start.29 = (bf16[256,256]{1,0:T(8,128)(2,1)S(1)}, bf16[256,256]{1,0:T(8,128)(2,1)S(1)}, u32[]{:S(2)}, u32[]{:S(2)}) collective-permute-start(bf16[256,256]{1,0:T(8,128)(2,1)S(1)} %get-tuple-element.136), channel_id=1, source_target_pairs={{0,31},{1,2},{2,1},{3,4},{4,3},{5,6},{6,5},{7,8},{8,7},{9,10},{10,... | collective-permute-start | bytes 393224 | tf_op jit(solution)/shard_map/ppermute | solution.py:225
  62.7 1.2 %layer.20 = (bf16[1024,256]{1,0:T(8,128)(2,1)S(1)}, bf16[1024,256]{1,0:T(8,128)(2,1)S(1)}, bf16[256,256]{1,0:T(8,128)(2,1)S(1)}, bf16[256,256]{1,0:T(8,128)(2,1)S(1)}) custom-call(s32[32,128]{1,0:T(8,128)S(1)} %get-tuple-element.75.idx_ref, bf16[1024,256]{1,0:T(8,128)(2,1)S(1)} %get-tuple-element.97.h_ref, bf16[1024,256]{1,0:T(8,128)(2,1)S(1)} %get-tuple-element.98.nrm_ref, ...), custom_call_target="tpu_custom_call" | custom-call | flops 1000000 | bytes 1024 | tf_op jit(solution)/shard_map/layer/pallas_call | solution.py:289
  64.0 0.1 collective-permute-start.14
  64.1 3.2 %collective-permute-start.15 = (bf16[256,256]{1,0:T(8,128)(2,1)S(1)}, bf16[256,256]{1,0:T(8,128)(2,1)S(1)}, u32[]{:S(2)}, u32[]{:S(2)}) collective-permute-start(bf16[256,256]{1,0:T(8,128)(2,1)S(1)} %get-tuple-element.104), channel_id=1, source_target_pairs={{0,31},{1,2},{2,1},{3,4},{4,3},{5,6},{6,5},{7,8},{8,7},{9,10},{10,... | collective-permute-start | bytes 393224 | tf_op jit(solution)/shard_map/ppermute | solution.py:225
  67.3 1.2 %collective-permute-done.29.off_in = bf16[256,256]{1,0:T(8,128)(2,1)S(1)} collective-permute-done((bf16[256,256]{1,0:T(8,128)(2,1)S(1)}, bf16[256,256]{1,0:T(8,128)(2,1)S(1)}, u32[]{:S(2)}, u32[]{:S(2)}) %collective-permute-start.29) | collective-permute-done | bytes 131104 | tf_op jit(solution)/shard_map/ppermute | solution.py:225
  68.5 1.2 %layer.28 = (bf16[1024,256]{1,0:T(8,128)(2,1)S(1)}, bf16[1024,256]{1,0:T(8,128)(2,1)S(1)}, bf16[256,256]{1,0:T(8,128)(2,1)S(1)}, bf16[256,256]{1,0:T(8,128)(2,1)S(1)}) custom-call(s32[32,128]{1,0:T(8,128)S(1)} %get-tuple-element.113.idx_ref, bf16[1024,256]{1,0:T(8,128)(2,1)S(1)} %get-tuple-element.133.h_ref, ...), custom_call_target="tpu_custom_call" | custom-call | flops 1000000 | bytes 1024 | tf_op jit(solution)/shard_map/layer/pallas_call | solution.py:289
  69.7 0.1 collective-permute-start.30
  69.8 2.0 %collective-permute-start.31 = (bf16[256,256]{1,0:T(8,128)(2,1)S(1)}, bf16[256,256]{1,0:T(8,128)(2,1)S(1)}, u32[]{:S(2)}, u32[]{:S(2)}) collective-permute-start(bf16[256,256]{1,0:T(8,128)(2,1)S(1)} %get-tuple-element.140), channel_id=1, source_target_pairs={{0,31},{1,2},{2,1},{3,4},{4,3},{5,6},{6,5},{7,8},{8,7},{9,10},{10,... | collective-permute-start | bytes 393224 | tf_op jit(solution)/shard_map/ppermute | solution.py:225
  71.9 1.2 %layer.21 = (bf16[1024,256]{1,0:T(8,128)(2,1)S(1)}, bf16[1024,256]{1,0:T(8,128)(2,1)S(1)}, bf16[256,256]{1,0:T(8,128)(2,1)S(1)}, bf16[256,256]{1,0:T(8,128)(2,1)S(1)}) custom-call(s32[32,128]{1,0:T(8,128)S(1)} %get-tuple-element.75.idx_ref, bf16[1024,256]{1,0:T(8,128)(2,1)S(1)} %get-tuple-element.101.h_ref, ...), custom_call_target="tpu_custom_call" | custom-call | flops 1000000 | bytes 1024 | tf_op jit(solution)/shard_map/layer/pallas_call | solution.py:289
  73.1 0.1 collective-permute-start.16
  73.2 3.4 %collective-permute-start.17 = (bf16[256,256]{1,0:T(8,128)(2,1)S(1)}, bf16[256,256]{1,0:T(8,128)(2,1)S(1)}, u32[]{:S(2)}, u32[]{:S(2)}) collective-permute-start(bf16[256,256]{1,0:T(8,128)(2,1)S(1)} %get-tuple-element.108), channel_id=1, source_target_pairs={{0,31},{1,2},{2,1},{3,4},{4,3},{5,6},{6,5},{7,8},{8,7},{9,10},{10,... | collective-permute-start | bytes 393224 | tf_op jit(solution)/shard_map/ppermute | solution.py:225
  76.6 1.0 %collective-permute-done.31.off_in = bf16[256,256]{1,0:T(8,128)(2,1)S(1)} collective-permute-done((bf16[256,256]{1,0:T(8,128)(2,1)S(1)}, bf16[256,256]{1,0:T(8,128)(2,1)S(1)}, u32[]{:S(2)}, u32[]{:S(2)}) %collective-permute-start.31) | collective-permute-done | bytes 131104 | tf_op jit(solution)/shard_map/ppermute | solution.py:225
  77.6 1.2 %layer.29 = (bf16[1024,256]{1,0:T(8,128)(2,1)S(1)}, bf16[1024,256]{1,0:T(8,128)(2,1)S(1)}, bf16[256,256]{1,0:T(8,128)(2,1)S(1)}, bf16[256,256]{1,0:T(8,128)(2,1)S(1)}) custom-call(s32[32,128]{1,0:T(8,128)S(1)} %get-tuple-element.113.idx_ref, bf16[1024,256]{1,0:T(8,128)(2,1)S(1)} %get-tuple-element.137.h_ref, ...), custom_call_target="tpu_custom_call" | custom-call | flops 1000000 | bytes 1024 | tf_op jit(solution)/shard_map/layer/pallas_call | solution.py:289
  78.9 0.1 collective-permute-start.32
  79.0 2.0 %collective-permute-start.33 = (bf16[256,256]{1,0:T(8,128)(2,1)S(1)}, bf16[256,256]{1,0:T(8,128)(2,1)S(1)}, u32[]{:S(2)}, u32[]{:S(2)}) collective-permute-start(bf16[256,256]{1,0:T(8,128)(2,1)S(1)} %get-tuple-element.144), channel_id=1, source_target_pairs={{0,31},{1,2},{2,1},{3,4},{4,3},{5,6},{6,5},{7,8},{8,7},{9,10},{10,... | collective-permute-start | bytes 393224 | tf_op jit(solution)/shard_map/ppermute | solution.py:225
  81.0 0.2 collective-permute-done.17.off_in
  81.2 1.2 %layer.22 = (bf16[1024,256]{1,0:T(8,128)(2,1)S(1)}, bf16[1024,256]{1,0:T(8,128)(2,1)S(1)}, bf16[256,256]{1,0:T(8,128)(2,1)S(1)}, bf16[256,256]{1,0:T(8,128)(2,1)S(1)}) custom-call(s32[32,128]{1,0:T(8,128)S(1)} %get-tuple-element.75.idx_ref, bf16[1024,256]{1,0:T(8,128)(2,1)S(1)} %get-tuple-element.105.h_ref, ...), custom_call_target="tpu_custom_call" | custom-call | flops 1000000 | bytes 1024 | tf_op jit(solution)/shard_map/layer/pallas_call | solution.py:289
  82.4 0.1 collective-permute-start.18
  82.5 3.2 %collective-permute-start.19 = (bf16[256,256]{1,0:T(8,128)(2,1)S(1)}, bf16[256,256]{1,0:T(8,128)(2,1)S(1)}, u32[]{:S(2)}, u32[]{:S(2)}) collective-permute-start(bf16[256,256]{1,0:T(8,128)(2,1)S(1)} %get-tuple-element.112), channel_id=1, source_target_pairs={{0,31},{1,2},{2,1},{3,4},{4,3},{5,6},{6,5},{7,8},{8,7},{9,10},{10,... | collective-permute-start | bytes 393224 | tf_op jit(solution)/shard_map/ppermute | solution.py:225
  85.7 1.0 %collective-permute-done.33.off_in = bf16[256,256]{1,0:T(8,128)(2,1)S(1)} collective-permute-done((bf16[256,256]{1,0:T(8,128)(2,1)S(1)}, bf16[256,256]{1,0:T(8,128)(2,1)S(1)}, u32[]{:S(2)}, u32[]{:S(2)}) %collective-permute-start.33) | collective-permute-done | bytes 131104 | tf_op jit(solution)/shard_map/ppermute | solution.py:225
  86.8 0.7 layer.30.rest_0_
  87.5 2.9 %collective-permute-done.19.off_in = bf16[256,256]{1,0:T(8,128)(2,1)S(1)} collective-permute-done((bf16[256,256]{1,0:T(8,128)(2,1)S(1)}, bf16[256,256]{1,0:T(8,128)(2,1)S(1)}, u32[]{:S(2)}, u32[]{:S(2)}) %collective-permute-start.19) | collective-permute-done | bytes 131104 | tf_op jit(solution)/shard_map/ppermute | solution.py:225
  90.3 1.4 %layer.31 = bf16[2,1024,256]{2,1,0:T(8,128)(2,1)} custom-call(s32[32,128]{1,0:T(8,128)S(1)} %get-tuple-element.75.idx_ref, bf16[1024,256]{1,0:T(8,128)(2,1)S(1)} %get-tuple-element.109.h_ref, bf16[1024,256]{1,0:T(8,128)(2,1)S(1)} %get-tuple-element.110.nrm_ref, bf16[256,256]{1,0:T(8,128)(2,1)S(1)} %collective-permute-done.18.on_in, ...), custom_call_target="tpu_custom_call" | custom-call | flops 1000000 | bytes 1024 | tf_op jit(solution)/shard_map/layer/pallas_call | solution.py:289
  (24 shorter events, 0.2 us)
Async XLA Ops:
  3.7 10.8 %collective-permute-start = (bf16[2,256,256]{2,1,0:T(8,128)(2,1)S(1)}, bf16[2,256,256]{2,1,0:T(8,128)(2,1)S(1)}, u32[]{:S(2)}, u32[]{:S(2)}) collective-permute-start(bf16[2,256,256]{2,1,0:T(8,128)(2,1)S(1)} %get-tuple-element.78), channel_id=1, source_target_pairs={{0,1},{1,0},{2,3},{3,2},{4,5},{5,4},{6,7},{7,6},{8,9},{9,8},{10,11... | collective-permute-start | bytes 786440 | tf_op jit(solution)/shard_map/ppermute | solution.py:254
  3.8 17.0 %collective-permute-start.1 = (bf16[2,256,256]{2,1,0:T(8,128)(2,1)S(1)}, bf16[2,256,256]{2,1,0:T(8,128)(2,1)S(1)}, u32[]{:S(2)}, u32[]{:S(2)}) collective-permute-start(bf16[2,256,256]{2,1,0:T(8,128)(2,1)S(1)} %get-tuple-element.79), channel_id=1, source_target_pairs={{0,31},{1,2},{2,1},{3,4},{4,3},{5,6},{6,5},{7,8},{8,7},{9,10},{10,... | collective-permute-start | bytes 786440 | tf_op jit(solution)/shard_map/ppermute | solution.py:255
  9.1 8.0 %collective-permute-start.4 = (bf16[256,256]{1,0:T(8,128)(2,1)S(1)}, bf16[256,256]{1,0:T(8,128)(2,1)S(1)}, u32[]{:S(2)}, u32[]{:S(2)}) collective-permute-start(bf16[256,256]{1,0:T(8,128)(2,1)S(1)} %get-tuple-element.84), channel_id=1, source_target_pairs={{0,96},{32,0},{64,32},{96,64},{1,97},{33,1},{65,33},{97,65},{2,98}... | collective-permute-start | bytes 393224 | tf_op jit(solution)/shard_map/ppermute | solution.py:268
  13.2 6.6 %collective-permute-start.3 = (bf16[256,256]{1,0:T(8,128)(2,1)S(1)}, bf16[256,256]{1,0:T(8,128)(2,1)S(1)}, u32[]{:S(2)}, u32[]{:S(2)}) collective-permute-start(bf16[256,256]{1,0:T(8,128)(2,1)S(1)} %get-tuple-element.84), channel_id=1, source_target_pairs={{0,64},{32,96},{64,0},{96,32},{1,65},{33,97},{65,1},{97,33},{2,66}... | collective-permute-start | bytes 393224 | tf_op jit(solution)/shard_map/ppermute | solution.py:268
  13.2 7.6 %collective-permute-start.2 = (bf16[256,256]{1,0:T(8,128)(2,1)S(1)}, bf16[256,256]{1,0:T(8,128)(2,1)S(1)}, u32[]{:S(2)}, u32[]{:S(2)}) collective-permute-start(bf16[256,256]{1,0:T(8,128)(2,1)S(1)} %get-tuple-element.84), channel_id=1, source_target_pairs={{0,32},{32,64},{64,96},{96,0},{1,33},{33,65},{65,97},{97,1},{2,34}... | collective-permute-start | bytes 393224 | tf_op jit(solution)/shard_map/ppermute | solution.py:268
  20.8 1.8 %collective-permute-start.5 = (bf16[3,256,256]{2,1,0:T(8,128)(2,1)S(1)}, bf16[3,256,256]{2,1,0:T(8,128)(2,1)S(1)}, u32[]{:S(2)}, u32[]{:S(2)}) collective-permute-start(bf16[3,256,256]{2,1,0:T(8,128)(2,1)S(1)} %pack.1.mine_ref), channel_id=1, source_target_pairs={{0,1},{1,0},{2,3},{3,2},{4,5},{5,4},{6,7},{7,6},{8,9},{9,8},{10,11... | collective-permute-start | bytes 1179656 | tf_op jit(solution)/shard_map/ppermute | solution.py:272
  23.9 6.7 %collective-permute-start.20 = (bf16[256,256]{1,0:T(8,128)(2,1)S(1)}, bf16[256,256]{1,0:T(8,128)(2,1)S(1)}, u32[]{:S(2)}, u32[]{:S(2)}) collective-permute-start(bf16[256,256]{1,0:T(8,128)(2,1)S(1)} %get-tuple-element.119), channel_id=1, source_target_pairs={{0,1},{1,0},{2,3},{3,2},{4,5},{5,4},{6,7},{7,6},{8,9},{9,8},{10,11... | collective-permute-start | bytes 393224 | tf_op jit(solution)/shard_map/ppermute | solution.py:225
  24.1 7.7 %collective-permute-start.21 = (bf16[256,256]{1,0:T(8,128)(2,1)S(1)}, bf16[256,256]{1,0:T(8,128)(2,1)S(1)}, u32[]{:S(2)}, u32[]{:S(2)}) collective-permute-start(bf16[256,256]{1,0:T(8,128)(2,1)S(1)} %get-tuple-element.120), channel_id=1, source_target_pairs={{0,31},{1,2},{2,1},{3,4},{4,3},{5,6},{6,5},{7,8},{8,7},{9,10},{10,... | collective-permute-start | bytes 393224 | tf_op jit(solution)/shard_map/ppermute | solution.py:225
  27.3 7.9 %collective-permute-start.6 = (bf16[256,256]{1,0:T(8,128)(2,1)S(1)}, bf16[256,256]{1,0:T(8,128)(2,1)S(1)}, u32[]{:S(2)}, u32[]{:S(2)}) collective-permute-start(bf16[256,256]{1,0:T(8,128)(2,1)S(1)} %get-tuple-element.87), channel_id=1, source_target_pairs={{0,1},{1,0},{2,3},{3,2},{4,5},{5,4},{6,7},{7,6},{8,9},{9,8},{10,11... | collective-permute-start | bytes 393224 | tf_op jit(solution)/shard_map/ppermute | solution.py:225
  27.4 7.8 %collective-permute-start.7 = (bf16[256,256]{1,0:T(8,128)(2,1)S(1)}, bf16[256,256]{1,0:T(8,128)(2,1)S(1)}, u32[]{:S(2)}, u32[]{:S(2)}) collective-permute-start(bf16[256,256]{1,0:T(8,128)(2,1)S(1)} %get-tuple-element.88), channel_id=1, source_target_pairs={{0,31},{1,2},{2,1},{3,4},{4,3},{5,6},{6,5},{7,8},{8,7},{9,10},{10,... | collective-permute-start | bytes 393224 | tf_op jit(solution)/shard_map/ppermute | solution.py:225
  33.1 6.7 %collective-permute-start.22 = (bf16[256,256]{1,0:T(8,128)(2,1)S(1)}, bf16[256,256]{1,0:T(8,128)(2,1)S(1)}, u32[]{:S(2)}, u32[]{:S(2)}) collective-permute-start(bf16[256,256]{1,0:T(8,128)(2,1)S(1)} %get-tuple-element.123), channel_id=1, source_target_pairs={{0,1},{1,0},{2,3},{3,2},{4,5},{5,4},{6,7},{7,6},{8,9},{9,8},{10,11... | collective-permute-start | bytes 393224 | tf_op jit(solution)/shard_map/ppermute | solution.py:225
  33.2 7.8 %collective-permute-start.23 = (bf16[256,256]{1,0:T(8,128)(2,1)S(1)}, bf16[256,256]{1,0:T(8,128)(2,1)S(1)}, u32[]{:S(2)}, u32[]{:S(2)}) collective-permute-start(bf16[256,256]{1,0:T(8,128)(2,1)S(1)} %get-tuple-element.124), channel_id=1, source_target_pairs={{0,31},{1,2},{2,1},{3,4},{4,3},{5,6},{6,5},{7,8},{8,7},{9,10},{10,... | collective-permute-start | bytes 393224 | tf_op jit(solution)/shard_map/ppermute | solution.py:225
  36.4 8.1 %collective-permute-start.8 = (bf16[256,256]{1,0:T(8,128)(2,1)S(1)}, bf16[256,256]{1,0:T(8,128)(2,1)S(1)}, u32[]{:S(2)}, u32[]{:S(2)}) collective-permute-start(bf16[256,256]{1,0:T(8,128)(2,1)S(1)} %get-tuple-element.91), channel_id=1, source_target_pairs={{0,1},{1,0},{2,3},{3,2},{4,5},{5,4},{6,7},{7,6},{8,9},{9,8},{10,11... | collective-permute-start | bytes 393224 | tf_op jit(solution)/shard_map/ppermute | solution.py:225
  36.5 8.0 %collective-permute-start.9 = (bf16[256,256]{1,0:T(8,128)(2,1)S(1)}, bf16[256,256]{1,0:T(8,128)(2,1)S(1)}, u32[]{:S(2)}, u32[]{:S(2)}) collective-permute-start(bf16[256,256]{1,0:T(8,128)(2,1)S(1)} %get-tuple-element.92), channel_id=1, source_target_pairs={{0,31},{1,2},{2,1},{3,4},{4,3},{5,6},{6,5},{7,8},{8,7},{9,10},{10,... | collective-permute-start | bytes 393224 | tf_op jit(solution)/shard_map/ppermute | solution.py:225
  42.2 6.8 %collective-permute-start.24 = (bf16[256,256]{1,0:T(8,128)(2,1)S(1)}, bf16[256,256]{1,0:T(8,128)(2,1)S(1)}, u32[]{:S(2)}, u32[]{:S(2)}) collective-permute-start(bf16[256,256]{1,0:T(8,128)(2,1)S(1)} %get-tuple-element.127), channel_id=1, source_target_pairs={{0,1},{1,0},{2,3},{3,2},{4,5},{5,4},{6,7},{7,6},{8,9},{9,8},{10,11... | collective-permute-start | bytes 393224 | tf_op jit(solution)/shard_map/ppermute | solution.py:225
  42.3 8.0 %collective-permute-start.25 = (bf16[256,256]{1,0:T(8,128)(2,1)S(1)}, bf16[256,256]{1,0:T(8,128)(2,1)S(1)}, u32[]{:S(2)}, u32[]{:S(2)}) collective-permute-start(bf16[256,256]{1,0:T(8,128)(2,1)S(1)} %get-tuple-element.128), channel_id=1, source_target_pairs={{0,31},{1,2},{2,1},{3,4},{4,3},{5,6},{6,5},{7,8},{8,7},{9,10},{10,... | collective-permute-start | bytes 393224 | tf_op jit(solution)/shard_map/ppermute | solution.py:225
  45.7 7.9 %collective-permute-start.10 = (bf16[256,256]{1,0:T(8,128)(2,1)S(1)}, bf16[256,256]{1,0:T(8,128)(2,1)S(1)}, u32[]{:S(2)}, u32[]{:S(2)}) collective-permute-start(bf16[256,256]{1,0:T(8,128)(2,1)S(1)} %get-tuple-element.95), channel_id=1, source_target_pairs={{0,1},{1,0},{2,3},{3,2},{4,5},{5,4},{6,7},{7,6},{8,9},{9,8},{10,11... | collective-permute-start | bytes 393224 | tf_op jit(solution)/shard_map/ppermute | solution.py:225
  45.8 7.8 %collective-permute-start.11 = (bf16[256,256]{1,0:T(8,128)(2,1)S(1)}, bf16[256,256]{1,0:T(8,128)(2,1)S(1)}, u32[]{:S(2)}, u32[]{:S(2)}) collective-permute-start(bf16[256,256]{1,0:T(8,128)(2,1)S(1)} %get-tuple-element.96), channel_id=1, source_target_pairs={{0,31},{1,2},{2,1},{3,4},{4,3},{5,6},{6,5},{7,8},{8,7},{9,10},{10,... | collective-permute-start | bytes 393224 | tf_op jit(solution)/shard_map/ppermute | solution.py:225
  51.5 6.7 %collective-permute-start.26 = (bf16[256,256]{1,0:T(8,128)(2,1)S(1)}, bf16[256,256]{1,0:T(8,128)(2,1)S(1)}, u32[]{:S(2)}, u32[]{:S(2)}) collective-permute-start(bf16[256,256]{1,0:T(8,128)(2,1)S(1)} %get-tuple-element.131), channel_id=1, source_target_pairs={{0,1},{1,0},{2,3},{3,2},{4,5},{5,4},{6,7},{7,6},{8,9},{9,8},{10,11... | collective-permute-start | bytes 393224 | tf_op jit(solution)/shard_map/ppermute | solution.py:225
  51.6 7.8 %collective-permute-start.27 = (bf16[256,256]{1,0:T(8,128)(2,1)S(1)}, bf16[256,256]{1,0:T(8,128)(2,1)S(1)}, u32[]{:S(2)}, u32[]{:S(2)}) collective-permute-start(bf16[256,256]{1,0:T(8,128)(2,1)S(1)} %get-tuple-element.132), channel_id=1, source_target_pairs={{0,31},{1,2},{2,1},{3,4},{4,3},{5,6},{6,5},{7,8},{8,7},{9,10},{10,... | collective-permute-start | bytes 393224 | tf_op jit(solution)/shard_map/ppermute | solution.py:225
  54.9 7.9 %collective-permute-start.12 = (bf16[256,256]{1,0:T(8,128)(2,1)S(1)}, bf16[256,256]{1,0:T(8,128)(2,1)S(1)}, u32[]{:S(2)}, u32[]{:S(2)}) collective-permute-start(bf16[256,256]{1,0:T(8,128)(2,1)S(1)} %get-tuple-element.99), channel_id=1, source_target_pairs={{0,1},{1,0},{2,3},{3,2},{4,5},{5,4},{6,7},{7,6},{8,9},{9,8},{10,11... | collective-permute-start | bytes 393224 | tf_op jit(solution)/shard_map/ppermute | solution.py:225
  55.0 7.8 %collective-permute-start.13 = (bf16[256,256]{1,0:T(8,128)(2,1)S(1)}, bf16[256,256]{1,0:T(8,128)(2,1)S(1)}, u32[]{:S(2)}, u32[]{:S(2)}) collective-permute-start(bf16[256,256]{1,0:T(8,128)(2,1)S(1)} %get-tuple-element.100), channel_id=1, source_target_pairs={{0,31},{1,2},{2,1},{3,4},{4,3},{5,6},{6,5},{7,8},{8,7},{9,10},{10,... | collective-permute-start | bytes 393224 | tf_op jit(solution)/shard_map/ppermute | solution.py:225
  60.6 6.7 %collective-permute-start.28 = (bf16[256,256]{1,0:T(8,128)(2,1)S(1)}, bf16[256,256]{1,0:T(8,128)(2,1)S(1)}, u32[]{:S(2)}, u32[]{:S(2)}) collective-permute-start(bf16[256,256]{1,0:T(8,128)(2,1)S(1)} %get-tuple-element.135), channel_id=1, source_target_pairs={{0,1},{1,0},{2,3},{3,2},{4,5},{5,4},{6,7},{7,6},{8,9},{9,8},{10,11... | collective-permute-start | bytes 393224 | tf_op jit(solution)/shard_map/ppermute | solution.py:225
  60.7 7.8 %collective-permute-start.29 = (bf16[256,256]{1,0:T(8,128)(2,1)S(1)}, bf16[256,256]{1,0:T(8,128)(2,1)S(1)}, u32[]{:S(2)}, u32[]{:S(2)}) collective-permute-start(bf16[256,256]{1,0:T(8,128)(2,1)S(1)} %get-tuple-element.136), channel_id=1, source_target_pairs={{0,31},{1,2},{2,1},{3,4},{4,3},{5,6},{6,5},{7,8},{8,7},{9,10},{10,... | collective-permute-start | bytes 393224 | tf_op jit(solution)/shard_map/ppermute | solution.py:225
  64.0 7.9 %collective-permute-start.14 = (bf16[256,256]{1,0:T(8,128)(2,1)S(1)}, bf16[256,256]{1,0:T(8,128)(2,1)S(1)}, u32[]{:S(2)}, u32[]{:S(2)}) collective-permute-start(bf16[256,256]{1,0:T(8,128)(2,1)S(1)} %get-tuple-element.103), channel_id=1, source_target_pairs={{0,1},{1,0},{2,3},{3,2},{4,5},{5,4},{6,7},{7,6},{8,9},{9,8},{10,11... | collective-permute-start | bytes 393224 | tf_op jit(solution)/shard_map/ppermute | solution.py:225
  64.1 7.8 %collective-permute-start.15 = (bf16[256,256]{1,0:T(8,128)(2,1)S(1)}, bf16[256,256]{1,0:T(8,128)(2,1)S(1)}, u32[]{:S(2)}, u32[]{:S(2)}) collective-permute-start(bf16[256,256]{1,0:T(8,128)(2,1)S(1)} %get-tuple-element.104), channel_id=1, source_target_pairs={{0,31},{1,2},{2,1},{3,4},{4,3},{5,6},{6,5},{7,8},{8,7},{9,10},{10,... | collective-permute-start | bytes 393224 | tf_op jit(solution)/shard_map/ppermute | solution.py:225
  69.7 6.9 %collective-permute-start.30 = (bf16[256,256]{1,0:T(8,128)(2,1)S(1)}, bf16[256,256]{1,0:T(8,128)(2,1)S(1)}, u32[]{:S(2)}, u32[]{:S(2)}) collective-permute-start(bf16[256,256]{1,0:T(8,128)(2,1)S(1)} %get-tuple-element.139), channel_id=1, source_target_pairs={{0,1},{1,0},{2,3},{3,2},{4,5},{5,4},{6,7},{7,6},{8,9},{9,8},{10,11... | collective-permute-start | bytes 393224 | tf_op jit(solution)/shard_map/ppermute | solution.py:225
  69.8 7.8 %collective-permute-start.31 = (bf16[256,256]{1,0:T(8,128)(2,1)S(1)}, bf16[256,256]{1,0:T(8,128)(2,1)S(1)}, u32[]{:S(2)}, u32[]{:S(2)}) collective-permute-start(bf16[256,256]{1,0:T(8,128)(2,1)S(1)} %get-tuple-element.140), channel_id=1, source_target_pairs={{0,31},{1,2},{2,1},{3,4},{4,3},{5,6},{6,5},{7,8},{8,7},{9,10},{10,... | collective-permute-start | bytes 393224 | tf_op jit(solution)/shard_map/ppermute | solution.py:225
  73.1 7.9 %collective-permute-start.16 = (bf16[256,256]{1,0:T(8,128)(2,1)S(1)}, bf16[256,256]{1,0:T(8,128)(2,1)S(1)}, u32[]{:S(2)}, u32[]{:S(2)}) collective-permute-start(bf16[256,256]{1,0:T(8,128)(2,1)S(1)} %get-tuple-element.107), channel_id=1, source_target_pairs={{0,1},{1,0},{2,3},{3,2},{4,5},{5,4},{6,7},{7,6},{8,9},{9,8},{10,11... | collective-permute-start | bytes 393224 | tf_op jit(solution)/shard_map/ppermute | solution.py:225
  73.2 8.0 %collective-permute-start.17 = (bf16[256,256]{1,0:T(8,128)(2,1)S(1)}, bf16[256,256]{1,0:T(8,128)(2,1)S(1)}, u32[]{:S(2)}, u32[]{:S(2)}) collective-permute-start(bf16[256,256]{1,0:T(8,128)(2,1)S(1)} %get-tuple-element.108), channel_id=1, source_target_pairs={{0,31},{1,2},{2,1},{3,4},{4,3},{5,6},{6,5},{7,8},{8,7},{9,10},{10,... | collective-permute-start | bytes 393224 | tf_op jit(solution)/shard_map/ppermute | solution.py:225
  78.9 6.9 %collective-permute-start.32 = (bf16[256,256]{1,0:T(8,128)(2,1)S(1)}, bf16[256,256]{1,0:T(8,128)(2,1)S(1)}, u32[]{:S(2)}, u32[]{:S(2)}) collective-permute-start(bf16[256,256]{1,0:T(8,128)(2,1)S(1)} %get-tuple-element.143), channel_id=1, source_target_pairs={{0,1},{1,0},{2,3},{3,2},{4,5},{5,4},{6,7},{7,6},{8,9},{9,8},{10,11... | collective-permute-start | bytes 393224 | tf_op jit(solution)/shard_map/ppermute | solution.py:225
  79.0 7.8 %collective-permute-start.33 = (bf16[256,256]{1,0:T(8,128)(2,1)S(1)}, bf16[256,256]{1,0:T(8,128)(2,1)S(1)}, u32[]{:S(2)}, u32[]{:S(2)}) collective-permute-start(bf16[256,256]{1,0:T(8,128)(2,1)S(1)} %get-tuple-element.144), channel_id=1, source_target_pairs={{0,31},{1,2},{2,1},{3,4},{4,3},{5,6},{6,5},{7,8},{8,7},{9,10},{10,... | collective-permute-start | bytes 393224 | tf_op jit(solution)/shard_map/ppermute | solution.py:225
  82.4 5.0 %collective-permute-start.18 = (bf16[256,256]{1,0:T(8,128)(2,1)S(1)}, bf16[256,256]{1,0:T(8,128)(2,1)S(1)}, u32[]{:S(2)}, u32[]{:S(2)}) collective-permute-start(bf16[256,256]{1,0:T(8,128)(2,1)S(1)} %get-tuple-element.111), channel_id=1, source_target_pairs={{0,1},{1,0},{2,3},{3,2},{4,5},{5,4},{6,7},{7,6},{8,9},{9,8},{10,11... | collective-permute-start | bytes 393224 | tf_op jit(solution)/shard_map/ppermute | solution.py:225
  82.5 7.8 %collective-permute-start.19 = (bf16[256,256]{1,0:T(8,128)(2,1)S(1)}, bf16[256,256]{1,0:T(8,128)(2,1)S(1)}, u32[]{:S(2)}, u32[]{:S(2)}) collective-permute-start(bf16[256,256]{1,0:T(8,128)(2,1)S(1)} %get-tuple-element.112), channel_id=1, source_target_pairs={{0,31},{1,2},{2,1},{3,4},{4,3},{5,6},{6,5},{7,8},{8,7},{9,10},{10,... | collective-permute-start | bytes 393224 | tf_op jit(solution)/shard_map/ppermute | solution.py:225

commit v5 on v1

--- a/solution.py
+++ b/solution.py
@@ -62,12 +62,18 @@
     return copies
 
 
-def prologue_body(local, per_section, early, *refs):
-    feat, rows_hbm, count_hbm, src_hbm = refs[:4]
-    refs = refs[4 + early :]
-    h_ref, nrm_ref, sel_ref, on_ref, off_ref, idx_ref = refs[:6]
-    rows_ref, count_ref, src_ref, sems, feat_sems = refs[6:]
-    graph, parity = graph_of(local, per_section), dom_parity()
+def prologue_body(local, per_section, *refs):
+    feat, rows_hbm, count_hbm, src_hbm, before_ref = refs[:5]
+    h_ref, nrm_ref, sel_ref, on_ref, off_ref, idx_ref = refs[5:11]
+    rows_ref, count_ref, src_ref, sems, feat_sems = refs[11:]
+    if local:
+        for g in range(local):
+            on_ref[g] = before_ref[g]
+        on_ref = on_ref.at[local]
+    else:
+        on_ref = on_ref.at[0]
+    even = dom_parity() == 0
+    graph = graph_of(local, per_section)
     small = [
         pltpu.make_async_copy(rows_hbm.at[graph], rows_ref, sems.at[0]),
         pltpu.make_async_copy(count_hbm, count_ref, sems.at[1]),
@@ -75,20 +81,20 @@
     ]
     for copy in small:
         copy.start()
-    copies = chunked(feat.at[graph], h_ref, feat_sems)
+    feat_copies = chunked(feat.at[graph], h_ref, feat_sems)
     for copy in small:
         copy.wait()
     rows_dev = h_ref.shape[0]
-    bnd = on_ref.shape[0]
+    bnd = off_ref.shape[0]
     own, half = rows_dev // TILE, bnd // TILE
     counts = count_ref[...]
     here = lax.broadcasted_iota(jnp.int32, counts.shape, 1) == graph
     live = jnp.sum(jnp.where(here, counts, 0), axis=1, keepdims=True)
-    lane = lax.broadcasted_iota(jnp.int32, rows_ref.shape, 1)
-    rows = jnp.where(lane < live, rows_ref[...], -1).astype(F32)
+    raw = rows_ref[...]
+    lane = lax.broadcasted_iota(jnp.int32, raw.shape, 1)
+    rows = jnp.where(lane < live, raw, -1).astype(F32)
     first = jnp.broadcast_to(rows[0:1, :], (TILE, bnd))
     second = jnp.broadcast_to(rows[1:2, :], (TILE, bnd))
-    even = parity == 0
     for at, picked in ((0, jnp.where(even, second, first)), (bnd, jnp.where(even, first, second))):
         column = picked.T
         for c in range(rows_dev // TILE):
@@ -102,14 +108,15 @@
     for i in range(own):
         for k in range(K):
             idx_ref[i * K + k : i * K + k + 1, :] = jnp.broadcast_to(table[k : k + 1, i : i + 1], (1, TILE))
-    for c, copy in enumerate(copies):
+    for c, copy in enumerate(feat_copies):
         copy.wait()
-        block = slice(c * rows_dev // len(copies), (c + 1) * rows_dev // len(copies))
+        step = rows_dev // len(feat_copies)
+        block = slice(c * step, (c + 1) * step)
         nrm_ref[block, :] = normalise(h_ref[block, :].astype(F32))
     send_rows(sel_ref, nrm_ref, on_ref, off_ref)
 
 
-def fetch_body(per_section, val_ref, after_ref, *refs):
+def fetch_body(per_section, val_ref, *refs):
     outs, sems = refs[:per_section], refs[per_section]
     copies = []
     for g, out in enumerate(outs):
@@ -118,25 +125,42 @@
         copy.wait()
 
 
-def scale_body(w_ref, gain_ref, after_ref, out_ref):
+def scale_body(w_hbm, gain_hbm, out_ref, mine_ref, w_ref, gain_ref, sems):
+    copies = [
+        pltpu.make_async_copy(w_hbm, w_ref, sems.at[0]),
+        pltpu.make_async_copy(gain_hbm, gain_ref, sems.at[1]),
+    ]
+    for copy in copies:
+        copy.start()
+    for copy in copies:
+        copy.wait()
     width = w_ref.shape[1]
     gain = gain_ref[...].astype(F32)
     for k in range(w_ref.shape[0]):
         column = jnp.broadcast_to(gain[k : k + 1, :], (width, width)).T
         out_ref[k] = (w_ref[k].astype(F32) * column).astype(BF)
-
-
-def order_body(count, *refs):
-    parts, out = refs[:count], refs[count]
+    mine_ref[...] = out_ref[dom_parity()]
+
+
+def pack_body(*refs):
+    refs = refs[-4:]
+    for k, part in enumerate(refs[:-1]):
+        refs[-1][k] = part[...]
+
+
+def order_body(scaled_ref, mine_ref, swapped_ref, out_ref):
     section = lax.axis_index("section")
-    per = parts[0].shape[0]
-    for shift, part in enumerate(parts):
+    parity = dom_parity()
+    count = mine_ref.shape[0] + 1
+    for k in range(2):
+        out_ref[section * 2 + k] = scaled_ref[k]
+    for shift in range(1, count):
         source = lax.rem(section - shift + count, count)
-        for k in range(per):
-            out[source * per + k] = part[k]
-
-
-def layer_body(layer, last, others, idx_ref, h_ref, nrm_ref, on_in, off_in, tv_ref, sel_ref, w_ref, *rest):
+        out_ref[source * 2 + parity] = mine_ref[shift - 1]
+        out_ref[source * 2 + 1 - parity] = swapped_ref[shift - 1]
+
+
+def layer_body(layer, graph, last, others, idx_ref, h_ref, nrm_ref, on_in, off_in, tv_ref, sel_ref, w_ref, *rest):
     done, rest = rest[:others], rest[others:]
     if last and others:
         out_ref, ext, agg, out_h, sems = rest
@@ -147,6 +171,8 @@
         out_h, ext, agg = rest
     else:
         out_h, out_n, on_ref, off_ref, ext, agg = rest
+    if len(on_in.shape) == 3:
+        on_in = on_in.at[graph]
     rows_dev = h_ref.shape[0]
     bnd = on_in.shape[0]
     own, half = rows_dev // TILE, bnd // TILE
@@ -165,13 +191,15 @@
         update = jnp.dot(agg[rows, :], w_ref[layer], preferred_element_type=F32)
         new = (h_ref[rows, :].astype(F32) + update).astype(BF)
         out_h[rows, :] = new
+        if last and others:
+            at = pl.ds(r, step)
+            copies.append(pltpu.make_async_copy(out_h.at[at], out_ref.at[others, at], sems.at[others + r // step]))
+            copies[-1].start()
         if not last:
             out_n[rows, :] = normalise(new.astype(F32))
     if not last:
         send_rows(sel_ref, out_n, on_ref, off_ref)
     elif others:
-        copies.append(pltpu.make_async_copy(out_h, out_ref.at[others], sems.at[others]))
-        copies[-1].start()
         for copy in copies:
             copy.wait()
 
@@ -192,17 +220,26 @@
 
     tile_src = jnp.swapaxes(tile_src, 1, 2)
     boundary_count = jnp.swapaxes(boundary_count, 0, 1)
-    features, tile_val, boundary_rows, boundary_count, tile_src = (
+    features, tile_val, boundary_rows, boundary_count, tile_src, weights, gains = (
         pltpu.with_memory_space_constraint(x, pltpu.HBM)
-        for x in (features, tile_val, boundary_rows, boundary_count, tile_src)
+        for x in (features, tile_val, boundary_rows, boundary_count, tile_src, weights, gains)
     )
+    square = (width, width)
+    square = (width, width)
+    scaled, mine = call(
+        scale_body,
+        [weights.shape, square],
+        [HBM] * 2,
+        "scale",
+        [pltpu.VMEM(weights.shape, BF), pltpu.VMEM(gains.shape, BF), pltpu.SemaphoreType.DMA((2,))],
+    )(weights, gains)
+    on_all = mine
     state = []
-    early = ()
     for g in range(per_section):
-        h, nrm, sel, on, off, idx = call(
-            functools.partial(prologue_body, g, per_section, len(early)),
-            [(rows_dev, width), (rows_dev, width), (2 * bnd, rows_dev), (bnd, width), (bnd, width)],
-            [HBM] * 4 + [VMEM] * len(early),
+        h, nrm, sel, on_all, off, idx = call(
+            functools.partial(prologue_body, g, per_section),
+            [(rows_dev, width), (rows_dev, width), (2 * bnd, rows_dev), (g + 1, bnd, width), (bnd, width)],
+            [HBM] * 4 + [VMEM],
             "prologue",
             [
                 pltpu.VMEM((2, bnd), jnp.int32),
@@ -212,25 +249,26 @@
                 pltpu.SemaphoreType.DMA((4,)),
             ],
             ints=[(tiles * K, TILE)],
-        )(features, boundary_rows, boundary_count, tile_src, *early)
-        on, off = exchange(on, off)
-        state.append([h, nrm, on, off, sel, idx])
-        early = (state[0][2],)
-    scaled = call(scale_body, [weights.shape], [VMEM] * 3, "scale")(weights, gains, *early)[0]
-    parts = [scaled] + [
-        lax.ppermute(scaled, "section", [(i, (i + shift) % sections) for i in range(sections)])
-        for shift in range(1, sections)
-    ]
+        )(features, boundary_rows, boundary_count, tile_src, on_all)
+        state.append([h, nrm, None, lax.ppermute(off, "dom", off_pairs), sel, idx])
+    on_all = lax.ppermute(on_all, "dom", on_pairs)
+    for entry in state:
+        entry[2] = on_all
     values = call(
         functools.partial(fetch_body, per_section),
         [(rows_dev, K * TILE)] * per_section,
-        [HBM, VMEM],
+        [HBM],
         "fetch",
         [pltpu.SemaphoreType.DMA((per_section, 4))],
-    )(tile_val, *early)
-    w_all = call(functools.partial(order_body, sections), [(layers, width, width)], [VMEM] * sections, "order")(
-        *parts
-    )[0]
+    )(tile_val)
+    parts = [
+        lax.ppermute(mine, "section", [(i, (i + shift) % sections) for i in range(sections)])
+        for shift in range(1, sections)
+    ]
+    packed = call(pack_body, [(sections - 1, *square)], [VMEM] * (sections + 1), "pack", flops=3_000_000_000)(values[0], state[-1][1], *parts)[0]
+    packed, state[0][3] = lax.optimization_barrier((packed, state[0][3]))
+    swapped = lax.ppermute(packed, "dom", on_pairs)
+    w_all = call(order_body, [(layers, *square)], [VMEM] * 3, "order")(scaled, packed, swapped)[0]
     outputs = []
     for layer in range(layers):
         last = layer == layers - 1
@@ -241,13 +279,13 @@
             others = len(outputs) if final else 0
             if final:
                 outs = [(per_section, rows_dev, width)]
-                scratch += [pltpu.VMEM((rows_dev, width), BF), pltpu.SemaphoreType.DMA((per_section,))]
+                scratch += [pltpu.VMEM((rows_dev, width), BF), pltpu.SemaphoreType.DMA((others + 4,))]
             elif last:
                 outs = [(rows_dev, width)]
             else:
                 outs = [(rows_dev, width), (rows_dev, width), (bnd, width), (bnd, width)]
             result = call(
-                functools.partial(layer_body, layer, last, others),
+                functools.partial(layer_body, layer, g, last, others),
                 outs,
                 [VMEM] * (8 + others),
                 "layer",

time: 97.3 us -> 90.8 us (0.933)
  waiting for transfers between devices: 17.5 us -> 9.7 us
  starting transfers between devices: 52 us -> 53.8 us
  local copies, waits for them, and re-layouts: 1.63 us -> 0 us
  Pallas kernels: 25.4 us -> 26.4 us
    ppermute x3 -> x7, starting transfers between devices: 5.45 us -> 13.7 us  [the longest x2 7.72 us: on_device(): state.append([h, nrm, None, lax.ppermute(off, 'dom', off_pairs), sel, idx])]
    ppermute x16 -> x14, starting transfers between devices: 45.2 us -> 38.8 us  [exchange(): lax.ppermute(off, 'dom', off_pairs)]
    ppermute x16 -> x14, waiting for transfers between devices: 12.3 us -> 8.7 us  [exchange(): lax.ppermute(off, 'dom', off_pairs)]
    ppermute x3 -> x7, waiting for transfers between devices: 3.88 us -> 0.96 us  [the longest x2 0.95 us: on_device(): state.append([h, nrm, None, lax.ppermute(off, 'dom', off_pairs), sel, idx])]
    unnamed x4 -> x0, local copies, waits for them, and re-layouts: 1.63 us -> none
    ppermute x16 -> x14, waiting for transfers between devices: 1.37 us -> 0.04 us  [exchange(): lax.ppermute(on, 'dom', on_pairs)]
    pallas_call x20 -> x21, Pallas kernels: 23.9 us -> 24.8 us  [the longest x16 19.3 us: on_device(): call(functools.partial(layer_body, layer, g, last, others), outs, [VMEM]...]
  transfers between devices with their start and end apart: 35 -> 35, of which waited for: 11 -> 14; matrix products, arithmetic and copies ran while one was open for 0% -> 0% of each run, Pallas kernels for 22% -> 26%
where the time goes in v5:
time: 90.8 us; the launch traced here: 90.4 us
  starting transfers between devices  53.8 us (59%)
  Pallas kernels  26.4 us (29%)
  waiting for transfers between devices  9.7 us (11%)
    ppermute x14, starting transfers between devices, exchange(): lax.ppermute(off, 'dom', off_pairs)  38.8 us
    pallas_call x16, Pallas kernels, on_device(): call(functools.partial(layer_body, layer, g, last, others), outs, [VMEM]...  19.3 us
    ppermute x14, waiting for transfers between devices, exchange(): lax.ppermute(off, 'dom', off_pairs)  8.7 us
    ppermute x2, starting transfers between devices, on_device(): state.append([h, nrm, None, lax.ppermute(off, 'dom', off_pairs), sel, idx])  7.72 us
    ppermute x3, starting transfers between devices, on_device(): lax.ppermute(mine, 'section', [(i, (i + shift) % sections) for i in range...  5.45 us
    pallas_call x2, Pallas kernels, on_device(): call(functools.partial(prologue_body, g, per_section), [(rows_dev, width)...  4.29 us
  transfers between devices with their start and end apart: 35, of which 14 were waited for; matrix products, arithmetic and copies ran while one was open for 0% of the time, Pallas kernels for 26%

profile of v5, /device:TPU:0, one launch (start us, length us, event | category | flops | bytes accessed | tf_op | source)
XLA Modules:
  0.0 90.4 jit_solution(8712240526288904142)
XLA Ops:
  0.0 1.1 %scale.1 = (bf16[2,256,256]{2,1,0:T(8,128)(2,1)S(1)}, bf16[256,256]{1,0:T(8,128)(2,1)S(1)}) custom-call(bf16[2,256,256]{2,1,0:T(8,128)(2,1)} %w_hbm.1, bf16[2,256]{1,0:T(2,128)(2,1)} %gain_hbm.1), custom_call_target="tpu_custom_call" | custom-call | bytes 1024 | tf_op jit(solution)/shard_map/scale/pallas_call | solution.py:229
  1.1 4.2 %collective-permute-start.4 = (bf16[256,256]{1,0:T(8,128)(2,1)S(1)}, bf16[256,256]{1,0:T(8,128)(2,1)S(1)}, u32[]{:S(2)}, u32[]{:S(2)}) collective-permute-start(bf16[256,256]{1,0:T(8,128)(2,1)S(1)} %get-tuple-element.79.refs_4_), channel_id=1, source_target_pairs={{0,96},{32,0},{64,32},{96,64},{1,97},{33,1},{65,33},{97,65},{2,98}... | collective-permute-start | bytes 393224 | tf_op jit(solution)/shard_map/ppermute | solution.py:265
  5.3 1.3 %collective-permute-start.2 = (bf16[256,256]{1,0:T(8,128)(2,1)S(1)}, bf16[256,256]{1,0:T(8,128)(2,1)S(1)}, u32[]{:S(2)}, u32[]{:S(2)}) collective-permute-start(bf16[256,256]{1,0:T(8,128)(2,1)S(1)} %get-tuple-element.79.refs_4_), channel_id=1, source_target_pairs={{0,32},{32,64},{64,96},{96,0},{1,33},{33,65},{65,97},{97,1},{2,34}... | collective-permute-start | bytes 393224 | tf_op jit(solution)/shard_map/ppermute | solution.py:265
  6.6 2.1 %prologue.2 = (bf16[1024,256]{1,0:T(8,128)(2,1)S(1)}, bf16[1024,256]{1,0:T(8,128)(2,1)S(1)}, bf16[512,1024]{1,0:T(8,128)(2,1)S(1)}, bf16[1,256,256]{2,1,0:T(8,12...) custom-call(bf16[8,1024,256]{2,1,0:T(8,128)(2,1)} %refs_0_.3, s32[8,2,256]{2,1,0:T(2,128)} %refs_1_.3, ...), custom_call_target="tpu_custom_call" | custom-call | bytes 1024 | tf_op jit(solution)/shard_map/prologue/pallas_call | solution.py:239
  8.7 3.9 %collective-permute-start.5 = (bf16[256,256]{1,0:T(8,128)(2,1)S(1)}, bf16[256,256]{1,0:T(8,128)(2,1)S(1)}, u32[]{:S(2)}, u32[]{:S(2)}) collective-permute-start(bf16[256,256]{1,0:T(8,128)(2,1)S(1)} %get-tuple-element.90), channel_id=1, source_target_pairs={{0,31},{1,2},{2,1},{3,4},{4,3},{5,6},{6,5},{7,8},{8,7},{9,10},{10,... | collective-permute-start | bytes 393224 | tf_op jit(solution)/shard_map/ppermute | solution.py:253
  12.6 1.6 %fetch.1 = (bf16[1024,512]{1,0:T(8,128)(2,1)S(1)}, bf16[1024,512]{1,0:T(8,128)(2,1)S(1)}) custom-call(bf16[8,1024,512]{2,1,0:T(8,128)(2,1)} %val_ref.1), custom_call_target="tpu_custom_call" | custom-call | bytes 1024 | tf_op jit(solution)/shard_map/fetch/pallas_call | solution.py:257
  14.2 2.2 %prologue.3 = (bf16[1024,256]{1,0:T(8,128)(2,1)S(1)}, bf16[1024,256]{1,0:T(8,128)(2,1)S(1)}, bf16[512,1024]{1,0:T(8,128)(2,1)S(1)}, bf16[2,256,256]{2,1,0:T(8,12...) custom-call(bf16[8,1024,256]{2,1,0:T(8,128)(2,1)} %refs_0_.3, s32[8,2,256]{2,1,0:T(2,128)} %refs_1_.3, ...), custom_call_target="tpu_custom_call" | custom-call | bytes 1024 | tf_op jit(solution)/shard_map/prologue/pallas_call | solution.py:239
  16.4 0.1 collective-permute-done.5.off_in
  16.5 0.5 collective-permute-start
  17.0 3.8 %collective-permute-start.1 = (bf16[256,256]{1,0:T(8,128)(2,1)S(1)}, bf16[256,256]{1,0:T(8,128)(2,1)S(1)}, u32[]{:S(2)}, u32[]{:S(2)}) collective-permute-start(bf16[256,256]{1,0:T(8,128)(2,1)S(1)} %get-tuple-element.85), channel_id=1, source_target_pairs={{0,31},{1,2},{2,1},{3,4},{4,3},{5,6},{6,5},{7,8},{8,7},{9,10},{10,... | collective-permute-start | bytes 393224 | tf_op jit(solution)/shard_map/ppermute | solution.py:253
  21.0 1.2 %layer.23 = (bf16[1024,256]{1,0:T(8,128)(2,1)S(1)}, bf16[1024,256]{1,0:T(8,128)(2,1)S(1)}, bf16[256,256]{1,0:T(8,128)(2,1)S(1)}, bf16[256,256]{1,0:T(8,128)(2,1)S(1)}) custom-call(s32[32,128]{1,0:T(8,128)S(1)} %get-tuple-element.120.idx_ref, bf16[1024,256]{1,0:T(8,128)(2,1)S(1)} %get-tuple-element.121.h_ref, ...), custom_call_target="tpu_custom_call" | custom-call | flops 1000000 | bytes 1024 | tf_op jit(solution)/shard_map/layer/pallas_call | solution.py:287
  22.2 0.1 collective-permute-start.21
  22.3 1.6 %collective-permute-start.22 = (bf16[256,256]{1,0:T(8,128)(2,1)S(1)}, bf16[256,256]{1,0:T(8,128)(2,1)S(1)}, u32[]{:S(2)}, u32[]{:S(2)}) collective-permute-start(bf16[256,256]{1,0:T(8,128)(2,1)S(1)} %get-tuple-element.128), channel_id=1, source_target_pairs={{0,31},{1,2},{2,1},{3,4},{4,3},{5,6},{6,5},{7,8},{8,7},{9,10},{10,... | collective-permute-start | bytes 393224 | tf_op jit(solution)/shard_map/ppermute | solution.py:219
  23.9 0.9 collective-permute-done.1.off_in
  24.8 1.2 %layer.16 = (bf16[1024,256]{1,0:T(8,128)(2,1)S(1)}, bf16[1024,256]{1,0:T(8,128)(2,1)S(1)}, bf16[256,256]{1,0:T(8,128)(2,1)S(1)}, bf16[256,256]{1,0:T(8,128)(2,1)S(1)}) custom-call(s32[32,128]{1,0:T(8,128)S(1)} %get-tuple-element.81.idx_ref, bf16[1024,256]{1,0:T(8,128)(2,1)S(1)} %get-tuple-element.82.h_ref, ...), custom_call_target="tpu_custom_call" | custom-call | flops 1000000 | bytes 1024 | tf_op jit(solution)/shard_map/layer/pallas_call | solution.py:287
  26.0 0.1 collective-permute-start.7
  26.1 3.9 %collective-permute-start.8 = (bf16[256,256]{1,0:T(8,128)(2,1)S(1)}, bf16[256,256]{1,0:T(8,128)(2,1)S(1)}, u32[]{:S(2)}, u32[]{:S(2)}) collective-permute-start(bf16[256,256]{1,0:T(8,128)(2,1)S(1)} %get-tuple-element.95), channel_id=1, source_target_pairs={{0,31},{1,2},{2,1},{3,4},{4,3},{5,6},{6,5},{7,8},{8,7},{9,10},{10,... | collective-permute-start | bytes 393224 | tf_op jit(solution)/shard_map/ppermute | solution.py:219
  30.0 0.1 collective-permute-done.22.off_in
  30.1 1.2 %layer.24 = (bf16[1024,256]{1,0:T(8,128)(2,1)S(1)}, bf16[1024,256]{1,0:T(8,128)(2,1)S(1)}, bf16[256,256]{1,0:T(8,128)(2,1)S(1)}, bf16[256,256]{1,0:T(8,128)(2,1)S(1)}) custom-call(s32[32,128]{1,0:T(8,128)S(1)} %get-tuple-element.120.idx_ref, bf16[1024,256]{1,0:T(8,128)(2,1)S(1)} %get-tuple-element.125.h_ref, ...), custom_call_target="tpu_custom_call" | custom-call | flops 1000000 | bytes 1024 | tf_op jit(solution)/shard_map/layer/pallas_call | solution.py:287
  31.3 0.1 collective-permute-start.23
  31.4 1.6 %collective-permute-start.24 = (bf16[256,256]{1,0:T(8,128)(2,1)S(1)}, bf16[256,256]{1,0:T(8,128)(2,1)S(1)}, u32[]{:S(2)}, u32[]{:S(2)}) collective-permute-start(bf16[256,256]{1,0:T(8,128)(2,1)S(1)} %get-tuple-element.132), channel_id=1, source_target_pairs={{0,31},{1,2},{2,1},{3,4},{4,3},{5,6},{6,5},{7,8},{8,7},{9,10},{10,... | collective-permute-start | bytes 393224 | tf_op jit(solution)/shard_map/ppermute | solution.py:219
  33.0 0.9 collective-permute-done.8.off_in
  33.9 1.2 %layer.17 = (bf16[1024,256]{1,0:T(8,128)(2,1)S(1)}, bf16[1024,256]{1,0:T(8,128)(2,1)S(1)}, bf16[256,256]{1,0:T(8,128)(2,1)S(1)}, bf16[256,256]{1,0:T(8,128)(2,1)S(1)}) custom-call(s32[32,128]{1,0:T(8,128)S(1)} %get-tuple-element.81.idx_ref, bf16[1024,256]{1,0:T(8,128)(2,1)S(1)} %get-tuple-element.92.h_ref, bf16[1024,256]{1,0:T(8,128)(2,1)S(1)} %get-tuple-element.93.nrm_ref, ...), custom_call_target="tpu_custom_call" | custom-call | flops 1000000 | bytes 1024 | tf_op jit(solution)/shard_map/layer/pallas_call | solution.py:287
  35.1 0.1 collective-permute-start.9
  35.2 3.9 %collective-permute-start.10 = (bf16[256,256]{1,0:T(8,128)(2,1)S(1)}, bf16[256,256]{1,0:T(8,128)(2,1)S(1)}, u32[]{:S(2)}, u32[]{:S(2)}) collective-permute-start(bf16[256,256]{1,0:T(8,128)(2,1)S(1)} %get-tuple-element.99), channel_id=1, source_target_pairs={{0,31},{1,2},{2,1},{3,4},{4,3},{5,6},{6,5},{7,8},{8,7},{9,10},{10,... | collective-permute-start | bytes 393224 | tf_op jit(solution)/shard_map/ppermute | solution.py:219
  39.1 0.1 collective-permute-done.24.off_in
  39.2 1.2 %layer.25 = (bf16[1024,256]{1,0:T(8,128)(2,1)S(1)}, bf16[1024,256]{1,0:T(8,128)(2,1)S(1)}, bf16[256,256]{1,0:T(8,128)(2,1)S(1)}, bf16[256,256]{1,0:T(8,128)(2,1)S(1)}) custom-call(s32[32,128]{1,0:T(8,128)S(1)} %get-tuple-element.120.idx_ref, bf16[1024,256]{1,0:T(8,128)(2,1)S(1)} %get-tuple-element.129.h_ref, ...), custom_call_target="tpu_custom_call" | custom-call | flops 1000000 | bytes 1024 | tf_op jit(solution)/shard_map/layer/pallas_call | solution.py:287
  40.4 0.3 collective-permute-start.25
  40.7 1.6 %collective-permute-start.26 = (bf16[256,256]{1,0:T(8,128)(2,1)S(1)}, bf16[256,256]{1,0:T(8,128)(2,1)S(1)}, u32[]{:S(2)}, u32[]{:S(2)}) collective-permute-start(bf16[256,256]{1,0:T(8,128)(2,1)S(1)} %get-tuple-element.136), channel_id=1, source_target_pairs={{0,31},{1,2},{2,1},{3,4},{4,3},{5,6},{6,5},{7,8},{8,7},{9,10},{10,... | collective-permute-start | bytes 393224 | tf_op jit(solution)/shard_map/ppermute | solution.py:219
  42.3 0.7 collective-permute-done.10.off_in
  43.0 1.2 %layer.18 = (bf16[1024,256]{1,0:T(8,128)(2,1)S(1)}, bf16[1024,256]{1,0:T(8,128)(2,1)S(1)}, bf16[256,256]{1,0:T(8,128)(2,1)S(1)}, bf16[256,256]{1,0:T(8,128)(2,1)S(1)}) custom-call(s32[32,128]{1,0:T(8,128)S(1)} %get-tuple-element.81.idx_ref, bf16[1024,256]{1,0:T(8,128)(2,1)S(1)} %get-tuple-element.96.h_ref, bf16[1024,256]{1,0:T(8,128)(2,1)S(1)} %get-tuple-element.97.nrm_ref, ...), custom_call_target="tpu_custom_call" | custom-call | flops 1000000 | bytes 1024 | tf_op jit(solution)/shard_map/layer/pallas_call | solution.py:287
  44.2 0.1 collective-permute-start.11
  44.3 3.9 %collective-permute-start.12 = (bf16[256,256]{1,0:T(8,128)(2,1)S(1)}, bf16[256,256]{1,0:T(8,128)(2,1)S(1)}, u32[]{:S(2)}, u32[]{:S(2)}) collective-permute-start(bf16[256,256]{1,0:T(8,128)(2,1)S(1)} %get-tuple-element.103), channel_id=1, source_target_pairs={{0,31},{1,2},{2,1},{3,4},{4,3},{5,6},{6,5},{7,8},{8,7},{9,10},{10,... | collective-permute-start | bytes 393224 | tf_op jit(solution)/shard_map/ppermute | solution.py:219
  48.2 0.3 collective-permute-done.26.off_in
  48.5 1.2 %layer.26 = (bf16[1024,256]{1,0:T(8,128)(2,1)S(1)}, bf16[1024,256]{1,0:T(8,128)(2,1)S(1)}, bf16[256,256]{1,0:T(8,128)(2,1)S(1)}, bf16[256,256]{1,0:T(8,128)(2,1)S(1)}) custom-call(s32[32,128]{1,0:T(8,128)S(1)} %get-tuple-element.120.idx_ref, bf16[1024,256]{1,0:T(8,128)(2,1)S(1)} %get-tuple-element.133.h_ref, ...), custom_call_target="tpu_custom_call" | custom-call | flops 1000000 | bytes 1024 | tf_op jit(solution)/shard_map/layer/pallas_call | solution.py:287
  49.7 0.1 collective-permute-start.27
  49.8 1.6 %collective-permute-start.28 = (bf16[256,256]{1,0:T(8,128)(2,1)S(1)}, bf16[256,256]{1,0:T(8,128)(2,1)S(1)}, u32[]{:S(2)}, u32[]{:S(2)}) collective-permute-start(bf16[256,256]{1,0:T(8,128)(2,1)S(1)} %get-tuple-element.140), channel_id=1, source_target_pairs={{0,31},{1,2},{2,1},{3,4},{4,3},{5,6},{6,5},{7,8},{8,7},{9,10},{10,... | collective-permute-start | bytes 393224 | tf_op jit(solution)/shard_map/ppermute | solution.py:219
  51.4 0.7 collective-permute-done.12.off_in
  52.1 1.2 %layer.19 = (bf16[1024,256]{1,0:T(8,128)(2,1)S(1)}, bf16[1024,256]{1,0:T(8,128)(2,1)S(1)}, bf16[256,256]{1,0:T(8,128)(2,1)S(1)}, bf16[256,256]{1,0:T(8,128)(2,1)S(1)}) custom-call(s32[32,128]{1,0:T(8,128)S(1)} %get-tuple-element.81.idx_ref, bf16[1024,256]{1,0:T(8,128)(2,1)S(1)} %get-tuple-element.100.h_ref, ...), custom_call_target="tpu_custom_call" | custom-call | flops 1000000 | bytes 1024 | tf_op jit(solution)/shard_map/layer/pallas_call | solution.py:287
  53.3 0.1 collective-permute-start.13
  53.4 3.9 %collective-permute-start.14 = (bf16[256,256]{1,0:T(8,128)(2,1)S(1)}, bf16[256,256]{1,0:T(8,128)(2,1)S(1)}, u32[]{:S(2)}, u32[]{:S(2)}) collective-permute-start(bf16[256,256]{1,0:T(8,128)(2,1)S(1)} %get-tuple-element.107), channel_id=1, source_target_pairs={{0,31},{1,2},{2,1},{3,4},{4,3},{5,6},{6,5},{7,8},{8,7},{9,10},{10,... | collective-permute-start | bytes 393224 | tf_op jit(solution)/shard_map/ppermute | solution.py:219
  57.3 0.3 collective-permute-done.28.off_in
  57.6 1.2 %layer.27 = (bf16[1024,256]{1,0:T(8,128)(2,1)S(1)}, bf16[1024,256]{1,0:T(8,128)(2,1)S(1)}, bf16[256,256]{1,0:T(8,128)(2,1)S(1)}, bf16[256,256]{1,0:T(8,128)(2,1)S(1)}) custom-call(s32[32,128]{1,0:T(8,128)S(1)} %get-tuple-element.120.idx_ref, bf16[1024,256]{1,0:T(8,128)(2,1)S(1)} %get-tuple-element.137.h_ref, ...), custom_call_target="tpu_custom_call" | custom-call | flops 1000000 | bytes 1024 | tf_op jit(solution)/shard_map/layer/pallas_call | solution.py:287
  58.8 0.1 collective-permute-start.29
  58.9 1.6 %collective-permute-start.30 = (bf16[256,256]{1,0:T(8,128)(2,1)S(1)}, bf16[256,256]{1,0:T(8,128)(2,1)S(1)}, u32[]{:S(2)}, u32[]{:S(2)}) collective-permute-start(bf16[256,256]{1,0:T(8,128)(2,1)S(1)} %get-tuple-element.144), channel_id=1, source_target_pairs={{0,31},{1,2},{2,1},{3,4},{4,3},{5,6},{6,5},{7,8},{8,7},{9,10},{10,... | collective-permute-start | bytes 393224 | tf_op jit(solution)/shard_map/ppermute | solution.py:219
  60.5 0.7 collective-permute-done.14.off_in
  61.2 1.2 %layer.20 = (bf16[1024,256]{1,0:T(8,128)(2,1)S(1)}, bf16[1024,256]{1,0:T(8,128)(2,1)S(1)}, bf16[256,256]{1,0:T(8,128)(2,1)S(1)}, bf16[256,256]{1,0:T(8,128)(2,1)S(1)}) custom-call(s32[32,128]{1,0:T(8,128)S(1)} %get-tuple-element.81.idx_ref, bf16[1024,256]{1,0:T(8,128)(2,1)S(1)} %get-tuple-element.104.h_ref, ...), custom_call_target="tpu_custom_call" | custom-call | flops 1000000 | bytes 1024 | tf_op jit(solution)/shard_map/layer/pallas_call | solution.py:287
  62.5 0.1 collective-permute-start.15
  62.6 3.9 %collective-permute-start.16 = (bf16[256,256]{1,0:T(8,128)(2,1)S(1)}, bf16[256,256]{1,0:T(8,128)(2,1)S(1)}, u32[]{:S(2)}, u32[]{:S(2)}) collective-permute-start(bf16[256,256]{1,0:T(8,128)(2,1)S(1)} %get-tuple-element.111), channel_id=1, source_target_pairs={{0,31},{1,2},{2,1},{3,4},{4,3},{5,6},{6,5},{7,8},{8,7},{9,10},{10,... | collective-permute-start | bytes 393224 | tf_op jit(solution)/shard_map/ppermute | solution.py:219
  66.5 0.3 collective-permute-done.30.off_in
  66.7 1.2 %layer.28 = (bf16[1024,256]{1,0:T(8,128)(2,1)S(1)}, bf16[1024,256]{1,0:T(8,128)(2,1)S(1)}, bf16[256,256]{1,0:T(8,128)(2,1)S(1)}, bf16[256,256]{1,0:T(8,128)(2,1)S(1)}) custom-call(s32[32,128]{1,0:T(8,128)S(1)} %get-tuple-element.120.idx_ref, bf16[1024,256]{1,0:T(8,128)(2,1)S(1)} %get-tuple-element.141.h_ref, ...), custom_call_target="tpu_custom_call" | custom-call | flops 1000000 | bytes 1024 | tf_op jit(solution)/shard_map/layer/pallas_call | solution.py:287
  68.1 1.6 %collective-permute-start.32 = (bf16[256,256]{1,0:T(8,128)(2,1)S(1)}, bf16[256,256]{1,0:T(8,128)(2,1)S(1)}, u32[]{:S(2)}, u32[]{:S(2)}) collective-permute-start(bf16[256,256]{1,0:T(8,128)(2,1)S(1)} %get-tuple-element.148), channel_id=1, source_target_pairs={{0,31},{1,2},{2,1},{3,4},{4,3},{5,6},{6,5},{7,8},{8,7},{9,10},{10,... | collective-permute-start | bytes 393224 | tf_op jit(solution)/shard_map/ppermute | solution.py:219
  69.7 0.7 collective-permute-done.16.off_in
  70.3 1.2 %layer.21 = (bf16[1024,256]{1,0:T(8,128)(2,1)S(1)}, bf16[1024,256]{1,0:T(8,128)(2,1)S(1)}, bf16[256,256]{1,0:T(8,128)(2,1)S(1)}, bf16[256,256]{1,0:T(8,128)(2,1)S(1)}) custom-call(s32[32,128]{1,0:T(8,128)S(1)} %get-tuple-element.81.idx_ref, bf16[1024,256]{1,0:T(8,128)(2,1)S(1)} %get-tuple-element.108.h_ref, ...), custom_call_target="tpu_custom_call" | custom-call | flops 1000000 | bytes 1024 | tf_op jit(solution)/shard_map/layer/pallas_call | solution.py:287
  71.6 0.1 collective-permute-start.17
  71.7 4.1 %collective-permute-start.18 = (bf16[256,256]{1,0:T(8,128)(2,1)S(1)}, bf16[256,256]{1,0:T(8,128)(2,1)S(1)}, u32[]{:S(2)}, u32[]{:S(2)}) collective-permute-start(bf16[256,256]{1,0:T(8,128)(2,1)S(1)} %get-tuple-element.115), channel_id=1, source_target_pairs={{0,31},{1,2},{2,1},{3,4},{4,3},{5,6},{6,5},{7,8},{8,7},{9,10},{10,... | collective-permute-start | bytes 393224 | tf_op jit(solution)/shard_map/ppermute | solution.py:219
  75.8 1.2 %layer.29 = (bf16[1024,256]{1,0:T(8,128)(2,1)S(1)}, bf16[1024,256]{1,0:T(8,128)(2,1)S(1)}, bf16[256,256]{1,0:T(8,128)(2,1)S(1)}, bf16[256,256]{1,0:T(8,128)(2,1)S(1)}) custom-call(s32[32,128]{1,0:T(8,128)S(1)} %get-tuple-element.120.idx_ref, bf16[1024,256]{1,0:T(8,128)(2,1)S(1)} %get-tuple-element.145.h_ref, ...), custom_call_target="tpu_custom_call" | custom-call | flops 1000000 | bytes 1024 | tf_op jit(solution)/shard_map/layer/pallas_call | solution.py:287
  77.2 1.6 %collective-permute-start.34 = (bf16[256,256]{1,0:T(8,128)(2,1)S(1)}, bf16[256,256]{1,0:T(8,128)(2,1)S(1)}, u32[]{:S(2)}, u32[]{:S(2)}) collective-permute-start(bf16[256,256]{1,0:T(8,128)(2,1)S(1)} %get-tuple-element.152), channel_id=1, source_target_pairs={{0,31},{1,2},{2,1},{3,4},{4,3},{5,6},{6,5},{7,8},{8,7},{9,10},{10,... | collective-permute-start | bytes 393224 | tf_op jit(solution)/shard_map/ppermute | solution.py:219
  78.8 0.9 collective-permute-done.18.off_in
  79.7 1.2 %layer.22 = (bf16[1024,256]{1,0:T(8,128)(2,1)S(1)}, bf16[1024,256]{1,0:T(8,128)(2,1)S(1)}, bf16[256,256]{1,0:T(8,128)(2,1)S(1)}, bf16[256,256]{1,0:T(8,128)(2,1)S(1)}) custom-call(s32[32,128]{1,0:T(8,128)S(1)} %get-tuple-element.81.idx_ref, bf16[1024,256]{1,0:T(8,128)(2,1)S(1)} %get-tuple-element.112.h_ref, ...), custom_call_target="tpu_custom_call" | custom-call | flops 1000000 | bytes 1024 | tf_op jit(solution)/shard_map/layer/pallas_call | solution.py:287
  81.0 3.9 %collective-permute-start.20 = (bf16[256,256]{1,0:T(8,128)(2,1)S(1)}, bf16[256,256]{1,0:T(8,128)(2,1)S(1)}, u32[]{:S(2)}, u32[]{:S(2)}) collective-permute-start(bf16[256,256]{1,0:T(8,128)(2,1)S(1)} %get-tuple-element.119), channel_id=1, source_target_pairs={{0,31},{1,2},{2,1},{3,4},{4,3},{5,6},{6,5},{7,8},{8,7},{9,10},{10,... | collective-permute-start | bytes 393224 | tf_op jit(solution)/shard_map/ppermute | solution.py:219
  85.0 0.7 layer.30.rest_0_
  85.7 3.1 %collective-permute-done.20.off_in = bf16[256,256]{1,0:T(8,128)(2,1)S(1)} collective-permute-done((bf16[256,256]{1,0:T(8,128)(2,1)S(1)}, bf16[256,256]{1,0:T(8,128)(2,1)S(1)}, u32[]{:S(2)}, u32[]{:S(2)}) %collective-permute-start.20) | collective-permute-done | bytes 131104 | tf_op jit(solution)/shard_map/ppermute | solution.py:219
  88.8 1.4 %layer.31 = bf16[2,1024,256]{2,1,0:T(8,128)(2,1)} custom-call(s32[32,128]{1,0:T(8,128)S(1)} %get-tuple-element.81.idx_ref, bf16[1024,256]{1,0:T(8,128)(2,1)S(1)} %get-tuple-element.116.h_ref, bf16[1024,256]{1,0:T(8,128)(2,1)S(1)} %get-tuple-element.117.nrm_ref, bf16[256,256]{1,0:T(8,128)(2,1)S(1)} %collective-permute-done.19.on_in, ...), custom_call_target="tpu_custom_call" | custom-call | flops 1000000 | bytes 1024 | tf_op jit(solution)/shard_map/layer/pallas_call | solution.py:287
  (28 shorter events, 0.5 us)
Async XLA Ops:
  1.1 15.2 %collective-permute-start.4 = (bf16[256,256]{1,0:T(8,128)(2,1)S(1)}, bf16[256,256]{1,0:T(8,128)(2,1)S(1)}, u32[]{:S(2)}, u32[]{:S(2)}) collective-permute-start(bf16[256,256]{1,0:T(8,128)(2,1)S(1)} %get-tuple-element.79.refs_4_), channel_id=1, source_target_pairs={{0,96},{32,0},{64,32},{96,64},{1,97},{33,1},{65,33},{97,65},{2,98}... | collective-permute-start | bytes 393224 | tf_op jit(solution)/shard_map/ppermute | solution.py:265
  5.3 11.1 %collective-permute-start.3 = (bf16[256,256]{1,0:T(8,128)(2,1)S(1)}, bf16[256,256]{1,0:T(8,128)(2,1)S(1)}, u32[]{:S(2)}, u32[]{:S(2)}) collective-permute-start(bf16[256,256]{1,0:T(8,128)(2,1)S(1)} %get-tuple-element.79.refs_4_), channel_id=1, source_target_pairs={{0,64},{32,96},{64,0},{96,32},{1,65},{33,97},{65,1},{97,33},{2,66}... | collective-permute-start | bytes 393224 | tf_op jit(solution)/shard_map/ppermute | solution.py:265
  5.3 11.1 %collective-permute-start.2 = (bf16[256,256]{1,0:T(8,128)(2,1)S(1)}, bf16[256,256]{1,0:T(8,128)(2,1)S(1)}, u32[]{:S(2)}, u32[]{:S(2)}) collective-permute-start(bf16[256,256]{1,0:T(8,128)(2,1)S(1)} %get-tuple-element.79.refs_4_), channel_id=1, source_target_pairs={{0,32},{32,64},{64,96},{96,0},{1,33},{33,65},{65,97},{97,1},{2,34}... | collective-permute-start | bytes 393224 | tf_op jit(solution)/shard_map/ppermute | solution.py:265
  8.7 7.8 %collective-permute-start.5 = (bf16[256,256]{1,0:T(8,128)(2,1)S(1)}, bf16[256,256]{1,0:T(8,128)(2,1)S(1)}, u32[]{:S(2)}, u32[]{:S(2)}) collective-permute-start(bf16[256,256]{1,0:T(8,128)(2,1)S(1)} %get-tuple-element.90), channel_id=1, source_target_pairs={{0,31},{1,2},{2,1},{3,4},{4,3},{5,6},{6,5},{7,8},{8,7},{9,10},{10,... | collective-permute-start | bytes 393224 | tf_op jit(solution)/shard_map/ppermute | solution.py:253
  16.5 4.3 %collective-permute-start.6 = (bf16[3,256,256]{2,1,0:T(8,128)(2,1)S(1)}, bf16[3,256,256]{2,1,0:T(8,128)(2,1)S(1)}, u32[]{:S(2)}, u32[]{:S(2)}) collective-permute-start(bf16[3,256,256]{2,1,0:T(8,128)(2,1)S(1)} %pack.1.mine_ref), channel_id=1, source_target_pairs={{0,1},{1,0},{2,3},{3,2},{4,5},{5,4},{6,7},{7,6},{8,9},{9,8},{10,11... | collective-permute-start | bytes 1179656 | tf_op jit(solution)/shard_map/ppermute | solution.py:270
  16.5 4.4 %collective-permute-start = (bf16[2,256,256]{2,1,0:T(8,128)(2,1)S(1)}, bf16[2,256,256]{2,1,0:T(8,128)(2,1)S(1)}, u32[]{:S(2)}, u32[]{:S(2)}) collective-permute-start(bf16[2,256,256]{2,1,0:T(8,128)(2,1)S(1)} %get-tuple-element.84), channel_id=1, source_target_pairs={{0,1},{1,0},{2,3},{3,2},{4,5},{5,4},{6,7},{7,6},{8,9},{9,8},{10,11... | collective-permute-start | bytes 786440 | tf_op jit(solution)/shard_map/ppermute | solution.py:254
  17.0 7.7 %collective-permute-start.1 = (bf16[256,256]{1,0:T(8,128)(2,1)S(1)}, bf16[256,256]{1,0:T(8,128)(2,1)S(1)}, u32[]{:S(2)}, u32[]{:S(2)}) collective-permute-start(bf16[256,256]{1,0:T(8,128)(2,1)S(1)} %get-tuple-element.85), channel_id=1, source_target_pairs={{0,31},{1,2},{2,1},{3,4},{4,3},{5,6},{6,5},{7,8},{8,7},{9,10},{10,... | collective-permute-start | bytes 393224 | tf_op jit(solution)/shard_map/ppermute | solution.py:253
  22.2 7.8 %collective-permute-start.21 = (bf16[256,256]{1,0:T(8,128)(2,1)S(1)}, bf16[256,256]{1,0:T(8,128)(2,1)S(1)}, u32[]{:S(2)}, u32[]{:S(2)}) collective-permute-start(bf16[256,256]{1,0:T(8,128)(2,1)S(1)} %get-tuple-element.127), channel_id=1, source_target_pairs={{0,1},{1,0},{2,3},{3,2},{4,5},{5,4},{6,7},{7,6},{8,9},{9,8},{10,11... | collective-permute-start | bytes 393224 | tf_op jit(solution)/shard_map/ppermute | solution.py:219
  22.3 7.8 %collective-permute-start.22 = (bf16[256,256]{1,0:T(8,128)(2,1)S(1)}, bf16[256,256]{1,0:T(8,128)(2,1)S(1)}, u32[]{:S(2)}, u32[]{:S(2)}) collective-permute-start(bf16[256,256]{1,0:T(8,128)(2,1)S(1)} %get-tuple-element.128), channel_id=1, source_target_pairs={{0,31},{1,2},{2,1},{3,4},{4,3},{5,6},{6,5},{7,8},{8,7},{9,10},{10,... | collective-permute-start | bytes 393224 | tf_op jit(solution)/shard_map/ppermute | solution.py:219
  26.0 7.0 %collective-permute-start.7 = (bf16[256,256]{1,0:T(8,128)(2,1)S(1)}, bf16[256,256]{1,0:T(8,128)(2,1)S(1)}, u32[]{:S(2)}, u32[]{:S(2)}) collective-permute-start(bf16[256,256]{1,0:T(8,128)(2,1)S(1)} %get-tuple-element.94), channel_id=1, source_target_pairs={{0,1},{1,0},{2,3},{3,2},{4,5},{5,4},{6,7},{7,6},{8,9},{9,8},{10,11... | collective-permute-start | bytes 393224 | tf_op jit(solution)/shard_map/ppermute | solution.py:219
  26.1 7.8 %collective-permute-start.8 = (bf16[256,256]{1,0:T(8,128)(2,1)S(1)}, bf16[256,256]{1,0:T(8,128)(2,1)S(1)}, u32[]{:S(2)}, u32[]{:S(2)}) collective-permute-start(bf16[256,256]{1,0:T(8,128)(2,1)S(1)} %get-tuple-element.95), channel_id=1, source_target_pairs={{0,31},{1,2},{2,1},{3,4},{4,3},{5,6},{6,5},{7,8},{8,7},{9,10},{10,... | collective-permute-start | bytes 393224 | tf_op jit(solution)/shard_map/ppermute | solution.py:219
  31.3 7.8 %collective-permute-start.23 = (bf16[256,256]{1,0:T(8,128)(2,1)S(1)}, bf16[256,256]{1,0:T(8,128)(2,1)S(1)}, u32[]{:S(2)}, u32[]{:S(2)}) collective-permute-start(bf16[256,256]{1,0:T(8,128)(2,1)S(1)} %get-tuple-element.131), channel_id=1, source_target_pairs={{0,1},{1,0},{2,3},{3,2},{4,5},{5,4},{6,7},{7,6},{8,9},{9,8},{10,11... | collective-permute-start | bytes 393224 | tf_op jit(solution)/shard_map/ppermute | solution.py:219
  31.4 7.8 %collective-permute-start.24 = (bf16[256,256]{1,0:T(8,128)(2,1)S(1)}, bf16[256,256]{1,0:T(8,128)(2,1)S(1)}, u32[]{:S(2)}, u32[]{:S(2)}) collective-permute-start(bf16[256,256]{1,0:T(8,128)(2,1)S(1)} %get-tuple-element.132), channel_id=1, source_target_pairs={{0,31},{1,2},{2,1},{3,4},{4,3},{5,6},{6,5},{7,8},{8,7},{9,10},{10,... | collective-permute-start | bytes 393224 | tf_op jit(solution)/shard_map/ppermute | solution.py:219
  35.1 7.2 %collective-permute-start.9 = (bf16[256,256]{1,0:T(8,128)(2,1)S(1)}, bf16[256,256]{1,0:T(8,128)(2,1)S(1)}, u32[]{:S(2)}, u32[]{:S(2)}) collective-permute-start(bf16[256,256]{1,0:T(8,128)(2,1)S(1)} %get-tuple-element.98), channel_id=1, source_target_pairs={{0,1},{1,0},{2,3},{3,2},{4,5},{5,4},{6,7},{7,6},{8,9},{9,8},{10,11... | collective-permute-start | bytes 393224 | tf_op jit(solution)/shard_map/ppermute | solution.py:219
  35.2 7.8 %collective-permute-start.10 = (bf16[256,256]{1,0:T(8,128)(2,1)S(1)}, bf16[256,256]{1,0:T(8,128)(2,1)S(1)}, u32[]{:S(2)}, u32[]{:S(2)}) collective-permute-start(bf16[256,256]{1,0:T(8,128)(2,1)S(1)} %get-tuple-element.99), channel_id=1, source_target_pairs={{0,31},{1,2},{2,1},{3,4},{4,3},{5,6},{6,5},{7,8},{8,7},{9,10},{10,... | collective-permute-start | bytes 393224 | tf_op jit(solution)/shard_map/ppermute | solution.py:219
  40.4 7.8 %collective-permute-start.25 = (bf16[256,256]{1,0:T(8,128)(2,1)S(1)}, bf16[256,256]{1,0:T(8,128)(2,1)S(1)}, u32[]{:S(2)}, u32[]{:S(2)}) collective-permute-start(bf16[256,256]{1,0:T(8,128)(2,1)S(1)} %get-tuple-element.135), channel_id=1, source_target_pairs={{0,1},{1,0},{2,3},{3,2},{4,5},{5,4},{6,7},{7,6},{8,9},{9,8},{10,11... | collective-permute-start | bytes 393224 | tf_op jit(solution)/shard_map/ppermute | solution.py:219
  40.7 7.8 %collective-permute-start.26 = (bf16[256,256]{1,0:T(8,128)(2,1)S(1)}, bf16[256,256]{1,0:T(8,128)(2,1)S(1)}, u32[]{:S(2)}, u32[]{:S(2)}) collective-permute-start(bf16[256,256]{1,0:T(8,128)(2,1)S(1)} %get-tuple-element.136), channel_id=1, source_target_pairs={{0,31},{1,2},{2,1},{3,4},{4,3},{5,6},{6,5},{7,8},{8,7},{9,10},{10,... | collective-permute-start | bytes 393224 | tf_op jit(solution)/shard_map/ppermute | solution.py:219
  44.2 7.2 %collective-permute-start.11 = (bf16[256,256]{1,0:T(8,128)(2,1)S(1)}, bf16[256,256]{1,0:T(8,128)(2,1)S(1)}, u32[]{:S(2)}, u32[]{:S(2)}) collective-permute-start(bf16[256,256]{1,0:T(8,128)(2,1)S(1)} %get-tuple-element.102), channel_id=1, source_target_pairs={{0,1},{1,0},{2,3},{3,2},{4,5},{5,4},{6,7},{7,6},{8,9},{9,8},{10,11... | collective-permute-start | bytes 393224 | tf_op jit(solution)/shard_map/ppermute | solution.py:219
  44.3 7.8 %collective-permute-start.12 = (bf16[256,256]{1,0:T(8,128)(2,1)S(1)}, bf16[256,256]{1,0:T(8,128)(2,1)S(1)}, u32[]{:S(2)}, u32[]{:S(2)}) collective-permute-start(bf16[256,256]{1,0:T(8,128)(2,1)S(1)} %get-tuple-element.103), channel_id=1, source_target_pairs={{0,31},{1,2},{2,1},{3,4},{4,3},{5,6},{6,5},{7,8},{8,7},{9,10},{10,... | collective-permute-start | bytes 393224 | tf_op jit(solution)/shard_map/ppermute | solution.py:219
  49.7 7.6 %collective-permute-start.27 = (bf16[256,256]{1,0:T(8,128)(2,1)S(1)}, bf16[256,256]{1,0:T(8,128)(2,1)S(1)}, u32[]{:S(2)}, u32[]{:S(2)}) collective-permute-start(bf16[256,256]{1,0:T(8,128)(2,1)S(1)} %get-tuple-element.139), channel_id=1, source_target_pairs={{0,1},{1,0},{2,3},{3,2},{4,5},{5,4},{6,7},{7,6},{8,9},{9,8},{10,11... | collective-permute-start | bytes 393224 | tf_op jit(solution)/shard_map/ppermute | solution.py:219
  49.8 7.8 %collective-permute-start.28 = (bf16[256,256]{1,0:T(8,128)(2,1)S(1)}, bf16[256,256]{1,0:T(8,128)(2,1)S(1)}, u32[]{:S(2)}, u32[]{:S(2)}) collective-permute-start(bf16[256,256]{1,0:T(8,128)(2,1)S(1)} %get-tuple-element.140), channel_id=1, source_target_pairs={{0,31},{1,2},{2,1},{3,4},{4,3},{5,6},{6,5},{7,8},{8,7},{9,10},{10,... | collective-permute-start | bytes 393224 | tf_op jit(solution)/shard_map/ppermute | solution.py:219
  53.3 7.2 %collective-permute-start.13 = (bf16[256,256]{1,0:T(8,128)(2,1)S(1)}, bf16[256,256]{1,0:T(8,128)(2,1)S(1)}, u32[]{:S(2)}, u32[]{:S(2)}) collective-permute-start(bf16[256,256]{1,0:T(8,128)(2,1)S(1)} %get-tuple-element.106), channel_id=1, source_target_pairs={{0,1},{1,0},{2,3},{3,2},{4,5},{5,4},{6,7},{7,6},{8,9},{9,8},{10,11... | collective-permute-start | bytes 393224 | tf_op jit(solution)/shard_map/ppermute | solution.py:219
  53.4 7.8 %collective-permute-start.14 = (bf16[256,256]{1,0:T(8,128)(2,1)S(1)}, bf16[256,256]{1,0:T(8,128)(2,1)S(1)}, u32[]{:S(2)}, u32[]{:S(2)}) collective-permute-start(bf16[256,256]{1,0:T(8,128)(2,1)S(1)} %get-tuple-element.107), channel_id=1, source_target_pairs={{0,31},{1,2},{2,1},{3,4},{4,3},{5,6},{6,5},{7,8},{8,7},{9,10},{10,... | collective-permute-start | bytes 393224 | tf_op jit(solution)/shard_map/ppermute | solution.py:219
  58.8 7.6 %collective-permute-start.29 = (bf16[256,256]{1,0:T(8,128)(2,1)S(1)}, bf16[256,256]{1,0:T(8,128)(2,1)S(1)}, u32[]{:S(2)}, u32[]{:S(2)}) collective-permute-start(bf16[256,256]{1,0:T(8,128)(2,1)S(1)} %get-tuple-element.143), channel_id=1, source_target_pairs={{0,1},{1,0},{2,3},{3,2},{4,5},{5,4},{6,7},{7,6},{8,9},{9,8},{10,11... | collective-permute-start | bytes 393224 | tf_op jit(solution)/shard_map/ppermute | solution.py:219
  58.9 7.8 %collective-permute-start.30 = (bf16[256,256]{1,0:T(8,128)(2,1)S(1)}, bf16[256,256]{1,0:T(8,128)(2,1)S(1)}, u32[]{:S(2)}, u32[]{:S(2)}) collective-permute-start(bf16[256,256]{1,0:T(8,128)(2,1)S(1)} %get-tuple-element.144), channel_id=1, source_target_pairs={{0,31},{1,2},{2,1},{3,4},{4,3},{5,6},{6,5},{7,8},{8,7},{9,10},{10,... | collective-permute-start | bytes 393224 | tf_op jit(solution)/shard_map/ppermute | solution.py:219
  62.5 7.2 %collective-permute-start.15 = (bf16[256,256]{1,0:T(8,128)(2,1)S(1)}, bf16[256,256]{1,0:T(8,128)(2,1)S(1)}, u32[]{:S(2)}, u32[]{:S(2)}) collective-permute-start(bf16[256,256]{1,0:T(8,128)(2,1)S(1)} %get-tuple-element.110), channel_id=1, source_target_pairs={{0,1},{1,0},{2,3},{3,2},{4,5},{5,4},{6,7},{7,6},{8,9},{9,8},{10,11... | collective-permute-start | bytes 393224 | tf_op jit(solution)/shard_map/ppermute | solution.py:219
  62.6 7.8 %collective-permute-start.16 = (bf16[256,256]{1,0:T(8,128)(2,1)S(1)}, bf16[256,256]{1,0:T(8,128)(2,1)S(1)}, u32[]{:S(2)}, u32[]{:S(2)}) collective-permute-start(bf16[256,256]{1,0:T(8,128)(2,1)S(1)} %get-tuple-element.111), channel_id=1, source_target_pairs={{0,31},{1,2},{2,1},{3,4},{4,3},{5,6},{6,5},{7,8},{8,7},{9,10},{10,... | collective-permute-start | bytes 393224 | tf_op jit(solution)/shard_map/ppermute | solution.py:219
  68.0 7.8 %collective-permute-start.31 = (bf16[256,256]{1,0:T(8,128)(2,1)S(1)}, bf16[256,256]{1,0:T(8,128)(2,1)S(1)}, u32[]{:S(2)}, u32[]{:S(2)}) collective-permute-start(bf16[256,256]{1,0:T(8,128)(2,1)S(1)} %get-tuple-element.147), channel_id=1, source_target_pairs={{0,1},{1,0},{2,3},{3,2},{4,5},{5,4},{6,7},{7,6},{8,9},{9,8},{10,11... | collective-permute-start | bytes 393224 | tf_op jit(solution)/shard_map/ppermute | solution.py:219
  68.1 7.8 %collective-permute-start.32 = (bf16[256,256]{1,0:T(8,128)(2,1)S(1)}, bf16[256,256]{1,0:T(8,128)(2,1)S(1)}, u32[]{:S(2)}, u32[]{:S(2)}) collective-permute-start(bf16[256,256]{1,0:T(8,128)(2,1)S(1)} %get-tuple-element.148), channel_id=1, source_target_pairs={{0,31},{1,2},{2,1},{3,4},{4,3},{5,6},{6,5},{7,8},{8,7},{9,10},{10,... | collective-permute-start | bytes 393224 | tf_op jit(solution)/shard_map/ppermute | solution.py:219
  71.6 7.2 %collective-permute-start.17 = (bf16[256,256]{1,0:T(8,128)(2,1)S(1)}, bf16[256,256]{1,0:T(8,128)(2,1)S(1)}, u32[]{:S(2)}, u32[]{:S(2)}) collective-permute-start(bf16[256,256]{1,0:T(8,128)(2,1)S(1)} %get-tuple-element.114), channel_id=1, source_target_pairs={{0,1},{1,0},{2,3},{3,2},{4,5},{5,4},{6,7},{7,6},{8,9},{9,8},{10,11... | collective-permute-start | bytes 393224 | tf_op jit(solution)/shard_map/ppermute | solution.py:219
  71.7 8.0 %collective-permute-start.18 = (bf16[256,256]{1,0:T(8,128)(2,1)S(1)}, bf16[256,256]{1,0:T(8,128)(2,1)S(1)}, u32[]{:S(2)}, u32[]{:S(2)}) collective-permute-start(bf16[256,256]{1,0:T(8,128)(2,1)S(1)} %get-tuple-element.115), channel_id=1, source_target_pairs={{0,31},{1,2},{2,1},{3,4},{4,3},{5,6},{6,5},{7,8},{8,7},{9,10},{10,... | collective-permute-start | bytes 393224 | tf_op jit(solution)/shard_map/ppermute | solution.py:219
  77.1 7.8 %collective-permute-start.33 = (bf16[256,256]{1,0:T(8,128)(2,1)S(1)}, bf16[256,256]{1,0:T(8,128)(2,1)S(1)}, u32[]{:S(2)}, u32[]{:S(2)}) collective-permute-start(bf16[256,256]{1,0:T(8,128)(2,1)S(1)} %get-tuple-element.151), channel_id=1, source_target_pairs={{0,1},{1,0},{2,3},{3,2},{4,5},{5,4},{6,7},{7,6},{8,9},{9,8},{10,11... | collective-permute-start | bytes 393224 | tf_op jit(solution)/shard_map/ppermute | solution.py:219
  77.2 7.8 %collective-permute-start.34 = (bf16[256,256]{1,0:T(8,128)(2,1)S(1)}, bf16[256,256]{1,0:T(8,128)(2,1)S(1)}, u32[]{:S(2)}, u32[]{:S(2)}) collective-permute-start(bf16[256,256]{1,0:T(8,128)(2,1)S(1)} %get-tuple-element.152), channel_id=1, source_target_pairs={{0,31},{1,2},{2,1},{3,4},{4,3},{5,6},{6,5},{7,8},{8,7},{9,10},{10,... | collective-permute-start | bytes 393224 | tf_op jit(solution)/shard_map/ppermute | solution.py:219
  80.9 4.8 %collective-permute-start.19 = (bf16[256,256]{1,0:T(8,128)(2,1)S(1)}, bf16[256,256]{1,0:T(8,128)(2,1)S(1)}, u32[]{:S(2)}, u32[]{:S(2)}) collective-permute-start(bf16[256,256]{1,0:T(8,128)(2,1)S(1)} %get-tuple-element.118), channel_id=1, source_target_pairs={{0,1},{1,0},{2,3},{3,2},{4,5},{5,4},{6,7},{7,6},{8,9},{9,8},{10,11... | collective-permute-start | bytes 393224 | tf_op jit(solution)/shard_map/ppermute | solution.py:219
  81.0 7.8 %collective-permute-start.20 = (bf16[256,256]{1,0:T(8,128)(2,1)S(1)}, bf16[256,256]{1,0:T(8,128)(2,1)S(1)}, u32[]{:S(2)}, u32[]{:S(2)}) collective-permute-start(bf16[256,256]{1,0:T(8,128)(2,1)S(1)} %get-tuple-element.119), channel_id=1, source_target_pairs={{0,31},{1,2},{2,1},{3,4},{4,3},{5,6},{6,5},{7,8},{8,7},{9,10},{10,... | collective-permute-start | bytes 393224 | tf_op jit(solution)/shard_map/ppermute | solution.py:219

commit v6 on v5

--- a/solution.py
+++ b/solution.py
@@ -63,9 +63,13 @@
 
 
 def prologue_body(local, per_section, *refs):
-    feat, rows_hbm, count_hbm, src_hbm, before_ref = refs[:5]
-    h_ref, nrm_ref, sel_ref, on_ref, off_ref, idx_ref = refs[5:11]
-    rows_ref, count_ref, src_ref, sems, feat_sems = refs[11:]
+    if local:
+        feat, rows_hbm, count_hbm, src_hbm, before_ref = refs[:5]
+        h_ref, nrm_ref, sel_ref, on_ref, off_ref, idx_ref = refs[5:11]
+        rows_ref, count_ref, src_ref, sems, feat_sems = refs[11:]
+    else:
+        h_ref, rows_ref, count_ref, src_ref, _ = refs[:5]
+        nrm_ref, sel_ref, on_ref, off_ref, idx_ref = refs[5:10]
     if local:
         for g in range(local):
             on_ref[g] = before_ref[g]
@@ -74,16 +78,18 @@
         on_ref = on_ref.at[0]
     even = dom_parity() == 0
     graph = graph_of(local, per_section)
-    small = [
-        pltpu.make_async_copy(rows_hbm.at[graph], rows_ref, sems.at[0]),
-        pltpu.make_async_copy(count_hbm, count_ref, sems.at[1]),
-        pltpu.make_async_copy(src_hbm.at[graph], src_ref, sems.at[2]),
-    ]
-    for copy in small:
-        copy.start()
-    feat_copies = chunked(feat.at[graph], h_ref, feat_sems)
-    for copy in small:
-        copy.wait()
+    feat_copies = [None] * 4
+    if local:
+        small = [
+            pltpu.make_async_copy(rows_hbm.at[graph], rows_ref, sems.at[0]),
+            pltpu.make_async_copy(count_hbm, count_ref, sems.at[1]),
+            pltpu.make_async_copy(src_hbm.at[graph], src_ref, sems.at[2]),
+        ]
+        for copy in small:
+            copy.start()
+        feat_copies = chunked(feat.at[graph], h_ref, feat_sems)
+        for copy in small:
+            copy.wait()
     rows_dev = h_ref.shape[0]
     bnd = off_ref.shape[0]
     own, half = rows_dev // TILE, bnd // TILE
@@ -109,7 +115,8 @@
         for k in range(K):
             idx_ref[i * K + k : i * K + k + 1, :] = jnp.broadcast_to(table[k : k + 1, i : i + 1], (1, TILE))
     for c, copy in enumerate(feat_copies):
-        copy.wait()
+        if local:
+            copy.wait()
         step = rows_dev // len(feat_copies)
         block = slice(c * step, (c + 1) * step)
         nrm_ref[block, :] = normalise(h_ref[block, :].astype(F32))
@@ -125,13 +132,21 @@
         copy.wait()
 
 
-def scale_body(w_hbm, gain_hbm, out_ref, mine_ref, w_ref, gain_ref, sems):
+def scale_body(per_section, w_hbm, gain_hbm, feat, rows_hbm, count_hbm, src_hbm, *refs):
+    out_ref, mine_ref, h_ref, rows_ref, count_ref, src_ref, w_ref, gain_ref, sems, feat_sems = refs
+    graph = graph_of(0, per_section)
     copies = [
         pltpu.make_async_copy(w_hbm, w_ref, sems.at[0]),
         pltpu.make_async_copy(gain_hbm, gain_ref, sems.at[1]),
     ]
-    for copy in copies:
+    others = [
+        pltpu.make_async_copy(rows_hbm.at[graph], rows_ref, sems.at[2]),
+        pltpu.make_async_copy(count_hbm, count_ref, sems.at[3]),
+        pltpu.make_async_copy(src_hbm.at[graph], src_ref, sems.at[4]),
+    ]
+    for copy in copies + others:
         copy.start()
+    others += chunked(feat.at[graph], h_ref, feat_sems)
     for copy in copies:
         copy.wait()
     width = w_ref.shape[1]
@@ -140,6 +155,8 @@
         column = jnp.broadcast_to(gain[k : k + 1, :], (width, width)).T
         out_ref[k] = (w_ref[k].astype(F32) * column).astype(BF)
     mine_ref[...] = out_ref[dom_parity()]
+    for copy in others:
+        copy.wait()
 
 
 def pack_body(*refs):
@@ -226,20 +243,26 @@
     )
     square = (width, width)
     square = (width, width)
-    scaled, mine = call(
-        scale_body,
-        [weights.shape, square],
-        [HBM] * 2,
+    scaled, mine, *given = call(
+        functools.partial(scale_body, per_section),
+        [weights.shape, square, (rows_dev, width)],
+        [HBM] * 6,
         "scale",
-        [pltpu.VMEM(weights.shape, BF), pltpu.VMEM(gains.shape, BF), pltpu.SemaphoreType.DMA((2,))],
-    )(weights, gains)
+        [
+            pltpu.VMEM(weights.shape, BF),
+            pltpu.VMEM(gains.shape, BF),
+            pltpu.SemaphoreType.DMA((5,)),
+            pltpu.SemaphoreType.DMA((4,)),
+        ],
+        ints=[(2, bnd), (2, graphs), (K, tiles)],
+    )(weights, gains, features, boundary_rows, boundary_count, tile_src)
     on_all = mine
     state = []
     for g in range(per_section):
-        h, nrm, sel, on_all, off, idx = call(
+        *h, nrm, sel, on_all, off, idx = call(
             functools.partial(prologue_body, g, per_section),
-            [(rows_dev, width), (rows_dev, width), (2 * bnd, rows_dev), (g + 1, bnd, width), (bnd, width)],
-            [HBM] * 4 + [VMEM],
+            [(rows_dev, width)] * (2 if g else 1) + [(2 * bnd, rows_dev), (g + 1, bnd, width), (bnd, width)],
+            [HBM if g else VMEM] * 4 + [VMEM],
             "prologue",
             [
                 pltpu.VMEM((2, bnd), jnp.int32),
@@ -247,9 +270,10 @@
                 pltpu.VMEM((K, tiles), jnp.int32),
                 pltpu.SemaphoreType.DMA((3,)),
                 pltpu.SemaphoreType.DMA((4,)),
-            ],
+            ] if g else [],
             ints=[(tiles * K, TILE)],
-        )(features, boundary_rows, boundary_count, tile_src, on_all)
+        )(*((features, boundary_rows, boundary_count, tile_src) if g else given), on_all)
+        h = h[0] if g else given[0]
         state.append([h, nrm, None, lax.ppermute(off, "dom", off_pairs), sel, idx])
     on_all = lax.ppermute(on_all, "dom", on_pairs)
     for entry in state:

time: 90.8 us -> 89.7 us (0.988)
  waiting for transfers between devices: 9.7 us -> 5.46 us
  starting transfers between devices: 53.8 us -> 58 us
  Pallas kernels: 26.4 us -> 25.3 us
    ppermute x14, starting transfers between devices: 38.8 us -> 42.9 us  [exchange(): lax.ppermute(off, 'dom', off_pairs)]
    ppermute x14, waiting for transfers between devices: 8.7 us -> 5.03 us  [exchange(): lax.ppermute(off, 'dom', off_pairs)]
    pallas_call x2, Pallas kernels: 4.29 us -> 2.99 us  [on_device(): call(functools.partial(prologue_body, g, per_section), [(rows_dev, width)...]
  transfers between devices with their start and end apart: 35 -> 35, of which waited for: 14 -> 16; matrix products, arithmetic and copies ran while one was open for 0% -> 0% of each run, Pallas kernels for 26% -> 25%
where the time goes in v6:
time: 89.7 us; the launch traced here: 89.3 us
  starting transfers between devices  58 us (65%)
  Pallas kernels  25.3 us (28%)
  waiting for transfers between devices  5.46 us (6%)
    ppermute x14, starting transfers between devices, exchange(): lax.ppermute(off, 'dom', off_pairs)  42.9 us
    pallas_call x16, Pallas kernels, on_device(): call(functools.partial(layer_body, layer, g, last, others), outs, [VMEM]...  19.3 us
    ppermute x2, starting transfers between devices, on_device(): state.append([h, nrm, None, lax.ppermute(off, 'dom', off_pairs), sel, idx])  7.99 us
    ppermute x3, starting transfers between devices, on_device(): lax.ppermute(mine, 'section', [(i, (i + shift) % sections) for i in range...  5.45 us
    ppermute x14, waiting for transfers between devices, exchange(): lax.ppermute(off, 'dom', off_pairs)  5.03 us
    pallas_call x2, Pallas kernels, on_device(): call(functools.partial(prologue_body, g, per_section), [(rows_dev, width)...  2.99 us
  transfers between devices with their start and end apart: 35, of which 16 were waited for; matrix products, arithmetic and copies ran while one was open for 0% of the time, Pallas kernels for 25%

profile of v6, /device:TPU:0, one launch (start us, length us, event | category | flops | bytes accessed | tf_op | source)
XLA Modules:
  0.0 89.3 jit_solution(4816317712358264724)
XLA Ops:
  0.0 1.3 %scale.1 = (bf16[2,256,256]{2,1,0:T(8,128)(2,1)S(1)}, bf16[256,256]{1,0:T(8,128)(2,1)S(1)}, bf16[1024,256]{1,0:T(8,128)(2,1)S(1)}, s32[2,256]{1,0:T(2,128)S(1)}, s32[2,8]{1,0:T(2,128)S(1)}, /*index=5*/s32[4,8]{1,0:T(4,128)S(1)}) custom-call(bf16[2,256,256]{2,1,0:T(8,128)(2,1)} %w_hbm.1, bf16[2,256]{1,0:T(2,128)(2,1)} %gain_hbm.1, ...), custom_call_target="tpu_custom_call" | custom-call | bytes 1024 | tf_op jit(solution)/shard_map/scale/pallas_call | solution.py:246
  1.3 4.2 %collective-permute-start.4 = (bf16[256,256]{1,0:T(8,128)(2,1)S(1)}, bf16[256,256]{1,0:T(8,128)(2,1)S(1)}, u32[]{:S(2)}, u32[]{:S(2)}) collective-permute-start(bf16[256,256]{1,0:T(8,128)(2,1)S(1)} %get-tuple-element.86.refs_4_), channel_id=1, source_target_pairs={{0,96},{32,0},{64,32},{96,64},{1,97},{33,1},{65,33},{97,65},{2,98}... | collective-permute-start | bytes 393224 | tf_op jit(solution)/shard_map/ppermute | solution.py:289
  5.5 1.3 %collective-permute-start.2 = (bf16[256,256]{1,0:T(8,128)(2,1)S(1)}, bf16[256,256]{1,0:T(8,128)(2,1)S(1)}, u32[]{:S(2)}, u32[]{:S(2)}) collective-permute-start(bf16[256,256]{1,0:T(8,128)(2,1)S(1)} %get-tuple-element.86.refs_4_), channel_id=1, source_target_pairs={{0,32},{32,64},{64,96},{96,0},{1,33},{33,65},{65,97},{97,1},{2,34}... | collective-permute-start | bytes 393224 | tf_op jit(solution)/shard_map/ppermute | solution.py:289
  6.7 0.8 prologue.2
  7.6 3.9 %collective-permute-start.5 = (bf16[256,256]{1,0:T(8,128)(2,1)S(1)}, bf16[256,256]{1,0:T(8,128)(2,1)S(1)}, u32[]{:S(2)}, u32[]{:S(2)}) collective-permute-start(bf16[256,256]{1,0:T(8,128)(2,1)S(1)} %get-tuple-element.97), channel_id=1, source_target_pairs={{0,31},{1,2},{2,1},{3,4},{4,3},{5,6},{6,5},{7,8},{8,7},{9,10},{10,... | collective-permute-start | bytes 393224 | tf_op jit(solution)/shard_map/ppermute | solution.py:277
  11.5 1.6 %fetch.1 = (bf16[1024,512]{1,0:T(8,128)(2,1)S(1)}, bf16[1024,512]{1,0:T(8,128)(2,1)S(1)}) custom-call(bf16[8,1024,512]{2,1,0:T(8,128)(2,1)} %val_ref.1), custom_call_target="tpu_custom_call" | custom-call | bytes 1024 | tf_op jit(solution)/shard_map/fetch/pallas_call | solution.py:281
  13.1 2.2 %prologue.3 = (bf16[1024,256]{1,0:T(8,128)(2,1)S(1)}, bf16[1024,256]{1,0:T(8,128)(2,1)S(1)}, bf16[512,1024]{1,0:T(8,128)(2,1)S(1)}, bf16[2,256,256]{2,1,0:T(8,12...) custom-call(bf16[8,1024,256]{2,1,0:T(8,128)(2,1)} %refs_0_.1, s32[8,2,256]{2,1,0:T(2,128)} %refs_1_.1, ...), custom_call_target="tpu_custom_call" | custom-call | bytes 1024 | tf_op jit(solution)/shard_map/prologue/pallas_call | solution.py:262
  15.3 0.1 collective-permute-done.5.off_in
  15.4 0.5 collective-permute-start
  15.9 4.1 %collective-permute-start.1 = (bf16[256,256]{1,0:T(8,128)(2,1)S(1)}, bf16[256,256]{1,0:T(8,128)(2,1)S(1)}, u32[]{:S(2)}, u32[]{:S(2)}) collective-permute-start(bf16[256,256]{1,0:T(8,128)(2,1)S(1)} %get-tuple-element.92), channel_id=1, source_target_pairs={{0,31},{1,2},{2,1},{3,4},{4,3},{5,6},{6,5},{7,8},{8,7},{9,10},{10,... | collective-permute-start | bytes 393224 | tf_op jit(solution)/shard_map/ppermute | solution.py:277
  20.1 1.2 %layer.23 = (bf16[1024,256]{1,0:T(8,128)(2,1)S(1)}, bf16[1024,256]{1,0:T(8,128)(2,1)S(1)}, bf16[256,256]{1,0:T(8,128)(2,1)S(1)}, bf16[256,256]{1,0:T(8,128)(2,1)S(1)}) custom-call(s32[32,128]{1,0:T(8,128)S(1)} %get-tuple-element.127.idx_ref, bf16[1024,256]{1,0:T(8,128)(2,1)S(1)} %get-tuple-element.82.refs_0_.h_ref, ...), custom_call_target="tpu_custom_call" | custom-call | flops 1000000 | bytes 1024 | tf_op jit(solution)/shard_map/layer/pallas_call | solution.py:311
  21.3 0.1 collective-permute-start.21
  21.4 1.9 %collective-permute-start.22 = (bf16[256,256]{1,0:T(8,128)(2,1)S(1)}, bf16[256,256]{1,0:T(8,128)(2,1)S(1)}, u32[]{:S(2)}, u32[]{:S(2)}) collective-permute-start(bf16[256,256]{1,0:T(8,128)(2,1)S(1)} %get-tuple-element.134), channel_id=1, source_target_pairs={{0,31},{1,2},{2,1},{3,4},{4,3},{5,6},{6,5},{7,8},{8,7},{9,10},{10,... | collective-permute-start | bytes 393224 | tf_op jit(solution)/shard_map/ppermute | solution.py:236
  23.3 0.3 collective-permute-done.1.off_in
  23.6 1.2 %layer.16 = (bf16[1024,256]{1,0:T(8,128)(2,1)S(1)}, bf16[1024,256]{1,0:T(8,128)(2,1)S(1)}, bf16[256,256]{1,0:T(8,128)(2,1)S(1)}, bf16[256,256]{1,0:T(8,128)(2,1)S(1)}) custom-call(s32[32,128]{1,0:T(8,128)S(1)} %get-tuple-element.88.idx_ref, bf16[1024,256]{1,0:T(8,128)(2,1)S(1)} %get-tuple-element.89.h_ref, ...), custom_call_target="tpu_custom_call" | custom-call | flops 1000000 | bytes 1024 | tf_op jit(solution)/shard_map/layer/pallas_call | solution.py:311
  24.8 0.1 collective-permute-start.7
  24.9 4.2 %collective-permute-start.8 = (bf16[256,256]{1,0:T(8,128)(2,1)S(1)}, bf16[256,256]{1,0:T(8,128)(2,1)S(1)}, u32[]{:S(2)}, u32[]{:S(2)}) collective-permute-start(bf16[256,256]{1,0:T(8,128)(2,1)S(1)} %get-tuple-element.102), channel_id=1, source_target_pairs={{0,31},{1,2},{2,1},{3,4},{4,3},{5,6},{6,5},{7,8},{8,7},{9,10},{10,... | collective-permute-start | bytes 393224 | tf_op jit(solution)/shard_map/ppermute | solution.py:236
  29.1 0.1 collective-permute-done.22.off_in
  29.2 1.2 %layer.24 = (bf16[1024,256]{1,0:T(8,128)(2,1)S(1)}, bf16[1024,256]{1,0:T(8,128)(2,1)S(1)}, bf16[256,256]{1,0:T(8,128)(2,1)S(1)}, bf16[256,256]{1,0:T(8,128)(2,1)S(1)}) custom-call(s32[32,128]{1,0:T(8,128)S(1)} %get-tuple-element.127.idx_ref, bf16[1024,256]{1,0:T(8,128)(2,1)S(1)} %get-tuple-element.131.h_ref, ...), custom_call_target="tpu_custom_call" | custom-call | flops 1000000 | bytes 1024 | tf_op jit(solution)/shard_map/layer/pallas_call | solution.py:311
  30.5 0.1 collective-permute-start.23
  30.6 1.9 %collective-permute-start.24 = (bf16[256,256]{1,0:T(8,128)(2,1)S(1)}, bf16[256,256]{1,0:T(8,128)(2,1)S(1)}, u32[]{:S(2)}, u32[]{:S(2)}) collective-permute-start(bf16[256,256]{1,0:T(8,128)(2,1)S(1)} %get-tuple-element.138), channel_id=1, source_target_pairs={{0,31},{1,2},{2,1},{3,4},{4,3},{5,6},{6,5},{7,8},{8,7},{9,10},{10,... | collective-permute-start | bytes 393224 | tf_op jit(solution)/shard_map/ppermute | solution.py:236
  32.5 0.3 collective-permute-done.8.off_in
  32.7 1.2 %layer.17 = (bf16[1024,256]{1,0:T(8,128)(2,1)S(1)}, bf16[1024,256]{1,0:T(8,128)(2,1)S(1)}, bf16[256,256]{1,0:T(8,128)(2,1)S(1)}, bf16[256,256]{1,0:T(8,128)(2,1)S(1)}) custom-call(s32[32,128]{1,0:T(8,128)S(1)} %get-tuple-element.88.idx_ref, bf16[1024,256]{1,0:T(8,128)(2,1)S(1)} %get-tuple-element.99.h_ref, bf16[1024,256]{1,0:T(8,128)(2,1)S(1)} %get-tuple-element.100.nrm_ref, ...), custom_call_target="tpu_custom_call" | custom-call | flops 1000000 | bytes 1024 | tf_op jit(solution)/shard_map/layer/pallas_call | solution.py:311
  34.0 0.1 collective-permute-start.9
  34.1 4.2 %collective-permute-start.10 = (bf16[256,256]{1,0:T(8,128)(2,1)S(1)}, bf16[256,256]{1,0:T(8,128)(2,1)S(1)}, u32[]{:S(2)}, u32[]{:S(2)}) collective-permute-start(bf16[256,256]{1,0:T(8,128)(2,1)S(1)} %get-tuple-element.106), channel_id=1, source_target_pairs={{0,31},{1,2},{2,1},{3,4},{4,3},{5,6},{6,5},{7,8},{8,7},{9,10},{10,... | collective-permute-start | bytes 393224 | tf_op jit(solution)/shard_map/ppermute | solution.py:236
  38.2 0.1 collective-permute-done.24.off_in
  38.4 1.2 %layer.25 = (bf16[1024,256]{1,0:T(8,128)(2,1)S(1)}, bf16[1024,256]{1,0:T(8,128)(2,1)S(1)}, bf16[256,256]{1,0:T(8,128)(2,1)S(1)}, bf16[256,256]{1,0:T(8,128)(2,1)S(1)}) custom-call(s32[32,128]{1,0:T(8,128)S(1)} %get-tuple-element.127.idx_ref, bf16[1024,256]{1,0:T(8,128)(2,1)S(1)} %get-tuple-element.135.h_ref, ...), custom_call_target="tpu_custom_call" | custom-call | flops 1000000 | bytes 1024 | tf_op jit(solution)/shard_map/layer/pallas_call | solution.py:311
  39.6 0.1 collective-permute-start.25
  39.7 2.1 %collective-permute-start.26 = (bf16[256,256]{1,0:T(8,128)(2,1)S(1)}, bf16[256,256]{1,0:T(8,128)(2,1)S(1)}, u32[]{:S(2)}, u32[]{:S(2)}) collective-permute-start(bf16[256,256]{1,0:T(8,128)(2,1)S(1)} %get-tuple-element.142), channel_id=1, source_target_pairs={{0,31},{1,2},{2,1},{3,4},{4,3},{5,6},{6,5},{7,8},{8,7},{9,10},{10,... | collective-permute-start | bytes 393224 | tf_op jit(solution)/shard_map/ppermute | solution.py:236
  41.8 0.1 collective-permute-done.10.off_in
  41.9 1.2 %layer.18 = (bf16[1024,256]{1,0:T(8,128)(2,1)S(1)}, bf16[1024,256]{1,0:T(8,128)(2,1)S(1)}, bf16[256,256]{1,0:T(8,128)(2,1)S(1)}, bf16[256,256]{1,0:T(8,128)(2,1)S(1)}) custom-call(s32[32,128]{1,0:T(8,128)S(1)} %get-tuple-element.88.idx_ref, bf16[1024,256]{1,0:T(8,128)(2,1)S(1)} %get-tuple-element.103.h_ref, ...), custom_call_target="tpu_custom_call" | custom-call | flops 1000000 | bytes 1024 | tf_op jit(solution)/shard_map/layer/pallas_call | solution.py:311
  43.1 0.1 collective-permute-start.11
  43.2 4.2 %collective-permute-start.12 = (bf16[256,256]{1,0:T(8,128)(2,1)S(1)}, bf16[256,256]{1,0:T(8,128)(2,1)S(1)}, u32[]{:S(2)}, u32[]{:S(2)}) collective-permute-start(bf16[256,256]{1,0:T(8,128)(2,1)S(1)} %get-tuple-element.110), channel_id=1, source_target_pairs={{0,31},{1,2},{2,1},{3,4},{4,3},{5,6},{6,5},{7,8},{8,7},{9,10},{10,... | collective-permute-start | bytes 393224 | tf_op jit(solution)/shard_map/ppermute | solution.py:236
  47.4 0.3 collective-permute-done.26.off_in
  47.7 1.2 %layer.26 = (bf16[1024,256]{1,0:T(8,128)(2,1)S(1)}, bf16[1024,256]{1,0:T(8,128)(2,1)S(1)}, bf16[256,256]{1,0:T(8,128)(2,1)S(1)}, bf16[256,256]{1,0:T(8,128)(2,1)S(1)}) custom-call(s32[32,128]{1,0:T(8,128)S(1)} %get-tuple-element.127.idx_ref, bf16[1024,256]{1,0:T(8,128)(2,1)S(1)} %get-tuple-element.139.h_ref, ...), custom_call_target="tpu_custom_call" | custom-call | flops 1000000 | bytes 1024 | tf_op jit(solution)/shard_map/layer/pallas_call | solution.py:311
  48.9 0.1 collective-permute-start.27
  49.0 1.9 %collective-permute-start.28 = (bf16[256,256]{1,0:T(8,128)(2,1)S(1)}, bf16[256,256]{1,0:T(8,128)(2,1)S(1)}, u32[]{:S(2)}, u32[]{:S(2)}) collective-permute-start(bf16[256,256]{1,0:T(8,128)(2,1)S(1)} %get-tuple-element.146), channel_id=1, source_target_pairs={{0,31},{1,2},{2,1},{3,4},{4,3},{5,6},{6,5},{7,8},{8,7},{9,10},{10,... | collective-permute-start | bytes 393224 | tf_op jit(solution)/shard_map/ppermute | solution.py:236
  50.9 0.1 collective-permute-done.12.off_in
  51.0 1.2 %layer.19 = (bf16[1024,256]{1,0:T(8,128)(2,1)S(1)}, bf16[1024,256]{1,0:T(8,128)(2,1)S(1)}, bf16[256,256]{1,0:T(8,128)(2,1)S(1)}, bf16[256,256]{1,0:T(8,128)(2,1)S(1)}) custom-call(s32[32,128]{1,0:T(8,128)S(1)} %get-tuple-element.88.idx_ref, bf16[1024,256]{1,0:T(8,128)(2,1)S(1)} %get-tuple-element.107.h_ref, ...), custom_call_target="tpu_custom_call" | custom-call | flops 1000000 | bytes 1024 | tf_op jit(solution)/shard_map/layer/pallas_call | solution.py:311
  52.2 0.1 collective-permute-start.13
  52.3 4.2 %collective-permute-start.14 = (bf16[256,256]{1,0:T(8,128)(2,1)S(1)}, bf16[256,256]{1,0:T(8,128)(2,1)S(1)}, u32[]{:S(2)}, u32[]{:S(2)}) collective-permute-start(bf16[256,256]{1,0:T(8,128)(2,1)S(1)} %get-tuple-element.114), channel_id=1, source_target_pairs={{0,31},{1,2},{2,1},{3,4},{4,3},{5,6},{6,5},{7,8},{8,7},{9,10},{10,... | collective-permute-start | bytes 393224 | tf_op jit(solution)/shard_map/ppermute | solution.py:236
  56.5 0.3 collective-permute-done.28.off_in
  56.8 1.2 %layer.27 = (bf16[1024,256]{1,0:T(8,128)(2,1)S(1)}, bf16[1024,256]{1,0:T(8,128)(2,1)S(1)}, bf16[256,256]{1,0:T(8,128)(2,1)S(1)}, bf16[256,256]{1,0:T(8,128)(2,1)S(1)}) custom-call(s32[32,128]{1,0:T(8,128)S(1)} %get-tuple-element.127.idx_ref, bf16[1024,256]{1,0:T(8,128)(2,1)S(1)} %get-tuple-element.143.h_ref, ...), custom_call_target="tpu_custom_call" | custom-call | flops 1000000 | bytes 1024 | tf_op jit(solution)/shard_map/layer/pallas_call | solution.py:311
  58.0 0.1 collective-permute-start.29
  58.1 1.9 %collective-permute-start.30 = (bf16[256,256]{1,0:T(8,128)(2,1)S(1)}, bf16[256,256]{1,0:T(8,128)(2,1)S(1)}, u32[]{:S(2)}, u32[]{:S(2)}) collective-permute-start(bf16[256,256]{1,0:T(8,128)(2,1)S(1)} %get-tuple-element.150), channel_id=1, source_target_pairs={{0,31},{1,2},{2,1},{3,4},{4,3},{5,6},{6,5},{7,8},{8,7},{9,10},{10,... | collective-permute-start | bytes 393224 | tf_op jit(solution)/shard_map/ppermute | solution.py:236
  60.0 0.1 collective-permute-done.14.off_in
  60.1 1.2 %layer.20 = (bf16[1024,256]{1,0:T(8,128)(2,1)S(1)}, bf16[1024,256]{1,0:T(8,128)(2,1)S(1)}, bf16[256,256]{1,0:T(8,128)(2,1)S(1)}, bf16[256,256]{1,0:T(8,128)(2,1)S(1)}) custom-call(s32[32,128]{1,0:T(8,128)S(1)} %get-tuple-element.88.idx_ref, bf16[1024,256]{1,0:T(8,128)(2,1)S(1)} %get-tuple-element.111.h_ref, ...), custom_call_target="tpu_custom_call" | custom-call | flops 1000000 | bytes 1024 | tf_op jit(solution)/shard_map/layer/pallas_call | solution.py:311
  61.3 0.1 collective-permute-start.15
  61.4 4.2 %collective-permute-start.16 = (bf16[256,256]{1,0:T(8,128)(2,1)S(1)}, bf16[256,256]{1,0:T(8,128)(2,1)S(1)}, u32[]{:S(2)}, u32[]{:S(2)}) collective-permute-start(bf16[256,256]{1,0:T(8,128)(2,1)S(1)} %get-tuple-element.118), channel_id=1, source_target_pairs={{0,31},{1,2},{2,1},{3,4},{4,3},{5,6},{6,5},{7,8},{8,7},{9,10},{10,... | collective-permute-start | bytes 393224 | tf_op jit(solution)/shard_map/ppermute | solution.py:236
  65.6 0.3 collective-permute-done.30.off_in
  65.9 1.2 %layer.28 = (bf16[1024,256]{1,0:T(8,128)(2,1)S(1)}, bf16[1024,256]{1,0:T(8,128)(2,1)S(1)}, bf16[256,256]{1,0:T(8,128)(2,1)S(1)}, bf16[256,256]{1,0:T(8,128)(2,1)S(1)}) custom-call(s32[32,128]{1,0:T(8,128)S(1)} %get-tuple-element.127.idx_ref, bf16[1024,256]{1,0:T(8,128)(2,1)S(1)} %get-tuple-element.147.h_ref, ...), custom_call_target="tpu_custom_call" | custom-call | flops 1000000 | bytes 1024 | tf_op jit(solution)/shard_map/layer/pallas_call | solution.py:311
  67.2 1.9 %collective-permute-start.32 = (bf16[256,256]{1,0:T(8,128)(2,1)S(1)}, bf16[256,256]{1,0:T(8,128)(2,1)S(1)}, u32[]{:S(2)}, u32[]{:S(2)}) collective-permute-start(bf16[256,256]{1,0:T(8,128)(2,1)S(1)} %get-tuple-element.154), channel_id=1, source_target_pairs={{0,31},{1,2},{2,1},{3,4},{4,3},{5,6},{6,5},{7,8},{8,7},{9,10},{10,... | collective-permute-start | bytes 393224 | tf_op jit(solution)/shard_map/ppermute | solution.py:236
  69.1 0.1 collective-permute-done.16.off_in
  69.2 1.2 %layer.21 = (bf16[1024,256]{1,0:T(8,128)(2,1)S(1)}, bf16[1024,256]{1,0:T(8,128)(2,1)S(1)}, bf16[256,256]{1,0:T(8,128)(2,1)S(1)}, bf16[256,256]{1,0:T(8,128)(2,1)S(1)}) custom-call(s32[32,128]{1,0:T(8,128)S(1)} %get-tuple-element.88.idx_ref, bf16[1024,256]{1,0:T(8,128)(2,1)S(1)} %get-tuple-element.115.h_ref, ...), custom_call_target="tpu_custom_call" | custom-call | flops 1000000 | bytes 1024 | tf_op jit(solution)/shard_map/layer/pallas_call | solution.py:311
  70.6 4.4 %collective-permute-start.18 = (bf16[256,256]{1,0:T(8,128)(2,1)S(1)}, bf16[256,256]{1,0:T(8,128)(2,1)S(1)}, u32[]{:S(2)}, u32[]{:S(2)}) collective-permute-start(bf16[256,256]{1,0:T(8,128)(2,1)S(1)} %get-tuple-element.122), channel_id=1, source_target_pairs={{0,31},{1,2},{2,1},{3,4},{4,3},{5,6},{6,5},{7,8},{8,7},{9,10},{10,... | collective-permute-start | bytes 393224 | tf_op jit(solution)/shard_map/ppermute | solution.py:236
  75.0 1.2 %layer.29 = (bf16[1024,256]{1,0:T(8,128)(2,1)S(1)}, bf16[1024,256]{1,0:T(8,128)(2,1)S(1)}, bf16[256,256]{1,0:T(8,128)(2,1)S(1)}, bf16[256,256]{1,0:T(8,128)(2,1)S(1)}) custom-call(s32[32,128]{1,0:T(8,128)S(1)} %get-tuple-element.127.idx_ref, bf16[1024,256]{1,0:T(8,128)(2,1)S(1)} %get-tuple-element.151.h_ref, ...), custom_call_target="tpu_custom_call" | custom-call | flops 1000000 | bytes 1024 | tf_op jit(solution)/shard_map/layer/pallas_call | solution.py:311
  76.3 1.9 %collective-permute-start.34 = (bf16[256,256]{1,0:T(8,128)(2,1)S(1)}, bf16[256,256]{1,0:T(8,128)(2,1)S(1)}, u32[]{:S(2)}, u32[]{:S(2)}) collective-permute-start(bf16[256,256]{1,0:T(8,128)(2,1)S(1)} %get-tuple-element.158), channel_id=1, source_target_pairs={{0,31},{1,2},{2,1},{3,4},{4,3},{5,6},{6,5},{7,8},{8,7},{9,10},{10,... | collective-permute-start | bytes 393224 | tf_op jit(solution)/shard_map/ppermute | solution.py:236
  78.2 0.3 collective-permute-done.18.off_in
  78.6 1.2 %layer.22 = (bf16[1024,256]{1,0:T(8,128)(2,1)S(1)}, bf16[1024,256]{1,0:T(8,128)(2,1)S(1)}, bf16[256,256]{1,0:T(8,128)(2,1)S(1)}, bf16[256,256]{1,0:T(8,128)(2,1)S(1)}) custom-call(s32[32,128]{1,0:T(8,128)S(1)} %get-tuple-element.88.idx_ref, bf16[1024,256]{1,0:T(8,128)(2,1)S(1)} %get-tuple-element.119.h_ref, ...), custom_call_target="tpu_custom_call" | custom-call | flops 1000000 | bytes 1024 | tf_op jit(solution)/shard_map/layer/pallas_call | solution.py:311
  79.8 0.1 collective-permute-start.19
  79.9 4.2 %collective-permute-start.20 = (bf16[256,256]{1,0:T(8,128)(2,1)S(1)}, bf16[256,256]{1,0:T(8,128)(2,1)S(1)}, u32[]{:S(2)}, u32[]{:S(2)}) collective-permute-start(bf16[256,256]{1,0:T(8,128)(2,1)S(1)} %get-tuple-element.126), channel_id=1, source_target_pairs={{0,31},{1,2},{2,1},{3,4},{4,3},{5,6},{6,5},{7,8},{8,7},{9,10},{10,... | collective-permute-start | bytes 393224 | tf_op jit(solution)/shard_map/ppermute | solution.py:236
  84.1 0.7 layer.30.rest_0_
  84.8 2.8 %collective-permute-done.20.off_in = bf16[256,256]{1,0:T(8,128)(2,1)S(1)} collective-permute-done((bf16[256,256]{1,0:T(8,128)(2,1)S(1)}, bf16[256,256]{1,0:T(8,128)(2,1)S(1)}, u32[]{:S(2)}, u32[]{:S(2)}) %collective-permute-start.20) | collective-permute-done | bytes 131104 | tf_op jit(solution)/shard_map/ppermute | solution.py:236
  87.7 1.4 %layer.31 = bf16[2,1024,256]{2,1,0:T(8,128)(2,1)} custom-call(s32[32,128]{1,0:T(8,128)S(1)} %get-tuple-element.88.idx_ref, bf16[1024,256]{1,0:T(8,128)(2,1)S(1)} %get-tuple-element.123.h_ref, bf16[1024,256]{1,0:T(8,128)(2,1)S(1)} %get-tuple-element.124.nrm_ref, bf16[256,256]{1,0:T(8,128)(2,1)S(1)} %collective-permute-done.19.on_in, ...), custom_call_target="tpu_custom_call" | custom-call | flops 1000000 | bytes 1024 | tf_op jit(solution)/shard_map/layer/pallas_call | solution.py:311
  (28 shorter events, 0.5 us)
Async XLA Ops:
  1.3 13.9 %collective-permute-start.4 = (bf16[256,256]{1,0:T(8,128)(2,1)S(1)}, bf16[256,256]{1,0:T(8,128)(2,1)S(1)}, u32[]{:S(2)}, u32[]{:S(2)}) collective-permute-start(bf16[256,256]{1,0:T(8,128)(2,1)S(1)} %get-tuple-element.86.refs_4_), channel_id=1, source_target_pairs={{0,96},{32,0},{64,32},{96,64},{1,97},{33,1},{65,33},{97,65},{2,98}... | collective-permute-start | bytes 393224 | tf_op jit(solution)/shard_map/ppermute | solution.py:289
  5.5 9.7 %collective-permute-start.3 = (bf16[256,256]{1,0:T(8,128)(2,1)S(1)}, bf16[256,256]{1,0:T(8,128)(2,1)S(1)}, u32[]{:S(2)}, u32[]{:S(2)}) collective-permute-start(bf16[256,256]{1,0:T(8,128)(2,1)S(1)} %get-tuple-element.86.refs_4_), channel_id=1, source_target_pairs={{0,64},{32,96},{64,0},{96,32},{1,65},{33,97},{65,1},{97,33},{2,66}... | collective-permute-start | bytes 393224 | tf_op jit(solution)/shard_map/ppermute | solution.py:289
  5.5 9.8 %collective-permute-start.2 = (bf16[256,256]{1,0:T(8,128)(2,1)S(1)}, bf16[256,256]{1,0:T(8,128)(2,1)S(1)}, u32[]{:S(2)}, u32[]{:S(2)}) collective-permute-start(bf16[256,256]{1,0:T(8,128)(2,1)S(1)} %get-tuple-element.86.refs_4_), channel_id=1, source_target_pairs={{0,32},{32,64},{64,96},{96,0},{1,33},{33,65},{65,97},{97,1},{2,34}... | collective-permute-start | bytes 393224 | tf_op jit(solution)/shard_map/ppermute | solution.py:289
  7.6 7.8 %collective-permute-start.5 = (bf16[256,256]{1,0:T(8,128)(2,1)S(1)}, bf16[256,256]{1,0:T(8,128)(2,1)S(1)}, u32[]{:S(2)}, u32[]{:S(2)}) collective-permute-start(bf16[256,256]{1,0:T(8,128)(2,1)S(1)} %get-tuple-element.97), channel_id=1, source_target_pairs={{0,31},{1,2},{2,1},{3,4},{4,3},{5,6},{6,5},{7,8},{8,7},{9,10},{10,... | collective-permute-start | bytes 393224 | tf_op jit(solution)/shard_map/ppermute | solution.py:277
  15.4 4.6 %collective-permute-start.6 = (bf16[3,256,256]{2,1,0:T(8,128)(2,1)S(1)}, bf16[3,256,256]{2,1,0:T(8,128)(2,1)S(1)}, u32[]{:S(2)}, u32[]{:S(2)}) collective-permute-start(bf16[3,256,256]{2,1,0:T(8,128)(2,1)S(1)} %pack.1.mine_ref), channel_id=1, source_target_pairs={{0,1},{1,0},{2,3},{3,2},{4,5},{5,4},{6,7},{7,6},{8,9},{9,8},{10,11... | collective-permute-start | bytes 1179656 | tf_op jit(solution)/shard_map/ppermute | solution.py:294
  15.4 4.7 %collective-permute-start = (bf16[2,256,256]{2,1,0:T(8,128)(2,1)S(1)}, bf16[2,256,256]{2,1,0:T(8,128)(2,1)S(1)}, u32[]{:S(2)}, u32[]{:S(2)}) collective-permute-start(bf16[2,256,256]{2,1,0:T(8,128)(2,1)S(1)} %get-tuple-element.91), channel_id=1, source_target_pairs={{0,1},{1,0},{2,3},{3,2},{4,5},{5,4},{6,7},{7,6},{8,9},{9,8},{10,11... | collective-permute-start | bytes 786440 | tf_op jit(solution)/shard_map/ppermute | solution.py:278
  15.9 7.7 %collective-permute-start.1 = (bf16[256,256]{1,0:T(8,128)(2,1)S(1)}, bf16[256,256]{1,0:T(8,128)(2,1)S(1)}, u32[]{:S(2)}, u32[]{:S(2)}) collective-permute-start(bf16[256,256]{1,0:T(8,128)(2,1)S(1)} %get-tuple-element.92), channel_id=1, source_target_pairs={{0,31},{1,2},{2,1},{3,4},{4,3},{5,6},{6,5},{7,8},{8,7},{9,10},{10,... | collective-permute-start | bytes 393224 | tf_op jit(solution)/shard_map/ppermute | solution.py:277
  21.3 7.8 %collective-permute-start.21 = (bf16[256,256]{1,0:T(8,128)(2,1)S(1)}, bf16[256,256]{1,0:T(8,128)(2,1)S(1)}, u32[]{:S(2)}, u32[]{:S(2)}) collective-permute-start(bf16[256,256]{1,0:T(8,128)(2,1)S(1)} %get-tuple-element.133), channel_id=1, source_target_pairs={{0,1},{1,0},{2,3},{3,2},{4,5},{5,4},{6,7},{7,6},{8,9},{9,8},{10,11... | collective-permute-start | bytes 393224 | tf_op jit(solution)/shard_map/ppermute | solution.py:236
  21.4 7.8 %collective-permute-start.22 = (bf16[256,256]{1,0:T(8,128)(2,1)S(1)}, bf16[256,256]{1,0:T(8,128)(2,1)S(1)}, u32[]{:S(2)}, u32[]{:S(2)}) collective-permute-start(bf16[256,256]{1,0:T(8,128)(2,1)S(1)} %get-tuple-element.134), channel_id=1, source_target_pairs={{0,31},{1,2},{2,1},{3,4},{4,3},{5,6},{6,5},{7,8},{8,7},{9,10},{10,... | collective-permute-start | bytes 393224 | tf_op jit(solution)/shard_map/ppermute | solution.py:236
  24.8 7.6 %collective-permute-start.7 = (bf16[256,256]{1,0:T(8,128)(2,1)S(1)}, bf16[256,256]{1,0:T(8,128)(2,1)S(1)}, u32[]{:S(2)}, u32[]{:S(2)}) collective-permute-start(bf16[256,256]{1,0:T(8,128)(2,1)S(1)} %get-tuple-element.101), channel_id=1, source_target_pairs={{0,1},{1,0},{2,3},{3,2},{4,5},{5,4},{6,7},{7,6},{8,9},{9,8},{10,11... | collective-permute-start | bytes 393224 | tf_op jit(solution)/shard_map/ppermute | solution.py:236
  24.9 7.8 %collective-permute-start.8 = (bf16[256,256]{1,0:T(8,128)(2,1)S(1)}, bf16[256,256]{1,0:T(8,128)(2,1)S(1)}, u32[]{:S(2)}, u32[]{:S(2)}) collective-permute-start(bf16[256,256]{1,0:T(8,128)(2,1)S(1)} %get-tuple-element.102), channel_id=1, source_target_pairs={{0,31},{1,2},{2,1},{3,4},{4,3},{5,6},{6,5},{7,8},{8,7},{9,10},{10,... | collective-permute-start | bytes 393224 | tf_op jit(solution)/shard_map/ppermute | solution.py:236
  30.5 7.8 %collective-permute-start.23 = (bf16[256,256]{1,0:T(8,128)(2,1)S(1)}, bf16[256,256]{1,0:T(8,128)(2,1)S(1)}, u32[]{:S(2)}, u32[]{:S(2)}) collective-permute-start(bf16[256,256]{1,0:T(8,128)(2,1)S(1)} %get-tuple-element.137), channel_id=1, source_target_pairs={{0,1},{1,0},{2,3},{3,2},{4,5},{5,4},{6,7},{7,6},{8,9},{9,8},{10,11... | collective-permute-start | bytes 393224 | tf_op jit(solution)/shard_map/ppermute | solution.py:236
  30.6 7.8 %collective-permute-start.24 = (bf16[256,256]{1,0:T(8,128)(2,1)S(1)}, bf16[256,256]{1,0:T(8,128)(2,1)S(1)}, u32[]{:S(2)}, u32[]{:S(2)}) collective-permute-start(bf16[256,256]{1,0:T(8,128)(2,1)S(1)} %get-tuple-element.138), channel_id=1, source_target_pairs={{0,31},{1,2},{2,1},{3,4},{4,3},{5,6},{6,5},{7,8},{8,7},{9,10},{10,... | collective-permute-start | bytes 393224 | tf_op jit(solution)/shard_map/ppermute | solution.py:236
  34.0 7.8 %collective-permute-start.9 = (bf16[256,256]{1,0:T(8,128)(2,1)S(1)}, bf16[256,256]{1,0:T(8,128)(2,1)S(1)}, u32[]{:S(2)}, u32[]{:S(2)}) collective-permute-start(bf16[256,256]{1,0:T(8,128)(2,1)S(1)} %get-tuple-element.105), channel_id=1, source_target_pairs={{0,1},{1,0},{2,3},{3,2},{4,5},{5,4},{6,7},{7,6},{8,9},{9,8},{10,11... | collective-permute-start | bytes 393224 | tf_op jit(solution)/shard_map/ppermute | solution.py:236
  34.1 7.8 %collective-permute-start.10 = (bf16[256,256]{1,0:T(8,128)(2,1)S(1)}, bf16[256,256]{1,0:T(8,128)(2,1)S(1)}, u32[]{:S(2)}, u32[]{:S(2)}) collective-permute-start(bf16[256,256]{1,0:T(8,128)(2,1)S(1)} %get-tuple-element.106), channel_id=1, source_target_pairs={{0,31},{1,2},{2,1},{3,4},{4,3},{5,6},{6,5},{7,8},{8,7},{9,10},{10,... | collective-permute-start | bytes 393224 | tf_op jit(solution)/shard_map/ppermute | solution.py:236
  39.6 7.8 %collective-permute-start.25 = (bf16[256,256]{1,0:T(8,128)(2,1)S(1)}, bf16[256,256]{1,0:T(8,128)(2,1)S(1)}, u32[]{:S(2)}, u32[]{:S(2)}) collective-permute-start(bf16[256,256]{1,0:T(8,128)(2,1)S(1)} %get-tuple-element.141), channel_id=1, source_target_pairs={{0,1},{1,0},{2,3},{3,2},{4,5},{5,4},{6,7},{7,6},{8,9},{9,8},{10,11... | collective-permute-start | bytes 393224 | tf_op jit(solution)/shard_map/ppermute | solution.py:236
  39.7 8.0 %collective-permute-start.26 = (bf16[256,256]{1,0:T(8,128)(2,1)S(1)}, bf16[256,256]{1,0:T(8,128)(2,1)S(1)}, u32[]{:S(2)}, u32[]{:S(2)}) collective-permute-start(bf16[256,256]{1,0:T(8,128)(2,1)S(1)} %get-tuple-element.142), channel_id=1, source_target_pairs={{0,31},{1,2},{2,1},{3,4},{4,3},{5,6},{6,5},{7,8},{8,7},{9,10},{10,... | collective-permute-start | bytes 393224 | tf_op jit(solution)/shard_map/ppermute | solution.py:236
  43.1 7.8 %collective-permute-start.11 = (bf16[256,256]{1,0:T(8,128)(2,1)S(1)}, bf16[256,256]{1,0:T(8,128)(2,1)S(1)}, u32[]{:S(2)}, u32[]{:S(2)}) collective-permute-start(bf16[256,256]{1,0:T(8,128)(2,1)S(1)} %get-tuple-element.109), channel_id=1, source_target_pairs={{0,1},{1,0},{2,3},{3,2},{4,5},{5,4},{6,7},{7,6},{8,9},{9,8},{10,11... | collective-permute-start | bytes 393224 | tf_op jit(solution)/shard_map/ppermute | solution.py:236
  43.2 7.8 %collective-permute-start.12 = (bf16[256,256]{1,0:T(8,128)(2,1)S(1)}, bf16[256,256]{1,0:T(8,128)(2,1)S(1)}, u32[]{:S(2)}, u32[]{:S(2)}) collective-permute-start(bf16[256,256]{1,0:T(8,128)(2,1)S(1)} %get-tuple-element.110), channel_id=1, source_target_pairs={{0,31},{1,2},{2,1},{3,4},{4,3},{5,6},{6,5},{7,8},{8,7},{9,10},{10,... | collective-permute-start | bytes 393224 | tf_op jit(solution)/shard_map/ppermute | solution.py:236
  48.9 7.6 %collective-permute-start.27 = (bf16[256,256]{1,0:T(8,128)(2,1)S(1)}, bf16[256,256]{1,0:T(8,128)(2,1)S(1)}, u32[]{:S(2)}, u32[]{:S(2)}) collective-permute-start(bf16[256,256]{1,0:T(8,128)(2,1)S(1)} %get-tuple-element.145), channel_id=1, source_target_pairs={{0,1},{1,0},{2,3},{3,2},{4,5},{5,4},{6,7},{7,6},{8,9},{9,8},{10,11... | collective-permute-start | bytes 393224 | tf_op jit(solution)/shard_map/ppermute | solution.py:236
  49.0 7.8 %collective-permute-start.28 = (bf16[256,256]{1,0:T(8,128)(2,1)S(1)}, bf16[256,256]{1,0:T(8,128)(2,1)S(1)}, u32[]{:S(2)}, u32[]{:S(2)}) collective-permute-start(bf16[256,256]{1,0:T(8,128)(2,1)S(1)} %get-tuple-element.146), channel_id=1, source_target_pairs={{0,31},{1,2},{2,1},{3,4},{4,3},{5,6},{6,5},{7,8},{8,7},{9,10},{10,... | collective-permute-start | bytes 393224 | tf_op jit(solution)/shard_map/ppermute | solution.py:236
  52.2 7.8 %collective-permute-start.13 = (bf16[256,256]{1,0:T(8,128)(2,1)S(1)}, bf16[256,256]{1,0:T(8,128)(2,1)S(1)}, u32[]{:S(2)}, u32[]{:S(2)}) collective-permute-start(bf16[256,256]{1,0:T(8,128)(2,1)S(1)} %get-tuple-element.113), channel_id=1, source_target_pairs={{0,1},{1,0},{2,3},{3,2},{4,5},{5,4},{6,7},{7,6},{8,9},{9,8},{10,11... | collective-permute-start | bytes 393224 | tf_op jit(solution)/shard_map/ppermute | solution.py:236
  52.3 7.8 %collective-permute-start.14 = (bf16[256,256]{1,0:T(8,128)(2,1)S(1)}, bf16[256,256]{1,0:T(8,128)(2,1)S(1)}, u32[]{:S(2)}, u32[]{:S(2)}) collective-permute-start(bf16[256,256]{1,0:T(8,128)(2,1)S(1)} %get-tuple-element.114), channel_id=1, source_target_pairs={{0,31},{1,2},{2,1},{3,4},{4,3},{5,6},{6,5},{7,8},{8,7},{9,10},{10,... | collective-permute-start | bytes 393224 | tf_op jit(solution)/shard_map/ppermute | solution.py:236
  58.0 7.6 %collective-permute-start.29 = (bf16[256,256]{1,0:T(8,128)(2,1)S(1)}, bf16[256,256]{1,0:T(8,128)(2,1)S(1)}, u32[]{:S(2)}, u32[]{:S(2)}) collective-permute-start(bf16[256,256]{1,0:T(8,128)(2,1)S(1)} %get-tuple-element.149), channel_id=1, source_target_pairs={{0,1},{1,0},{2,3},{3,2},{4,5},{5,4},{6,7},{7,6},{8,9},{9,8},{10,11... | collective-permute-start | bytes 393224 | tf_op jit(solution)/shard_map/ppermute | solution.py:236
  58.1 7.8 %collective-permute-start.30 = (bf16[256,256]{1,0:T(8,128)(2,1)S(1)}, bf16[256,256]{1,0:T(8,128)(2,1)S(1)}, u32[]{:S(2)}, u32[]{:S(2)}) collective-permute-start(bf16[256,256]{1,0:T(8,128)(2,1)S(1)} %get-tuple-element.150), channel_id=1, source_target_pairs={{0,31},{1,2},{2,1},{3,4},{4,3},{5,6},{6,5},{7,8},{8,7},{9,10},{10,... | collective-permute-start | bytes 393224 | tf_op jit(solution)/shard_map/ppermute | solution.py:236
  61.3 7.8 %collective-permute-start.15 = (bf16[256,256]{1,0:T(8,128)(2,1)S(1)}, bf16[256,256]{1,0:T(8,128)(2,1)S(1)}, u32[]{:S(2)}, u32[]{:S(2)}) collective-permute-start(bf16[256,256]{1,0:T(8,128)(2,1)S(1)} %get-tuple-element.117), channel_id=1, source_target_pairs={{0,1},{1,0},{2,3},{3,2},{4,5},{5,4},{6,7},{7,6},{8,9},{9,8},{10,11... | collective-permute-start | bytes 393224 | tf_op jit(solution)/shard_map/ppermute | solution.py:236
  61.4 7.8 %collective-permute-start.16 = (bf16[256,256]{1,0:T(8,128)(2,1)S(1)}, bf16[256,256]{1,0:T(8,128)(2,1)S(1)}, u32[]{:S(2)}, u32[]{:S(2)}) collective-permute-start(bf16[256,256]{1,0:T(8,128)(2,1)S(1)} %get-tuple-element.118), channel_id=1, source_target_pairs={{0,31},{1,2},{2,1},{3,4},{4,3},{5,6},{6,5},{7,8},{8,7},{9,10},{10,... | collective-permute-start | bytes 393224 | tf_op jit(solution)/shard_map/ppermute | solution.py:236
  67.1 7.8 %collective-permute-start.31 = (bf16[256,256]{1,0:T(8,128)(2,1)S(1)}, bf16[256,256]{1,0:T(8,128)(2,1)S(1)}, u32[]{:S(2)}, u32[]{:S(2)}) collective-permute-start(bf16[256,256]{1,0:T(8,128)(2,1)S(1)} %get-tuple-element.153), channel_id=1, source_target_pairs={{0,1},{1,0},{2,3},{3,2},{4,5},{5,4},{6,7},{7,6},{8,9},{9,8},{10,11... | collective-permute-start | bytes 393224 | tf_op jit(solution)/shard_map/ppermute | solution.py:236
  67.2 7.8 %collective-permute-start.32 = (bf16[256,256]{1,0:T(8,128)(2,1)S(1)}, bf16[256,256]{1,0:T(8,128)(2,1)S(1)}, u32[]{:S(2)}, u32[]{:S(2)}) collective-permute-start(bf16[256,256]{1,0:T(8,128)(2,1)S(1)} %get-tuple-element.154), channel_id=1, source_target_pairs={{0,31},{1,2},{2,1},{3,4},{4,3},{5,6},{6,5},{7,8},{8,7},{9,10},{10,... | collective-permute-start | bytes 393224 | tf_op jit(solution)/shard_map/ppermute | solution.py:236
  70.5 7.8 %collective-permute-start.17 = (bf16[256,256]{1,0:T(8,128)(2,1)S(1)}, bf16[256,256]{1,0:T(8,128)(2,1)S(1)}, u32[]{:S(2)}, u32[]{:S(2)}) collective-permute-start(bf16[256,256]{1,0:T(8,128)(2,1)S(1)} %get-tuple-element.121), channel_id=1, source_target_pairs={{0,1},{1,0},{2,3},{3,2},{4,5},{5,4},{6,7},{7,6},{8,9},{9,8},{10,11... | collective-permute-start | bytes 393224 | tf_op jit(solution)/shard_map/ppermute | solution.py:236
  70.6 8.0 %collective-permute-start.18 = (bf16[256,256]{1,0:T(8,128)(2,1)S(1)}, bf16[256,256]{1,0:T(8,128)(2,1)S(1)}, u32[]{:S(2)}, u32[]{:S(2)}) collective-permute-start(bf16[256,256]{1,0:T(8,128)(2,1)S(1)} %get-tuple-element.122), channel_id=1, source_target_pairs={{0,31},{1,2},{2,1},{3,4},{4,3},{5,6},{6,5},{7,8},{8,7},{9,10},{10,... | collective-permute-start | bytes 393224 | tf_op jit(solution)/shard_map/ppermute | solution.py:236
  76.3 7.8 %collective-permute-start.33 = (bf16[256,256]{1,0:T(8,128)(2,1)S(1)}, bf16[256,256]{1,0:T(8,128)(2,1)S(1)}, u32[]{:S(2)}, u32[]{:S(2)}) collective-permute-start(bf16[256,256]{1,0:T(8,128)(2,1)S(1)} %get-tuple-element.157), channel_id=1, source_target_pairs={{0,1},{1,0},{2,3},{3,2},{4,5},{5,4},{6,7},{7,6},{8,9},{9,8},{10,11... | collective-permute-start | bytes 393224 | tf_op jit(solution)/shard_map/ppermute | solution.py:236
  76.3 7.8 %collective-permute-start.34 = (bf16[256,256]{1,0:T(8,128)(2,1)S(1)}, bf16[256,256]{1,0:T(8,128)(2,1)S(1)}, u32[]{:S(2)}, u32[]{:S(2)}) collective-permute-start(bf16[256,256]{1,0:T(8,128)(2,1)S(1)} %get-tuple-element.158), channel_id=1, source_target_pairs={{0,31},{1,2},{2,1},{3,4},{4,3},{5,6},{6,5},{7,8},{8,7},{9,10},{10,... | collective-permute-start | bytes 393224 | tf_op jit(solution)/shard_map/ppermute | solution.py:236
  79.8 5.0 %collective-permute-start.19 = (bf16[256,256]{1,0:T(8,128)(2,1)S(1)}, bf16[256,256]{1,0:T(8,128)(2,1)S(1)}, u32[]{:S(2)}, u32[]{:S(2)}) collective-permute-start(bf16[256,256]{1,0:T(8,128)(2,1)S(1)} %get-tuple-element.125), channel_id=1, source_target_pairs={{0,1},{1,0},{2,3},{3,2},{4,5},{5,4},{6,7},{7,6},{8,9},{9,8},{10,11... | collective-permute-start | bytes 393224 | tf_op jit(solution)/shard_map/ppermute | solution.py:236
  79.9 7.8 %collective-permute-start.20 = (bf16[256,256]{1,0:T(8,128)(2,1)S(1)}, bf16[256,256]{1,0:T(8,128)(2,1)S(1)}, u32[]{:S(2)}, u32[]{:S(2)}) collective-permute-start(bf16[256,256]{1,0:T(8,128)(2,1)S(1)} %get-tuple-element.126), channel_id=1, source_target_pairs={{0,31},{1,2},{2,1},{3,4},{4,3},{5,6},{6,5},{7,8},{8,7},{9,10},{10,... | collective-permute-start | bytes 393224 | tf_op jit(solution)/shard_map/ppermute | solution.py:236

commit v7 on v6

--- a/solution.py
+++ b/solution.py
@@ -159,6 +159,10 @@
         copy.wait()
 
 
+def gate_body(after_ref, out_ref):
+    out_ref[...] = jnp.zeros_like(out_ref)
+
+
 def pack_body(*refs):
     refs = refs[-4:]
     for k, part in enumerate(refs[:-1]):
@@ -177,7 +181,8 @@
         out_ref[source * 2 + 1 - parity] = swapped_ref[shift - 1]
 
 
-def layer_body(layer, graph, last, others, idx_ref, h_ref, nrm_ref, on_in, off_in, tv_ref, sel_ref, w_ref, *rest):
+def layer_body(layer, graph, last, gated, others, idx_ref, h_ref, nrm_ref, on_in, off_in, tv_ref, sel_ref, w_ref, *rest):
+    rest = rest[gated:]
     done, rest = rest[:others], rest[others:]
     if last and others:
         out_ref, ext, agg, out_h, sems = rest
@@ -308,15 +313,16 @@
                 outs = [(rows_dev, width)]
             else:
                 outs = [(rows_dev, width), (rows_dev, width), (bnd, width), (bnd, width)]
+            gate = [call(gate_body, [(16, TILE)], [VMEM], "gate")(off)[0]] if layer else []
             result = call(
-                functools.partial(layer_body, layer, g, last, others),
+                functools.partial(layer_body, layer, g, last, len(gate), others),
                 outs,
-                [VMEM] * (8 + others),
+                [VMEM] * (8 + len(gate) + others),
                 "layer",
                 scratch,
                 flops=1_000_000,
                 hbm_out=final,
-            )(idx, h, nrm, on, off, values[g], sel, w_all, *outputs[:others])
+            )(idx, h, nrm, on, off, values[g], sel, w_all, *gate, *outputs[:others])
             if last:
                 outputs.append(result[0])
             else:

time: 89.7 us -> 89.6 us (level)
  starting transfers between devices: 58 us -> 54.8 us
  waiting for transfers between devices: 5.46 us -> 8.63 us
    ppermute x14, starting transfers between devices: 42.9 us -> 39.8 us  [exchange(): lax.ppermute(off, 'dom', off_pairs)]
    ppermute x14, waiting for transfers between devices: 5.03 us -> 7.82 us  [exchange(): lax.ppermute(off, 'dom', off_pairs)]
    pallas_call x16 -> x30, Pallas kernels: 19.3 us -> 19.4 us  [the longest x16 19.4 us: on_device(): call(functools.partial(layer_body, layer, g, last, len(gate), others), ou...]
  transfers between devices with their start and end apart: 35 -> 35, of which waited for: 16 -> 15; matrix products, arithmetic and copies ran while one was open for 0% -> 0% of each run, Pallas kernels for 25% -> 25%
where the time goes in v7:
time: 89.6 us; the launch traced here: 89.2 us
  starting transfers between devices  54.8 us (61%)
  Pallas kernels  25.4 us (28%)
  waiting for transfers between devices  8.63 us (10%)
    ppermute x14, starting transfers between devices, exchange(): lax.ppermute(off, 'dom', off_pairs)  39.8 us
    pallas_call x16, Pallas kernels, on_device(): call(functools.partial(layer_body, layer, g, last, len(gate), others), ou...  19.4 us
    ppermute x2, starting transfers between devices, on_device(): state.append([h, nrm, None, lax.ppermute(off, 'dom', off_pairs), sel, idx])  7.99 us
    ppermute x14, waiting for transfers between devices, exchange(): lax.ppermute(off, 'dom', off_pairs)  7.82 us
    ppermute x3, starting transfers between devices, on_device(): lax.ppermute(mine, 'section', [(i, (i + shift) % sections) for i in range...  5.45 us
    pallas_call x2, Pallas kernels, on_device(): call(functools.partial(prologue_body, g, per_section), [(rows_dev, width)...  2.99 us
  transfers between devices with their start and end apart: 35, of which 15 were waited for; matrix products, arithmetic and copies ran while one was open for 0% of the time, Pallas kernels for 25%

profile of v7, /device:TPU:0, one launch (start us, length us, event | category | flops | bytes accessed | tf_op | source)
XLA Modules:
  0.0 89.2 jit_solution(17131981311361222739)
XLA Ops:
  0.0 1.3 %scale.1 = (bf16[2,256,256]{2,1,0:T(8,128)(2,1)S(1)}, bf16[256,256]{1,0:T(8,128)(2,1)S(1)}, bf16[1024,256]{1,0:T(8,128)(2,1)S(1)}, s32[2,256]{1,0:T(2,128)S(1)}, s32[2,8]{1,0:T(2,128)S(1)}, /*index=5*/s32[4,8]{1,0:T(4,128)S(1)}) custom-call(bf16[2,256,256]{2,1,0:T(8,128)(2,1)} %w_hbm.1, bf16[2,256]{1,0:T(2,128)(2,1)} %gain_hbm.1, ...), custom_call_target="tpu_custom_call" | custom-call | bytes 1024 | tf_op jit(solution)/shard_map/scale/pallas_call | solution.py:251
  1.3 4.2 %collective-permute-start.4 = (bf16[256,256]{1,0:T(8,128)(2,1)S(1)}, bf16[256,256]{1,0:T(8,128)(2,1)S(1)}, u32[]{:S(2)}, u32[]{:S(2)}) collective-permute-start(bf16[256,256]{1,0:T(8,128)(2,1)S(1)} %get-tuple-element.86.refs_4_), channel_id=1, source_target_pairs={{0,96},{32,0},{64,32},{96,64},{1,97},{33,1},{65,33},{97,65},{2,98}... | collective-permute-start | bytes 393224 | tf_op jit(solution)/shard_map/ppermute | solution.py:294
  5.5 1.3 %collective-permute-start.2 = (bf16[256,256]{1,0:T(8,128)(2,1)S(1)}, bf16[256,256]{1,0:T(8,128)(2,1)S(1)}, u32[]{:S(2)}, u32[]{:S(2)}) collective-permute-start(bf16[256,256]{1,0:T(8,128)(2,1)S(1)} %get-tuple-element.86.refs_4_), channel_id=1, source_target_pairs={{0,32},{32,64},{64,96},{96,0},{1,33},{33,65},{65,97},{97,1},{2,34}... | collective-permute-start | bytes 393224 | tf_op jit(solution)/shard_map/ppermute | solution.py:294
  6.7 0.8 prologue.2
  7.6 3.9 %collective-permute-start.5 = (bf16[256,256]{1,0:T(8,128)(2,1)S(1)}, bf16[256,256]{1,0:T(8,128)(2,1)S(1)}, u32[]{:S(2)}, u32[]{:S(2)}) collective-permute-start(bf16[256,256]{1,0:T(8,128)(2,1)S(1)} %get-tuple-element.97), channel_id=1, source_target_pairs={{0,31},{1,2},{2,1},{3,4},{4,3},{5,6},{6,5},{7,8},{8,7},{9,10},{10,... | collective-permute-start | bytes 393224 | tf_op jit(solution)/shard_map/ppermute | solution.py:282
  11.5 1.6 %fetch.1 = (bf16[1024,512]{1,0:T(8,128)(2,1)S(1)}, bf16[1024,512]{1,0:T(8,128)(2,1)S(1)}) custom-call(bf16[8,1024,512]{2,1,0:T(8,128)(2,1)} %val_ref.1), custom_call_target="tpu_custom_call" | custom-call | bytes 1024 | tf_op jit(solution)/shard_map/fetch/pallas_call | solution.py:286
  13.1 2.2 %prologue.3 = (bf16[1024,256]{1,0:T(8,128)(2,1)S(1)}, bf16[1024,256]{1,0:T(8,128)(2,1)S(1)}, bf16[512,1024]{1,0:T(8,128)(2,1)S(1)}, bf16[2,256,256]{2,1,0:T(8,12...) custom-call(bf16[8,1024,256]{2,1,0:T(8,128)(2,1)} %refs_0_.1, s32[8,2,256]{2,1,0:T(2,128)} %refs_1_.1, ...), custom_call_target="tpu_custom_call" | custom-call | bytes 1024 | tf_op jit(solution)/shard_map/prologue/pallas_call | solution.py:267
  15.2 0.0 collective-permute-done.3.refs_3_
  15.2 0.0 collective-permute-done.2.refs_2_
  15.3 0.1 collective-permute-done.5.off_in
  15.4 0.0 collective-permute-start.6
  15.4 0.5 collective-permute-start
  15.9 4.1 %collective-permute-start.1 = (bf16[256,256]{1,0:T(8,128)(2,1)S(1)}, bf16[256,256]{1,0:T(8,128)(2,1)S(1)}, u32[]{:S(2)}, u32[]{:S(2)}) collective-permute-start(bf16[256,256]{1,0:T(8,128)(2,1)S(1)} %get-tuple-element.92), channel_id=1, source_target_pairs={{0,31},{1,2},{2,1},{3,4},{4,3},{5,6},{6,5},{7,8},{8,7},{9,10},{10,... | collective-permute-start | bytes 393224 | tf_op jit(solution)/shard_map/ppermute | solution.py:282
  20.0 0.1 order.1.w_ref
  20.1 0.0 collective-permute-done.on_in
  20.1 1.2 %layer.23 = (bf16[1024,256]{1,0:T(8,128)(2,1)S(1)}, bf16[1024,256]{1,0:T(8,128)(2,1)S(1)}, bf16[256,256]{1,0:T(8,128)(2,1)S(1)}, bf16[256,256]{1,0:T(8,128)(2,1)S(1)}) custom-call(s32[32,128]{1,0:T(8,128)S(1)} %get-tuple-element.127.idx_ref, bf16[1024,256]{1,0:T(8,128)(2,1)S(1)} %get-tuple-element.82.refs_0_.h_ref, ...), custom_call_target="tpu_custom_call" | custom-call | flops 1000000 | bytes 1024 | tf_op jit(solution)/shard_map/layer/pallas_call | solution.py:317
  21.3 1.6 %collective-permute-start.22 = (bf16[256,256]{1,0:T(8,128)(2,1)S(1)}, bf16[256,256]{1,0:T(8,128)(2,1)S(1)}, u32[]{:S(2)}, u32[]{:S(2)}) collective-permute-start(bf16[256,256]{1,0:T(8,128)(2,1)S(1)} %get-tuple-element.134), channel_id=1, source_target_pairs={{0,31},{1,2},{2,1},{3,4},{4,3},{5,6},{6,5},{7,8},{8,7},{9,10},{10,... | collective-permute-start | bytes 393224 | tf_op jit(solution)/shard_map/ppermute | solution.py:241
  23.0 0.0 collective-permute-start.21
  23.0 0.7 collective-permute-done.1.off_in
  23.6 1.2 %layer.16 = (bf16[1024,256]{1,0:T(8,128)(2,1)S(1)}, bf16[1024,256]{1,0:T(8,128)(2,1)S(1)}, bf16[256,256]{1,0:T(8,128)(2,1)S(1)}, bf16[256,256]{1,0:T(8,128)(2,1)S(1)}) custom-call(s32[32,128]{1,0:T(8,128)S(1)} %get-tuple-element.88.idx_ref, bf16[1024,256]{1,0:T(8,128)(2,1)S(1)} %get-tuple-element.89.h_ref, ...), custom_call_target="tpu_custom_call" | custom-call | flops 1000000 | bytes 1024 | tf_op jit(solution)/shard_map/layer/pallas_call | solution.py:317
  24.9 4.2 %collective-permute-start.8 = (bf16[256,256]{1,0:T(8,128)(2,1)S(1)}, bf16[256,256]{1,0:T(8,128)(2,1)S(1)}, u32[]{:S(2)}, u32[]{:S(2)}) collective-permute-start(bf16[256,256]{1,0:T(8,128)(2,1)S(1)} %get-tuple-element.102), channel_id=1, source_target_pairs={{0,31},{1,2},{2,1},{3,4},{4,3},{5,6},{6,5},{7,8},{8,7},{9,10},{10,... | collective-permute-start | bytes 393224 | tf_op jit(solution)/shard_map/ppermute | solution.py:241
  29.0 0.1 collective-permute-done.22.after_ref.off_in
  29.1 1.2 %layer.24 = (bf16[1024,256]{1,0:T(8,128)(2,1)S(1)}, bf16[1024,256]{1,0:T(8,128)(2,1)S(1)}, bf16[256,256]{1,0:T(8,128)(2,1)S(1)}, bf16[256,256]{1,0:T(8,128)(2,1)S(1)}) custom-call(s32[32,128]{1,0:T(8,128)S(1)} %get-tuple-element.127.idx_ref, bf16[1024,256]{1,0:T(8,128)(2,1)S(1)} %get-tuple-element.131.h_ref, ...), custom_call_target="tpu_custom_call" | custom-call | flops 1000000 | bytes 1024 | tf_op jit(solution)/shard_map/layer/pallas_call | solution.py:317
  30.4 1.6 %collective-permute-start.24 = (bf16[256,256]{1,0:T(8,128)(2,1)S(1)}, bf16[256,256]{1,0:T(8,128)(2,1)S(1)}, u32[]{:S(2)}, u32[]{:S(2)}) collective-permute-start(bf16[256,256]{1,0:T(8,128)(2,1)S(1)} %get-tuple-element.138), channel_id=1, source_target_pairs={{0,31},{1,2},{2,1},{3,4},{4,3},{5,6},{6,5},{7,8},{8,7},{9,10},{10,... | collective-permute-start | bytes 393224 | tf_op jit(solution)/shard_map/ppermute | solution.py:241
  32.0 0.7 collective-permute-done.8.after_ref.off_in
  32.7 1.2 %layer.17 = (bf16[1024,256]{1,0:T(8,128)(2,1)S(1)}, bf16[1024,256]{1,0:T(8,128)(2,1)S(1)}, bf16[256,256]{1,0:T(8,128)(2,1)S(1)}, bf16[256,256]{1,0:T(8,128)(2,1)S(1)}) custom-call(s32[32,128]{1,0:T(8,128)S(1)} %get-tuple-element.88.idx_ref, bf16[1024,256]{1,0:T(8,128)(2,1)S(1)} %get-tuple-element.99.h_ref, bf16[1024,256]{1,0:T(8,128)(2,1)S(1)} %get-tuple-element.100.nrm_ref, ...), custom_call_target="tpu_custom_call" | custom-call | flops 1000000 | bytes 1024 | tf_op jit(solution)/shard_map/layer/pallas_call | solution.py:317
  33.9 4.2 %collective-permute-start.10 = (bf16[256,256]{1,0:T(8,128)(2,1)S(1)}, bf16[256,256]{1,0:T(8,128)(2,1)S(1)}, u32[]{:S(2)}, u32[]{:S(2)}) collective-permute-start(bf16[256,256]{1,0:T(8,128)(2,1)S(1)} %get-tuple-element.106), channel_id=1, source_target_pairs={{0,31},{1,2},{2,1},{3,4},{4,3},{5,6},{6,5},{7,8},{8,7},{9,10},{10,... | collective-permute-start | bytes 393224 | tf_op jit(solution)/shard_map/ppermute | solution.py:241
  38.1 0.1 collective-permute-done.24.after_ref.off_in
  38.2 1.2 %layer.25 = (bf16[1024,256]{1,0:T(8,128)(2,1)S(1)}, bf16[1024,256]{1,0:T(8,128)(2,1)S(1)}, bf16[256,256]{1,0:T(8,128)(2,1)S(1)}, bf16[256,256]{1,0:T(8,128)(2,1)S(1)}) custom-call(s32[32,128]{1,0:T(8,128)S(1)} %get-tuple-element.127.idx_ref, bf16[1024,256]{1,0:T(8,128)(2,1)S(1)} %get-tuple-element.135.h_ref, ...), custom_call_target="tpu_custom_call" | custom-call | flops 1000000 | bytes 1024 | tf_op jit(solution)/shard_map/layer/pallas_call | solution.py:317
  39.4 1.6 %collective-permute-start.26 = (bf16[256,256]{1,0:T(8,128)(2,1)S(1)}, bf16[256,256]{1,0:T(8,128)(2,1)S(1)}, u32[]{:S(2)}, u32[]{:S(2)}) collective-permute-start(bf16[256,256]{1,0:T(8,128)(2,1)S(1)} %get-tuple-element.142), channel_id=1, source_target_pairs={{0,31},{1,2},{2,1},{3,4},{4,3},{5,6},{6,5},{7,8},{8,7},{9,10},{10,... | collective-permute-start | bytes 393224 | tf_op jit(solution)/shard_map/ppermute | solution.py:241
  41.0 0.0 collective-permute-start.25
  41.0 0.7 collective-permute-done.10.after_ref.off_in
  41.7 1.2 %layer.18 = (bf16[1024,256]{1,0:T(8,128)(2,1)S(1)}, bf16[1024,256]{1,0:T(8,128)(2,1)S(1)}, bf16[256,256]{1,0:T(8,128)(2,1)S(1)}, bf16[256,256]{1,0:T(8,128)(2,1)S(1)}) custom-call(s32[32,128]{1,0:T(8,128)S(1)} %get-tuple-element.88.idx_ref, bf16[1024,256]{1,0:T(8,128)(2,1)S(1)} %get-tuple-element.103.h_ref, ...), custom_call_target="tpu_custom_call" | custom-call | flops 1000000 | bytes 1024 | tf_op jit(solution)/shard_map/layer/pallas_call | solution.py:317
  42.9 4.2 %collective-permute-start.12 = (bf16[256,256]{1,0:T(8,128)(2,1)S(1)}, bf16[256,256]{1,0:T(8,128)(2,1)S(1)}, u32[]{:S(2)}, u32[]{:S(2)}) collective-permute-start(bf16[256,256]{1,0:T(8,128)(2,1)S(1)} %get-tuple-element.110), channel_id=1, source_target_pairs={{0,31},{1,2},{2,1},{3,4},{4,3},{5,6},{6,5},{7,8},{8,7},{9,10},{10,... | collective-permute-start | bytes 393224 | tf_op jit(solution)/shard_map/ppermute | solution.py:241
  47.1 0.1 collective-permute-done.26.after_ref.off_in
  47.2 1.2 %layer.26 = (bf16[1024,256]{1,0:T(8,128)(2,1)S(1)}, bf16[1024,256]{1,0:T(8,128)(2,1)S(1)}, bf16[256,256]{1,0:T(8,128)(2,1)S(1)}, bf16[256,256]{1,0:T(8,128)(2,1)S(1)}) custom-call(s32[32,128]{1,0:T(8,128)S(1)} %get-tuple-element.127.idx_ref, bf16[1024,256]{1,0:T(8,128)(2,1)S(1)} %get-tuple-element.139.h_ref, ...), custom_call_target="tpu_custom_call" | custom-call | flops 1000000 | bytes 1024 | tf_op jit(solution)/shard_map/layer/pallas_call | solution.py:317
  48.5 1.6 %collective-permute-start.28 = (bf16[256,256]{1,0:T(8,128)(2,1)S(1)}, bf16[256,256]{1,0:T(8,128)(2,1)S(1)}, u32[]{:S(2)}, u32[]{:S(2)}) collective-permute-start(bf16[256,256]{1,0:T(8,128)(2,1)S(1)} %get-tuple-element.146), channel_id=1, source_target_pairs={{0,31},{1,2},{2,1},{3,4},{4,3},{5,6},{6,5},{7,8},{8,7},{9,10},{10,... | collective-permute-start | bytes 393224 | tf_op jit(solution)/shard_map/ppermute | solution.py:241
  50.1 0.7 collective-permute-done.12.after_ref.off_in
  50.7 1.2 %layer.19 = (bf16[1024,256]{1,0:T(8,128)(2,1)S(1)}, bf16[1024,256]{1,0:T(8,128)(2,1)S(1)}, bf16[256,256]{1,0:T(8,128)(2,1)S(1)}, bf16[256,256]{1,0:T(8,128)(2,1)S(1)}) custom-call(s32[32,128]{1,0:T(8,128)S(1)} %get-tuple-element.88.idx_ref, bf16[1024,256]{1,0:T(8,128)(2,1)S(1)} %get-tuple-element.107.h_ref, ...), custom_call_target="tpu_custom_call" | custom-call | flops 1000000 | bytes 1024 | tf_op jit(solution)/shard_map/layer/pallas_call | solution.py:317
  52.0 4.2 %collective-permute-start.14 = (bf16[256,256]{1,0:T(8,128)(2,1)S(1)}, bf16[256,256]{1,0:T(8,128)(2,1)S(1)}, u32[]{:S(2)}, u32[]{:S(2)}) collective-permute-start(bf16[256,256]{1,0:T(8,128)(2,1)S(1)} %get-tuple-element.114), channel_id=1, source_target_pairs={{0,31},{1,2},{2,1},{3,4},{4,3},{5,6},{6,5},{7,8},{8,7},{9,10},{10,... | collective-permute-start | bytes 393224 | tf_op jit(solution)/shard_map/ppermute | solution.py:241
  56.2 0.1 collective-permute-done.28.after_ref.off_in
  56.2 1.2 %layer.27 = (bf16[1024,256]{1,0:T(8,128)(2,1)S(1)}, bf16[1024,256]{1,0:T(8,128)(2,1)S(1)}, bf16[256,256]{1,0:T(8,128)(2,1)S(1)}, bf16[256,256]{1,0:T(8,128)(2,1)S(1)}) custom-call(s32[32,128]{1,0:T(8,128)S(1)} %get-tuple-element.127.idx_ref, bf16[1024,256]{1,0:T(8,128)(2,1)S(1)} %get-tuple-element.143.h_ref, ...), custom_call_target="tpu_custom_call" | custom-call | flops 1000000 | bytes 1024 | tf_op jit(solution)/shard_map/layer/pallas_call | solution.py:317
  57.5 1.6 %collective-permute-start.30 = (bf16[256,256]{1,0:T(8,128)(2,1)S(1)}, bf16[256,256]{1,0:T(8,128)(2,1)S(1)}, u32[]{:S(2)}, u32[]{:S(2)}) collective-permute-start(bf16[256,256]{1,0:T(8,128)(2,1)S(1)} %get-tuple-element.150), channel_id=1, source_target_pairs={{0,31},{1,2},{2,1},{3,4},{4,3},{5,6},{6,5},{7,8},{8,7},{9,10},{10,... | collective-permute-start | bytes 393224 | tf_op jit(solution)/shard_map/ppermute | solution.py:241
  59.1 0.7 collective-permute-done.14.after_ref.off_in
  59.8 1.2 %layer.20 = (bf16[1024,256]{1,0:T(8,128)(2,1)S(1)}, bf16[1024,256]{1,0:T(8,128)(2,1)S(1)}, bf16[256,256]{1,0:T(8,128)(2,1)S(1)}, bf16[256,256]{1,0:T(8,128)(2,1)S(1)}) custom-call(s32[32,128]{1,0:T(8,128)S(1)} %get-tuple-element.88.idx_ref, bf16[1024,256]{1,0:T(8,128)(2,1)S(1)} %get-tuple-element.111.h_ref, ...), custom_call_target="tpu_custom_call" | custom-call | flops 1000000 | bytes 1024 | tf_op jit(solution)/shard_map/layer/pallas_call | solution.py:317
  61.0 4.2 %collective-permute-start.16 = (bf16[256,256]{1,0:T(8,128)(2,1)S(1)}, bf16[256,256]{1,0:T(8,128)(2,1)S(1)}, u32[]{:S(2)}, u32[]{:S(2)}) collective-permute-start(bf16[256,256]{1,0:T(8,128)(2,1)S(1)} %get-tuple-element.118), channel_id=1, source_target_pairs={{0,31},{1,2},{2,1},{3,4},{4,3},{5,6},{6,5},{7,8},{8,7},{9,10},{10,... | collective-permute-start | bytes 393224 | tf_op jit(solution)/shard_map/ppermute | solution.py:241
  65.2 0.1 collective-permute-done.30.after_ref.off_in
  65.3 1.2 %layer.28 = (bf16[1024,256]{1,0:T(8,128)(2,1)S(1)}, bf16[1024,256]{1,0:T(8,128)(2,1)S(1)}, bf16[256,256]{1,0:T(8,128)(2,1)S(1)}, bf16[256,256]{1,0:T(8,128)(2,1)S(1)}) custom-call(s32[32,128]{1,0:T(8,128)S(1)} %get-tuple-element.127.idx_ref, bf16[1024,256]{1,0:T(8,128)(2,1)S(1)} %get-tuple-element.147.h_ref, ...), custom_call_target="tpu_custom_call" | custom-call | flops 1000000 | bytes 1024 | tf_op jit(solution)/shard_map/layer/pallas_call | solution.py:317
  66.5 0.5 collective-permute-start.31
  67.0 1.2 %collective-permute-start.32 = (bf16[256,256]{1,0:T(8,128)(2,1)S(1)}, bf16[256,256]{1,0:T(8,128)(2,1)S(1)}, u32[]{:S(2)}, u32[]{:S(2)}) collective-permute-start(bf16[256,256]{1,0:T(8,128)(2,1)S(1)} %get-tuple-element.154), channel_id=1, source_target_pairs={{0,31},{1,2},{2,1},{3,4},{4,3},{5,6},{6,5},{7,8},{8,7},{9,10},{10,... | collective-permute-start | bytes 393224 | tf_op jit(solution)/shard_map/ppermute | solution.py:241
  68.2 0.6 collective-permute-done.16.after_ref.off_in
  68.8 1.2 %layer.21 = (bf16[1024,256]{1,0:T(8,128)(2,1)S(1)}, bf16[1024,256]{1,0:T(8,128)(2,1)S(1)}, bf16[256,256]{1,0:T(8,128)(2,1)S(1)}, bf16[256,256]{1,0:T(8,128)(2,1)S(1)}) custom-call(s32[32,128]{1,0:T(8,128)S(1)} %get-tuple-element.88.idx_ref, bf16[1024,256]{1,0:T(8,128)(2,1)S(1)} %get-tuple-element.115.h_ref, ...), custom_call_target="tpu_custom_call" | custom-call | flops 1000000 | bytes 1024 | tf_op jit(solution)/shard_map/layer/pallas_call | solution.py:317
  70.0 4.2 %collective-permute-start.18 = (bf16[256,256]{1,0:T(8,128)(2,1)S(1)}, bf16[256,256]{1,0:T(8,128)(2,1)S(1)}, u32[]{:S(2)}, u32[]{:S(2)}) collective-permute-start(bf16[256,256]{1,0:T(8,128)(2,1)S(1)} %get-tuple-element.122), channel_id=1, source_target_pairs={{0,31},{1,2},{2,1},{3,4},{4,3},{5,6},{6,5},{7,8},{8,7},{9,10},{10,... | collective-permute-start | bytes 393224 | tf_op jit(solution)/shard_map/ppermute | solution.py:241
  74.2 0.0 collective-permute-start.17
  74.2 0.5 collective-permute-done.32.after_ref.off_in
  74.8 1.2 %layer.29 = (bf16[1024,256]{1,0:T(8,128)(2,1)S(1)}, bf16[1024,256]{1,0:T(8,128)(2,1)S(1)}, bf16[256,256]{1,0:T(8,128)(2,1)S(1)}, bf16[256,256]{1,0:T(8,128)(2,1)S(1)}) custom-call(s32[32,128]{1,0:T(8,128)S(1)} %get-tuple-element.127.idx_ref, bf16[1024,256]{1,0:T(8,128)(2,1)S(1)} %get-tuple-element.151.h_ref, ...), custom_call_target="tpu_custom_call" | custom-call | flops 1000000 | bytes 1024 | tf_op jit(solution)/shard_map/layer/pallas_call | solution.py:317
  76.0 1.3 %collective-permute-start.34 = (bf16[256,256]{1,0:T(8,128)(2,1)S(1)}, bf16[256,256]{1,0:T(8,128)(2,1)S(1)}, u32[]{:S(2)}, u32[]{:S(2)}) collective-permute-start(bf16[256,256]{1,0:T(8,128)(2,1)S(1)} %get-tuple-element.158), channel_id=1, source_target_pairs={{0,31},{1,2},{2,1},{3,4},{4,3},{5,6},{6,5},{7,8},{8,7},{9,10},{10,... | collective-permute-start | bytes 393224 | tf_op jit(solution)/shard_map/ppermute | solution.py:241
  77.3 0.6 collective-permute-done.18.after_ref.off_in
  77.8 1.2 %layer.22 = (bf16[1024,256]{1,0:T(8,128)(2,1)S(1)}, bf16[1024,256]{1,0:T(8,128)(2,1)S(1)}, bf16[256,256]{1,0:T(8,128)(2,1)S(1)}, bf16[256,256]{1,0:T(8,128)(2,1)S(1)}) custom-call(s32[32,128]{1,0:T(8,128)S(1)} %get-tuple-element.88.idx_ref, bf16[1024,256]{1,0:T(8,128)(2,1)S(1)} %get-tuple-element.119.h_ref, ...), custom_call_target="tpu_custom_call" | custom-call | flops 1000000 | bytes 1024 | tf_op jit(solution)/shard_map/layer/pallas_call | solution.py:317
  79.1 4.2 %collective-permute-start.20 = (bf16[256,256]{1,0:T(8,128)(2,1)S(1)}, bf16[256,256]{1,0:T(8,128)(2,1)S(1)}, u32[]{:S(2)}, u32[]{:S(2)}) collective-permute-start(bf16[256,256]{1,0:T(8,128)(2,1)S(1)} %get-tuple-element.126), channel_id=1, source_target_pairs={{0,31},{1,2},{2,1},{3,4},{4,3},{5,6},{6,5},{7,8},{8,7},{9,10},{10,... | collective-permute-start | bytes 393224 | tf_op jit(solution)/shard_map/ppermute | solution.py:241
  83.3 0.5 collective-permute-start.19
  83.8 3.1 %collective-permute-done.20.after_ref.off_in = bf16[256,256]{1,0:T(8,128)(2,1)S(1)} collective-permute-done((bf16[256,256]{1,0:T(8,128)(2,1)S(1)}, bf16[256,256]{1,0:T(8,128)(2,1)S(1)}, u32[]{:S(2)}, u32[]{:S(2)}) %collective-permute-start.20) | collective-permute-done | bytes 131104 | tf_op jit(solution)/shard_map/ppermute | solution.py:241
  86.9 0.7 layer.30.rest_1_
  87.6 1.4 %layer.31 = bf16[2,1024,256]{2,1,0:T(8,128)(2,1)} custom-call(s32[32,128]{1,0:T(8,128)S(1)} %get-tuple-element.88.idx_ref, bf16[1024,256]{1,0:T(8,128)(2,1)S(1)} %get-tuple-element.123.h_ref, bf16[1024,256]{1,0:T(8,128)(2,1)S(1)} %get-tuple-element.124.nrm_ref, bf16[256,256]{1,0:T(8,128)(2,1)S(1)} %collective-permute-done.19.on_in, ...), custom_call_target="tpu_custom_call" | custom-call | flops 1000000 | bytes 1024 | tf_op jit(solution)/shard_map/layer/pallas_call | solution.py:317
  (42 shorter events, 0.1 us)
Async XLA Ops:
  1.3 13.9 %collective-permute-start.4 = (bf16[256,256]{1,0:T(8,128)(2,1)S(1)}, bf16[256,256]{1,0:T(8,128)(2,1)S(1)}, u32[]{:S(2)}, u32[]{:S(2)}) collective-permute-start(bf16[256,256]{1,0:T(8,128)(2,1)S(1)} %get-tuple-element.86.refs_4_), channel_id=1, source_target_pairs={{0,96},{32,0},{64,32},{96,64},{1,97},{33,1},{65,33},{97,65},{2,98}... | collective-permute-start | bytes 393224 | tf_op jit(solution)/shard_map/ppermute | solution.py:294
  5.5 9.7 %collective-permute-start.3 = (bf16[256,256]{1,0:T(8,128)(2,1)S(1)}, bf16[256,256]{1,0:T(8,128)(2,1)S(1)}, u32[]{:S(2)}, u32[]{:S(2)}) collective-permute-start(bf16[256,256]{1,0:T(8,128)(2,1)S(1)} %get-tuple-element.86.refs_4_), channel_id=1, source_target_pairs={{0,64},{32,96},{64,0},{96,32},{1,65},{33,97},{65,1},{97,33},{2,66}... | collective-permute-start | bytes 393224 | tf_op jit(solution)/shard_map/ppermute | solution.py:294
  5.5 9.8 %collective-permute-start.2 = (bf16[256,256]{1,0:T(8,128)(2,1)S(1)}, bf16[256,256]{1,0:T(8,128)(2,1)S(1)}, u32[]{:S(2)}, u32[]{:S(2)}) collective-permute-start(bf16[256,256]{1,0:T(8,128)(2,1)S(1)} %get-tuple-element.86.refs_4_), channel_id=1, source_target_pairs={{0,32},{32,64},{64,96},{96,0},{1,33},{33,65},{65,97},{97,1},{2,34}... | collective-permute-start | bytes 393224 | tf_op jit(solution)/shard_map/ppermute | solution.py:294
  7.6 7.8 %collective-permute-start.5 = (bf16[256,256]{1,0:T(8,128)(2,1)S(1)}, bf16[256,256]{1,0:T(8,128)(2,1)S(1)}, u32[]{:S(2)}, u32[]{:S(2)}) collective-permute-start(bf16[256,256]{1,0:T(8,128)(2,1)S(1)} %get-tuple-element.97), channel_id=1, source_target_pairs={{0,31},{1,2},{2,1},{3,4},{4,3},{5,6},{6,5},{7,8},{8,7},{9,10},{10,... | collective-permute-start | bytes 393224 | tf_op jit(solution)/shard_map/ppermute | solution.py:282
  15.4 4.6 %collective-permute-start.6 = (bf16[3,256,256]{2,1,0:T(8,128)(2,1)S(1)}, bf16[3,256,256]{2,1,0:T(8,128)(2,1)S(1)}, u32[]{:S(2)}, u32[]{:S(2)}) collective-permute-start(bf16[3,256,256]{2,1,0:T(8,128)(2,1)S(1)} %pack.1.mine_ref), channel_id=1, source_target_pairs={{0,1},{1,0},{2,3},{3,2},{4,5},{5,4},{6,7},{7,6},{8,9},{9,8},{10,11... | collective-permute-start | bytes 1179656 | tf_op jit(solution)/shard_map/ppermute | solution.py:299
  15.4 4.7 %collective-permute-start = (bf16[2,256,256]{2,1,0:T(8,128)(2,1)S(1)}, bf16[2,256,256]{2,1,0:T(8,128)(2,1)S(1)}, u32[]{:S(2)}, u32[]{:S(2)}) collective-permute-start(bf16[2,256,256]{2,1,0:T(8,128)(2,1)S(1)} %get-tuple-element.91), channel_id=1, source_target_pairs={{0,1},{1,0},{2,3},{3,2},{4,5},{5,4},{6,7},{7,6},{8,9},{9,8},{10,11... | collective-permute-start | bytes 786440 | tf_op jit(solution)/shard_map/ppermute | solution.py:283
  15.9 7.7 %collective-permute-start.1 = (bf16[256,256]{1,0:T(8,128)(2,1)S(1)}, bf16[256,256]{1,0:T(8,128)(2,1)S(1)}, u32[]{:S(2)}, u32[]{:S(2)}) collective-permute-start(bf16[256,256]{1,0:T(8,128)(2,1)S(1)} %get-tuple-element.92), channel_id=1, source_target_pairs={{0,31},{1,2},{2,1},{3,4},{4,3},{5,6},{6,5},{7,8},{8,7},{9,10},{10,... | collective-permute-start | bytes 393224 | tf_op jit(solution)/shard_map/ppermute | solution.py:282
  21.3 7.8 %collective-permute-start.22 = (bf16[256,256]{1,0:T(8,128)(2,1)S(1)}, bf16[256,256]{1,0:T(8,128)(2,1)S(1)}, u32[]{:S(2)}, u32[]{:S(2)}) collective-permute-start(bf16[256,256]{1,0:T(8,128)(2,1)S(1)} %get-tuple-element.134), channel_id=1, source_target_pairs={{0,31},{1,2},{2,1},{3,4},{4,3},{5,6},{6,5},{7,8},{8,7},{9,10},{10,... | collective-permute-start | bytes 393224 | tf_op jit(solution)/shard_map/ppermute | solution.py:241
  23.0 6.2 %collective-permute-start.21 = (bf16[256,256]{1,0:T(8,128)(2,1)S(1)}, bf16[256,256]{1,0:T(8,128)(2,1)S(1)}, u32[]{:S(2)}, u32[]{:S(2)}) collective-permute-start(bf16[256,256]{1,0:T(8,128)(2,1)S(1)} %get-tuple-element.133), channel_id=1, source_target_pairs={{0,1},{1,0},{2,3},{3,2},{4,5},{5,4},{6,7},{7,6},{8,9},{9,8},{10,11... | collective-permute-start | bytes 393224 | tf_op jit(solution)/shard_map/ppermute | solution.py:241
  24.9 7.8 %collective-permute-start.8 = (bf16[256,256]{1,0:T(8,128)(2,1)S(1)}, bf16[256,256]{1,0:T(8,128)(2,1)S(1)}, u32[]{:S(2)}, u32[]{:S(2)}) collective-permute-start(bf16[256,256]{1,0:T(8,128)(2,1)S(1)} %get-tuple-element.102), channel_id=1, source_target_pairs={{0,31},{1,2},{2,1},{3,4},{4,3},{5,6},{6,5},{7,8},{8,7},{9,10},{10,... | collective-permute-start | bytes 393224 | tf_op jit(solution)/shard_map/ppermute | solution.py:241
  29.0 3.6 %collective-permute-start.7 = (bf16[256,256]{1,0:T(8,128)(2,1)S(1)}, bf16[256,256]{1,0:T(8,128)(2,1)S(1)}, u32[]{:S(2)}, u32[]{:S(2)}) collective-permute-start(bf16[256,256]{1,0:T(8,128)(2,1)S(1)} %get-tuple-element.101), channel_id=1, source_target_pairs={{0,1},{1,0},{2,3},{3,2},{4,5},{5,4},{6,7},{7,6},{8,9},{9,8},{10,11... | collective-permute-start | bytes 393224 | tf_op jit(solution)/shard_map/ppermute | solution.py:241
  30.4 7.8 %collective-permute-start.24 = (bf16[256,256]{1,0:T(8,128)(2,1)S(1)}, bf16[256,256]{1,0:T(8,128)(2,1)S(1)}, u32[]{:S(2)}, u32[]{:S(2)}) collective-permute-start(bf16[256,256]{1,0:T(8,128)(2,1)S(1)} %get-tuple-element.138), channel_id=1, source_target_pairs={{0,31},{1,2},{2,1},{3,4},{4,3},{5,6},{6,5},{7,8},{8,7},{9,10},{10,... | collective-permute-start | bytes 393224 | tf_op jit(solution)/shard_map/ppermute | solution.py:241
  32.0 6.2 %collective-permute-start.23 = (bf16[256,256]{1,0:T(8,128)(2,1)S(1)}, bf16[256,256]{1,0:T(8,128)(2,1)S(1)}, u32[]{:S(2)}, u32[]{:S(2)}) collective-permute-start(bf16[256,256]{1,0:T(8,128)(2,1)S(1)} %get-tuple-element.137), channel_id=1, source_target_pairs={{0,1},{1,0},{2,3},{3,2},{4,5},{5,4},{6,7},{7,6},{8,9},{9,8},{10,11... | collective-permute-start | bytes 393224 | tf_op jit(solution)/shard_map/ppermute | solution.py:241
  33.9 7.8 %collective-permute-start.10 = (bf16[256,256]{1,0:T(8,128)(2,1)S(1)}, bf16[256,256]{1,0:T(8,128)(2,1)S(1)}, u32[]{:S(2)}, u32[]{:S(2)}) collective-permute-start(bf16[256,256]{1,0:T(8,128)(2,1)S(1)} %get-tuple-element.106), channel_id=1, source_target_pairs={{0,31},{1,2},{2,1},{3,4},{4,3},{5,6},{6,5},{7,8},{8,7},{9,10},{10,... | collective-permute-start | bytes 393224 | tf_op jit(solution)/shard_map/ppermute | solution.py:241
  38.1 3.6 %collective-permute-start.9 = (bf16[256,256]{1,0:T(8,128)(2,1)S(1)}, bf16[256,256]{1,0:T(8,128)(2,1)S(1)}, u32[]{:S(2)}, u32[]{:S(2)}) collective-permute-start(bf16[256,256]{1,0:T(8,128)(2,1)S(1)} %get-tuple-element.105), channel_id=1, source_target_pairs={{0,1},{1,0},{2,3},{3,2},{4,5},{5,4},{6,7},{7,6},{8,9},{9,8},{10,11... | collective-permute-start | bytes 393224 | tf_op jit(solution)/shard_map/ppermute | solution.py:241
  39.4 7.8 %collective-permute-start.26 = (bf16[256,256]{1,0:T(8,128)(2,1)S(1)}, bf16[256,256]{1,0:T(8,128)(2,1)S(1)}, u32[]{:S(2)}, u32[]{:S(2)}) collective-permute-start(bf16[256,256]{1,0:T(8,128)(2,1)S(1)} %get-tuple-element.142), channel_id=1, source_target_pairs={{0,31},{1,2},{2,1},{3,4},{4,3},{5,6},{6,5},{7,8},{8,7},{9,10},{10,... | collective-permute-start | bytes 393224 | tf_op jit(solution)/shard_map/ppermute | solution.py:241
  41.0 6.2 %collective-permute-start.25 = (bf16[256,256]{1,0:T(8,128)(2,1)S(1)}, bf16[256,256]{1,0:T(8,128)(2,1)S(1)}, u32[]{:S(2)}, u32[]{:S(2)}) collective-permute-start(bf16[256,256]{1,0:T(8,128)(2,1)S(1)} %get-tuple-element.141), channel_id=1, source_target_pairs={{0,1},{1,0},{2,3},{3,2},{4,5},{5,4},{6,7},{7,6},{8,9},{9,8},{10,11... | collective-permute-start | bytes 393224 | tf_op jit(solution)/shard_map/ppermute | solution.py:241
  42.9 7.8 %collective-permute-start.12 = (bf16[256,256]{1,0:T(8,128)(2,1)S(1)}, bf16[256,256]{1,0:T(8,128)(2,1)S(1)}, u32[]{:S(2)}, u32[]{:S(2)}) collective-permute-start(bf16[256,256]{1,0:T(8,128)(2,1)S(1)} %get-tuple-element.110), channel_id=1, source_target_pairs={{0,31},{1,2},{2,1},{3,4},{4,3},{5,6},{6,5},{7,8},{8,7},{9,10},{10,... | collective-permute-start | bytes 393224 | tf_op jit(solution)/shard_map/ppermute | solution.py:241
  47.1 3.6 %collective-permute-start.11 = (bf16[256,256]{1,0:T(8,128)(2,1)S(1)}, bf16[256,256]{1,0:T(8,128)(2,1)S(1)}, u32[]{:S(2)}, u32[]{:S(2)}) collective-permute-start(bf16[256,256]{1,0:T(8,128)(2,1)S(1)} %get-tuple-element.109), channel_id=1, source_target_pairs={{0,1},{1,0},{2,3},{3,2},{4,5},{5,4},{6,7},{7,6},{8,9},{9,8},{10,11... | collective-permute-start | bytes 393224 | tf_op jit(solution)/shard_map/ppermute | solution.py:241
  48.5 7.8 %collective-permute-start.28 = (bf16[256,256]{1,0:T(8,128)(2,1)S(1)}, bf16[256,256]{1,0:T(8,128)(2,1)S(1)}, u32[]{:S(2)}, u32[]{:S(2)}) collective-permute-start(bf16[256,256]{1,0:T(8,128)(2,1)S(1)} %get-tuple-element.146), channel_id=1, source_target_pairs={{0,31},{1,2},{2,1},{3,4},{4,3},{5,6},{6,5},{7,8},{8,7},{9,10},{10,... | collective-permute-start | bytes 393224 | tf_op jit(solution)/shard_map/ppermute | solution.py:241
  50.1 6.2 %collective-permute-start.27 = (bf16[256,256]{1,0:T(8,128)(2,1)S(1)}, bf16[256,256]{1,0:T(8,128)(2,1)S(1)}, u32[]{:S(2)}, u32[]{:S(2)}) collective-permute-start(bf16[256,256]{1,0:T(8,128)(2,1)S(1)} %get-tuple-element.145), channel_id=1, source_target_pairs={{0,1},{1,0},{2,3},{3,2},{4,5},{5,4},{6,7},{7,6},{8,9},{9,8},{10,11... | collective-permute-start | bytes 393224 | tf_op jit(solution)/shard_map/ppermute | solution.py:241
  52.0 7.8 %collective-permute-start.14 = (bf16[256,256]{1,0:T(8,128)(2,1)S(1)}, bf16[256,256]{1,0:T(8,128)(2,1)S(1)}, u32[]{:S(2)}, u32[]{:S(2)}) collective-permute-start(bf16[256,256]{1,0:T(8,128)(2,1)S(1)} %get-tuple-element.114), channel_id=1, source_target_pairs={{0,31},{1,2},{2,1},{3,4},{4,3},{5,6},{6,5},{7,8},{8,7},{9,10},{10,... | collective-permute-start | bytes 393224 | tf_op jit(solution)/shard_map/ppermute | solution.py:241
  56.1 3.6 %collective-permute-start.13 = (bf16[256,256]{1,0:T(8,128)(2,1)S(1)}, bf16[256,256]{1,0:T(8,128)(2,1)S(1)}, u32[]{:S(2)}, u32[]{:S(2)}) collective-permute-start(bf16[256,256]{1,0:T(8,128)(2,1)S(1)} %get-tuple-element.113), channel_id=1, source_target_pairs={{0,1},{1,0},{2,3},{3,2},{4,5},{5,4},{6,7},{7,6},{8,9},{9,8},{10,11... | collective-permute-start | bytes 393224 | tf_op jit(solution)/shard_map/ppermute | solution.py:241
  57.5 7.8 %collective-permute-start.30 = (bf16[256,256]{1,0:T(8,128)(2,1)S(1)}, bf16[256,256]{1,0:T(8,128)(2,1)S(1)}, u32[]{:S(2)}, u32[]{:S(2)}) collective-permute-start(bf16[256,256]{1,0:T(8,128)(2,1)S(1)} %get-tuple-element.150), channel_id=1, source_target_pairs={{0,31},{1,2},{2,1},{3,4},{4,3},{5,6},{6,5},{7,8},{8,7},{9,10},{10,... | collective-permute-start | bytes 393224 | tf_op jit(solution)/shard_map/ppermute | solution.py:241
  59.1 6.2 %collective-permute-start.29 = (bf16[256,256]{1,0:T(8,128)(2,1)S(1)}, bf16[256,256]{1,0:T(8,128)(2,1)S(1)}, u32[]{:S(2)}, u32[]{:S(2)}) collective-permute-start(bf16[256,256]{1,0:T(8,128)(2,1)S(1)} %get-tuple-element.149), channel_id=1, source_target_pairs={{0,1},{1,0},{2,3},{3,2},{4,5},{5,4},{6,7},{7,6},{8,9},{9,8},{10,11... | collective-permute-start | bytes 393224 | tf_op jit(solution)/shard_map/ppermute | solution.py:241
  61.0 7.8 %collective-permute-start.16 = (bf16[256,256]{1,0:T(8,128)(2,1)S(1)}, bf16[256,256]{1,0:T(8,128)(2,1)S(1)}, u32[]{:S(2)}, u32[]{:S(2)}) collective-permute-start(bf16[256,256]{1,0:T(8,128)(2,1)S(1)} %get-tuple-element.118), channel_id=1, source_target_pairs={{0,31},{1,2},{2,1},{3,4},{4,3},{5,6},{6,5},{7,8},{8,7},{9,10},{10,... | collective-permute-start | bytes 393224 | tf_op jit(solution)/shard_map/ppermute | solution.py:241
  65.2 3.6 %collective-permute-start.15 = (bf16[256,256]{1,0:T(8,128)(2,1)S(1)}, bf16[256,256]{1,0:T(8,128)(2,1)S(1)}, u32[]{:S(2)}, u32[]{:S(2)}) collective-permute-start(bf16[256,256]{1,0:T(8,128)(2,1)S(1)} %get-tuple-element.117), channel_id=1, source_target_pairs={{0,1},{1,0},{2,3},{3,2},{4,5},{5,4},{6,7},{7,6},{8,9},{9,8},{10,11... | collective-permute-start | bytes 393224 | tf_op jit(solution)/shard_map/ppermute | solution.py:241
  66.5 8.2 %collective-permute-start.31 = (bf16[256,256]{1,0:T(8,128)(2,1)S(1)}, bf16[256,256]{1,0:T(8,128)(2,1)S(1)}, u32[]{:S(2)}, u32[]{:S(2)}) collective-permute-start(bf16[256,256]{1,0:T(8,128)(2,1)S(1)} %get-tuple-element.153), channel_id=1, source_target_pairs={{0,1},{1,0},{2,3},{3,2},{4,5},{5,4},{6,7},{7,6},{8,9},{9,8},{10,11... | collective-permute-start | bytes 393224 | tf_op jit(solution)/shard_map/ppermute | solution.py:241
  67.0 7.7 %collective-permute-start.32 = (bf16[256,256]{1,0:T(8,128)(2,1)S(1)}, bf16[256,256]{1,0:T(8,128)(2,1)S(1)}, u32[]{:S(2)}, u32[]{:S(2)}) collective-permute-start(bf16[256,256]{1,0:T(8,128)(2,1)S(1)} %get-tuple-element.154), channel_id=1, source_target_pairs={{0,31},{1,2},{2,1},{3,4},{4,3},{5,6},{6,5},{7,8},{8,7},{9,10},{10,... | collective-permute-start | bytes 393224 | tf_op jit(solution)/shard_map/ppermute | solution.py:241
  70.0 7.8 %collective-permute-start.18 = (bf16[256,256]{1,0:T(8,128)(2,1)S(1)}, bf16[256,256]{1,0:T(8,128)(2,1)S(1)}, u32[]{:S(2)}, u32[]{:S(2)}) collective-permute-start(bf16[256,256]{1,0:T(8,128)(2,1)S(1)} %get-tuple-element.122), channel_id=1, source_target_pairs={{0,31},{1,2},{2,1},{3,4},{4,3},{5,6},{6,5},{7,8},{8,7},{9,10},{10,... | collective-permute-start | bytes 393224 | tf_op jit(solution)/shard_map/ppermute | solution.py:241
  74.2 3.6 %collective-permute-start.17 = (bf16[256,256]{1,0:T(8,128)(2,1)S(1)}, bf16[256,256]{1,0:T(8,128)(2,1)S(1)}, u32[]{:S(2)}, u32[]{:S(2)}) collective-permute-start(bf16[256,256]{1,0:T(8,128)(2,1)S(1)} %get-tuple-element.121), channel_id=1, source_target_pairs={{0,1},{1,0},{2,3},{3,2},{4,5},{5,4},{6,7},{7,6},{8,9},{9,8},{10,11... | collective-permute-start | bytes 393224 | tf_op jit(solution)/shard_map/ppermute | solution.py:241
  76.0 7.8 %collective-permute-start.34 = (bf16[256,256]{1,0:T(8,128)(2,1)S(1)}, bf16[256,256]{1,0:T(8,128)(2,1)S(1)}, u32[]{:S(2)}, u32[]{:S(2)}) collective-permute-start(bf16[256,256]{1,0:T(8,128)(2,1)S(1)} %get-tuple-element.158), channel_id=1, source_target_pairs={{0,31},{1,2},{2,1},{3,4},{4,3},{5,6},{6,5},{7,8},{8,7},{9,10},{10,... | collective-permute-start | bytes 393224 | tf_op jit(solution)/shard_map/ppermute | solution.py:241
  79.1 7.8 %collective-permute-start.20 = (bf16[256,256]{1,0:T(8,128)(2,1)S(1)}, bf16[256,256]{1,0:T(8,128)(2,1)S(1)}, u32[]{:S(2)}, u32[]{:S(2)}) collective-permute-start(bf16[256,256]{1,0:T(8,128)(2,1)S(1)} %get-tuple-element.126), channel_id=1, source_target_pairs={{0,31},{1,2},{2,1},{3,4},{4,3},{5,6},{6,5},{7,8},{8,7},{9,10},{10,... | collective-permute-start | bytes 393224 | tf_op jit(solution)/shard_map/ppermute | solution.py:241
  83.3 3.6 %collective-permute-start.33 = (bf16[256,256]{1,0:T(8,128)(2,1)S(1)}, bf16[256,256]{1,0:T(8,128)(2,1)S(1)}, u32[]{:S(2)}, u32[]{:S(2)}) collective-permute-start(bf16[256,256]{1,0:T(8,128)(2,1)S(1)} %get-tuple-element.157), channel_id=1, source_target_pairs={{0,1},{1,0},{2,3},{3,2},{4,5},{5,4},{6,7},{7,6},{8,9},{9,8},{10,11... | collective-permute-start | bytes 393224 | tf_op jit(solution)/shard_map/ppermute | solution.py:241
  83.3 4.3 %collective-permute-start.19 = (bf16[256,256]{1,0:T(8,128)(2,1)S(1)}, bf16[256,256]{1,0:T(8,128)(2,1)S(1)}, u32[]{:S(2)}, u32[]{:S(2)}) collective-permute-start(bf16[256,256]{1,0:T(8,128)(2,1)S(1)} %get-tuple-element.125), channel_id=1, source_target_pairs={{0,1},{1,0},{2,3},{3,2},{4,5},{5,4},{6,7},{7,6},{8,9},{9,8},{10,11... | collective-permute-start | bytes 393224 | tf_op jit(solution)/shard_map/ppermute | solution.py:241
